TPU v7x, 128 devices: a whole 4x4x4 slice. The times are simulated.
128 devices in a mesh: row: 16 (over y, x_lo, core), col: 8 (over x_hi, z).
Axes of the slice: x: 4 (x_hi: 2, x_lo: 2; x = x_hi * 2 + x_lo), y: 4, z: 4, core: 2. Of those that a mesh axis runs over, the one named last changes fastest.
Arguments:
- tiles: bfloat16 [2, 32768, 16384], P(None, 'row', 'col'), may hold values from -0.046875 to 0.046875
- probe: bfloat16 [2, 32768, 256], P(None, ('row', 'col')), may hold values from -6 to 6
- cluster_perm: int32 [2, 16, 2048], P(None, 'row'), may hold values from 0 to 2047, each once within a row
- tile_keep: int32 [2, 16, 8], P(None, 'row', 'col'), may hold values 0 or 1
Outputs:
- samples: float32 [2, 32768, 256], P(None, ('row', 'col'))
- leaf_basis: float32 [2, 32768, 256], P(None, ('row', 'col'))
Inputs may be any that keep to these rules, and one draw needn't show every extreme that they name: Each row of cluster_perm is a permutation. `tile_keep`: entries with c = 0 are not read.
All inputs are finite; a program needn't handle non-finite values. No bound on the sum of `tile_keep` on one device may be relied on, other than what follows from the above.
Results may differ from a plain program's by a relative error of at most 0.0003.
Values may be sent and summed in bfloat16 or wider, within the bound.
No kernel may reach another device: no remote copies, remote signals or barrier semaphores. Data moves between devices by JAX's collectives and lax.ppermute only.
A program may use at most 128 MiB of HBM per device.

v0:
```python
import functools

import jax
import jax.numpy as jnp
from jax import lax
from jax.experimental import pallas as pl
from jax.experimental.pallas import tpu as pltpu
from jax.sharding import PartitionSpec as P


AXES = ("row", "col")
EXACT = lax.Precision.HIGHEST
LEVELS = 32767.0
EXTRA = 16


def sent(value, to):
    nrows, ncols = lax.axis_size("row"), lax.axis_size("col")
    pairs = []
    for r in range(nrows):
        for c in range(ncols):
            r_to, c_to = to(r, c)
            pairs.append((r * ncols + c, (r_to % nrows) * ncols + c_to))
    return lax.ppermute(value, AXES, pairs)


def scale_of(exponent, mantissa):
    return jnp.exp2(exponent) * (mantissa * (1.0 / (LEVELS * LEVELS)))


def coded(block):
    largest = jnp.maximum(jnp.max(jnp.abs(block), axis=0, keepdims=True), 1e-30)
    exponent = jnp.floor(jnp.log2(largest * 1.0001)) + 1.0
    mantissa = jnp.ceil(largest * jnp.exp2(-exponent) * LEVELS)
    scale = scale_of(exponent, mantissa)
    values = jnp.clip(jnp.round(block * (1.0 / scale)), -LEVELS, LEVELS)
    at = lax.broadcasted_iota(jnp.int32, (EXTRA, block.shape[1]), 0)
    tail = jnp.where(at == 0, exponent, mantissa)
    return jnp.concatenate([values, tail], axis=0).astype(jnp.int32).astype(jnp.int16)


def decoded(code):
    wide = code.astype(jnp.int32).astype(jnp.float32)
    rows = code.shape[0] - EXTRA
    return wide[:rows] * scale_of(wide[rows : rows + 1], wide[rows + 1 : rows + 2])


def product_kernel(back, part, ids_ref, weight_ref, perm_ref, *refs):
    *pair_refs, plane_ref, cross_ref, tiles_ref = refs[:7]
    *out_refs, tile_ref, raw_ref, omega_ref, sems = refs[7:]
    nz, points, _ = plane_ref.shape
    length = raw_ref.shape[1]
    step = 512
    k = ids_ref[3] ^ ids_ref[2] ^ part
    tile_slot = k if back else k ^ ids_ref[2]

    def piece_copy(q):
        rows = pl.ds(q * step, step)
        return pltpu.make_async_copy(tiles_ref.at[tile_slot, rows], tile_ref.at[rows], sems.at[q])

    for q in range(length // step):
        piece_copy(q).start()
    for slot in range(2):

        @pl.when(k == slot)
        def _(slot=slot):
            for d in range(nz):
                for a in range(2):
                    piece = (cross_ref[d] if a else plane_ref[d]) if slot else pair_refs[d][a]
                    at = (nz * a + d) * points
                    raw_ref[:, at : at + points] = piece.T

    def order_step(i, carry):
        at = pl.multiple_of(i * step, step)
        index = perm_ref[k, :, pl.ds(at, step)] ^ (ids_ref[0] * points)
        place = lax.broadcasted_iota(jnp.int32, (length, step), 0)
        chosen = jnp.where(place == index, 1.0, 0.0).astype(jnp.bfloat16)
        found = jnp.dot(raw_ref[...], chosen, preferred_element_type=jnp.float32)
        if back:
            omega_ref[:, pl.ds(at, step)] = found.astype(jnp.bfloat16)
        else:
            omega_ref[pl.ds(at, step), :] = found.T.astype(jnp.bfloat16)
        return carry

    lax.fori_loop(0, length // step, order_step, 0)
    for q in range(length // step):
        piece_copy(q).wait()
    weight = weight_ref[tile_slot]
    for d in range(nz):
        for a in range(2):
            at = pl.multiple_of((a * nz + (ids_ref[1] ^ d)) * points, points)
            if back:
                value = jnp.dot(omega_ref[...], tile_ref[:, pl.ds(at, points)], preferred_element_type=jnp.float32).T
            else:
                value = jnp.dot(tile_ref[pl.ds(at, points), :], omega_ref[...], preferred_element_type=jnp.float32)
            code = coded(value * weight)
            if len(out_refs) == 1:
                out_refs[0][d, a] = code
            else:
                out_refs[d][a] = code


def products(ids, weight, perm, pairs, plane, cross, tiles, back, part):
    nz, points, probes = plane.shape
    length = tiles.shape[1]
    block = (2, points + EXTRA, probes)
    shapes = [(nz, *block)] if back and part else [block] * nz
    smem, vmem = pl.BlockSpec(memory_space=pltpu.SMEM), pl.BlockSpec(memory_space=pltpu.VMEM)
    return pl.pallas_call(
        functools.partial(product_kernel, back, part),
        out_shape=[jax.ShapeDtypeStruct(shape, jnp.int16) for shape in shapes],
        in_specs=[smem, smem] + [vmem] * (3 + nz) + [pl.BlockSpec(memory_space=pl.ANY)],
        out_specs=[vmem] * len(shapes),
        scratch_shapes=[
            pltpu.VMEM(tiles.shape[1:], jnp.bfloat16),
            pltpu.VMEM((probes, length), jnp.bfloat16),
            pltpu.VMEM((probes, length) if back else (length, probes), jnp.bfloat16),
            pltpu.SemaphoreType.DMA((length // 512,)),
        ],
        compiler_params=pltpu.CompilerParams(vmem_limit_bytes=32 << 20),
        cost_estimate=pl.CostEstimate(flops=4 * length * length * probes, bytes_accessed=11 << 20, transcendentals=0),
    )(ids, weight, perm, *pairs, plane, cross, tiles)


def sum_kernel(*refs):
    *in_refs, unread_ref, out_ref = refs
    for a in range(2):
        total = decoded(in_refs[0][a])
        for ref in in_refs[1:]:
            total = total + decoded(ref[a])
        out_ref[a] = coded(total)


def summed(codes, after):
    return pl.pallas_call(
        sum_kernel,
        in_specs=[pl.BlockSpec(memory_space=pltpu.VMEM)] * len(codes) + [pl.BlockSpec(memory_space=pl.ANY)],
        out_shape=jax.ShapeDtypeStruct(codes[0].shape, jnp.int16),
        name="sum_back",
    )(*codes, after)


def join_kernel(nz, *refs):
    more_ref = refs[nz]
    for d in range(nz):
        for a in range(2):
            refs[nz + 1 + d][a] = coded(decoded(refs[d][a]) + decoded(more_ref[d, a]))


def joined(codes, more):
    return pl.pallas_call(
        functools.partial(join_kernel, len(codes)),
        out_shape=[jax.ShapeDtypeStruct(x.shape, jnp.int16) for x in codes],
        name="join",
    )(*codes, more)


def gram_kernel(ids_ref, *refs):
    *in_refs, samples_ref, other_ref, gram_ref = refs
    plane = ids_ref[3]
    half = gram_ref.shape[1]
    total = None
    for a in (plane, 1 - plane):
        block = decoded(in_refs[0][a])
        for ref in in_refs[1:]:
            block = block + decoded(ref[a])
        if total is None:
            samples_ref[plane] = block
        else:
            other_ref[...] = block
        left, right = block[:, :half], block[:, half:]
        parts = [
            lax.dot_general(x, y, (((0,), (0,)), ((), ())), preferred_element_type=jnp.float32, precision=EXACT)
            for x, y in ((left, left), (left, right), (right, right))
        ]
        total = parts if total is None else [x + y for x, y in zip(total, parts)]
    for n, part in enumerate(total):
        gram_ref[n * half : (n + 1) * half, :] = part


def gram_of(ids, codes):
    _, rows, probes = codes[0].shape
    points = rows - EXTRA
    return pl.pallas_call(
        gram_kernel,
        in_specs=[pl.BlockSpec(memory_space=pltpu.SMEM)] + [pl.BlockSpec(memory_space=pltpu.VMEM)] * len(codes),
        out_shape=[
            jax.ShapeDtypeStruct((2, points, probes), jnp.float32),
            jax.ShapeDtypeStruct((points, probes), jnp.float32),
            jax.ShapeDtypeStruct((3 * probes // 2, probes // 2), jnp.float32),
        ],
        name="gram",
    )(ids, *codes)


def half_inverse(a_ref, out_ref, m_ref, tall_ref, u_ref, v_ref):
    n, size = a_ref.shape[0], u_ref.shape[0]
    rows = lax.broadcasted_iota(jnp.int32, (n, n), 0)
    cols = lax.broadcasted_iota(jnp.int32, (n, n), 1)
    m_ref[...] = (rows == cols).astype(jnp.float32)
    for ref in (tall_ref, u_ref, v_ref):
        ref[...] = jnp.zeros_like(ref)
    lane = lax.broadcasted_iota(jnp.int32, (size, n), 1)
    sub = lax.broadcasted_iota(jnp.int32, (size, n), 0)

    def spread(array, i):
        return jnp.broadcast_to(array[i : i + 1, :], (size, n))

    def group(b, carry):
        at = pl.multiple_of(b * size, size)
        u, v, near = u_ref[...], v_ref[...], tall_ref[pl.ds(at, size), :]
        panel, inverse = a_ref[pl.ds(at, size), :], m_ref[pl.ds(at, size), :]
        old_a, old_m, tall = a_ref[...], m_ref[...], tall_ref[...]
        for t in range(size):
            factor = jnp.broadcast_to(near[:, t : t + 1], (size, n))
            panel = panel - factor * u[t : t + 1, :]
            inverse = inverse - factor * v[t : t + 1, :]
        small = pltpu.roll(panel, n - at, axis=1)
        s = [[None] * size for _ in range(size)]
        e = [[None] * size for _ in range(size)]
        for t in range(size):
            column = jnp.broadcast_to(small[:, t : t + 1], (size, n))
            for i in range(t, size):
                s[i][t] = spread(column, i)
        for t in range(size - 1):
            ratio = 1.0 / s[t][t]
            for i in range(t + 1, size):
                factor = s[i][t] * ratio
                for j in range(t + 1, i + 1):
                    s[i][j] = s[i][j] - factor * s[j][t]
                for j in range(t):
                    e[i][j] = e[i][j] - factor * e[t][j]
                e[i][t] = -factor
        scale = s[0][0]
        for t in range(1, size):
            scale = jnp.where(sub == t, s[t][t], scale)
        scale = lax.rsqrt(scale)
        new_u, new_v = panel, inverse
        for t in range(size - 1):
            factor = jnp.zeros((size, n), jnp.float32)
            for i in range(t + 1, size):
                factor = jnp.where(sub == i, e[i][t], factor)
            new_u = new_u + factor * panel[t : t + 1, :]
            new_v = new_v + factor * inverse[t : t + 1, :]
        new_u = jnp.where(lane >= at + sub, new_u * scale, 0.0)
        new_v = new_v * scale
        for t in range(size):
            factor = jnp.broadcast_to(tall[:, t : t + 1], (n, n))
            old_a = old_a - factor * u[t : t + 1, :]
            old_m = old_m - factor * v[t : t + 1, :]
        a_ref[...], m_ref[...] = old_a, old_m
        out_ref[pl.ds(at, size), :] = new_v
        u_ref[...], v_ref[...] = new_u, new_v
        tall_ref[...] = new_u.T
        return carry

    lax.fori_loop(0, n // size, group, 0)


def factor_kernel(scale, ids_ref, samples_ref, other_ref, *refs):
    *gram_refs, basis_ref, out_ref, a_ref, m1_ref, m2_ref = refs[:9]
    work = refs[9:]
    half = a_ref.shape[0]
    plane = ids_ref[3]

    def product(a, b, over):
        return lax.dot_general(
            a, b, ((over[:1], over[1:]), ((), ())), preferred_element_type=jnp.float32, precision=EXACT
        )

    def gram(n):
        rows = slice(n * half, (n + 1) * half)
        one, two, three, four = (ref[rows, :] for ref in gram_refs)
        return ((one + two) + (three + four)) * scale

    a_ref[...] = gram(0)
    half_inverse(a_ref, m1_ref, *work)
    first = m1_ref[...]
    cross = product(first, gram(1), (1, 0))
    a_ref[...] = gram(2) - product(cross, cross, (0, 0))
    half_inverse(a_ref, m2_ref, *work)
    second = m2_ref[...]
    mixed = -product(second, product(cross, first, (0, 0)), (1, 0))
    for n, block in enumerate((samples_ref[plane], other_ref[...])):
        left, right = block[:, :half], block[:, half:]
        made = (product(left, first, (1, 1)), product(left, mixed, (1, 1)) + product(right, second, (1, 1)))
        for m, value in enumerate(made):
            columns = slice(m * half, (m + 1) * half)
            if n:
                out_ref[:, columns] = value
            else:
                basis_ref[plane, :, columns] = value


def orthogonal(ids, samples, other, grams, scale):
    half = grams[0].shape[1]
    return pl.pallas_call(
        functools.partial(factor_kernel, scale),
        in_specs=[pl.BlockSpec(memory_space=pltpu.SMEM)] + [pl.BlockSpec(memory_space=pltpu.VMEM)] * (2 + len(grams)),
        out_shape=[jax.ShapeDtypeStruct(x.shape, jnp.float32) for x in (samples, other)],
        scratch_shapes=[
            pltpu.VMEM(shape, jnp.float32) for shape in [(half, half)] * 4 + [(half, 8), (8, half), (8, half)]
        ],
        name="orthogonal",
    )(ids, samples, other, *grams)


def whole_step(tiles, probe, cluster_perm, tile_keep):
    row_id = lax.axis_index("row")
    col_id = lax.axis_index("col")
    nrows = lax.axis_size("row")
    ncols = lax.axis_size("col")
    tile_len = tiles.shape[1]
    nz = ncols // 2
    plane, depth = col_id // nz, col_id % nz
    wraps = (row_id + col_id >= nrows).astype(jnp.int32)
    ids = jnp.stack([col_id, depth, wraps, plane]).astype(jnp.int32)
    weight = jnp.where(col_id == 0, 0.5, tile_keep[:, 0, 0].astype(jnp.float32))

    def same(d):
        return lambda r, c: (r, c ^ d)

    def slanted(d):
        return lambda r, c: (r + c - (c ^ d), c ^ d)

    def far(r, c):
        return (r - c, c)

    depths = range(1, nz)
    other = sent(probe[0], same(nz))
    singles = [sent(probe[1], same(d)) for d in depths]
    pair = jnp.stack([probe[0], other])
    line = jnp.stack([probe[1], *singles])
    pairs = [sent(pair, same(d)) for d in depths]
    cross = sent(line, same(nz))

    far_pair = sent(pair, far)
    far_line = sent(line, far)
    far_perm = sent(cluster_perm, far)
    far_pairs = [sent(far_pair, slanted(d)) for d in depths]
    far_cross = sent(cross, far)

    perm, far_perm = (x.reshape(-1, 1, tile_len) for x in (cluster_perm, far_perm))
    own_blocks = ([pair, *pairs], line, cross)
    far_blocks = ([far_pair, *far_pairs], far_line, far_cross)

    def home(r, c):
        return (r + c, c)

    (more,) = products(ids, weight, perm, *own_blocks, tiles, True, 1)
    more = sent(more, home)
    back = products(ids, weight, perm, *own_blocks, tiles, True, 0)
    back, far_pairs = lax.optimization_barrier((back, far_pairs))
    back = [back[0]] + [sent(back[d], slanted(d)) for d in depths]
    kept = products(ids, weight, far_perm, *far_blocks, tiles, False, 0)
    kept = [kept[0]] + [sent(kept[d], same(d)) for d in depths]
    given = products(ids, weight, far_perm, *far_blocks, tiles, False, 1)
    arrived = sent(summed(back, given[0]), home)
    given = [sent(code, same(nz + d)) for d, code in enumerate(joined(given, more))]
    samples, swapped, gram = gram_of(ids, [*kept, *given, arrived])
    grams = [gram] + [sent(gram, same(d)) for d in depths]
    basis, swapped_basis = orthogonal(ids, samples, swapped, grams, 1.0 / tile_len)

    def placed(array, theirs):
        return lax.dynamic_update_index_in_dim(array, sent(theirs, same(nz)), 1 - plane, 0)

    return (placed(samples, swapped), placed(basis, swapped_basis))


def solution(mesh):
    whole = P(None, ("row", "col"), None)
    return jax.shard_map(
        whole_step,
        mesh=mesh,
        in_specs=(P(None, "row", "col"), whole, P(None, "row", None), P(None, "row", "col")),
        out_specs=(whole, whole),
        check_vma=False,
    )
```

profile of v0, /device:TPU:0, one launch (start us, length us, event | category | flops | bytes accessed | tf_op | source)
XLA Modules:
  0.0 208.6 jit_solution(10572871790654336834)
XLA Ops:
  0.7 1.0 fusion.1
  1.7 4.2 %collective-permute-start.8 = (bf16[256,256]{1,0:T(8,128)(2,1)S(1)}, bf16[256,256]{1,0:T(8,128)(2,1)S(1)}, u32[]{:S(2)}, u32[]{:S(2)}) collective-permute-start(bf16[256,256]{1,0:T(8,128)(2,1)S(1)} %get-tuple-element.54), channel_id=1, source_target_pairs={{0,3},{1,2},{2,1},{3,0},{4,7},{5,6},{6,5},{7,4},{8,11},{9,10},{10,... | collective-permute-start | bytes 393224 | tf_op jit(solution)/shard_map/ppermute | solution.py:24
  5.9 0.9 collective-permute-start.6
  6.8 3.0 %collective-permute-start.1 = (bf16[256,256]{1,0:T(8,128)(2,1)S(1)}, bf16[256,256]{1,0:T(8,128)(2,1)S(1)}, u32[]{:S(2)}, u32[]{:S(2)}) collective-permute-start(bf16[256,256]{1,0:T(8,128)(2,1)S(1)} %get-tuple-element.53), channel_id=1, source_target_pairs={{0,4},{1,5},{2,6},{3,7},{4,0},{5,1},{6,2},{7,3},{8,12},{9,13},{10,... | collective-permute-start | bytes 393224 | tf_op jit(solution)/shard_map/ppermute | solution.py:24
  9.9 1.6 collective-permute-done.8
  11.5 2.3 %collective-permute-done.7 = bf16[256,256]{1,0:T(8,128)(2,1)S(1)} collective-permute-done((bf16[256,256]{1,0:T(8,128)(2,1)S(1)}, bf16[256,256]{1,0:T(8,128)(2,1)S(1)}, u32[]{:S(2)}, u32[]{:S(2)}) %collective-permute-start.7) | collective-permute-done | bytes 131104 | tf_op jit(solution)/shard_map/ppermute | solution.py:24
  13.8 0.1 pad_maximum_fusion.refs_4_
  13.8 3.1 %collective-permute-start.10 = (bf16[4,256,256]{2,1,0:T(8,128)(2,1)S(1)}, bf16[4,256,256]{2,1,0:T(8,128)(2,1)S(1)}, u32[]{:S(2)}, u32[]{:S(2)}) collective-permute-start(bf16[4,256,256]{2,1,0:T(8,128)(2,1)S(1)} %pad_maximum_fusion.refs_4_), channel_id=1, source_target_pairs={{0,4},{1,5},{2,6},{3,7},{4,0},{5,1},{6,2},{7,3},{8,12},{9,13},{10,... | collective-permute-start | bytes 1572872 | tf_op jit(solution)/shard_map/ppermute | solution.py:24
  17.0 2.0 collective-permute-start.17
  19.0 0.3 collective-permute-start.16
  19.3 1.8 collective-permute-start.15
  21.1 0.7 collective-permute-start.2
  21.8 0.1 pad_add_fusion.ids_ref
  21.9 8.1 %collective-permute-done.17.refs_3_ = bf16[2,256,256]{2,1,0:T(8,128)(2,1)S(1)} collective-permute-done((bf16[2,256,256]{2,1,0:T(8,128)(2,1)S(1)}, bf16[2,256,256]{2,1,0:T(8,128)(2,1)S(1)}, u32[]{:S(2)}, u32[]{:S(2)}) %collective-permute-start.17) | collective-permute-done | bytes 262176 | tf_op jit(solution)/shard_map/ppermute | solution.py:24
  30.0 0.7 collective-permute-start
  30.7 0.7 collective-permute-start.9
  31.4 8.3 %collective-permute-start.5 = (bf16[2,256,256]{2,1,0:T(8,128)(2,1)S(1)}, bf16[2,256,256]{2,1,0:T(8,128)(2,1)S(1)}, u32[]{:S(2)}, u32[]{:S(2)}) collective-permute-start(bf16[2,256,256]{2,1,0:T(8,128)(2,1)S(1)} %collective-permute-done.2.refs_0_), channel_id=1, source_target_pairs={{0,107},{1,122},{2,9},{3,24},{4,111},{5,126},{6,13},{7,28},{8,115}... | collective-permute-start | bytes 786440 | tf_op jit(solution)/shard_map/ppermute | solution.py:24
  39.7 0.7 collective-permute-start.11
  40.4 0.0 copy-start
  40.4 5.8 %copy-done = bf16[2,2048,2048]{2,1,0:T(8,128)(2,1)S(1)} copy-done((bf16[2,2048,2048]{2,1,0:T(8,128)(2,1)S(1)}, bf16[2,2048,2048]{2,1,0:T(8,128)(2,1)}, u32[]{:S(2)}) %copy-start) | copy-done | bytes 16777240
  46.2 7.2 %shard_map.61 = s16[4,2,272,256]{3,2,1,0:T(8,128)(2,1)S(1)} custom-call(s32[4]{0:T(128)S(1)} %pad_add_fusion.ids_ref, f32[2]{0:T(128)S(1)} %fusion.weight_ref, s32[2,1,2048]{2,1,0:T(1,128)S(1)} %copy-done.8, bf16[2,256,256]{2,1,0:T(8,128)(2,1)S(1)} %pad_maximum_fusion.1.refs_0_, bf16[2,256,256]{2,1,0:T(8,128)(2,1)S(1)} %collective-permute-done.15.refs_1_, ...), custom_call_target="tpu_custom_call" | custom-call | flops 4294967296 | bytes 11534336 | tf_op jit(solution)/shard_map/pallas_call | solution.py:109
  53.4 3.7 %collective-permute-start.3 = (bf16[2,256,256]{2,1,0:T(8,128)(2,1)S(1)}, bf16[2,256,256]{2,1,0:T(8,128)(2,1)S(1)}, u32[]{:S(2)}, u32[]{:S(2)}) collective-permute-start(bf16[2,256,256]{2,1,0:T(8,128)(2,1)S(1)} %collective-permute-done.2.refs_0_), channel_id=1, source_target_pairs={{0,121},{1,8},{2,123},{3,10},{4,125},{5,12},{6,127},{7,14},{8,1},{... | collective-permute-start | bytes 786440 | tf_op jit(solution)/shard_map/ppermute | solution.py:24
  57.1 0.6 collective-permute-done.4.refs_2_
  57.7 1.7 collective-permute-start.18
  59.4 7.2 %shard_map.62 = (s16[2,272,256]{2,1,0:T(8,128)(2,1)S(1)}, s16[2,272,256]{2,1,0:T(8,128)(2,1)S(1)}, s16[2,272,256]{2,1,0:T(8,128)(2,1)S(1)}, s16[2,272,256]{2,1,0:T(8,128)(2,1)S(1)}) custom-call(s32[4]{0:T(128)S(1)} %pad_add_fusion.ids_ref, f32[2]{0:T(128)S(1)} %fusion.weight_ref, s32[2,1,2048]{2,1,0:T(1,128)S(1)} %copy-done.8, ...), custom_call_target="tpu_custom_call" | custom-call | flops 4294967296 | bytes 11534336 | tf_op jit(solution)/shard_map/pallas_call | solution.py:109
  66.6 0.7 copy-done.3
  67.3 3.1 %collective-permute-start.23 = (s16[2,272,256]{2,1,0:T(8,128)(2,1)S(1)}, s16[2,272,256]{2,1,0:T(8,128)(2,1)S(1)}, u32[]{:S(2)}, u32[]{:S(2)}) collective-permute-start(s16[2,272,256]{2,1,0:T(8,128)(2,1)S(1)} %get-tuple-element.44), channel_id=1, source_target_pairs={{0,121},{1,8},{2,123},{3,10},{4,125},{5,12},{6,127},{7,14},{8,1},{... | collective-permute-start | bytes 835592 | tf_op jit(solution)/shard_map/ppermute | solution.py:24
  70.4 7.1 %collective-permute-start.24 = (s16[2,272,256]{2,1,0:T(8,128)(2,1)S(1)}, s16[2,272,256]{2,1,0:T(8,128)(2,1)S(1)}, u32[]{:S(2)}, u32[]{:S(2)}) collective-permute-start(s16[2,272,256]{2,1,0:T(8,128)(2,1)S(1)} %get-tuple-element.45), channel_id=1, source_target_pairs={{0,114},{1,115},{2,16},{3,17},{4,118},{5,119},{6,20},{7,21},{8,122... | collective-permute-start | bytes 835592 | tf_op jit(solution)/shard_map/ppermute | solution.py:24
  77.5 0.0 copy-start.1
  77.5 5.8 %copy-done.1 = bf16[2,2048,2048]{2,1,0:T(8,128)(2,1)S(1)} copy-done((bf16[2,2048,2048]{2,1,0:T(8,128)(2,1)S(1)}, bf16[2,2048,2048]{2,1,0:T(8,128)(2,1)}, u32[]{:S(2)}) %copy-start.1) | copy-done | bytes 16777240
  83.3 7.5 %shard_map.59 = (s16[2,272,256]{2,1,0:T(8,128)(2,1)S(1)}, s16[2,272,256]{2,1,0:T(8,128)(2,1)S(1)}, s16[2,272,256]{2,1,0:T(8,128)(2,1)S(1)}, s16[2,272,256]{2,1,0:T(8,128)(2,1)S(1)}) custom-call(s32[4]{0:T(128)S(1)} %pad_add_fusion.ids_ref, f32[2]{0:T(128)S(1)} %fusion.weight_ref, s32[2,1,2048]{2,1,0:T(1,128)S(1)} %collective-permute-done.perm_ref, ...), custom_call_target="tpu_custom_call" | custom-call | flops 4294967296 | bytes 11534336 | tf_op jit(solution)/shard_map/pallas_call | solution.py:109
  90.8 0.0 copy-start.7
  90.8 0.7 copy-done.7
  91.5 10.2 %collective-permute-start.13 = (s16[2,272,256]{2,1,0:T(8,128)(2,1)S(1)}, s16[2,272,256]{2,1,0:T(8,128)(2,1)S(1)}, u32[]{:S(2)}, u32[]{:S(2)}) collective-permute-start(s16[2,272,256]{2,1,0:T(8,128)(2,1)S(1)} %get-tuple-element.29), channel_id=1, source_target_pairs={{0,2},{1,3},{2,0},{3,1},{4,6},{5,7},{6,4},{7,5},{8,10},{9,11},{10,... | collective-permute-start | bytes 835592 | tf_op jit(solution)/shard_map/ppermute | solution.py:24
  101.7 7.7 %collective-permute-done.24.refs_2_ = s16[2,272,256]{2,1,0:T(8,128)(2,1)S(1)} collective-permute-done((s16[2,272,256]{2,1,0:T(8,128)(2,1)S(1)}, s16[2,272,256]{2,1,0:T(8,128)(2,1)S(1)}, u32[]{:S(2)}, u32[]{:S(2)}) %collective-permute-start.24) | collective-permute-done | bytes 278560 | tf_op jit(solution)/shard_map/ppermute | solution.py:24
  109.4 7.3 %shard_map.60 = (s16[2,272,256]{2,1,0:T(8,128)(2,1)S(1)}, s16[2,272,256]{2,1,0:T(8,128)(2,1)S(1)}, s16[2,272,256]{2,1,0:T(8,128)(2,1)S(1)}, s16[2,272,256]{2,1,0:T(8,128)(2,1)S(1)}) custom-call(s32[4]{0:T(128)S(1)} %pad_add_fusion.ids_ref, f32[2]{0:T(128)S(1)} %fusion.weight_ref, s32[2,1,2048]{2,1,0:T(1,128)S(1)} %collective-permute-done.perm_ref, ...), custom_call_target="tpu_custom_call" | custom-call | flops 4294967296 | bytes 11534336 | tf_op jit(solution)/shard_map/pallas_call | solution.py:109
  116.8 0.7 copy-done.2
  117.5 0.7 copy-done.4
  118.2 0.7 copy-done.5
  118.9 0.7 copy-done.6
  119.6 0.7 copy-done.14
  120.3 2.3 %sum_back.1 = s16[2,272,256]{2,1,0:T(8,128)(2,1)} custom-call(s16[2,272,256]{2,1,0:T(8,128)(2,1)} %copy-done.3, s16[2,272,256]{2,1,0:T(8,128)(2,1)} %copy-done.12, s16[2,272,256]{2,1,0:T(8,128)(2,1)} %copy-done.13, s16[2,272,256]{2,1,0:T(8,128)(2,1)} %copy-done.14, s16[2,272,256]{2,1,0:T(8,128)(2,1)} %copy-done.2), custom_call_target="tpu_custom_call" | custom-call | tf_op jit(solution)/shard_map/sum_back/pallas_call | solution.py:135
  122.6 1.6 collective-permute-start.26
  124.2 3.2 %join.1 = (s16[2,272,256]{2,1,0:T(8,128)(2,1)}, s16[2,272,256]{2,1,0:T(8,128)(2,1)}, s16[2,272,256]{2,1,0:T(8,128)(2,1)}, s16[2,272,256]{2,1,0:T(8,128)(2,1)}) custom-call(s16[2,272,256]{2,1,0:T(8,128)(2,1)} %copy-done.2, s16[2,272,256]{2,1,0:T(8,128)(2,1)} %copy-done.4, s16[2,272,256]{2,1,0:T(8,128)(2,1)} %copy-done.5, s16[2,272,256]{2,1,0:T(8,128)(2,1)} %copy-done.6, ...), custom_call_target="tpu_custom_call" | custom-call | tf_op jit(solution)/shard_map/join/pallas_call | solution.py:151
  127.4 1.0 collective-permute-start.19
  128.4 6.5 %collective-permute-start.21 = (s16[2,272,256]{2,1,0:T(8,128)(2,1)}, s16[2,272,256]{2,1,0:T(8,128)(2,1)S(1)}, u32[]{:S(2)}, u32[]{:S(2)}) collective-permute-start(s16[2,272,256]{2,1,0:T(8,128)(2,1)} %get-tuple-element.37), channel_id=1, source_target_pairs={{0,6},{1,7},{2,4},{3,5},{4,2},{5,3},{6,0},{7,1},{8,14},{9,15},{10,... | collective-permute-start | bytes 835592 | tf_op jit(solution)/shard_map/ppermute | solution.py:24
  134.9 2.6 %collective-permute-start.22 = (s16[2,272,256]{2,1,0:T(8,128)(2,1)}, s16[2,272,256]{2,1,0:T(8,128)(2,1)S(1)}, u32[]{:S(2)}, u32[]{:S(2)}) collective-permute-start(s16[2,272,256]{2,1,0:T(8,128)(2,1)} %get-tuple-element.38), channel_id=1, source_target_pairs={{0,7},{1,6},{2,5},{3,4},{4,3},{5,2},{6,1},{7,0},{8,15},{9,14},{10,... | collective-permute-start | bytes 835592 | tf_op jit(solution)/shard_map/ppermute | solution.py:24
  137.5 3.0 %collective-permute-done.20.refs_5_ = s16[2,272,256]{2,1,0:T(8,128)(2,1)S(1)} collective-permute-done((s16[2,272,256]{2,1,0:T(8,128)(2,1)}, s16[2,272,256]{2,1,0:T(8,128)(2,1)S(1)}, u32[]{:S(2)}, u32[]{:S(2)}) %collective-permute-start.20) | collective-permute-done | bytes 278560 | tf_op jit(solution)/shard_map/ppermute | solution.py:24
  140.5 8.1 %collective-permute-done.21.refs_6_ = s16[2,272,256]{2,1,0:T(8,128)(2,1)S(1)} collective-permute-done((s16[2,272,256]{2,1,0:T(8,128)(2,1)}, s16[2,272,256]{2,1,0:T(8,128)(2,1)S(1)}, u32[]{:S(2)}, u32[]{:S(2)}) %collective-permute-start.21) | collective-permute-done | bytes 278560 | tf_op jit(solution)/shard_map/ppermute | solution.py:24
  148.6 10.1 %collective-permute-done.22.refs_7_ = s16[2,272,256]{2,1,0:T(8,128)(2,1)S(1)} collective-permute-done((s16[2,272,256]{2,1,0:T(8,128)(2,1)}, s16[2,272,256]{2,1,0:T(8,128)(2,1)S(1)}, u32[]{:S(2)}, u32[]{:S(2)}) %collective-permute-start.22) | collective-permute-done | bytes 278560 | tf_op jit(solution)/shard_map/ppermute | solution.py:24
  158.7 0.7 copy-done.21
  159.4 3.7 %gram.1 = (f32[2,256,256]{2,1,0:T(8,128)}, f32[256,256]{1,0:T(8,128)}, f32[384,128]{1,0:T(8,128)}) custom-call(s32[4]{0:T(128)} %copy-done.9, s16[2,272,256]{2,1,0:T(8,128)(2,1)} %copy-done.7, s16[2,272,256]{2,1,0:T(8,128)(2,1)} %copy-done.15, s16[2,272,256]{2,1,0:T(8,128)(2,1)} %copy-done.16, s16[2,272,256]{2,1,0:T(8,128)(2,1)} %collective-permute-done.14.refs_3_, ...), custom_call_target="tpu_custom_call" | custom-call | tf_op jit(solution)/shard_map/gram/pallas_call | solution.py:184
  163.1 3.1 %collective-permute-start.27 = (f32[256,256]{1,0:T(8,128)}, f32[256,256]{1,0:T(8,128)S(1)}, u32[]{:S(2)}, u32[]{:S(2)}) collective-permute-start(f32[256,256]{1,0:T(8,128)} %get-tuple-element.48.other_ref), channel_id=1, source_target_pairs={{0,4},{1,5},{2,6},{3,7},{4,0},{5,1},{6,2},{7,3},{8,12},{9,13},{10,... | collective-permute-start | bytes 786440 | tf_op jit(solution)/shard_map/ppermute | solution.py:24
  166.2 0.7 collective-permute-start.29
  167.0 3.4 %collective-permute-start.28 = (f32[384,128]{1,0:T(8,128)}, f32[384,128]{1,0:T(8,128)S(1)}, u32[]{:S(2)}, u32[]{:S(2)}) collective-permute-start(f32[384,128]{1,0:T(8,128)} %get-tuple-element.49.refs_0_), channel_id=1, source_target_pairs={{0,1},{1,0},{2,3},{3,2},{4,5},{5,4},{6,7},{7,6},{8,9},{9,8},{10,11... | collective-permute-start | bytes 589832 | tf_op jit(solution)/shard_map/ppermute | solution.py:24
  170.3 8.1 %collective-permute-done.30.refs_3_ = f32[384,128]{1,0:T(8,128)S(1)} collective-permute-done((f32[384,128]{1,0:T(8,128)}, f32[384,128]{1,0:T(8,128)S(1)}, u32[]{:S(2)}, u32[]{:S(2)}) %collective-permute-start.30) | collective-permute-done | bytes 196640 | tf_op jit(solution)/shard_map/ppermute | solution.py:24
  178.5 0.6 collective-permute-done.28.refs_1_
  179.1 0.1 copy-done.22
  179.1 0.1 copy-done.23
  179.2 0.6 copy-done.24
  179.8 19.0 %orthogonal.1 = (f32[2,256,256]{2,1,0:T(8,128)}, f32[256,256]{1,0:T(8,128)}) custom-call(s32[4]{0:T(128)} %copy-done.9, f32[2,256,256]{2,1,0:T(8,128)} %get-tuple-element.47.samples_ref, f32[256,256]{1,0:T(8,128)} %get-tuple-element.48.other_ref, f32[384,128]{1,0:T(8,128)} %get-tuple-element.49.refs_0_, f32[384,128]{1,0:T(8,128)} %copy-done.24, ...), custom_call_target="tpu_custom_call" | custom-call | tf_op jit(solution)/shard_map/orthogonal/pallas_call | solution.py:297
  198.7 0.4 collective-permute-start.31
  199.1 8.8 %collective-permute-done.31 = f32[256,256]{1,0:T(8,128)S(1)} collective-permute-done((f32[256,256]{1,0:T(8,128)}, f32[256,256]{1,0:T(8,128)S(1)}, u32[]{:S(2)}, u32[]{:S(2)}) %collective-permute-start.31) | collective-permute-done | bytes 262176 | tf_op jit(solution)/shard_map/ppermute | solution.py:24
  207.9 0.7 bitcast_dynamic-update-slice_fusion
  (67 shorter events, 0.2 us)
Async XLA Ops:
  0.6 21.3 %copy-start.25 = (s32[2,1,1]{0,2,1:T(1,128)S(1)}, s32[2,1,1]{0,2,1:T(1,128)}, u32[]{:S(2)}) copy-start(s32[2,1,1]{0,2,1:T(1,128)} %param.7) | copy-start | bytes 28
  0.6 29.4 %copy-start.8 = (s32[2,1,2048]{2,1,0:T(1,128)S(1)}, s32[2,1,2048]{2,1,0:T(1,128)}, u32[]{:S(2)}) copy-start(s32[2,1,2048]{2,1,0:T(1,128)} %perm_ref.3) | copy-start | bytes 49156
  1.7 9.8 %collective-permute-start.8 = (bf16[256,256]{1,0:T(8,128)(2,1)S(1)}, bf16[256,256]{1,0:T(8,128)(2,1)S(1)}, u32[]{:S(2)}, u32[]{:S(2)}) collective-permute-start(bf16[256,256]{1,0:T(8,128)(2,1)S(1)} %get-tuple-element.54), channel_id=1, source_target_pairs={{0,3},{1,2},{2,1},{3,0},{4,7},{5,6},{6,5},{7,4},{8,11},{9,10},{10,... | collective-permute-start | bytes 393224 | tf_op jit(solution)/shard_map/ppermute | solution.py:24
  5.9 7.9 %collective-permute-start.7 = (bf16[256,256]{1,0:T(8,128)(2,1)S(1)}, bf16[256,256]{1,0:T(8,128)(2,1)S(1)}, u32[]{:S(2)}, u32[]{:S(2)}) collective-permute-start(bf16[256,256]{1,0:T(8,128)(2,1)S(1)} %get-tuple-element.54), channel_id=1, source_target_pairs={{0,2},{1,3},{2,0},{3,1},{4,6},{5,7},{6,4},{7,5},{8,10},{9,11},{10,... | collective-permute-start | bytes 393224 | tf_op jit(solution)/shard_map/ppermute | solution.py:24
  5.9 7.9 %collective-permute-start.6 = (bf16[256,256]{1,0:T(8,128)(2,1)S(1)}, bf16[256,256]{1,0:T(8,128)(2,1)S(1)}, u32[]{:S(2)}, u32[]{:S(2)}) collective-permute-start(bf16[256,256]{1,0:T(8,128)(2,1)S(1)} %get-tuple-element.54), channel_id=1, source_target_pairs={{0,1},{1,0},{2,3},{3,2},{4,5},{5,4},{6,7},{7,6},{8,9},{9,8},{10,11... | collective-permute-start | bytes 393224 | tf_op jit(solution)/shard_map/ppermute | solution.py:24
  6.8 10.1 %collective-permute-start.1 = (bf16[256,256]{1,0:T(8,128)(2,1)S(1)}, bf16[256,256]{1,0:T(8,128)(2,1)S(1)}, u32[]{:S(2)}, u32[]{:S(2)}) collective-permute-start(bf16[256,256]{1,0:T(8,128)(2,1)S(1)} %get-tuple-element.53), channel_id=1, source_target_pairs={{0,4},{1,5},{2,6},{3,7},{4,0},{5,1},{6,2},{7,3},{8,12},{9,13},{10,... | collective-permute-start | bytes 393224 | tf_op jit(solution)/shard_map/ppermute | solution.py:24
  13.8 25.9 %collective-permute-start.10 = (bf16[4,256,256]{2,1,0:T(8,128)(2,1)S(1)}, bf16[4,256,256]{2,1,0:T(8,128)(2,1)S(1)}, u32[]{:S(2)}, u32[]{:S(2)}) collective-permute-start(bf16[4,256,256]{2,1,0:T(8,128)(2,1)S(1)} %pad_maximum_fusion.refs_4_), channel_id=1, source_target_pairs={{0,4},{1,5},{2,6},{3,7},{4,0},{5,1},{6,2},{7,3},{8,12},{9,13},{10,... | collective-permute-start | bytes 1572872 | tf_op jit(solution)/shard_map/ppermute | solution.py:24
  17.0 13.1 %collective-permute-start.17 = (bf16[2,256,256]{2,1,0:T(8,128)(2,1)S(1)}, bf16[2,256,256]{2,1,0:T(8,128)(2,1)S(1)}, u32[]{:S(2)}, u32[]{:S(2)}) collective-permute-start(bf16[2,256,256]{2,1,0:T(8,128)(2,1)S(1)} %pad_maximum_fusion.1.refs_0_), channel_id=1, source_target_pairs={{0,3},{1,2},{2,1},{3,0},{4,7},{5,6},{6,5},{7,4},{8,11},{9,10},{10,... | collective-permute-start | bytes 786440 | tf_op jit(solution)/shard_map/ppermute | solution.py:24
  19.0 11.7 %collective-permute-start.16 = (bf16[2,256,256]{2,1,0:T(8,128)(2,1)S(1)}, bf16[2,256,256]{2,1,0:T(8,128)(2,1)S(1)}, u32[]{:S(2)}, u32[]{:S(2)}) collective-permute-start(bf16[2,256,256]{2,1,0:T(8,128)(2,1)S(1)} %pad_maximum_fusion.1.refs_0_), channel_id=1, source_target_pairs={{0,2},{1,3},{2,0},{3,1},{4,6},{5,7},{6,4},{7,5},{8,10},{9,11},{10,... | collective-permute-start | bytes 786440 | tf_op jit(solution)/shard_map/ppermute | solution.py:24
  19.3 20.4 %collective-permute-start.15 = (bf16[2,256,256]{2,1,0:T(8,128)(2,1)S(1)}, bf16[2,256,256]{2,1,0:T(8,128)(2,1)S(1)}, u32[]{:S(2)}, u32[]{:S(2)}) collective-permute-start(bf16[2,256,256]{2,1,0:T(8,128)(2,1)S(1)} %pad_maximum_fusion.1.refs_0_), channel_id=1, source_target_pairs={{0,1},{1,0},{2,3},{3,2},{4,5},{5,4},{6,7},{7,6},{8,9},{9,8},{10,11... | collective-permute-start | bytes 786440 | tf_op jit(solution)/shard_map/ppermute | solution.py:24
  21.1 10.3 %collective-permute-start.2 = (bf16[2,256,256]{2,1,0:T(8,128)(2,1)S(1)}, bf16[2,256,256]{2,1,0:T(8,128)(2,1)S(1)}, u32[]{:S(2)}, u32[]{:S(2)}) collective-permute-start(bf16[2,256,256]{2,1,0:T(8,128)(2,1)S(1)} %pad_maximum_fusion.1.refs_0_), channel_id=1, source_target_pairs={{0,0},{1,121},{2,114},{3,107},{4,100},{5,93},{6,86},{7,79},{8,8},{... | collective-permute-start | bytes 786440 | tf_op jit(solution)/shard_map/ppermute | solution.py:24
  21.9 87.5 %copy-start.9 = (s32[4]{0:T(128)}, s32[4]{0:T(128)S(1)}, u32[]{:S(2)}) copy-start(s32[4]{0:T(128)S(1)} %pad_add_fusion.ids_ref) | copy-start | bytes 52
  30.0 40.3 %collective-permute-start = (s32[2,1,2048]{2,1,0:T(1,128)S(1)}, s32[2,1,2048]{2,1,0:T(1,128)S(1)}, u32[]{:S(2)}, u32[]{:S(2)}) collective-permute-start(s32[2,1,2048]{2,1,0:T(1,128)S(1)} %copy-done.8), channel_id=1, source_target_pairs={{0,0},{1,121},{2,114},{3,107},{4,100},{5,93},{6,86},{7,79},{8,8},{... | collective-permute-start | bytes 49160 | tf_op jit(solution)/shard_map/ppermute | solution.py:24
  30.7 46.8 %collective-permute-start.9 = (bf16[4,256,256]{2,1,0:T(8,128)(2,1)S(1)}, bf16[4,256,256]{2,1,0:T(8,128)(2,1)S(1)}, u32[]{:S(2)}, u32[]{:S(2)}) collective-permute-start(bf16[4,256,256]{2,1,0:T(8,128)(2,1)S(1)} %pad_maximum_fusion.refs_4_), channel_id=1, source_target_pairs={{0,0},{1,121},{2,114},{3,107},{4,100},{5,93},{6,86},{7,79},{8,8},{... | collective-permute-start | bytes 1572872 | tf_op jit(solution)/shard_map/ppermute | solution.py:24
  31.4 22.0 %collective-permute-start.5 = (bf16[2,256,256]{2,1,0:T(8,128)(2,1)S(1)}, bf16[2,256,256]{2,1,0:T(8,128)(2,1)S(1)}, u32[]{:S(2)}, u32[]{:S(2)}) collective-permute-start(bf16[2,256,256]{2,1,0:T(8,128)(2,1)S(1)} %collective-permute-done.2.refs_0_), channel_id=1, source_target_pairs={{0,107},{1,122},{2,9},{3,24},{4,111},{5,126},{6,13},{7,28},{8,115}... | collective-permute-start | bytes 786440 | tf_op jit(solution)/shard_map/ppermute | solution.py:24
  39.7 18.0 %collective-permute-start.4 = (bf16[2,256,256]{2,1,0:T(8,128)(2,1)S(1)}, bf16[2,256,256]{2,1,0:T(8,128)(2,1)S(1)}, u32[]{:S(2)}, u32[]{:S(2)}) collective-permute-start(bf16[2,256,256]{2,1,0:T(8,128)(2,1)S(1)} %collective-permute-done.2.refs_0_), channel_id=1, source_target_pairs={{0,114},{1,115},{2,16},{3,17},{4,118},{5,119},{6,20},{7,21},{8,122... | collective-permute-start | bytes 786440 | tf_op jit(solution)/shard_map/ppermute | solution.py:24
  39.7 37.8 %collective-permute-start.11 = (bf16[4,256,256]{2,1,0:T(8,128)(2,1)S(1)}, bf16[4,256,256]{2,1,0:T(8,128)(2,1)S(1)}, u32[]{:S(2)}, u32[]{:S(2)}) collective-permute-start(bf16[4,256,256]{2,1,0:T(8,128)(2,1)S(1)} %collective-permute-done.10.refs_5_), channel_id=1, source_target_pairs={{0,0},{1,121},{2,114},{3,107},{4,100},{5,93},{6,86},{7,79},{8,8},{... | collective-permute-start | bytes 1572872 | tf_op jit(solution)/shard_map/ppermute | solution.py:24
  40.4 5.8 %copy-start = (bf16[2,2048,2048]{2,1,0:T(8,128)(2,1)S(1)}, bf16[2,2048,2048]{2,1,0:T(8,128)(2,1)}, u32[]{:S(2)}) copy-start(bf16[2,2048,2048]{2,1,0:T(8,128)(2,1)} %refs_6_.7) | copy-start | bytes 50331652
  53.4 13.9 %collective-permute-start.3 = (bf16[2,256,256]{2,1,0:T(8,128)(2,1)S(1)}, bf16[2,256,256]{2,1,0:T(8,128)(2,1)S(1)}, u32[]{:S(2)}, u32[]{:S(2)}) collective-permute-start(bf16[2,256,256]{2,1,0:T(8,128)(2,1)S(1)} %collective-permute-done.2.refs_0_), channel_id=1, source_target_pairs={{0,121},{1,8},{2,123},{3,10},{4,125},{5,12},{6,127},{7,14},{8,1},{... | collective-permute-start | bytes 786440 | tf_op jit(solution)/shard_map/ppermute | solution.py:24
  57.7 66.5 %collective-permute-start.18 = (s16[4,2,272,256]{3,2,1,0:T(8,128)(2,1)S(1)}, s16[4,2,272,256]{3,2,1,0:T(8,128)(2,1)}, u32[]{:S(2)}, u32[]{:S(2)}) collective-permute-start(s16[4,2,272,256]{3,2,1,0:T(8,128)(2,1)S(1)} %shard_map.61), channel_id=1, source_target_pairs={{0,0},{1,9},{2,18},{3,27},{4,36},{5,45},{6,54},{7,63},{8,8},{9,17}... | collective-permute-start | bytes 3342344 | tf_op jit(solution)/shard_map/ppermute | solution.py:24
  66.6 0.7 copy-start.3
  67.3 24.2 %collective-permute-start.23 = (s16[2,272,256]{2,1,0:T(8,128)(2,1)S(1)}, s16[2,272,256]{2,1,0:T(8,128)(2,1)S(1)}, u32[]{:S(2)}, u32[]{:S(2)}) collective-permute-start(s16[2,272,256]{2,1,0:T(8,128)(2,1)S(1)} %get-tuple-element.44), channel_id=1, source_target_pairs={{0,121},{1,8},{2,123},{3,10},{4,125},{5,12},{6,127},{7,14},{8,1},{... | collective-permute-start | bytes 835592 | tf_op jit(solution)/shard_map/ppermute | solution.py:24
  70.4 39.0 %collective-permute-start.24 = (s16[2,272,256]{2,1,0:T(8,128)(2,1)S(1)}, s16[2,272,256]{2,1,0:T(8,128)(2,1)S(1)}, u32[]{:S(2)}, u32[]{:S(2)}) collective-permute-start(s16[2,272,256]{2,1,0:T(8,128)(2,1)S(1)} %get-tuple-element.45), channel_id=1, source_target_pairs={{0,114},{1,115},{2,16},{3,17},{4,118},{5,119},{6,20},{7,21},{8,122... | collective-permute-start | bytes 835592 | tf_op jit(solution)/shard_map/ppermute | solution.py:24
  77.5 42.1 %collective-permute-start.25 = (s16[2,272,256]{2,1,0:T(8,128)(2,1)S(1)}, s16[2,272,256]{2,1,0:T(8,128)(2,1)S(1)}, u32[]{:S(2)}, u32[]{:S(2)}) collective-permute-start(s16[2,272,256]{2,1,0:T(8,128)(2,1)S(1)} %get-tuple-element.46), channel_id=1, source_target_pairs={{0,107},{1,122},{2,9},{3,24},{4,111},{5,126},{6,13},{7,28},{8,115}... | collective-permute-start | bytes 835592 | tf_op jit(solution)/shard_map/ppermute | solution.py:24
  77.5 5.8 %copy-start.1 = (bf16[2,2048,2048]{2,1,0:T(8,128)(2,1)S(1)}, bf16[2,2048,2048]{2,1,0:T(8,128)(2,1)}, u32[]{:S(2)}) copy-start(bf16[2,2048,2048]{2,1,0:T(8,128)(2,1)} %refs_6_.7) | copy-start | bytes 50331652
  90.8 0.7 copy-start.7
  91.5 36.9 %collective-permute-start.12 = (s16[2,272,256]{2,1,0:T(8,128)(2,1)S(1)}, s16[2,272,256]{2,1,0:T(8,128)(2,1)S(1)}, u32[]{:S(2)}, u32[]{:S(2)}) collective-permute-start(s16[2,272,256]{2,1,0:T(8,128)(2,1)S(1)} %get-tuple-element.28), channel_id=1, source_target_pairs={{0,1},{1,0},{2,3},{3,2},{4,5},{5,4},{6,7},{7,6},{8,9},{9,8},{10,11... | collective-permute-start | bytes 835592 | tf_op jit(solution)/shard_map/ppermute | solution.py:24
  91.5 17.9 %copy-start.12 = (s16[2,272,256]{2,1,0:T(8,128)(2,1)}, s16[2,272,256]{2,1,0:T(8,128)(2,1)S(1)}, u32[]{:S(2)}) copy-start(s16[2,272,256]{2,1,0:T(8,128)(2,1)S(1)} %collective-permute-done.23.refs_1_) | copy-start | bytes 835588
  91.5 36.9 %collective-permute-start.13 = (s16[2,272,256]{2,1,0:T(8,128)(2,1)S(1)}, s16[2,272,256]{2,1,0:T(8,128)(2,1)S(1)}, u32[]{:S(2)}, u32[]{:S(2)}) collective-permute-start(s16[2,272,256]{2,1,0:T(8,128)(2,1)S(1)} %get-tuple-element.29), channel_id=1, source_target_pairs={{0,2},{1,3},{2,0},{3,1},{4,6},{5,7},{6,4},{7,5},{8,10},{9,11},{10,... | collective-permute-start | bytes 835592 | tf_op jit(solution)/shard_map/ppermute | solution.py:24
  109.4 7.4 %copy-start.13 = (s16[2,272,256]{2,1,0:T(8,128)(2,1)}, s16[2,272,256]{2,1,0:T(8,128)(2,1)S(1)}, u32[]{:S(2)}) copy-start(s16[2,272,256]{2,1,0:T(8,128)(2,1)S(1)} %collective-permute-done.24.refs_2_) | copy-start | bytes 835588
  109.4 25.6 %collective-permute-start.14 = (s16[2,272,256]{2,1,0:T(8,128)(2,1)S(1)}, s16[2,272,256]{2,1,0:T(8,128)(2,1)}, u32[]{:S(2)}, u32[]{:S(2)}) collective-permute-start(s16[2,272,256]{2,1,0:T(8,128)(2,1)S(1)} %get-tuple-element.30), channel_id=1, source_target_pairs={{0,3},{1,2},{2,1},{3,0},{4,7},{5,6},{6,5},{7,4},{8,11},{9,10},{10,... | collective-permute-start | bytes 835592 | tf_op jit(solution)/shard_map/ppermute | solution.py:24
  116.8 0.7 copy-start.2
  117.5 0.7 copy-start.4
  118.2 0.7 copy-start.5
  118.9 0.7 copy-start.6
  119.6 0.7 copy-start.14
  122.6 14.9 %collective-permute-start.26 = (s16[2,272,256]{2,1,0:T(8,128)(2,1)}, s16[2,272,256]{2,1,0:T(8,128)(2,1)S(1)}, u32[]{:S(2)}, u32[]{:S(2)}) collective-permute-start(s16[2,272,256]{2,1,0:T(8,128)(2,1)} %sum_back.1), channel_id=1, source_target_pairs={{0,0},{1,9},{2,18},{3,27},{4,36},{5,45},{6,54},{7,63},{8,8},{9,17}... | collective-permute-start | bytes 835592 | tf_op jit(solution)/shard_map/ppermute | solution.py:24
  127.4 10.1 %collective-permute-start.19 = (s16[2,272,256]{2,1,0:T(8,128)(2,1)}, s16[2,272,256]{2,1,0:T(8,128)(2,1)S(1)}, u32[]{:S(2)}, u32[]{:S(2)}) collective-permute-start(s16[2,272,256]{2,1,0:T(8,128)(2,1)} %get-tuple-element.35), channel_id=1, source_target_pairs={{0,4},{1,5},{2,6},{3,7},{4,0},{5,1},{6,2},{7,3},{8,12},{9,13},{10,... | collective-permute-start | bytes 835592 | tf_op jit(solution)/shard_map/ppermute | solution.py:24
  128.4 30.3 %copy-start.15 = (s16[2,272,256]{2,1,0:T(8,128)(2,1)}, s16[2,272,256]{2,1,0:T(8,128)(2,1)S(1)}, u32[]{:S(2)}) copy-start(s16[2,272,256]{2,1,0:T(8,128)(2,1)S(1)} %collective-permute-done.12.refs_1_) | copy-start | bytes 835588
  128.4 12.1 %collective-permute-start.20 = (s16[2,272,256]{2,1,0:T(8,128)(2,1)}, s16[2,272,256]{2,1,0:T(8,128)(2,1)S(1)}, u32[]{:S(2)}, u32[]{:S(2)}) collective-permute-start(s16[2,272,256]{2,1,0:T(8,128)(2,1)} %get-tuple-element.36), channel_id=1, source_target_pairs={{0,5},{1,4},{2,7},{3,6},{4,1},{5,0},{6,3},{7,2},{8,13},{9,12},{10,... | collective-permute-start | bytes 835592 | tf_op jit(solution)/shard_map/ppermute | solution.py:24
  128.4 30.3 %copy-start.16 = (s16[2,272,256]{2,1,0:T(8,128)(2,1)}, s16[2,272,256]{2,1,0:T(8,128)(2,1)S(1)}, u32[]{:S(2)}) copy-start(s16[2,272,256]{2,1,0:T(8,128)(2,1)S(1)} %collective-permute-done.13.refs_2_) | copy-start | bytes 835588
  128.4 20.2 %collective-permute-start.21 = (s16[2,272,256]{2,1,0:T(8,128)(2,1)}, s16[2,272,256]{2,1,0:T(8,128)(2,1)S(1)}, u32[]{:S(2)}, u32[]{:S(2)}) collective-permute-start(s16[2,272,256]{2,1,0:T(8,128)(2,1)} %get-tuple-element.37), channel_id=1, source_target_pairs={{0,6},{1,7},{2,4},{3,5},{4,2},{5,3},{6,0},{7,1},{8,14},{9,15},{10,... | collective-permute-start | bytes 835592 | tf_op jit(solution)/shard_map/ppermute | solution.py:24
  134.9 23.7 %collective-permute-start.22 = (s16[2,272,256]{2,1,0:T(8,128)(2,1)}, s16[2,272,256]{2,1,0:T(8,128)(2,1)S(1)}, u32[]{:S(2)}, u32[]{:S(2)}) collective-permute-start(s16[2,272,256]{2,1,0:T(8,128)(2,1)} %get-tuple-element.38), channel_id=1, source_target_pairs={{0,7},{1,6},{2,5},{3,4},{4,3},{5,2},{6,1},{7,0},{8,15},{9,14},{10,... | collective-permute-start | bytes 835592 | tf_op jit(solution)/shard_map/ppermute | solution.py:24
  137.5 21.2 %copy-start.17 = (s16[2,272,256]{2,1,0:T(8,128)(2,1)}, s16[2,272,256]{2,1,0:T(8,128)(2,1)S(1)}, u32[]{:S(2)}) copy-start(s16[2,272,256]{2,1,0:T(8,128)(2,1)S(1)} %collective-permute-done.26.refs_8_) | copy-start | bytes 835588
  137.5 21.2 %copy-start.18 = (s16[2,272,256]{2,1,0:T(8,128)(2,1)}, s16[2,272,256]{2,1,0:T(8,128)(2,1)S(1)}, u32[]{:S(2)}) copy-start(s16[2,272,256]{2,1,0:T(8,128)(2,1)S(1)} %collective-permute-done.19.refs_4_) | copy-start | bytes 835588
  140.5 18.2 %copy-start.19 = (s16[2,272,256]{2,1,0:T(8,128)(2,1)}, s16[2,272,256]{2,1,0:T(8,128)(2,1)S(1)}, u32[]{:S(2)}) copy-start(s16[2,272,256]{2,1,0:T(8,128)(2,1)S(1)} %collective-permute-done.20.refs_5_) | copy-start | bytes 835588
  148.6 10.1 %copy-start.20 = (s16[2,272,256]{2,1,0:T(8,128)(2,1)}, s16[2,272,256]{2,1,0:T(8,128)(2,1)S(1)}, u32[]{:S(2)}) copy-start(s16[2,272,256]{2,1,0:T(8,128)(2,1)S(1)} %collective-permute-done.21.refs_6_) | copy-start | bytes 835588
  158.7 0.7 copy-start.21
  163.1 36.0 %copy-start.10 = (f32[2,256,256]{2,1,0:T(8,128)S(1)}, f32[2,256,256]{2,1,0:T(8,128)}, u32[]{:S(2)}) copy-start(f32[2,256,256]{2,1,0:T(8,128)} %get-tuple-element.47.samples_ref) | copy-start | bytes 1572868
  163.1 35.9 %collective-permute-start.27 = (f32[256,256]{1,0:T(8,128)}, f32[256,256]{1,0:T(8,128)S(1)}, u32[]{:S(2)}, u32[]{:S(2)}) collective-permute-start(f32[256,256]{1,0:T(8,128)} %get-tuple-element.48.other_ref), channel_id=1, source_target_pairs={{0,4},{1,5},{2,6},{3,7},{4,0},{5,1},{6,2},{7,3},{8,12},{9,13},{10,... | collective-permute-start | bytes 786440 | tf_op jit(solution)/shard_map/ppermute | solution.py:24
  166.2 12.2 %collective-permute-start.30 = (f32[384,128]{1,0:T(8,128)}, f32[384,128]{1,0:T(8,128)S(1)}, u32[]{:S(2)}, u32[]{:S(2)}) collective-permute-start(f32[384,128]{1,0:T(8,128)} %get-tuple-element.49.refs_0_), channel_id=1, source_target_pairs={{0,3},{1,2},{2,1},{3,0},{4,7},{5,6},{6,5},{7,4},{8,11},{9,10},{10,... | collective-permute-start | bytes 589832 | tf_op jit(solution)/shard_map/ppermute | solution.py:24
  166.2 12.2 %collective-permute-start.29 = (f32[384,128]{1,0:T(8,128)}, f32[384,128]{1,0:T(8,128)S(1)}, u32[]{:S(2)}, u32[]{:S(2)}) collective-permute-start(f32[384,128]{1,0:T(8,128)} %get-tuple-element.49.refs_0_), channel_id=1, source_target_pairs={{0,2},{1,3},{2,0},{3,1},{4,6},{5,7},{6,4},{7,5},{8,10},{9,11},{10,... | collective-permute-start | bytes 589832 | tf_op jit(solution)/shard_map/ppermute | solution.py:24
  167.0 12.1 %collective-permute-start.28 = (f32[384,128]{1,0:T(8,128)}, f32[384,128]{1,0:T(8,128)S(1)}, u32[]{:S(2)}, u32[]{:S(2)}) collective-permute-start(f32[384,128]{1,0:T(8,128)} %get-tuple-element.49.refs_0_), channel_id=1, source_target_pairs={{0,1},{1,0},{2,3},{3,2},{4,5},{5,4},{6,7},{7,6},{8,9},{9,8},{10,11... | collective-permute-start | bytes 589832 | tf_op jit(solution)/shard_map/ppermute | solution.py:24
  178.4 0.7 copy-start.22
  178.4 0.7 copy-start.23
  179.1 0.7 copy-start.24
  198.7 9.2 %collective-permute-start.31 = (f32[256,256]{1,0:T(8,128)}, f32[256,256]{1,0:T(8,128)S(1)}, u32[]{:S(2)}, u32[]{:S(2)}) collective-permute-start(f32[256,256]{1,0:T(8,128)} %get-tuple-element.51), channel_id=1, source_target_pairs={{0,4},{1,5},{2,6},{3,7},{4,0},{5,1},{6,2},{7,3},{8,12},{9,13},{10,... | collective-permute-start | bytes 786440 | tf_op jit(solution)/shard_map/ppermute | solution.py:24
  199.1 9.5 %copy-start.11 = (f32[2,256,256]{2,1,0:T(8,128)}, f32[2,256,256]{2,1,0:T(8,128)S(1)}, u32[]{:S(2)}) copy-start(f32[2,256,256]{2,1,0:T(8,128)S(1)} %bitcast_dynamic-update-slice_fusion.1) | copy-start | bytes 1572868
where the time goes:
time: 209 us
  starting transfers between devices  71.4 us (34%)
  waiting for transfers between devices  59 us (28%)
  Pallas kernels  57.4 us (27%)
  local copies, waits for them, and re-layouts  19.7 us (9%)
    ppermute x32, starting transfers between devices, sent(): return lax.ppermute(value, AXES, pairs)  71.4 us
    ppermute x32, waiting for transfers between devices, sent(): return lax.ppermute(value, AXES, pairs)  59 us
    pallas_call x4, Pallas kernels, products(): pl.pallas_call(functools.partial(product_kernel, back, part), out_shape=[...  29.2 us
    pallas_call x1, Pallas kernels, orthogonal(): pl.pallas_call(functools.partial(factor_kernel, scale), in_specs=[pl.Bloc...  19 us
    unnamed x52, local copies, waits for them, and re-layouts  17.9 us
  transfers between devices with their start and end apart: 32, of which 11 were waited for; matrix products, arithmetic and copies ran while one was open for 0% of the time, Pallas kernels for 26%

commit v1 on v0

--- a/solution.py
+++ b/solution.py
@@ -47,7 +47,9 @@
 
 def product_kernel(back, part, ids_ref, weight_ref, perm_ref, *refs):
     *pair_refs, plane_ref, cross_ref, tiles_ref = refs[:7]
-    *out_refs, tile_ref, raw_ref, omega_ref, sems = refs[7:]
+    joins = not back and part == 0
+    more_ref = refs[7] if joins else None
+    *out_refs, tile_ref, raw_ref, omega_ref, sems = refs[8 if joins else 7 :]
     nz, points, _ = plane_ref.shape
     length = raw_ref.shape[1]
     step = 512
@@ -93,23 +95,26 @@
                 value = jnp.dot(omega_ref[...], tile_ref[:, pl.ds(at, points)], preferred_element_type=jnp.float32).T
             else:
                 value = jnp.dot(tile_ref[pl.ds(at, points), :], omega_ref[...], preferred_element_type=jnp.float32)
-            code = coded(value * weight)
+            value = value * weight
+            if joins:
+                value = value + decoded(more_ref[d, a])
+            code = coded(value)
             if len(out_refs) == 1:
                 out_refs[0][d, a] = code
             else:
                 out_refs[d][a] = code
 
 
-def products(ids, weight, perm, pairs, plane, cross, tiles, back, part):
+def products(ids, weight, perm, pairs, plane, cross, tiles, back, part, more=()):
     nz, points, probes = plane.shape
     length = tiles.shape[1]
     block = (2, points + EXTRA, probes)
-    shapes = [(nz, *block)] if back and part else [block] * nz
+    shapes = [(nz, *block)] if back and part == 0 else [block] * nz
     smem, vmem = pl.BlockSpec(memory_space=pltpu.SMEM), pl.BlockSpec(memory_space=pltpu.VMEM)
     return pl.pallas_call(
         functools.partial(product_kernel, back, part),
         out_shape=[jax.ShapeDtypeStruct(shape, jnp.int16) for shape in shapes],
-        in_specs=[smem, smem] + [vmem] * (3 + nz) + [pl.BlockSpec(memory_space=pl.ANY)],
+        in_specs=[smem, smem] + [vmem] * (3 + nz) + [pl.BlockSpec(memory_space=pl.ANY)] + [vmem] * len(more),
         out_specs=[vmem] * len(shapes),
         scratch_shapes=[
             pltpu.VMEM(tiles.shape[1:], jnp.bfloat16),
@@ -117,13 +122,13 @@
             pltpu.VMEM((probes, length) if back else (length, probes), jnp.bfloat16),
             pltpu.SemaphoreType.DMA((length // 512,)),
         ],
-        compiler_params=pltpu.CompilerParams(vmem_limit_bytes=32 << 20),
+        compiler_params=pltpu.CompilerParams(vmem_limit_bytes=56 << 20),
         cost_estimate=pl.CostEstimate(flops=4 * length * length * probes, bytes_accessed=11 << 20, transcendentals=0),
-    )(ids, weight, perm, *pairs, plane, cross, tiles)
+    )(ids, weight, perm, *pairs, plane, cross, tiles, *more)
 
 
 def sum_kernel(*refs):
-    *in_refs, unread_ref, out_ref = refs
+    *in_refs, out_ref = refs
     for a in range(2):
         total = decoded(in_refs[0][a])
         for ref in in_refs[1:]:
@@ -131,28 +136,8 @@
         out_ref[a] = coded(total)
 
 
-def summed(codes, after):
-    return pl.pallas_call(
-        sum_kernel,
-        in_specs=[pl.BlockSpec(memory_space=pltpu.VMEM)] * len(codes) + [pl.BlockSpec(memory_space=pl.ANY)],
-        out_shape=jax.ShapeDtypeStruct(codes[0].shape, jnp.int16),
-        name="sum_back",
-    )(*codes, after)
-
-
-def join_kernel(nz, *refs):
-    more_ref = refs[nz]
-    for d in range(nz):
-        for a in range(2):
-            refs[nz + 1 + d][a] = coded(decoded(refs[d][a]) + decoded(more_ref[d, a]))
-
-
-def joined(codes, more):
-    return pl.pallas_call(
-        functools.partial(join_kernel, len(codes)),
-        out_shape=[jax.ShapeDtypeStruct(x.shape, jnp.int16) for x in codes],
-        name="join",
-    )(*codes, more)
+def summed(codes):
+    return pl.pallas_call(sum_kernel, out_shape=jax.ShapeDtypeStruct(codes[0].shape, jnp.int16), name="sum_back")(*codes)
 
 
 def gram_kernel(ids_ref, *refs):
@@ -344,19 +329,17 @@
     own_blocks = ([pair, *pairs], line, cross)
     far_blocks = ([far_pair, *far_pairs], far_line, far_cross)
 
-    def home(r, c):
-        return (r + c, c)
-
-    (more,) = products(ids, weight, perm, *own_blocks, tiles, True, 1)
-    more = sent(more, home)
-    back = products(ids, weight, perm, *own_blocks, tiles, True, 0)
+    (more,) = products(ids, weight, perm, *own_blocks, tiles, True, 0)
+    more = sent(more, lambda r, c: (r + c, c))
+    back = products(ids, weight, perm, *own_blocks, tiles, True, 1)
     back, far_pairs = lax.optimization_barrier((back, far_pairs))
     back = [back[0]] + [sent(back[d], slanted(d)) for d in depths]
-    kept = products(ids, weight, far_perm, *far_blocks, tiles, False, 0)
+    given = products(ids, weight, far_perm, *far_blocks, tiles, False, 1)
+    given = [sent(code, same(nz + d)) for d, code in enumerate(given)]
+    kept = products(ids, weight, far_perm, *far_blocks, tiles, False, 0, (more,))
     kept = [kept[0]] + [sent(kept[d], same(d)) for d in depths]
-    given = products(ids, weight, far_perm, *far_blocks, tiles, False, 1)
-    arrived = sent(summed(back, given[0]), home)
-    given = [sent(code, same(nz + d)) for d, code in enumerate(joined(given, more))]
+    arrived = summed(back)
+    arrived = sent(arrived, lambda r, c: (r + c, c ^ nz))
     samples, swapped, gram = gram_of(ids, [*kept, *given, arrived])
     grams = [gram] + [sent(gram, same(d)) for d in depths]
     basis, swapped_basis = orthogonal(ids, samples, swapped, grams, 1.0 / tile_len)

time: 209 us -> 212 us (1.014); the launches traced: 209 us -> 209 us
  starting transfers between devices: 71.4 us -> 88.8 us
  local copies, waits for them, and re-layouts: 19.7 us -> 7.13 us
  waiting for transfers between devices: 59 us -> 50.7 us
  Pallas kernels: 57.4 us -> 59.8 us
    ppermute x32, starting transfers between devices: 71.4 us -> 88.8 us  [sent(): return lax.ppermute(value, AXES, pairs)]
    unnamed x52 -> x64, local copies, waits for them, and re-layouts: 17.9 us -> 5.38 us
    ppermute x32, waiting for transfers between devices: 59 us -> 50.7 us  [sent(): return lax.ppermute(value, AXES, pairs)]
    pallas_call x4, Pallas kernels: 29.2 us -> 34.8 us  [products(): pl.pallas_call(functools.partial(product_kernel, back, part), out_shape=[...]
    pallas_call x2 -> x1, Pallas kernels: 5.5 us -> 2.33 us  [summed(): pl.pallas_call(sum_kernel, out_shape=jax.ShapeDtypeStruct(codes[0].shape,...]
  transfers between devices with their start and end apart: 32 -> 32, of which waited for: 11 -> 10; matrix products, arithmetic and copies ran while one was open for 0% -> 1% of each run, Pallas kernels for 26% -> 27%
where the time goes in v1:
time: 212 us; the launch traced here: 209 us
  starting transfers between devices  88.8 us (42%)
  Pallas kernels  59.8 us (28%)
  waiting for transfers between devices  50.7 us (24%)
  local copies, waits for them, and re-layouts  7.13 us (3%)
    ppermute x32, starting transfers between devices, sent(): return lax.ppermute(value, AXES, pairs)  88.8 us
    ppermute x32, waiting for transfers between devices, sent(): return lax.ppermute(value, AXES, pairs)  50.7 us
    pallas_call x4, Pallas kernels, products(): pl.pallas_call(functools.partial(product_kernel, back, part), out_shape=[...  34.8 us
    pallas_call x1, Pallas kernels, orthogonal(): pl.pallas_call(functools.partial(factor_kernel, scale), in_specs=[pl.Bloc...  19 us
    unnamed x64, local copies, waits for them, and re-layouts  5.38 us
  transfers between devices with their start and end apart: 32, of which 10 were waited for; matrix products, arithmetic and copies ran while one was open for 1% of the time, Pallas kernels for 27%

profile of v1, /device:TPU:0, one launch (start us, length us, event | category | flops | bytes accessed | tf_op | source)
XLA Modules:
  0.0 208.8 jit_solution(9628585807805739867)
XLA Ops:
  0.6 1.0 fusion.1
  1.7 4.2 %collective-permute-start.8 = (bf16[256,256]{1,0:T(8,128)(2,1)S(1)}, bf16[256,256]{1,0:T(8,128)(2,1)S(1)}, u32[]{:S(2)}, u32[]{:S(2)}) collective-permute-start(bf16[256,256]{1,0:T(8,128)(2,1)S(1)} %get-tuple-element.46), channel_id=1, source_target_pairs={{0,3},{1,2},{2,1},{3,0},{4,7},{5,6},{6,5},{7,4},{8,11},{9,10},{10,... | collective-permute-start | bytes 393224 | tf_op jit(solution)/shard_map/ppermute | solution.py:24
  5.9 0.9 collective-permute-start.6
  6.8 3.0 %collective-permute-start.1 = (bf16[256,256]{1,0:T(8,128)(2,1)S(1)}, bf16[256,256]{1,0:T(8,128)(2,1)S(1)}, u32[]{:S(2)}, u32[]{:S(2)}) collective-permute-start(bf16[256,256]{1,0:T(8,128)(2,1)S(1)} %get-tuple-element.45), channel_id=1, source_target_pairs={{0,4},{1,5},{2,6},{3,7},{4,0},{5,1},{6,2},{7,3},{8,12},{9,13},{10,... | collective-permute-start | bytes 393224 | tf_op jit(solution)/shard_map/ppermute | solution.py:24
  9.9 1.6 collective-permute-done.8
  11.4 2.3 %collective-permute-done.7 = bf16[256,256]{1,0:T(8,128)(2,1)S(1)} collective-permute-done((bf16[256,256]{1,0:T(8,128)(2,1)S(1)}, bf16[256,256]{1,0:T(8,128)(2,1)S(1)}, u32[]{:S(2)}, u32[]{:S(2)}) %collective-permute-start.7) | collective-permute-done | bytes 131104 | tf_op jit(solution)/shard_map/ppermute | solution.py:24
  13.7 0.1 pad_maximum_fusion.refs_4_
  13.8 3.1 %collective-permute-start.10 = (bf16[4,256,256]{2,1,0:T(8,128)(2,1)S(1)}, bf16[4,256,256]{2,1,0:T(8,128)(2,1)S(1)}, u32[]{:S(2)}, u32[]{:S(2)}) collective-permute-start(bf16[4,256,256]{2,1,0:T(8,128)(2,1)S(1)} %pad_maximum_fusion.refs_4_), channel_id=1, source_target_pairs={{0,4},{1,5},{2,6},{3,7},{4,0},{5,1},{6,2},{7,3},{8,12},{9,13},{10,... | collective-permute-start | bytes 1572872 | tf_op jit(solution)/shard_map/ppermute | solution.py:24
  17.0 2.0 collective-permute-start.14
  19.0 0.3 collective-permute-start.13
  19.4 1.8 collective-permute-start.12
  21.2 0.7 collective-permute-start.2
  21.8 0.6 pad_add_fusion.ids_ref
  22.4 0.6 fusion.weight_ref
  23.0 11.2 %collective-permute-start.5 = (bf16[2,256,256]{2,1,0:T(8,128)(2,1)S(1)}, bf16[2,256,256]{2,1,0:T(8,128)(2,1)S(1)}, u32[]{:S(2)}, u32[]{:S(2)}) collective-permute-start(bf16[2,256,256]{2,1,0:T(8,128)(2,1)S(1)} %collective-permute-done.2.refs_0_), channel_id=1, source_target_pairs={{0,107},{1,122},{2,9},{3,24},{4,111},{5,126},{6,13},{7,28},{8,115}... | collective-permute-start | bytes 786440 | tf_op jit(solution)/shard_map/ppermute | solution.py:24
  34.3 4.9 %collective-permute-start.4 = (bf16[2,256,256]{2,1,0:T(8,128)(2,1)S(1)}, bf16[2,256,256]{2,1,0:T(8,128)(2,1)S(1)}, u32[]{:S(2)}, u32[]{:S(2)}) collective-permute-start(bf16[2,256,256]{2,1,0:T(8,128)(2,1)S(1)} %collective-permute-done.2.refs_0_), channel_id=1, source_target_pairs={{0,114},{1,115},{2,16},{3,17},{4,118},{5,119},{6,20},{7,21},{8,122... | collective-permute-start | bytes 786440 | tf_op jit(solution)/shard_map/ppermute | solution.py:24
  39.3 0.6 copy-done.13
  40.0 0.1 copy-done.14
  40.1 0.8 copy-done.3
  40.9 8.9 %shard_map.59 = s16[4,2,272,256]{3,2,1,0:T(8,128)(2,1)} custom-call(s32[4]{0:T(128)} %pad_add_fusion.ids_ref, f32[2]{0:T(128)} %fusion.weight_ref, s32[2,1,2048]{2,1,0:T(1,128)} %perm_ref.3, bf16[2,256,256]{2,1,0:T(8,128)(2,1)} %copy-done.2, bf16[2,256,256]{2,1,0:T(8,128)(2,1)} %copy-done.14, bf16[2,256,256]{2,1,0:T(8,128)(2,1)} %copy-done.13, ...), custom_call_target="tpu_custom_call" | custom-call | flops 4294967296 | bytes 11534336 | tf_op jit(solution)/shard_map/pallas_call | solution.py:114
  49.8 0.0 copy-start.1
  49.8 0.0 copy-start.4
  49.8 2.0 collective-permute-start.15
  51.8 8.6 %shard_map.62 = (s16[2,272,256]{2,1,0:T(8,128)(2,1)}, s16[2,272,256]{2,1,0:T(8,128)(2,1)}, s16[2,272,256]{2,1,0:T(8,128)(2,1)}, s16[2,272,256]{2,1,0:T(8,128)(2,1)}) custom-call(s32[4]{0:T(128)} %pad_add_fusion.ids_ref, f32[2]{0:T(128)} %fusion.weight_ref, s32[2,1,2048]{2,1,0:T(1,128)} %perm_ref.3, bf16[2,256,256]{2,1,0:T(8,128)(2,1)} %copy-done.2, ...), custom_call_target="tpu_custom_call" | custom-call | flops 4294967296 | bytes 11534336 | tf_op jit(solution)/shard_map/pallas_call | solution.py:114
  60.4 0.7 copy-done.9
  61.1 0.1 copy-done.10
  61.2 4.6 %collective-permute-start.23 = (s16[2,272,256]{2,1,0:T(8,128)(2,1)}, s16[2,272,256]{2,1,0:T(8,128)(2,1)S(1)}, u32[]{:S(2)}, u32[]{:S(2)}) collective-permute-start(s16[2,272,256]{2,1,0:T(8,128)(2,1)} %get-tuple-element.36), channel_id=1, source_target_pairs={{0,121},{1,8},{2,123},{3,10},{4,125},{5,12},{6,127},{7,14},{8,1},{... | collective-permute-start | bytes 835592 | tf_op jit(solution)/shard_map/ppermute | solution.py:24
  65.9 0.7 collective-permute-start.9
  66.6 0.7 collective-permute-start.11
  67.3 6.5 %collective-permute-start.24 = (s16[2,272,256]{2,1,0:T(8,128)(2,1)}, s16[2,272,256]{2,1,0:T(8,128)(2,1)}, u32[]{:S(2)}, u32[]{:S(2)}) collective-permute-start(s16[2,272,256]{2,1,0:T(8,128)(2,1)} %get-tuple-element.37), channel_id=1, source_target_pairs={{0,114},{1,115},{2,16},{3,17},{4,118},{5,119},{6,20},{7,21},{8,122... | collective-permute-start | bytes 835592 | tf_op jit(solution)/shard_map/ppermute | solution.py:24
  73.7 2.2 %collective-permute-done.23.refs_1_ = s16[2,272,256]{2,1,0:T(8,128)(2,1)S(1)} collective-permute-done((s16[2,272,256]{2,1,0:T(8,128)(2,1)}, s16[2,272,256]{2,1,0:T(8,128)(2,1)S(1)}, u32[]{:S(2)}, u32[]{:S(2)}) %collective-permute-start.23) | collective-permute-done | bytes 278560 | tf_op jit(solution)/shard_map/ppermute | solution.py:24
  75.9 13.8 %collective-permute-start.25 = (s16[2,272,256]{2,1,0:T(8,128)(2,1)}, s16[2,272,256]{2,1,0:T(8,128)(2,1)}, u32[]{:S(2)}, u32[]{:S(2)}) collective-permute-start(s16[2,272,256]{2,1,0:T(8,128)(2,1)} %get-tuple-element.38), channel_id=1, source_target_pairs={{0,107},{1,122},{2,9},{3,24},{4,111},{5,126},{6,13},{7,28},{8,115}... | collective-permute-start | bytes 835592 | tf_op jit(solution)/shard_map/ppermute | solution.py:24
  89.7 25.0 %collective-permute-done.24.refs_2_ = s16[2,272,256]{2,1,0:T(8,128)(2,1)} collective-permute-done((s16[2,272,256]{2,1,0:T(8,128)(2,1)}, s16[2,272,256]{2,1,0:T(8,128)(2,1)}, u32[]{:S(2)}, u32[]{:S(2)}) %collective-permute-start.24) | collective-permute-done | bytes 278560 | tf_op jit(solution)/shard_map/ppermute | solution.py:24
  114.7 0.8 collective-permute-start
  115.6 2.3 %sum_back.1 = s16[2,272,256]{2,1,0:T(8,128)(2,1)} custom-call(s16[2,272,256]{2,1,0:T(8,128)(2,1)} %get-tuple-element.35.refs_0_, s16[2,272,256]{2,1,0:T(8,128)(2,1)} %copy-done.17, s16[2,272,256]{2,1,0:T(8,128)(2,1)} %collective-permute-done.24.refs_2_, s16[2,272,256]{2,1,0:T(8,128)(2,1)} %collective-permute-done.25.refs_3_), custom_call_target="tpu_custom_call" | custom-call | tf_op jit(solution)/shard_map/sum_back/pallas_call | solution.py:140
  117.9 4.4 %collective-permute-start.26 = (s16[2,272,256]{2,1,0:T(8,128)(2,1)}, s16[2,272,256]{2,1,0:T(8,128)(2,1)S(1)}, u32[]{:S(2)}, u32[]{:S(2)}) collective-permute-start(s16[2,272,256]{2,1,0:T(8,128)(2,1)} %sum_back.1), channel_id=1, source_target_pairs={{0,4},{1,13},{2,22},{3,31},{4,32},{5,41},{6,50},{7,59},{8,12},{9,2... | collective-permute-start | bytes 835592 | tf_op jit(solution)/shard_map/ppermute | solution.py:24
  122.4 0.6 copy-done.30
  122.9 0.2 copy-done.5
  123.1 0.8 copy-done.6
  123.9 8.5 %shard_map.61 = (s16[2,272,256]{2,1,0:T(8,128)(2,1)}, s16[2,272,256]{2,1,0:T(8,128)(2,1)}, s16[2,272,256]{2,1,0:T(8,128)(2,1)}, s16[2,272,256]{2,1,0:T(8,128)(2,1)}) custom-call(s32[4]{0:T(128)} %pad_add_fusion.ids_ref, f32[2]{0:T(128)} %fusion.weight_ref, s32[2,1,2048]{2,1,0:T(1,128)} %copy-done.30, bf16[2,256,256]{2,1,0:T(8,128)(2,1)} %copy-done.8, ...), custom_call_target="tpu_custom_call" | custom-call | flops 4294967296 | bytes 11534336 | tf_op jit(solution)/shard_map/pallas_call | solution.py:114
  132.5 1.2 collective-permute-start.19
  133.7 1.0 collective-permute-start.21
  134.8 7.9 %collective-permute-start.22 = (s16[2,272,256]{2,1,0:T(8,128)(2,1)}, s16[2,272,256]{2,1,0:T(8,128)(2,1)S(1)}, u32[]{:S(2)}, u32[]{:S(2)}) collective-permute-start(s16[2,272,256]{2,1,0:T(8,128)(2,1)} %get-tuple-element.30), channel_id=1, source_target_pairs={{0,7},{1,6},{2,5},{3,4},{4,3},{5,2},{6,1},{7,0},{8,15},{9,14},{10,... | collective-permute-start | bytes 835592 | tf_op jit(solution)/shard_map/ppermute | solution.py:24
  142.6 8.9 %shard_map.60 = (s16[2,272,256]{2,1,0:T(8,128)(2,1)}, s16[2,272,256]{2,1,0:T(8,128)(2,1)}, s16[2,272,256]{2,1,0:T(8,128)(2,1)}, s16[2,272,256]{2,1,0:T(8,128)(2,1)}) custom-call(s32[4]{0:T(128)} %pad_add_fusion.ids_ref, f32[2]{0:T(128)} %fusion.weight_ref, s32[2,1,2048]{2,1,0:T(1,128)} %copy-done.30, bf16[2,256,256]{2,1,0:T(8,128)(2,1)} %copy-done.8, ...), custom_call_target="tpu_custom_call" | custom-call | flops 4294967296 | bytes 11534336 | tf_op jit(solution)/shard_map/pallas_call | solution.py:114
  151.5 0.1 collective-permute-start.16
  151.7 0.7 collective-permute-start.17
  152.3 4.0 %collective-permute-start.18 = (s16[2,272,256]{2,1,0:T(8,128)(2,1)}, s16[2,272,256]{2,1,0:T(8,128)(2,1)S(1)}, u32[]{:S(2)}, u32[]{:S(2)}) collective-permute-start(s16[2,272,256]{2,1,0:T(8,128)(2,1)} %get-tuple-element.26), channel_id=1, source_target_pairs={{0,3},{1,2},{2,1},{3,0},{4,7},{5,6},{6,5},{7,4},{8,11},{9,10},{10,... | collective-permute-start | bytes 835592 | tf_op jit(solution)/shard_map/ppermute | solution.py:24
  156.4 2.2 %collective-permute-done.16.refs_1_ = s16[2,272,256]{2,1,0:T(8,128)(2,1)S(1)} collective-permute-done((s16[2,272,256]{2,1,0:T(8,128)(2,1)}, s16[2,272,256]{2,1,0:T(8,128)(2,1)S(1)}, u32[]{:S(2)}, u32[]{:S(2)}) %collective-permute-start.16) | collective-permute-done | bytes 278560 | tf_op jit(solution)/shard_map/ppermute | solution.py:24
  158.6 2.6 %collective-permute-done.17.refs_2_ = s16[2,272,256]{2,1,0:T(8,128)(2,1)S(1)} collective-permute-done((s16[2,272,256]{2,1,0:T(8,128)(2,1)}, s16[2,272,256]{2,1,0:T(8,128)(2,1)S(1)}, u32[]{:S(2)}, u32[]{:S(2)}) %collective-permute-start.17) | collective-permute-done | bytes 278560 | tf_op jit(solution)/shard_map/ppermute | solution.py:24
  161.2 2.9 %collective-permute-done.18.refs_3_ = s16[2,272,256]{2,1,0:T(8,128)(2,1)S(1)} collective-permute-done((s16[2,272,256]{2,1,0:T(8,128)(2,1)}, s16[2,272,256]{2,1,0:T(8,128)(2,1)S(1)}, u32[]{:S(2)}, u32[]{:S(2)}) %collective-permute-start.18) | collective-permute-done | bytes 278560 | tf_op jit(solution)/shard_map/ppermute | solution.py:24
  164.1 0.7 copy-done.25
  164.8 3.7 %gram.1 = (f32[2,256,256]{2,1,0:T(8,128)}, f32[256,256]{1,0:T(8,128)}, f32[384,128]{1,0:T(8,128)}) custom-call(s32[4]{0:T(128)} %pad_add_fusion.ids_ref, s16[2,272,256]{2,1,0:T(8,128)(2,1)} %get-tuple-element.23.refs_0_, s16[2,272,256]{2,1,0:T(8,128)(2,1)} %copy-done.23, s16[2,272,256]{2,1,0:T(8,128)(2,1)} %copy-done.24, s16[2,272,256]{2,1,0:T(8,128)(2,1)} %copy-done.25, ...), custom_call_target="tpu_custom_call" | custom-call | tf_op jit(solution)/shard_map/gram/pallas_call | solution.py:169
  168.5 1.6 collective-permute-start.27
  170.1 2.8 %collective-permute-start.30 = (f32[384,128]{1,0:T(8,128)}, f32[384,128]{1,0:T(8,128)S(1)}, u32[]{:S(2)}, u32[]{:S(2)}) collective-permute-start(f32[384,128]{1,0:T(8,128)} %get-tuple-element.41.refs_0_), channel_id=1, source_target_pairs={{0,3},{1,2},{2,1},{3,0},{4,7},{5,6},{6,5},{7,4},{8,11},{9,10},{10,... | collective-permute-start | bytes 589832 | tf_op jit(solution)/shard_map/ppermute | solution.py:24
  172.9 1.3 collective-permute-start.28
  174.2 4.4 %collective-permute-done.30.refs_3_ = f32[384,128]{1,0:T(8,128)S(1)} collective-permute-done((f32[384,128]{1,0:T(8,128)}, f32[384,128]{1,0:T(8,128)S(1)}, u32[]{:S(2)}, u32[]{:S(2)}) %collective-permute-start.30) | collective-permute-done | bytes 196640 | tf_op jit(solution)/shard_map/ppermute | solution.py:24
  178.5 1.8 collective-permute-done.29.refs_2_
  180.3 0.7 copy-done.27
  181.0 0.1 copy-done.28
  181.1 19.0 %orthogonal.1 = (f32[2,256,256]{2,1,0:T(8,128)}, f32[256,256]{1,0:T(8,128)}) custom-call(s32[4]{0:T(128)} %pad_add_fusion.ids_ref, f32[2,256,256]{2,1,0:T(8,128)} %get-tuple-element.39.samples_ref, f32[256,256]{1,0:T(8,128)} %get-tuple-element.40.other_ref, f32[384,128]{1,0:T(8,128)} %get-tuple-element.41.refs_0_, f32[384,128]{1,0:T(8,128)} %copy-done.28, ...), custom_call_target="tpu_custom_call" | custom-call | tf_op jit(solution)/shard_map/orthogonal/pallas_call | solution.py:282
  200.0 2.3 %collective-permute-start.31 = (f32[256,256]{1,0:T(8,128)}, f32[256,256]{1,0:T(8,128)S(1)}, u32[]{:S(2)}, u32[]{:S(2)}) collective-permute-start(f32[256,256]{1,0:T(8,128)} %get-tuple-element.43), channel_id=1, source_target_pairs={{0,4},{1,5},{2,6},{3,7},{4,0},{5,1},{6,2},{7,3},{8,12},{9,13},{10,... | collective-permute-start | bytes 786440 | tf_op jit(solution)/shard_map/ppermute | solution.py:24
  202.3 0.0 copy-start.16
  202.3 5.8 %collective-permute-done.31 = f32[256,256]{1,0:T(8,128)S(1)} collective-permute-done((f32[256,256]{1,0:T(8,128)}, f32[256,256]{1,0:T(8,128)S(1)}, u32[]{:S(2)}, u32[]{:S(2)}) %collective-permute-start.31) | collective-permute-done | bytes 262176 | tf_op jit(solution)/shard_map/ppermute | solution.py:24
  208.1 0.7 bitcast_dynamic-update-slice_fusion
  (78 shorter events, 0.2 us)
Async XLA Ops:
  0.6 21.8 %copy-start.31 = (s32[2,1,1]{0,2,1:T(1,128)S(1)}, s32[2,1,1]{0,2,1:T(1,128)}, u32[]{:S(2)}) copy-start(s32[2,1,1]{0,2,1:T(1,128)} %param.7) | copy-start | bytes 28
  1.7 9.8 %collective-permute-start.8 = (bf16[256,256]{1,0:T(8,128)(2,1)S(1)}, bf16[256,256]{1,0:T(8,128)(2,1)S(1)}, u32[]{:S(2)}, u32[]{:S(2)}) collective-permute-start(bf16[256,256]{1,0:T(8,128)(2,1)S(1)} %get-tuple-element.46), channel_id=1, source_target_pairs={{0,3},{1,2},{2,1},{3,0},{4,7},{5,6},{6,5},{7,4},{8,11},{9,10},{10,... | collective-permute-start | bytes 393224 | tf_op jit(solution)/shard_map/ppermute | solution.py:24
  5.9 7.9 %collective-permute-start.7 = (bf16[256,256]{1,0:T(8,128)(2,1)S(1)}, bf16[256,256]{1,0:T(8,128)(2,1)S(1)}, u32[]{:S(2)}, u32[]{:S(2)}) collective-permute-start(bf16[256,256]{1,0:T(8,128)(2,1)S(1)} %get-tuple-element.46), channel_id=1, source_target_pairs={{0,2},{1,3},{2,0},{3,1},{4,6},{5,7},{6,4},{7,5},{8,10},{9,11},{10,... | collective-permute-start | bytes 393224 | tf_op jit(solution)/shard_map/ppermute | solution.py:24
  5.9 7.9 %collective-permute-start.6 = (bf16[256,256]{1,0:T(8,128)(2,1)S(1)}, bf16[256,256]{1,0:T(8,128)(2,1)S(1)}, u32[]{:S(2)}, u32[]{:S(2)}) collective-permute-start(bf16[256,256]{1,0:T(8,128)(2,1)S(1)} %get-tuple-element.46), channel_id=1, source_target_pairs={{0,1},{1,0},{2,3},{3,2},{4,5},{5,4},{6,7},{7,6},{8,9},{9,8},{10,11... | collective-permute-start | bytes 393224 | tf_op jit(solution)/shard_map/ppermute | solution.py:24
  6.8 10.1 %collective-permute-start.1 = (bf16[256,256]{1,0:T(8,128)(2,1)S(1)}, bf16[256,256]{1,0:T(8,128)(2,1)S(1)}, u32[]{:S(2)}, u32[]{:S(2)}) collective-permute-start(bf16[256,256]{1,0:T(8,128)(2,1)S(1)} %get-tuple-element.45), channel_id=1, source_target_pairs={{0,4},{1,5},{2,6},{3,7},{4,0},{5,1},{6,2},{7,3},{8,12},{9,13},{10,... | collective-permute-start | bytes 393224 | tf_op jit(solution)/shard_map/ppermute | solution.py:24
  13.8 25.5 %copy-start = (bf16[4,256,256]{2,1,0:T(8,128)(2,1)}, bf16[4,256,256]{2,1,0:T(8,128)(2,1)S(1)}, u32[]{:S(2)}) copy-start(bf16[4,256,256]{2,1,0:T(8,128)(2,1)S(1)} %pad_maximum_fusion.refs_4_) | copy-start | bytes 1572868
  13.8 25.4 %collective-permute-start.10 = (bf16[4,256,256]{2,1,0:T(8,128)(2,1)S(1)}, bf16[4,256,256]{2,1,0:T(8,128)(2,1)S(1)}, u32[]{:S(2)}, u32[]{:S(2)}) collective-permute-start(bf16[4,256,256]{2,1,0:T(8,128)(2,1)S(1)} %pad_maximum_fusion.refs_4_), channel_id=1, source_target_pairs={{0,4},{1,5},{2,6},{3,7},{4,0},{5,1},{6,2},{7,3},{8,12},{9,13},{10,... | collective-permute-start | bytes 1572872 | tf_op jit(solution)/shard_map/ppermute | solution.py:24
  17.0 22.3 %copy-start.2 = (bf16[2,256,256]{2,1,0:T(8,128)(2,1)}, bf16[2,256,256]{2,1,0:T(8,128)(2,1)S(1)}, u32[]{:S(2)}) copy-start(bf16[2,256,256]{2,1,0:T(8,128)(2,1)S(1)} %pad_maximum_fusion.1.refs_0_) | copy-start | bytes 786436
  17.0 17.3 %collective-permute-start.14 = (bf16[2,256,256]{2,1,0:T(8,128)(2,1)S(1)}, bf16[2,256,256]{2,1,0:T(8,128)(2,1)S(1)}, u32[]{:S(2)}, u32[]{:S(2)}) collective-permute-start(bf16[2,256,256]{2,1,0:T(8,128)(2,1)S(1)} %pad_maximum_fusion.1.refs_0_), channel_id=1, source_target_pairs={{0,3},{1,2},{2,1},{3,0},{4,7},{5,6},{6,5},{7,4},{8,11},{9,10},{10,... | collective-permute-start | bytes 786440 | tf_op jit(solution)/shard_map/ppermute | solution.py:24
  19.0 20.2 %collective-permute-start.13 = (bf16[2,256,256]{2,1,0:T(8,128)(2,1)S(1)}, bf16[2,256,256]{2,1,0:T(8,128)(2,1)S(1)}, u32[]{:S(2)}, u32[]{:S(2)}) collective-permute-start(bf16[2,256,256]{2,1,0:T(8,128)(2,1)S(1)} %pad_maximum_fusion.1.refs_0_), channel_id=1, source_target_pairs={{0,2},{1,3},{2,0},{3,1},{4,6},{5,7},{6,4},{7,5},{8,10},{9,11},{10,... | collective-permute-start | bytes 786440 | tf_op jit(solution)/shard_map/ppermute | solution.py:24
  19.4 19.9 %collective-permute-start.12 = (bf16[2,256,256]{2,1,0:T(8,128)(2,1)S(1)}, bf16[2,256,256]{2,1,0:T(8,128)(2,1)S(1)}, u32[]{:S(2)}, u32[]{:S(2)}) collective-permute-start(bf16[2,256,256]{2,1,0:T(8,128)(2,1)S(1)} %pad_maximum_fusion.1.refs_0_), channel_id=1, source_target_pairs={{0,1},{1,0},{2,3},{3,2},{4,5},{5,4},{6,7},{7,6},{8,9},{9,8},{10,11... | collective-permute-start | bytes 786440 | tf_op jit(solution)/shard_map/ppermute | solution.py:24
  21.2 1.9 collective-permute-start.2
  23.0 26.7 %copy-start.8 = (bf16[2,256,256]{2,1,0:T(8,128)(2,1)}, bf16[2,256,256]{2,1,0:T(8,128)(2,1)S(1)}, u32[]{:S(2)}) copy-start(bf16[2,256,256]{2,1,0:T(8,128)(2,1)S(1)} %collective-permute-done.2.refs_0_) | copy-start | bytes 786436
  23.0 37.3 %collective-permute-start.5 = (bf16[2,256,256]{2,1,0:T(8,128)(2,1)S(1)}, bf16[2,256,256]{2,1,0:T(8,128)(2,1)S(1)}, u32[]{:S(2)}, u32[]{:S(2)}) collective-permute-start(bf16[2,256,256]{2,1,0:T(8,128)(2,1)S(1)} %collective-permute-done.2.refs_0_), channel_id=1, source_target_pairs={{0,107},{1,122},{2,9},{3,24},{4,111},{5,126},{6,13},{7,28},{8,115}... | collective-permute-start | bytes 786440 | tf_op jit(solution)/shard_map/ppermute | solution.py:24
  34.3 5.0 %copy-start.12 = (bf16[2,256,256]{2,1,0:T(8,128)(2,1)}, bf16[2,256,256]{2,1,0:T(8,128)(2,1)S(1)}, u32[]{:S(2)}) copy-start(bf16[2,256,256]{2,1,0:T(8,128)(2,1)S(1)} %collective-permute-done.14.refs_3_) | copy-start | bytes 786436
  34.3 26.1 %collective-permute-start.4 = (bf16[2,256,256]{2,1,0:T(8,128)(2,1)S(1)}, bf16[2,256,256]{2,1,0:T(8,128)(2,1)S(1)}, u32[]{:S(2)}, u32[]{:S(2)}) collective-permute-start(bf16[2,256,256]{2,1,0:T(8,128)(2,1)S(1)} %collective-permute-done.2.refs_0_), channel_id=1, source_target_pairs={{0,114},{1,115},{2,16},{3,17},{4,118},{5,119},{6,20},{7,21},{8,122... | collective-permute-start | bytes 786440 | tf_op jit(solution)/shard_map/ppermute | solution.py:24
  39.2 0.7 copy-start.13
  39.2 21.2 %collective-permute-start.3 = (bf16[2,256,256]{2,1,0:T(8,128)(2,1)S(1)}, bf16[2,256,256]{2,1,0:T(8,128)(2,1)S(1)}, u32[]{:S(2)}, u32[]{:S(2)}) collective-permute-start(bf16[2,256,256]{2,1,0:T(8,128)(2,1)S(1)} %collective-permute-done.2.refs_0_), channel_id=1, source_target_pairs={{0,121},{1,8},{2,123},{3,10},{4,125},{5,12},{6,127},{7,14},{8,1},{... | collective-permute-start | bytes 786440 | tf_op jit(solution)/shard_map/ppermute | solution.py:24
  39.3 0.8 copy-start.14
  40.1 0.8 copy-start.3
  49.8 16.1 %copy-start.1 = (bf16[4,256,256]{2,1,0:T(8,128)(2,1)S(1)}, bf16[4,256,256]{2,1,0:T(8,128)(2,1)}, u32[]{:S(2)}) copy-start(bf16[4,256,256]{2,1,0:T(8,128)(2,1)} %copy-done) | copy-start | bytes 1572868
  49.8 16.8 %copy-start.4 = (bf16[4,256,256]{2,1,0:T(8,128)(2,1)S(1)}, bf16[4,256,256]{2,1,0:T(8,128)(2,1)}, u32[]{:S(2)}) copy-start(bf16[4,256,256]{2,1,0:T(8,128)(2,1)} %copy-done.3) | copy-start | bytes 1572868
  49.8 64.9 %copy-start.29 = (s32[2,1,2048]{2,1,0:T(1,128)S(1)}, s32[2,1,2048]{2,1,0:T(1,128)}, u32[]{:S(2)}) copy-start(s32[2,1,2048]{2,1,0:T(1,128)} %perm_ref.3) | copy-start | bytes 49156
  49.8 85.0 %collective-permute-start.15 = (s16[4,2,272,256]{3,2,1,0:T(8,128)(2,1)}, s16[4,2,272,256]{3,2,1,0:T(8,128)(2,1)S(1)}, u32[]{:S(2)}, u32[]{:S(2)}) collective-permute-start(s16[4,2,272,256]{3,2,1,0:T(8,128)(2,1)} %shard_map.59), channel_id=1, source_target_pairs={{0,0},{1,9},{2,18},{3,27},{4,36},{5,45},{6,54},{7,63},{8,8},{9,17}... | collective-permute-start | bytes 3342344 | tf_op jit(solution)/shard_map/ppermute | solution.py:24
  60.4 0.7 copy-start.9
  60.4 0.8 copy-start.10
  60.4 5.4 %copy-start.11 = (bf16[2,256,256]{2,1,0:T(8,128)(2,1)}, bf16[2,256,256]{2,1,0:T(8,128)(2,1)S(1)}, u32[]{:S(2)}) copy-start(bf16[2,256,256]{2,1,0:T(8,128)(2,1)S(1)} %collective-permute-done.3.refs_1_) | copy-start | bytes 786436
  61.2 14.7 %collective-permute-start.23 = (s16[2,272,256]{2,1,0:T(8,128)(2,1)}, s16[2,272,256]{2,1,0:T(8,128)(2,1)S(1)}, u32[]{:S(2)}, u32[]{:S(2)}) collective-permute-start(s16[2,272,256]{2,1,0:T(8,128)(2,1)} %get-tuple-element.36), channel_id=1, source_target_pairs={{0,121},{1,8},{2,123},{3,10},{4,125},{5,12},{6,127},{7,14},{8,1},{... | collective-permute-start | bytes 835592 | tf_op jit(solution)/shard_map/ppermute | solution.py:24
  65.9 56.5 %collective-permute-start.9 = (bf16[4,256,256]{2,1,0:T(8,128)(2,1)S(1)}, bf16[4,256,256]{2,1,0:T(8,128)(2,1)S(1)}, u32[]{:S(2)}, u32[]{:S(2)}) collective-permute-start(bf16[4,256,256]{2,1,0:T(8,128)(2,1)S(1)} %copy-done.1), channel_id=1, source_target_pairs={{0,0},{1,121},{2,114},{3,107},{4,100},{5,93},{6,86},{7,79},{8,8},{... | collective-permute-start | bytes 1572872 | tf_op jit(solution)/shard_map/ppermute | solution.py:24
  66.6 55.8 %collective-permute-start.11 = (bf16[4,256,256]{2,1,0:T(8,128)(2,1)S(1)}, bf16[4,256,256]{2,1,0:T(8,128)(2,1)S(1)}, u32[]{:S(2)}, u32[]{:S(2)}) collective-permute-start(bf16[4,256,256]{2,1,0:T(8,128)(2,1)S(1)} %copy-done.4), channel_id=1, source_target_pairs={{0,0},{1,121},{2,114},{3,107},{4,100},{5,93},{6,86},{7,79},{8,8},{... | collective-permute-start | bytes 1572872 | tf_op jit(solution)/shard_map/ppermute | solution.py:24
  67.3 47.5 %collective-permute-start.24 = (s16[2,272,256]{2,1,0:T(8,128)(2,1)}, s16[2,272,256]{2,1,0:T(8,128)(2,1)}, u32[]{:S(2)}, u32[]{:S(2)}) collective-permute-start(s16[2,272,256]{2,1,0:T(8,128)(2,1)} %get-tuple-element.37), channel_id=1, source_target_pairs={{0,114},{1,115},{2,16},{3,17},{4,118},{5,119},{6,20},{7,21},{8,122... | collective-permute-start | bytes 835592 | tf_op jit(solution)/shard_map/ppermute | solution.py:24
  75.9 39.7 %copy-start.17 = (s16[2,272,256]{2,1,0:T(8,128)(2,1)}, s16[2,272,256]{2,1,0:T(8,128)(2,1)S(1)}, u32[]{:S(2)}) copy-start(s16[2,272,256]{2,1,0:T(8,128)(2,1)S(1)} %collective-permute-done.23.refs_1_) | copy-start | bytes 835588
  75.9 39.7 %collective-permute-start.25 = (s16[2,272,256]{2,1,0:T(8,128)(2,1)}, s16[2,272,256]{2,1,0:T(8,128)(2,1)}, u32[]{:S(2)}, u32[]{:S(2)}) collective-permute-start(s16[2,272,256]{2,1,0:T(8,128)(2,1)} %get-tuple-element.38), channel_id=1, source_target_pairs={{0,107},{1,122},{2,9},{3,24},{4,111},{5,126},{6,13},{7,28},{8,115}... | collective-permute-start | bytes 835592 | tf_op jit(solution)/shard_map/ppermute | solution.py:24
  114.7 7.6 %collective-permute-start = (s32[2,1,2048]{2,1,0:T(1,128)S(1)}, s32[2,1,2048]{2,1,0:T(1,128)S(1)}, u32[]{:S(2)}, u32[]{:S(2)}) collective-permute-start(s32[2,1,2048]{2,1,0:T(1,128)S(1)} %copy-done.29), channel_id=1, source_target_pairs={{0,0},{1,121},{2,114},{3,107},{4,100},{5,93},{6,86},{7,79},{8,8},{... | collective-permute-start | bytes 49160 | tf_op jit(solution)/shard_map/ppermute | solution.py:24
  117.9 33.6 %collective-permute-start.26 = (s16[2,272,256]{2,1,0:T(8,128)(2,1)}, s16[2,272,256]{2,1,0:T(8,128)(2,1)S(1)}, u32[]{:S(2)}, u32[]{:S(2)}) collective-permute-start(s16[2,272,256]{2,1,0:T(8,128)(2,1)} %sum_back.1), channel_id=1, source_target_pairs={{0,4},{1,13},{2,22},{3,31},{4,32},{5,41},{6,50},{7,59},{8,12},{9,2... | collective-permute-start | bytes 835592 | tf_op jit(solution)/shard_map/ppermute | solution.py:24
  122.3 0.6 copy-start.30
  122.3 0.8 copy-start.5
  123.1 0.8 copy-start.6
  132.5 19.2 %collective-permute-start.19 = (s16[2,272,256]{2,1,0:T(8,128)(2,1)}, s16[2,272,256]{2,1,0:T(8,128)(2,1)S(1)}, u32[]{:S(2)}, u32[]{:S(2)}) collective-permute-start(s16[2,272,256]{2,1,0:T(8,128)(2,1)} %get-tuple-element.27), channel_id=1, source_target_pairs={{0,4},{1,5},{2,6},{3,7},{4,0},{5,1},{6,2},{7,3},{8,12},{9,13},{10,... | collective-permute-start | bytes 835592 | tf_op jit(solution)/shard_map/ppermute | solution.py:24
  133.7 18.6 %collective-permute-start.20 = (s16[2,272,256]{2,1,0:T(8,128)(2,1)}, s16[2,272,256]{2,1,0:T(8,128)(2,1)S(1)}, u32[]{:S(2)}, u32[]{:S(2)}) collective-permute-start(s16[2,272,256]{2,1,0:T(8,128)(2,1)} %get-tuple-element.28), channel_id=1, source_target_pairs={{0,5},{1,4},{2,7},{3,6},{4,1},{5,0},{6,3},{7,2},{8,13},{9,12},{10,... | collective-permute-start | bytes 835592 | tf_op jit(solution)/shard_map/ppermute | solution.py:24
  133.7 22.6 %collective-permute-start.21 = (s16[2,272,256]{2,1,0:T(8,128)(2,1)}, s16[2,272,256]{2,1,0:T(8,128)(2,1)S(1)}, u32[]{:S(2)}, u32[]{:S(2)}) collective-permute-start(s16[2,272,256]{2,1,0:T(8,128)(2,1)} %get-tuple-element.29), channel_id=1, source_target_pairs={{0,6},{1,7},{2,4},{3,5},{4,2},{5,3},{6,0},{7,1},{8,14},{9,15},{10,... | collective-permute-start | bytes 835592 | tf_op jit(solution)/shard_map/ppermute | solution.py:24
  134.8 7.9 %copy-start.7 = (s16[4,2,272,256]{3,2,1,0:T(8,128)(2,1)}, s16[4,2,272,256]{3,2,1,0:T(8,128)(2,1)S(1)}, u32[]{:S(2)}) copy-start(s16[4,2,272,256]{3,2,1,0:T(8,128)(2,1)S(1)} %collective-permute-done.15.refs_7_) | copy-start | bytes 3342340
  134.8 21.6 %collective-permute-start.22 = (s16[2,272,256]{2,1,0:T(8,128)(2,1)}, s16[2,272,256]{2,1,0:T(8,128)(2,1)S(1)}, u32[]{:S(2)}, u32[]{:S(2)}) collective-permute-start(s16[2,272,256]{2,1,0:T(8,128)(2,1)} %get-tuple-element.30), channel_id=1, source_target_pairs={{0,7},{1,6},{2,5},{3,4},{4,3},{5,2},{6,1},{7,0},{8,15},{9,14},{10,... | collective-permute-start | bytes 835592 | tf_op jit(solution)/shard_map/ppermute | solution.py:24
  151.5 12.5 %copy-start.18 = (s16[2,272,256]{2,1,0:T(8,128)(2,1)}, s16[2,272,256]{2,1,0:T(8,128)(2,1)S(1)}, u32[]{:S(2)}) copy-start(s16[2,272,256]{2,1,0:T(8,128)(2,1)S(1)} %collective-permute-done.26.refs_8_) | copy-start | bytes 835588
  151.5 7.0 %collective-permute-start.16 = (s16[2,272,256]{2,1,0:T(8,128)(2,1)}, s16[2,272,256]{2,1,0:T(8,128)(2,1)S(1)}, u32[]{:S(2)}, u32[]{:S(2)}) collective-permute-start(s16[2,272,256]{2,1,0:T(8,128)(2,1)} %get-tuple-element.24), channel_id=1, source_target_pairs={{0,1},{1,0},{2,3},{3,2},{4,5},{5,4},{6,7},{7,6},{8,9},{9,8},{10,11... | collective-permute-start | bytes 835592 | tf_op jit(solution)/shard_map/ppermute | solution.py:24
  151.6 12.4 %copy-start.19 = (s16[2,272,256]{2,1,0:T(8,128)(2,1)}, s16[2,272,256]{2,1,0:T(8,128)(2,1)S(1)}, u32[]{:S(2)}) copy-start(s16[2,272,256]{2,1,0:T(8,128)(2,1)S(1)} %collective-permute-done.19.refs_4_) | copy-start | bytes 835588
  151.7 9.5 %collective-permute-start.17 = (s16[2,272,256]{2,1,0:T(8,128)(2,1)}, s16[2,272,256]{2,1,0:T(8,128)(2,1)S(1)}, u32[]{:S(2)}, u32[]{:S(2)}) collective-permute-start(s16[2,272,256]{2,1,0:T(8,128)(2,1)} %get-tuple-element.25), channel_id=1, source_target_pairs={{0,2},{1,3},{2,0},{3,1},{4,6},{5,7},{6,4},{7,5},{8,10},{9,11},{10,... | collective-permute-start | bytes 835592 | tf_op jit(solution)/shard_map/ppermute | solution.py:24
  152.3 11.7 %copy-start.20 = (s16[2,272,256]{2,1,0:T(8,128)(2,1)}, s16[2,272,256]{2,1,0:T(8,128)(2,1)S(1)}, u32[]{:S(2)}) copy-start(s16[2,272,256]{2,1,0:T(8,128)(2,1)S(1)} %collective-permute-done.20.refs_5_) | copy-start | bytes 835588
  152.3 11.7 %collective-permute-start.18 = (s16[2,272,256]{2,1,0:T(8,128)(2,1)}, s16[2,272,256]{2,1,0:T(8,128)(2,1)S(1)}, u32[]{:S(2)}, u32[]{:S(2)}) collective-permute-start(s16[2,272,256]{2,1,0:T(8,128)(2,1)} %get-tuple-element.26), channel_id=1, source_target_pairs={{0,3},{1,2},{2,1},{3,0},{4,7},{5,6},{6,5},{7,4},{8,11},{9,10},{10,... | collective-permute-start | bytes 835592 | tf_op jit(solution)/shard_map/ppermute | solution.py:24
  156.3 7.7 %copy-start.21 = (s16[2,272,256]{2,1,0:T(8,128)(2,1)}, s16[2,272,256]{2,1,0:T(8,128)(2,1)S(1)}, u32[]{:S(2)}) copy-start(s16[2,272,256]{2,1,0:T(8,128)(2,1)S(1)} %collective-permute-done.21.refs_6_) | copy-start | bytes 835588
  156.3 7.7 %copy-start.22 = (s16[2,272,256]{2,1,0:T(8,128)(2,1)}, s16[2,272,256]{2,1,0:T(8,128)(2,1)S(1)}, u32[]{:S(2)}) copy-start(s16[2,272,256]{2,1,0:T(8,128)(2,1)S(1)} %collective-permute-done.22.refs_7_) | copy-start | bytes 835588
  158.6 5.5 %copy-start.23 = (s16[2,272,256]{2,1,0:T(8,128)(2,1)}, s16[2,272,256]{2,1,0:T(8,128)(2,1)S(1)}, u32[]{:S(2)}) copy-start(s16[2,272,256]{2,1,0:T(8,128)(2,1)S(1)} %collective-permute-done.16.refs_1_) | copy-start | bytes 835588
  161.2 2.9 %copy-start.24 = (s16[2,272,256]{2,1,0:T(8,128)(2,1)}, s16[2,272,256]{2,1,0:T(8,128)(2,1)S(1)}, u32[]{:S(2)}) copy-start(s16[2,272,256]{2,1,0:T(8,128)(2,1)S(1)} %collective-permute-done.17.refs_2_) | copy-start | bytes 835588
  164.0 0.7 copy-start.25
  168.5 33.8 %copy-start.15 = (f32[2,256,256]{2,1,0:T(8,128)S(1)}, f32[2,256,256]{2,1,0:T(8,128)}, u32[]{:S(2)}) copy-start(f32[2,256,256]{2,1,0:T(8,128)} %get-tuple-element.39.samples_ref) | copy-start | bytes 1572868
  168.5 33.8 %collective-permute-start.27 = (f32[256,256]{1,0:T(8,128)}, f32[256,256]{1,0:T(8,128)S(1)}, u32[]{:S(2)}, u32[]{:S(2)}) collective-permute-start(f32[256,256]{1,0:T(8,128)} %get-tuple-element.40.other_ref), channel_id=1, source_target_pairs={{0,4},{1,5},{2,6},{3,7},{4,0},{5,1},{6,2},{7,3},{8,12},{9,13},{10,... | collective-permute-start | bytes 786440 | tf_op jit(solution)/shard_map/ppermute | solution.py:24
  170.1 8.4 %collective-permute-start.30 = (f32[384,128]{1,0:T(8,128)}, f32[384,128]{1,0:T(8,128)S(1)}, u32[]{:S(2)}, u32[]{:S(2)}) collective-permute-start(f32[384,128]{1,0:T(8,128)} %get-tuple-element.41.refs_0_), channel_id=1, source_target_pairs={{0,3},{1,2},{2,1},{3,0},{4,7},{5,6},{6,5},{7,4},{8,11},{9,10},{10,... | collective-permute-start | bytes 589832 | tf_op jit(solution)/shard_map/ppermute | solution.py:24
  172.9 7.4 %collective-permute-start.29 = (f32[384,128]{1,0:T(8,128)}, f32[384,128]{1,0:T(8,128)S(1)}, u32[]{:S(2)}, u32[]{:S(2)}) collective-permute-start(f32[384,128]{1,0:T(8,128)} %get-tuple-element.41.refs_0_), channel_id=1, source_target_pairs={{0,2},{1,3},{2,0},{3,1},{4,6},{5,7},{6,4},{7,5},{8,10},{9,11},{10,... | collective-permute-start | bytes 589832 | tf_op jit(solution)/shard_map/ppermute | solution.py:24
  172.9 7.4 %collective-permute-start.28 = (f32[384,128]{1,0:T(8,128)}, f32[384,128]{1,0:T(8,128)S(1)}, u32[]{:S(2)}, u32[]{:S(2)}) collective-permute-start(f32[384,128]{1,0:T(8,128)} %get-tuple-element.41.refs_0_), channel_id=1, source_target_pairs={{0,1},{1,0},{2,3},{3,2},{4,5},{5,4},{6,7},{7,6},{8,9},{9,8},{10,11... | collective-permute-start | bytes 589832 | tf_op jit(solution)/shard_map/ppermute | solution.py:24
  178.5 1.8 copy-start.26
  180.3 0.7 copy-start.27
  180.3 0.8 copy-start.28
  200.0 8.1 %collective-permute-start.31 = (f32[256,256]{1,0:T(8,128)}, f32[256,256]{1,0:T(8,128)S(1)}, u32[]{:S(2)}, u32[]{:S(2)}) collective-permute-start(f32[256,256]{1,0:T(8,128)} %get-tuple-element.43), channel_id=1, source_target_pairs={{0,4},{1,5},{2,6},{3,7},{4,0},{5,1},{6,2},{7,3},{8,12},{9,13},{10,... | collective-permute-start | bytes 786440 | tf_op jit(solution)/shard_map/ppermute | solution.py:24
  202.3 6.5 %copy-start.16 = (f32[2,256,256]{2,1,0:T(8,128)}, f32[2,256,256]{2,1,0:T(8,128)S(1)}, u32[]{:S(2)}) copy-start(f32[2,256,256]{2,1,0:T(8,128)S(1)} %bitcast_dynamic-update-slice_fusion.1) | copy-start | bytes 1572868

commit v2 on v1

--- a/solution.py
+++ b/solution.py
@@ -45,38 +45,49 @@
     return wide[:rows] * scale_of(wide[rows : rows + 1], wide[rows + 1 : rows + 2])
 
 
-def product_kernel(back, part, ids_ref, weight_ref, perm_ref, *refs):
-    *pair_refs, plane_ref, cross_ref, tiles_ref = refs[:7]
-    joins = not back and part == 0
-    more_ref = refs[7] if joins else None
-    *out_refs, tile_ref, raw_ref, omega_ref, sems = refs[8 if joins else 7 :]
-    nz, points, _ = plane_ref.shape
+def product_kernel(back, part, ids_ref, weight_ref, perm_ref, tiles_ref, *refs):
+    *in_refs, tile_ref, raw_ref, omega_ref, sems = refs
+    nz = sems.shape[0] // 2
     length = raw_ref.shape[1]
+    points = length // (2 * nz)
     step = 512
     k = ids_ref[3] ^ ids_ref[2] ^ part
     tile_slot = k if back else k ^ ids_ref[2]
-
-    def piece_copy(q):
-        rows = pl.ds(q * step, step)
-        return pltpu.make_async_copy(tiles_ref.at[tile_slot, rows], tile_ref.at[rows], sems.at[q])
-
-    for q in range(length // step):
-        piece_copy(q).start()
-    for slot in range(2):
-
-        @pl.when(k == slot)
-        def _(slot=slot):
-            for d in range(nz):
-                for a in range(2):
-                    piece = (cross_ref[d] if a else plane_ref[d]) if slot else pair_refs[d][a]
-                    at = (nz * a + d) * points
-                    raw_ref[:, at : at + points] = piece.T
+    blocks = [(d, a) for d in range(nz) for a in range(2)]
+
+    def place(d, a):
+        at = pl.ds(pl.multiple_of((a * nz + (ids_ref[1] ^ d)) * points, points), points)
+        return (slice(None), at) if back else (at, slice(None))
+
+    def block_copy(n):
+        at = place(*blocks[n])
+        return pltpu.make_async_copy(tiles_ref.at[(tile_slot, *at)], tile_ref.at[at], sems.at[n])
+
+    for n in range(len(blocks)):
+        block_copy(n).start()
+    if back:
+        out_refs = in_refs[2 * nz :]
+        for o in range(2 * nz):
+            raw_ref[:, o * points : (o + 1) * points] = in_refs[o][k].T
+    else:
+        out_refs = in_refs[nz + 2 - part :]
+
+        @pl.when(k == 0)
+        def _():
+            for d, a in blocks:
+                o = nz * a + d
+                raw_ref[:, o * points : (o + 1) * points] = in_refs[d][a].T
+
+        @pl.when(k == 1)
+        def _():
+            for o in range(2 * nz):
+                raw_ref[:, o * points : (o + 1) * points] = in_refs[nz][o].T
 
     def order_step(i, carry):
         at = pl.multiple_of(i * step, step)
         index = perm_ref[k, :, pl.ds(at, step)] ^ (ids_ref[0] * points)
-        place = lax.broadcasted_iota(jnp.int32, (length, step), 0)
-        chosen = jnp.where(place == index, 1.0, 0.0).astype(jnp.bfloat16)
+        places = lax.broadcasted_iota(jnp.int32, (length, step), 0)
+        chosen = jnp.where(places == index, 1.0, 0.0).astype(jnp.bfloat16)
         found = jnp.dot(raw_ref[...], chosen, preferred_element_type=jnp.float32)
         if back:
             omega_ref[:, pl.ds(at, step)] = found.astype(jnp.bfloat16)
@@ -85,46 +96,45 @@
         return carry
 
     lax.fori_loop(0, length // step, order_step, 0)
-    for q in range(length // step):
-        piece_copy(q).wait()
     weight = weight_ref[tile_slot]
-    for d in range(nz):
-        for a in range(2):
-            at = pl.multiple_of((a * nz + (ids_ref[1] ^ d)) * points, points)
-            if back:
-                value = jnp.dot(omega_ref[...], tile_ref[:, pl.ds(at, points)], preferred_element_type=jnp.float32).T
-            else:
-                value = jnp.dot(tile_ref[pl.ds(at, points), :], omega_ref[...], preferred_element_type=jnp.float32)
-            value = value * weight
-            if joins:
-                value = value + decoded(more_ref[d, a])
-            code = coded(value)
-            if len(out_refs) == 1:
-                out_refs[0][d, a] = code
-            else:
-                out_refs[d][a] = code
-
-
-def products(ids, weight, perm, pairs, plane, cross, tiles, back, part, more=()):
-    nz, points, probes = plane.shape
+    for n, (d, a) in enumerate(blocks):
+        block_copy(n).wait()
+        tile = tile_ref[place(d, a)]
+        if back:
+            value = jnp.dot(omega_ref[...], tile, preferred_element_type=jnp.float32).T
+        else:
+            value = jnp.dot(tile, omega_ref[...], preferred_element_type=jnp.float32)
+        value = value * weight
+        if not back and part == 0:
+            value = value + decoded(in_refs[nz + 1][d, a])
+        code = coded(value)
+        if len(out_refs) == 1:
+            out_refs[0][d, a] = code
+        else:
+            out_refs[d][a] = code
+
+
+def products(ids, weight, perm, tiles, blocks, back, part):
+    points, probes = blocks[0].shape[1:]
     length = tiles.shape[1]
+    nz = length // points // 2
     block = (2, points + EXTRA, probes)
     shapes = [(nz, *block)] if back and part == 0 else [block] * nz
     smem, vmem = pl.BlockSpec(memory_space=pltpu.SMEM), pl.BlockSpec(memory_space=pltpu.VMEM)
     return pl.pallas_call(
         functools.partial(product_kernel, back, part),
         out_shape=[jax.ShapeDtypeStruct(shape, jnp.int16) for shape in shapes],
-        in_specs=[smem, smem] + [vmem] * (3 + nz) + [pl.BlockSpec(memory_space=pl.ANY)] + [vmem] * len(more),
+        in_specs=[smem, smem, vmem, pl.BlockSpec(memory_space=pl.ANY)] + [vmem] * len(blocks),
         out_specs=[vmem] * len(shapes),
         scratch_shapes=[
             pltpu.VMEM(tiles.shape[1:], jnp.bfloat16),
             pltpu.VMEM((probes, length), jnp.bfloat16),
             pltpu.VMEM((probes, length) if back else (length, probes), jnp.bfloat16),
-            pltpu.SemaphoreType.DMA((length // 512,)),
+            pltpu.SemaphoreType.DMA((2 * nz,)),
         ],
         compiler_params=pltpu.CompilerParams(vmem_limit_bytes=56 << 20),
         cost_estimate=pl.CostEstimate(flops=4 * length * length * probes, bytes_accessed=11 << 20, transcendentals=0),
-    )(ids, weight, perm, *pairs, plane, cross, tiles, *more)
+    )(ids, weight, perm, tiles, *blocks)
 
 
 def sum_kernel(*refs):
@@ -312,31 +322,26 @@
         return (r - c, c)
 
     depths = range(1, nz)
-    other = sent(probe[0], same(nz))
-    singles = [sent(probe[1], same(d)) for d in depths]
-    pair = jnp.stack([probe[0], other])
-    line = jnp.stack([probe[1], *singles])
-    pairs = [sent(pair, same(d)) for d in depths]
-    cross = sent(line, same(nz))
-
+    blocks = {nz: sent(probe, same(nz))}
+    for o in (*depths, *range(nz + 1, ncols)):
+        blocks[o] = sent(probe, same(o))
+    blocks = [probe] + [blocks[o] for o in range(1, ncols)]
+
+    far_perm = sent(cluster_perm, far)
+    pair = jnp.stack([blocks[0][0], blocks[nz][0]])
     far_pair = sent(pair, far)
-    far_line = sent(line, far)
-    far_perm = sent(cluster_perm, far)
+    far_whole = sent(jnp.stack([block[1] for block in blocks]), far)
     far_pairs = [sent(far_pair, slanted(d)) for d in depths]
-    far_cross = sent(cross, far)
 
     perm, far_perm = (x.reshape(-1, 1, tile_len) for x in (cluster_perm, far_perm))
-    own_blocks = ([pair, *pairs], line, cross)
-    far_blocks = ([far_pair, *far_pairs], far_line, far_cross)
-
-    (more,) = products(ids, weight, perm, *own_blocks, tiles, True, 0)
+    far_blocks = [far_pair, *far_pairs, far_whole]
+    (more,) = products(ids, weight, perm, tiles, blocks, True, 0)
+    back = products(ids, weight, perm, tiles, blocks, True, 1)
     more = sent(more, lambda r, c: (r + c, c))
-    back = products(ids, weight, perm, *own_blocks, tiles, True, 1)
-    back, far_pairs = lax.optimization_barrier((back, far_pairs))
     back = [back[0]] + [sent(back[d], slanted(d)) for d in depths]
-    given = products(ids, weight, far_perm, *far_blocks, tiles, False, 1)
+    given = products(ids, weight, far_perm, tiles, far_blocks, False, 1)
     given = [sent(code, same(nz + d)) for d, code in enumerate(given)]
-    kept = products(ids, weight, far_perm, *far_blocks, tiles, False, 0, (more,))
+    kept = products(ids, weight, far_perm, tiles, [*far_blocks, more], False, 0)
     kept = [kept[0]] + [sent(kept[d], same(d)) for d in depths]
     arrived = summed(back)
     arrived = sent(arrived, lambda r, c: (r + c, c ^ nz))

time: 212 us -> 238 us (1.12)
  Pallas kernels: 59.8 us -> 74.6 us
  local copies, waits for them, and re-layouts: 7.13 us -> 15.3 us
  starting transfers between devices: 88.8 us -> 92 us
    pallas_call x4, Pallas kernels: 34.8 us -> 49.6 us  [products(): pl.pallas_call(functools.partial(product_kernel, back, part), out_shape=[...]
    unnamed x64 -> x69, local copies, waits for them, and re-layouts: 5.38 us -> 13.9 us
    ppermute x32 -> x30, starting transfers between devices: 88.8 us -> 92 us  [sent(): return lax.ppermute(value, AXES, pairs)]
    ppermute x32 -> x30, waiting for transfers between devices: 50.7 us -> 50 us  [sent(): return lax.ppermute(value, AXES, pairs)]
  transfers between devices with their start and end apart: 32 -> 30, of which waited for: 10 -> 12; matrix products, arithmetic and copies ran while one was open for 1% -> 5% of each run, Pallas kernels for 27% -> 30%
where the time goes in v2:
time: 238 us; the launch traced here: 235 us
  starting transfers between devices  92 us (39%)
  Pallas kernels  74.6 us (31%)
  waiting for transfers between devices  50 us (21%)
  local copies, waits for them, and re-layouts  15.3 us (6%)
    ppermute x30, starting transfers between devices, sent(): return lax.ppermute(value, AXES, pairs)  92 us
    ppermute x30, waiting for transfers between devices, sent(): return lax.ppermute(value, AXES, pairs)  50 us
    pallas_call x4, Pallas kernels, products(): pl.pallas_call(functools.partial(product_kernel, back, part), out_shape=[...  49.6 us
    pallas_call x1, Pallas kernels, orthogonal(): pl.pallas_call(functools.partial(factor_kernel, scale), in_specs=[pl.Bloc...  19 us
    unnamed x69, local copies, waits for them, and re-layouts  13.9 us
  transfers between devices with their start and end apart: 30, of which 12 were waited for; matrix products, arithmetic and copies ran while one was open for 5% of the time, Pallas kernels for 30%

profile of v2, /device:TPU:0, one launch (start us, length us, event | category | flops | bytes accessed | tf_op | source)
XLA Modules:
  0.0 234.8 jit_solution(11862492141222603962)
XLA Ops:
  0.6 6.5 %collective-permute-start.10 = (bf16[2,256,256]{2,1,0:T(8,128)(2,1)}, bf16[2,256,256]{2,1,0:T(8,128)(2,1)S(1)}, u32[]{:S(2)}, u32[]{:S(2)}) collective-permute-start(bf16[2,256,256]{2,1,0:T(8,128)(2,1)} %refs_0_.3), channel_id=1, source_target_pairs={{0,6},{1,7},{2,4},{3,5},{4,2},{5,3},{6,0},{7,1},{8,14},{9,15},{10,... | collective-permute-start | bytes 786440 | tf_op jit(solution)/shard_map/ppermute | solution.py:24
  7.2 1.0 collective-permute-start.9
  8.1 3.1 %collective-permute-start.7 = (bf16[2,256,256]{2,1,0:T(8,128)(2,1)}, bf16[2,256,256]{2,1,0:T(8,128)(2,1)S(1)}, u32[]{:S(2)}, u32[]{:S(2)}) collective-permute-start(bf16[2,256,256]{2,1,0:T(8,128)(2,1)} %refs_0_.3), channel_id=1, source_target_pairs={{0,2},{1,3},{2,0},{3,1},{4,6},{5,7},{6,4},{7,5},{8,10},{9,11},{10,... | collective-permute-start | bytes 786440 | tf_op jit(solution)/shard_map/ppermute | solution.py:24
  11.2 1.0 collective-permute-start.6
  12.2 1.2 fusion.weight_ref
  13.4 1.2 collective-permute-done.10.refs_6_
  14.6 2.6 %collective-permute-start.1 = (bf16[2,256,256]{2,1,0:T(8,128)(2,1)}, bf16[2,256,256]{2,1,0:T(8,128)(2,1)S(1)}, u32[]{:S(2)}, u32[]{:S(2)}) collective-permute-start(bf16[2,256,256]{2,1,0:T(8,128)(2,1)} %refs_0_.3), channel_id=1, source_target_pairs={{0,4},{1,5},{2,6},{3,7},{4,0},{5,1},{6,2},{7,3},{8,12},{9,13},{10,... | collective-permute-start | bytes 786440 | tf_op jit(solution)/shard_map/ppermute | solution.py:24
  17.2 3.9 %collective-permute-done.9.refs_5_ = bf16[2,256,256]{2,1,0:T(8,128)(2,1)S(1)} collective-permute-done((bf16[2,256,256]{2,1,0:T(8,128)(2,1)}, bf16[2,256,256]{2,1,0:T(8,128)(2,1)S(1)}, u32[]{:S(2)}, u32[]{:S(2)}) %collective-permute-start.9) | collective-permute-done | bytes 262176 | tf_op jit(solution)/shard_map/ppermute | solution.py:24
  21.2 0.5 collective-permute-start.11
  21.7 0.6 pad_add_fusion.ids_ref
  22.3 1.6 slice_dynamic-update-slice_fusion.7
  24.0 1.4 collective-permute-start
  25.3 6.1 %collective-permute-done.6.refs_1_ = bf16[2,256,256]{2,1,0:T(8,128)(2,1)S(1)} collective-permute-done((bf16[2,256,256]{2,1,0:T(8,128)(2,1)}, bf16[2,256,256]{2,1,0:T(8,128)(2,1)S(1)}, u32[]{:S(2)}, u32[]{:S(2)}) %collective-permute-start.6) | collective-permute-done | bytes 262176 | tf_op jit(solution)/shard_map/ppermute | solution.py:24
  31.5 0.6 copy-done.8
  32.1 0.1 copy-done.1
  32.2 0.7 copy-done.9
  33.0 12.8 %shard_map.59 = s16[4,2,272,256]{3,2,1,0:T(8,128)(2,1)} custom-call(s32[4]{0:T(128)} %pad_add_fusion.ids_ref, f32[2]{0:T(128)} %fusion.weight_ref, s32[2,1,2048]{2,1,0:T(1,128)} %perm_ref.3, bf16[2,2048,2048]{2,1,0:T(8,128)(2,1)} %tiles_ref.7, bf16[2,256,256]{2,1,0:T(8,128)(2,1)} %refs_0_.3, bf16[2,256,256]{2,1,0:T(8,128)(2,1)} %copy-done.8, ...), custom_call_target="tpu_custom_call" | custom-call | flops 4294967296 | bytes 11534336 | tf_op jit(solution)/shard_map/pallas_call | solution.py:124
  45.8 2.0 collective-permute-start.13
  47.8 1.6 slice_dynamic-update-slice_fusion.6
  49.4 1.6 slice_dynamic-update-slice_fusion.5
  50.9 1.6 slice_dynamic-update-slice_fusion.4
  52.5 1.6 slice_dynamic-update-slice_fusion.3
  54.1 0.7 slice_dynamic-update-slice_fusion.2
  54.8 0.7 slice_dynamic-update-slice_fusion.1
  55.5 0.7 slice_dynamic-update-slice_fusion
  56.1 1.9 collective-permute-start.12
  58.0 0.9 collective-permute-start.2
  58.9 12.4 %shard_map.62 = (s16[2,272,256]{2,1,0:T(8,128)(2,1)}, s16[2,272,256]{2,1,0:T(8,128)(2,1)}, s16[2,272,256]{2,1,0:T(8,128)(2,1)}, s16[2,272,256]{2,1,0:T(8,128)(2,1)}) custom-call(s32[4]{0:T(128)} %pad_add_fusion.ids_ref, f32[2]{0:T(128)} %fusion.weight_ref, s32[2,1,2048]{2,1,0:T(1,128)} %perm_ref.3, bf16[2,2048,2048]{2,1,0:T(8,128)(2,1)} %tiles_ref.7, ...), custom_call_target="tpu_custom_call" | custom-call | flops 4294967296 | bytes 11534336 | tf_op jit(solution)/shard_map/pallas_call | solution.py:124
  71.3 7.6 %collective-permute-start.21 = (s16[2,272,256]{2,1,0:T(8,128)(2,1)}, s16[2,272,256]{2,1,0:T(8,128)(2,1)S(1)}, u32[]{:S(2)}, u32[]{:S(2)}) collective-permute-start(s16[2,272,256]{2,1,0:T(8,128)(2,1)} %get-tuple-element.28), channel_id=1, source_target_pairs={{0,121},{1,8},{2,123},{3,10},{4,125},{5,12},{6,127},{7,14},{8,1},{... | collective-permute-start | bytes 835592 | tf_op jit(solution)/shard_map/ppermute | solution.py:24
  78.9 3.4 %collective-permute-start.22 = (s16[2,272,256]{2,1,0:T(8,128)(2,1)}, s16[2,272,256]{2,1,0:T(8,128)(2,1)}, u32[]{:S(2)}, u32[]{:S(2)}) collective-permute-start(s16[2,272,256]{2,1,0:T(8,128)(2,1)} %get-tuple-element.29), channel_id=1, source_target_pairs={{0,114},{1,115},{2,16},{3,17},{4,118},{5,119},{6,20},{7,21},{8,122... | collective-permute-start | bytes 835592 | tf_op jit(solution)/shard_map/ppermute | solution.py:24
  82.4 2.7 %collective-permute-done.21.refs_1_ = s16[2,272,256]{2,1,0:T(8,128)(2,1)S(1)} collective-permute-done((s16[2,272,256]{2,1,0:T(8,128)(2,1)}, s16[2,272,256]{2,1,0:T(8,128)(2,1)S(1)}, u32[]{:S(2)}, u32[]{:S(2)}) %collective-permute-start.21) | collective-permute-done | bytes 278560 | tf_op jit(solution)/shard_map/ppermute | solution.py:24
  85.1 28.6 %collective-permute-start.5 = (bf16[2,256,256]{2,1,0:T(8,128)(2,1)S(1)}, bf16[2,256,256]{2,1,0:T(8,128)(2,1)S(1)}, u32[]{:S(2)}, u32[]{:S(2)}) collective-permute-start(bf16[2,256,256]{2,1,0:T(8,128)(2,1)S(1)} %collective-permute-done.2.refs_0_), channel_id=1, source_target_pairs={{0,107},{1,122},{2,9},{3,24},{4,111},{5,126},{6,13},{7,28},{8,115}... | collective-permute-start | bytes 786440 | tf_op jit(solution)/shard_map/ppermute | solution.py:24
  113.6 6.2 %collective-permute-done.22.refs_2_ = s16[2,272,256]{2,1,0:T(8,128)(2,1)} collective-permute-done((s16[2,272,256]{2,1,0:T(8,128)(2,1)}, s16[2,272,256]{2,1,0:T(8,128)(2,1)}, u32[]{:S(2)}, u32[]{:S(2)}) %collective-permute-start.22) | collective-permute-done | bytes 278560 | tf_op jit(solution)/shard_map/ppermute | solution.py:24
  119.8 4.0 %collective-permute-start.3 = (bf16[2,256,256]{2,1,0:T(8,128)(2,1)S(1)}, bf16[2,256,256]{2,1,0:T(8,128)(2,1)S(1)}, u32[]{:S(2)}, u32[]{:S(2)}) collective-permute-start(bf16[2,256,256]{2,1,0:T(8,128)(2,1)S(1)} %collective-permute-done.2.refs_0_), channel_id=1, source_target_pairs={{0,121},{1,8},{2,123},{3,10},{4,125},{5,12},{6,127},{7,14},{8,1},{... | collective-permute-start | bytes 786440 | tf_op jit(solution)/shard_map/ppermute | solution.py:24
  123.8 2.3 sum_back.1
  126.1 1.2 collective-permute-start.24
  127.3 4.7 %collective-permute-done.4.refs_2_ = bf16[2,256,256]{2,1,0:T(8,128)(2,1)S(1)} collective-permute-done((bf16[2,256,256]{2,1,0:T(8,128)(2,1)S(1)}, bf16[2,256,256]{2,1,0:T(8,128)(2,1)S(1)}, u32[]{:S(2)}, u32[]{:S(2)}) %collective-permute-start.4) | collective-permute-done | bytes 262176 | tf_op jit(solution)/shard_map/ppermute | solution.py:24
  132.1 0.7 copy-done.14
  132.7 0.1 copy-done.15
  132.9 1.0 copy-done
  133.8 12.0 %shard_map.61 = (s16[2,272,256]{2,1,0:T(8,128)(2,1)}, s16[2,272,256]{2,1,0:T(8,128)(2,1)}, s16[2,272,256]{2,1,0:T(8,128)(2,1)}, s16[2,272,256]{2,1,0:T(8,128)(2,1)}) custom-call(s32[4]{0:T(128)} %pad_add_fusion.ids_ref, f32[2]{0:T(128)} %fusion.weight_ref, s32[2,1,2048]{2,1,0:T(1,128)} %copy-done.30, bf16[2,2048,2048]{2,1,0:T(8,128)(2,1)} %tiles_ref.7, ...), custom_call_target="tpu_custom_call" | custom-call | flops 4294967296 | bytes 11534336 | tf_op jit(solution)/shard_map/pallas_call | solution.py:124
  145.9 2.5 %collective-permute-start.17 = (s16[2,272,256]{2,1,0:T(8,128)(2,1)}, s16[2,272,256]{2,1,0:T(8,128)(2,1)S(1)}, u32[]{:S(2)}, u32[]{:S(2)}) collective-permute-start(s16[2,272,256]{2,1,0:T(8,128)(2,1)} %get-tuple-element.23), channel_id=1, source_target_pairs={{0,4},{1,5},{2,6},{3,7},{4,0},{5,1},{6,2},{7,3},{8,12},{9,13},{10,... | collective-permute-start | bytes 835592 | tf_op jit(solution)/shard_map/ppermute | solution.py:24
  148.4 7.7 %collective-permute-start.19 = (s16[2,272,256]{2,1,0:T(8,128)(2,1)}, s16[2,272,256]{2,1,0:T(8,128)(2,1)S(1)}, u32[]{:S(2)}, u32[]{:S(2)}) collective-permute-start(s16[2,272,256]{2,1,0:T(8,128)(2,1)} %get-tuple-element.25), channel_id=1, source_target_pairs={{0,6},{1,7},{2,4},{3,5},{4,2},{5,3},{6,0},{7,1},{8,14},{9,15},{10,... | collective-permute-start | bytes 835592 | tf_op jit(solution)/shard_map/ppermute | solution.py:24
  156.1 3.4 %collective-permute-start.20 = (s16[2,272,256]{2,1,0:T(8,128)(2,1)}, s16[2,272,256]{2,1,0:T(8,128)(2,1)S(1)}, u32[]{:S(2)}, u32[]{:S(2)}) collective-permute-start(s16[2,272,256]{2,1,0:T(8,128)(2,1)} %get-tuple-element.26), channel_id=1, source_target_pairs={{0,7},{1,6},{2,5},{3,4},{4,3},{5,2},{6,1},{7,0},{8,15},{9,14},{10,... | collective-permute-start | bytes 835592 | tf_op jit(solution)/shard_map/ppermute | solution.py:24
  159.6 12.4 %shard_map.60 = (s16[2,272,256]{2,1,0:T(8,128)(2,1)}, s16[2,272,256]{2,1,0:T(8,128)(2,1)}, s16[2,272,256]{2,1,0:T(8,128)(2,1)}, s16[2,272,256]{2,1,0:T(8,128)(2,1)}) custom-call(s32[4]{0:T(128)} %pad_add_fusion.ids_ref, f32[2]{0:T(128)} %fusion.weight_ref, s32[2,1,2048]{2,1,0:T(1,128)} %copy-done.30, bf16[2,2048,2048]{2,1,0:T(8,128)(2,1)} %tiles_ref.7, ...), custom_call_target="tpu_custom_call" | custom-call | flops 4294967296 | bytes 11534336 | tf_op jit(solution)/shard_map/pallas_call | solution.py:124
  172.0 1.9 collective-permute-start.14
  173.9 2.2 collective-permute-start.15
  176.1 0.6 collective-permute-start.16
  176.8 3.7 %collective-permute-done.14.refs_1_ = s16[2,272,256]{2,1,0:T(8,128)(2,1)S(1)} collective-permute-done((s16[2,272,256]{2,1,0:T(8,128)(2,1)}, s16[2,272,256]{2,1,0:T(8,128)(2,1)S(1)}, u32[]{:S(2)}, u32[]{:S(2)}) %collective-permute-start.14) | collective-permute-done | bytes 278560 | tf_op jit(solution)/shard_map/ppermute | solution.py:24
  180.5 5.2 %collective-permute-done.15.refs_2_ = s16[2,272,256]{2,1,0:T(8,128)(2,1)S(1)} collective-permute-done((s16[2,272,256]{2,1,0:T(8,128)(2,1)}, s16[2,272,256]{2,1,0:T(8,128)(2,1)S(1)}, u32[]{:S(2)}, u32[]{:S(2)}) %collective-permute-start.15) | collective-permute-done | bytes 278560 | tf_op jit(solution)/shard_map/ppermute | solution.py:24
  185.7 2.6 %collective-permute-done.16.refs_3_ = s16[2,272,256]{2,1,0:T(8,128)(2,1)S(1)} collective-permute-done((s16[2,272,256]{2,1,0:T(8,128)(2,1)}, s16[2,272,256]{2,1,0:T(8,128)(2,1)S(1)}, u32[]{:S(2)}, u32[]{:S(2)}) %collective-permute-start.16) | collective-permute-done | bytes 278560 | tf_op jit(solution)/shard_map/ppermute | solution.py:24
  188.4 0.7 copy-done.26
  189.1 3.7 %gram.1 = (f32[2,256,256]{2,1,0:T(8,128)}, f32[256,256]{1,0:T(8,128)}, f32[384,128]{1,0:T(8,128)}) custom-call(s32[4]{0:T(128)} %pad_add_fusion.ids_ref, s16[2,272,256]{2,1,0:T(8,128)(2,1)} %get-tuple-element.19.refs_0_, s16[2,272,256]{2,1,0:T(8,128)(2,1)} %copy-done.24, s16[2,272,256]{2,1,0:T(8,128)(2,1)} %copy-done.25, s16[2,272,256]{2,1,0:T(8,128)(2,1)} %copy-done.26, ...), custom_call_target="tpu_custom_call" | custom-call | tf_op jit(solution)/shard_map/gram/pallas_call | solution.py:179
  192.8 2.5 %collective-permute-start.25 = (f32[256,256]{1,0:T(8,128)}, f32[256,256]{1,0:T(8,128)S(1)}, u32[]{:S(2)}, u32[]{:S(2)}) collective-permute-start(f32[256,256]{1,0:T(8,128)} %get-tuple-element.32.other_ref), channel_id=1, source_target_pairs={{0,4},{1,5},{2,6},{3,7},{4,0},{5,1},{6,2},{7,3},{8,12},{9,13},{10,... | collective-permute-start | bytes 786440 | tf_op jit(solution)/shard_map/ppermute | solution.py:24
  195.3 0.3 collective-permute-start.28
  195.6 2.2 collective-permute-start.27
  197.8 1.6 collective-permute-start.26
  199.4 6.0 %collective-permute-done.28.refs_3_ = f32[384,128]{1,0:T(8,128)S(1)} collective-permute-done((f32[384,128]{1,0:T(8,128)}, f32[384,128]{1,0:T(8,128)S(1)}, u32[]{:S(2)}, u32[]{:S(2)}) %collective-permute-start.28) | collective-permute-done | bytes 196640 | tf_op jit(solution)/shard_map/ppermute | solution.py:24
  205.4 0.6 collective-permute-done.26.refs_1_
  206.2 0.6 copy-done.29
  206.7 19.0 %orthogonal.1 = (f32[2,256,256]{2,1,0:T(8,128)}, f32[256,256]{1,0:T(8,128)}) custom-call(s32[4]{0:T(128)} %pad_add_fusion.ids_ref, f32[2,256,256]{2,1,0:T(8,128)} %get-tuple-element.31.samples_ref, f32[256,256]{1,0:T(8,128)} %get-tuple-element.32.other_ref, f32[384,128]{1,0:T(8,128)} %get-tuple-element.33.refs_0_, f32[384,128]{1,0:T(8,128)} %copy-done.29, ...), custom_call_target="tpu_custom_call" | custom-call | tf_op jit(solution)/shard_map/orthogonal/pallas_call | solution.py:292
  225.7 1.3 collective-permute-start.29
  227.1 7.0 %collective-permute-done.29 = f32[256,256]{1,0:T(8,128)S(1)} collective-permute-done((f32[256,256]{1,0:T(8,128)}, f32[256,256]{1,0:T(8,128)S(1)}, u32[]{:S(2)}, u32[]{:S(2)}) %collective-permute-start.29) | collective-permute-done | bytes 262176 | tf_op jit(solution)/shard_map/ppermute | solution.py:24
  234.1 0.7 bitcast_dynamic-update-slice_fusion
  (78 shorter events, 0.3 us)
Async XLA Ops:
  0.6 14.0 %collective-permute-start.10 = (bf16[2,256,256]{2,1,0:T(8,128)(2,1)}, bf16[2,256,256]{2,1,0:T(8,128)(2,1)S(1)}, u32[]{:S(2)}, u32[]{:S(2)}) collective-permute-start(bf16[2,256,256]{2,1,0:T(8,128)(2,1)} %refs_0_.3), channel_id=1, source_target_pairs={{0,6},{1,7},{2,4},{3,5},{4,2},{5,3},{6,0},{7,1},{8,14},{9,15},{10,... | collective-permute-start | bytes 786440 | tf_op jit(solution)/shard_map/ppermute | solution.py:24
  7.2 14.0 %collective-permute-start.9 = (bf16[2,256,256]{2,1,0:T(8,128)(2,1)}, bf16[2,256,256]{2,1,0:T(8,128)(2,1)S(1)}, u32[]{:S(2)}, u32[]{:S(2)}) collective-permute-start(bf16[2,256,256]{2,1,0:T(8,128)(2,1)} %refs_0_.3), channel_id=1, source_target_pairs={{0,5},{1,4},{2,7},{3,6},{4,1},{5,0},{6,3},{7,2},{8,13},{9,12},{10,... | collective-permute-start | bytes 786440 | tf_op jit(solution)/shard_map/ppermute | solution.py:24
  8.1 15.9 %collective-permute-start.8 = (bf16[2,256,256]{2,1,0:T(8,128)(2,1)}, bf16[2,256,256]{2,1,0:T(8,128)(2,1)S(1)}, u32[]{:S(2)}, u32[]{:S(2)}) collective-permute-start(bf16[2,256,256]{2,1,0:T(8,128)(2,1)} %refs_0_.3), channel_id=1, source_target_pairs={{0,3},{1,2},{2,1},{3,0},{4,7},{5,6},{6,5},{7,4},{8,11},{9,10},{10,... | collective-permute-start | bytes 786440 | tf_op jit(solution)/shard_map/ppermute | solution.py:24
  8.1 17.2 %collective-permute-start.7 = (bf16[2,256,256]{2,1,0:T(8,128)(2,1)}, bf16[2,256,256]{2,1,0:T(8,128)(2,1)S(1)}, u32[]{:S(2)}, u32[]{:S(2)}) collective-permute-start(bf16[2,256,256]{2,1,0:T(8,128)(2,1)} %refs_0_.3), channel_id=1, source_target_pairs={{0,2},{1,3},{2,0},{3,1},{4,6},{5,7},{6,4},{7,5},{8,10},{9,11},{10,... | collective-permute-start | bytes 786440 | tf_op jit(solution)/shard_map/ppermute | solution.py:24
  11.2 20.3 %collective-permute-start.6 = (bf16[2,256,256]{2,1,0:T(8,128)(2,1)}, bf16[2,256,256]{2,1,0:T(8,128)(2,1)S(1)}, u32[]{:S(2)}, u32[]{:S(2)}) collective-permute-start(bf16[2,256,256]{2,1,0:T(8,128)(2,1)} %refs_0_.3), channel_id=1, source_target_pairs={{0,1},{1,0},{2,3},{3,2},{4,5},{5,4},{6,7},{7,6},{8,9},{9,8},{10,11... | collective-permute-start | bytes 786440 | tf_op jit(solution)/shard_map/ppermute | solution.py:24
  14.6 16.8 %copy-start.2 = (bf16[2,256,256]{2,1,0:T(8,128)(2,1)}, bf16[2,256,256]{2,1,0:T(8,128)(2,1)S(1)}, u32[]{:S(2)}) copy-start(bf16[2,256,256]{2,1,0:T(8,128)(2,1)S(1)} %collective-permute-done.10.refs_6_) | copy-start | bytes 786436
  14.6 16.8 %collective-permute-start.1 = (bf16[2,256,256]{2,1,0:T(8,128)(2,1)}, bf16[2,256,256]{2,1,0:T(8,128)(2,1)S(1)}, u32[]{:S(2)}, u32[]{:S(2)}) collective-permute-start(bf16[2,256,256]{2,1,0:T(8,128)(2,1)} %refs_0_.3), channel_id=1, source_target_pairs={{0,4},{1,5},{2,6},{3,7},{4,0},{5,1},{6,2},{7,3},{8,12},{9,13},{10,... | collective-permute-start | bytes 786440 | tf_op jit(solution)/shard_map/ppermute | solution.py:24
  21.2 10.3 %copy-start.4 = (bf16[2,256,256]{2,1,0:T(8,128)(2,1)}, bf16[2,256,256]{2,1,0:T(8,128)(2,1)S(1)}, u32[]{:S(2)}) copy-start(bf16[2,256,256]{2,1,0:T(8,128)(2,1)S(1)} %collective-permute-done.9.refs_5_) | copy-start | bytes 786436
  21.2 10.3 %collective-permute-start.11 = (bf16[2,256,256]{2,1,0:T(8,128)(2,1)}, bf16[2,256,256]{2,1,0:T(8,128)(2,1)S(1)}, u32[]{:S(2)}, u32[]{:S(2)}) collective-permute-start(bf16[2,256,256]{2,1,0:T(8,128)(2,1)} %refs_0_.3), channel_id=1, source_target_pairs={{0,7},{1,6},{2,5},{3,4},{4,3},{5,2},{6,1},{7,0},{8,15},{9,14},{10,... | collective-permute-start | bytes 786440 | tf_op jit(solution)/shard_map/ppermute | solution.py:24
  24.0 7.5 %copy-start.6 = (bf16[2,256,256]{2,1,0:T(8,128)(2,1)}, bf16[2,256,256]{2,1,0:T(8,128)(2,1)S(1)}, u32[]{:S(2)}) copy-start(bf16[2,256,256]{2,1,0:T(8,128)(2,1)S(1)} %collective-permute-done.8.refs_3_) | copy-start | bytes 786436
  24.0 55.0 %collective-permute-start = (s32[2,1,2048]{2,1,0:T(1,128)}, s32[2,1,2048]{2,1,0:T(1,128)S(1)}, u32[]{:S(2)}, u32[]{:S(2)}) collective-permute-start(s32[2,1,2048]{2,1,0:T(1,128)} %perm_ref.3), channel_id=1, source_target_pairs={{0,0},{1,121},{2,114},{3,107},{4,100},{5,93},{6,86},{7,79},{8,8},{... | collective-permute-start | bytes 49160 | tf_op jit(solution)/shard_map/ppermute | solution.py:24
  25.3 6.2 %copy-start.7 = (bf16[2,256,256]{2,1,0:T(8,128)(2,1)}, bf16[2,256,256]{2,1,0:T(8,128)(2,1)S(1)}, u32[]{:S(2)}) copy-start(bf16[2,256,256]{2,1,0:T(8,128)(2,1)S(1)} %collective-permute-done.7.refs_2_) | copy-start | bytes 786436
  31.5 0.7 copy-start.8
  31.5 0.8 copy-start.1
  32.2 0.7 copy-start.9
  45.8 8.4 %copy-start.5 = (bf16[2,256,256]{2,1,0:T(8,128)(2,1)S(1)}, bf16[2,256,256]{2,1,0:T(8,128)(2,1)}, u32[]{:S(2)}) copy-start(bf16[2,256,256]{2,1,0:T(8,128)(2,1)} %copy-done.4) | copy-start | bytes 786436
  45.8 9.0 %copy-start.3 = (bf16[2,256,256]{2,1,0:T(8,128)(2,1)S(1)}, bf16[2,256,256]{2,1,0:T(8,128)(2,1)}, u32[]{:S(2)}) copy-start(bf16[2,256,256]{2,1,0:T(8,128)(2,1)} %copy-done.2) | copy-start | bytes 786436
  45.8 9.7 %copy-start.10 = (bf16[2,256,256]{2,1,0:T(8,128)(2,1)S(1)}, bf16[2,256,256]{2,1,0:T(8,128)(2,1)}, u32[]{:S(2)}) copy-start(bf16[2,256,256]{2,1,0:T(8,128)(2,1)} %copy-done.9) | copy-start | bytes 786436
  45.8 110.3 %collective-permute-start.13 = (s16[4,2,272,256]{3,2,1,0:T(8,128)(2,1)}, s16[4,2,272,256]{3,2,1,0:T(8,128)(2,1)S(1)}, u32[]{:S(2)}, u32[]{:S(2)}) collective-permute-start(s16[4,2,272,256]{3,2,1,0:T(8,128)(2,1)} %shard_map.59), channel_id=1, source_target_pairs={{0,0},{1,9},{2,18},{3,27},{4,36},{5,45},{6,54},{7,63},{8,8},{9,17}... | collective-permute-start | bytes 3342344 | tf_op jit(solution)/shard_map/ppermute | solution.py:24
  56.1 75.9 %collective-permute-start.12 = (bf16[8,256,256]{2,1,0:T(8,128)(2,1)}, bf16[8,256,256]{2,1,0:T(8,128)(2,1)S(1)}, u32[]{:S(2)}, u32[]{:S(2)}) collective-permute-start(bf16[8,256,256]{2,1,0:T(8,128)(2,1)} %slice_dynamic-update-slice_fusion), channel_id=1, source_target_pairs={{0,0},{1,121},{2,114},{3,107},{4,100},{5,93},{6,86},{7,79},{8,8},{... | collective-permute-start | bytes 3145736 | tf_op jit(solution)/shard_map/ppermute | solution.py:24
  58.0 24.4 %collective-permute-start.2 = (bf16[2,256,256]{2,1,0:T(8,128)(2,1)S(1)}, bf16[2,256,256]{2,1,0:T(8,128)(2,1)S(1)}, u32[]{:S(2)}, u32[]{:S(2)}) collective-permute-start(bf16[2,256,256]{2,1,0:T(8,128)(2,1)S(1)} %pad_maximum_fusion), channel_id=1, source_target_pairs={{0,0},{1,121},{2,114},{3,107},{4,100},{5,93},{6,86},{7,79},{8,8},{... | collective-permute-start | bytes 786440 | tf_op jit(solution)/shard_map/ppermute | solution.py:24
  71.3 13.7 %collective-permute-start.21 = (s16[2,272,256]{2,1,0:T(8,128)(2,1)}, s16[2,272,256]{2,1,0:T(8,128)(2,1)S(1)}, u32[]{:S(2)}, u32[]{:S(2)}) collective-permute-start(s16[2,272,256]{2,1,0:T(8,128)(2,1)} %get-tuple-element.28), channel_id=1, source_target_pairs={{0,121},{1,8},{2,123},{3,10},{4,125},{5,12},{6,127},{7,14},{8,1},{... | collective-permute-start | bytes 835592 | tf_op jit(solution)/shard_map/ppermute | solution.py:24
  78.9 53.1 %copy-start.30 = (s32[2,1,2048]{2,1,0:T(1,128)}, s32[2,1,2048]{2,1,0:T(1,128)S(1)}, u32[]{:S(2)}) copy-start(s32[2,1,2048]{2,1,0:T(1,128)S(1)} %collective-permute-done.perm_ref) | copy-start | bytes 49156
  78.9 40.9 %collective-permute-start.22 = (s16[2,272,256]{2,1,0:T(8,128)(2,1)}, s16[2,272,256]{2,1,0:T(8,128)(2,1)}, u32[]{:S(2)}, u32[]{:S(2)}) collective-permute-start(s16[2,272,256]{2,1,0:T(8,128)(2,1)} %get-tuple-element.29), channel_id=1, source_target_pairs={{0,114},{1,115},{2,16},{3,17},{4,118},{5,119},{6,20},{7,21},{8,122... | collective-permute-start | bytes 835592 | tf_op jit(solution)/shard_map/ppermute | solution.py:24
  82.4 49.7 %copy-start.12 = (bf16[2,256,256]{2,1,0:T(8,128)(2,1)}, bf16[2,256,256]{2,1,0:T(8,128)(2,1)S(1)}, u32[]{:S(2)}) copy-start(bf16[2,256,256]{2,1,0:T(8,128)(2,1)S(1)} %collective-permute-done.2.refs_0_) | copy-start | bytes 786436
  82.4 37.4 %collective-permute-start.23 = (s16[2,272,256]{2,1,0:T(8,128)(2,1)}, s16[2,272,256]{2,1,0:T(8,128)(2,1)}, u32[]{:S(2)}, u32[]{:S(2)}) collective-permute-start(s16[2,272,256]{2,1,0:T(8,128)(2,1)} %get-tuple-element.30), channel_id=1, source_target_pairs={{0,107},{1,122},{2,9},{3,24},{4,111},{5,126},{6,13},{7,28},{8,115}... | collective-permute-start | bytes 835592 | tf_op jit(solution)/shard_map/ppermute | solution.py:24
  85.1 38.7 %copy-start.18 = (s16[2,272,256]{2,1,0:T(8,128)(2,1)}, s16[2,272,256]{2,1,0:T(8,128)(2,1)S(1)}, u32[]{:S(2)}) copy-start(s16[2,272,256]{2,1,0:T(8,128)(2,1)S(1)} %collective-permute-done.21.refs_1_) | copy-start | bytes 835588
  85.1 41.0 %collective-permute-start.5 = (bf16[2,256,256]{2,1,0:T(8,128)(2,1)S(1)}, bf16[2,256,256]{2,1,0:T(8,128)(2,1)S(1)}, u32[]{:S(2)}, u32[]{:S(2)}) collective-permute-start(bf16[2,256,256]{2,1,0:T(8,128)(2,1)S(1)} %collective-permute-done.2.refs_0_), channel_id=1, source_target_pairs={{0,107},{1,122},{2,9},{3,24},{4,111},{5,126},{6,13},{7,28},{8,115}... | collective-permute-start | bytes 786440 | tf_op jit(solution)/shard_map/ppermute | solution.py:24
  119.8 12.2 %collective-permute-start.4 = (bf16[2,256,256]{2,1,0:T(8,128)(2,1)S(1)}, bf16[2,256,256]{2,1,0:T(8,128)(2,1)S(1)}, u32[]{:S(2)}, u32[]{:S(2)}) collective-permute-start(bf16[2,256,256]{2,1,0:T(8,128)(2,1)S(1)} %collective-permute-done.2.refs_0_), channel_id=1, source_target_pairs={{0,114},{1,115},{2,16},{3,17},{4,118},{5,119},{6,20},{7,21},{8,122... | collective-permute-start | bytes 786440 | tf_op jit(solution)/shard_map/ppermute | solution.py:24
  119.8 12.2 %collective-permute-start.3 = (bf16[2,256,256]{2,1,0:T(8,128)(2,1)S(1)}, bf16[2,256,256]{2,1,0:T(8,128)(2,1)S(1)}, u32[]{:S(2)}, u32[]{:S(2)}) collective-permute-start(bf16[2,256,256]{2,1,0:T(8,128)(2,1)S(1)} %collective-permute-done.2.refs_0_), channel_id=1, source_target_pairs={{0,121},{1,8},{2,123},{3,10},{4,125},{5,12},{6,127},{7,14},{8,1},{... | collective-permute-start | bytes 786440 | tf_op jit(solution)/shard_map/ppermute | solution.py:24
  126.1 6.0 %copy-start.13 = (bf16[2,256,256]{2,1,0:T(8,128)(2,1)}, bf16[2,256,256]{2,1,0:T(8,128)(2,1)S(1)}, u32[]{:S(2)}) copy-start(bf16[2,256,256]{2,1,0:T(8,128)(2,1)S(1)} %collective-permute-done.5.refs_3_) | copy-start | bytes 786436
  126.1 45.9 %collective-permute-start.24 = (s16[2,272,256]{2,1,0:T(8,128)(2,1)}, s16[2,272,256]{2,1,0:T(8,128)(2,1)S(1)}, u32[]{:S(2)}, u32[]{:S(2)}) collective-permute-start(s16[2,272,256]{2,1,0:T(8,128)(2,1)} %sum_back.1), channel_id=1, source_target_pairs={{0,4},{1,13},{2,22},{3,31},{4,32},{5,41},{6,50},{7,59},{8,12},{9,2... | collective-permute-start | bytes 835592 | tf_op jit(solution)/shard_map/ppermute | solution.py:24
  132.0 0.7 copy-start.14
  132.0 0.8 copy-start.15
  132.9 1.0 copy-start
  145.9 28.0 %collective-permute-start.17 = (s16[2,272,256]{2,1,0:T(8,128)(2,1)}, s16[2,272,256]{2,1,0:T(8,128)(2,1)S(1)}, u32[]{:S(2)}, u32[]{:S(2)}) collective-permute-start(s16[2,272,256]{2,1,0:T(8,128)(2,1)} %get-tuple-element.23), channel_id=1, source_target_pairs={{0,4},{1,5},{2,6},{3,7},{4,0},{5,1},{6,2},{7,3},{8,12},{9,13},{10,... | collective-permute-start | bytes 835592 | tf_op jit(solution)/shard_map/ppermute | solution.py:24
  148.4 27.7 %collective-permute-start.18 = (s16[2,272,256]{2,1,0:T(8,128)(2,1)}, s16[2,272,256]{2,1,0:T(8,128)(2,1)S(1)}, u32[]{:S(2)}, u32[]{:S(2)}) collective-permute-start(s16[2,272,256]{2,1,0:T(8,128)(2,1)} %get-tuple-element.24), channel_id=1, source_target_pairs={{0,5},{1,4},{2,7},{3,6},{4,1},{5,0},{6,3},{7,2},{8,13},{9,12},{10,... | collective-permute-start | bytes 835592 | tf_op jit(solution)/shard_map/ppermute | solution.py:24
  148.4 28.4 %collective-permute-start.19 = (s16[2,272,256]{2,1,0:T(8,128)(2,1)}, s16[2,272,256]{2,1,0:T(8,128)(2,1)S(1)}, u32[]{:S(2)}, u32[]{:S(2)}) collective-permute-start(s16[2,272,256]{2,1,0:T(8,128)(2,1)} %get-tuple-element.25), channel_id=1, source_target_pairs={{0,6},{1,7},{2,4},{3,5},{4,2},{5,3},{6,0},{7,1},{8,14},{9,15},{10,... | collective-permute-start | bytes 835592 | tf_op jit(solution)/shard_map/ppermute | solution.py:24
  156.1 3.4 %copy-start.11 = (s16[4,2,272,256]{3,2,1,0:T(8,128)(2,1)}, s16[4,2,272,256]{3,2,1,0:T(8,128)(2,1)S(1)}, u32[]{:S(2)}) copy-start(s16[4,2,272,256]{3,2,1,0:T(8,128)(2,1)S(1)} %collective-permute-done.13.refs_5_) | copy-start | bytes 3342340
  156.1 20.6 %collective-permute-start.20 = (s16[2,272,256]{2,1,0:T(8,128)(2,1)}, s16[2,272,256]{2,1,0:T(8,128)(2,1)S(1)}, u32[]{:S(2)}, u32[]{:S(2)}) collective-permute-start(s16[2,272,256]{2,1,0:T(8,128)(2,1)} %get-tuple-element.26), channel_id=1, source_target_pairs={{0,7},{1,6},{2,5},{3,4},{4,3},{5,2},{6,1},{7,0},{8,15},{9,14},{10,... | collective-permute-start | bytes 835592 | tf_op jit(solution)/shard_map/ppermute | solution.py:24
  172.0 16.4 %copy-start.19 = (s16[2,272,256]{2,1,0:T(8,128)(2,1)}, s16[2,272,256]{2,1,0:T(8,128)(2,1)S(1)}, u32[]{:S(2)}) copy-start(s16[2,272,256]{2,1,0:T(8,128)(2,1)S(1)} %collective-permute-done.24.refs_8_) | copy-start | bytes 835588
  172.0 8.5 %collective-permute-start.14 = (s16[2,272,256]{2,1,0:T(8,128)(2,1)}, s16[2,272,256]{2,1,0:T(8,128)(2,1)S(1)}, u32[]{:S(2)}, u32[]{:S(2)}) collective-permute-start(s16[2,272,256]{2,1,0:T(8,128)(2,1)} %get-tuple-element.20), channel_id=1, source_target_pairs={{0,1},{1,0},{2,3},{3,2},{4,5},{5,4},{6,7},{7,6},{8,9},{9,8},{10,11... | collective-permute-start | bytes 835592 | tf_op jit(solution)/shard_map/ppermute | solution.py:24
  173.9 14.5 %copy-start.20 = (s16[2,272,256]{2,1,0:T(8,128)(2,1)}, s16[2,272,256]{2,1,0:T(8,128)(2,1)S(1)}, u32[]{:S(2)}) copy-start(s16[2,272,256]{2,1,0:T(8,128)(2,1)S(1)} %collective-permute-done.17.refs_4_) | copy-start | bytes 835588
  173.9 11.8 %collective-permute-start.15 = (s16[2,272,256]{2,1,0:T(8,128)(2,1)}, s16[2,272,256]{2,1,0:T(8,128)(2,1)S(1)}, u32[]{:S(2)}, u32[]{:S(2)}) collective-permute-start(s16[2,272,256]{2,1,0:T(8,128)(2,1)} %get-tuple-element.21), channel_id=1, source_target_pairs={{0,2},{1,3},{2,0},{3,1},{4,6},{5,7},{6,4},{7,5},{8,10},{9,11},{10,... | collective-permute-start | bytes 835592 | tf_op jit(solution)/shard_map/ppermute | solution.py:24
  176.1 12.3 %copy-start.21 = (s16[2,272,256]{2,1,0:T(8,128)(2,1)}, s16[2,272,256]{2,1,0:T(8,128)(2,1)S(1)}, u32[]{:S(2)}) copy-start(s16[2,272,256]{2,1,0:T(8,128)(2,1)S(1)} %collective-permute-done.18.refs_5_) | copy-start | bytes 835588
  176.1 12.2 %collective-permute-start.16 = (s16[2,272,256]{2,1,0:T(8,128)(2,1)}, s16[2,272,256]{2,1,0:T(8,128)(2,1)S(1)}, u32[]{:S(2)}, u32[]{:S(2)}) collective-permute-start(s16[2,272,256]{2,1,0:T(8,128)(2,1)} %get-tuple-element.22), channel_id=1, source_target_pairs={{0,3},{1,2},{2,1},{3,0},{4,7},{5,6},{6,5},{7,4},{8,11},{9,10},{10,... | collective-permute-start | bytes 835592 | tf_op jit(solution)/shard_map/ppermute | solution.py:24
  176.8 11.6 %copy-start.22 = (s16[2,272,256]{2,1,0:T(8,128)(2,1)}, s16[2,272,256]{2,1,0:T(8,128)(2,1)S(1)}, u32[]{:S(2)}) copy-start(s16[2,272,256]{2,1,0:T(8,128)(2,1)S(1)} %collective-permute-done.19.refs_6_) | copy-start | bytes 835588
  176.8 11.6 %copy-start.23 = (s16[2,272,256]{2,1,0:T(8,128)(2,1)}, s16[2,272,256]{2,1,0:T(8,128)(2,1)S(1)}, u32[]{:S(2)}) copy-start(s16[2,272,256]{2,1,0:T(8,128)(2,1)S(1)} %collective-permute-done.20.refs_7_) | copy-start | bytes 835588
  180.5 7.9 %copy-start.24 = (s16[2,272,256]{2,1,0:T(8,128)(2,1)}, s16[2,272,256]{2,1,0:T(8,128)(2,1)S(1)}, u32[]{:S(2)}) copy-start(s16[2,272,256]{2,1,0:T(8,128)(2,1)S(1)} %collective-permute-done.14.refs_1_) | copy-start | bytes 835588
  185.7 2.7 %copy-start.25 = (s16[2,272,256]{2,1,0:T(8,128)(2,1)}, s16[2,272,256]{2,1,0:T(8,128)(2,1)S(1)}, u32[]{:S(2)}) copy-start(s16[2,272,256]{2,1,0:T(8,128)(2,1)S(1)} %collective-permute-done.15.refs_2_) | copy-start | bytes 835588
  188.4 0.7 copy-start.26
  192.8 34.2 %copy-start.16 = (f32[2,256,256]{2,1,0:T(8,128)S(1)}, f32[2,256,256]{2,1,0:T(8,128)}, u32[]{:S(2)}) copy-start(f32[2,256,256]{2,1,0:T(8,128)} %get-tuple-element.31.samples_ref) | copy-start | bytes 1572868
  192.8 34.2 %collective-permute-start.25 = (f32[256,256]{1,0:T(8,128)}, f32[256,256]{1,0:T(8,128)S(1)}, u32[]{:S(2)}, u32[]{:S(2)}) collective-permute-start(f32[256,256]{1,0:T(8,128)} %get-tuple-element.32.other_ref), channel_id=1, source_target_pairs={{0,4},{1,5},{2,6},{3,7},{4,0},{5,1},{6,2},{7,3},{8,12},{9,13},{10,... | collective-permute-start | bytes 786440 | tf_op jit(solution)/shard_map/ppermute | solution.py:24
  195.3 10.1 %collective-permute-start.28 = (f32[384,128]{1,0:T(8,128)}, f32[384,128]{1,0:T(8,128)S(1)}, u32[]{:S(2)}, u32[]{:S(2)}) collective-permute-start(f32[384,128]{1,0:T(8,128)} %get-tuple-element.33.refs_0_), channel_id=1, source_target_pairs={{0,3},{1,2},{2,1},{3,0},{4,7},{5,6},{6,5},{7,4},{8,11},{9,10},{10,... | collective-permute-start | bytes 589832 | tf_op jit(solution)/shard_map/ppermute | solution.py:24
  195.6 9.8 %collective-permute-start.27 = (f32[384,128]{1,0:T(8,128)}, f32[384,128]{1,0:T(8,128)S(1)}, u32[]{:S(2)}, u32[]{:S(2)}) collective-permute-start(f32[384,128]{1,0:T(8,128)} %get-tuple-element.33.refs_0_), channel_id=1, source_target_pairs={{0,2},{1,3},{2,0},{3,1},{4,6},{5,7},{6,4},{7,5},{8,10},{9,11},{10,... | collective-permute-start | bytes 589832 | tf_op jit(solution)/shard_map/ppermute | solution.py:24
  197.8 8.2 %collective-permute-start.26 = (f32[384,128]{1,0:T(8,128)}, f32[384,128]{1,0:T(8,128)S(1)}, u32[]{:S(2)}, u32[]{:S(2)}) collective-permute-start(f32[384,128]{1,0:T(8,128)} %get-tuple-element.33.refs_0_), channel_id=1, source_target_pairs={{0,1},{1,0},{2,3},{3,2},{4,5},{5,4},{6,7},{7,6},{8,9},{9,8},{10,11... | collective-permute-start | bytes 589832 | tf_op jit(solution)/shard_map/ppermute | solution.py:24
  205.4 0.7 copy-start.27
  205.4 0.7 copy-start.28
  206.0 0.7 copy-start.29
  225.7 8.4 %collective-permute-start.29 = (f32[256,256]{1,0:T(8,128)}, f32[256,256]{1,0:T(8,128)S(1)}, u32[]{:S(2)}, u32[]{:S(2)}) collective-permute-start(f32[256,256]{1,0:T(8,128)} %get-tuple-element.35), channel_id=1, source_target_pairs={{0,4},{1,5},{2,6},{3,7},{4,0},{5,1},{6,2},{7,3},{8,12},{9,13},{10,... | collective-permute-start | bytes 786440 | tf_op jit(solution)/shard_map/ppermute | solution.py:24
  227.0 7.7 %copy-start.17 = (f32[2,256,256]{2,1,0:T(8,128)}, f32[2,256,256]{2,1,0:T(8,128)S(1)}, u32[]{:S(2)}) copy-start(f32[2,256,256]{2,1,0:T(8,128)S(1)} %bitcast_dynamic-update-slice_fusion.1) | copy-start | bytes 1572868

commit v3 on v1

--- a/solution.py
+++ b/solution.py
@@ -122,7 +122,7 @@
             pltpu.VMEM((probes, length) if back else (length, probes), jnp.bfloat16),
             pltpu.SemaphoreType.DMA((length // 512,)),
         ],
-        compiler_params=pltpu.CompilerParams(vmem_limit_bytes=56 << 20),
+        compiler_params=pltpu.CompilerParams(vmem_limit_bytes=40 << 20),
         cost_estimate=pl.CostEstimate(flops=4 * length * length * probes, bytes_accessed=11 << 20, transcendentals=0),
     )(ids, weight, perm, *pairs, plane, cross, tiles, *more)
 
@@ -314,14 +314,16 @@
     depths = range(1, nz)
     other = sent(probe[0], same(nz))
     singles = [sent(probe[1], same(d)) for d in depths]
+    far_own = sent(probe[0], far)
+    far_other = sent(probe[0], lambda r, c: (r - (c ^ nz), c ^ nz))
+    far_perm = sent(cluster_perm, far)
+
     pair = jnp.stack([probe[0], other])
     line = jnp.stack([probe[1], *singles])
+    far_pair = jnp.stack([far_own, far_other])
+    cross = sent(line, same(nz))
+    far_line = sent(line, far)
     pairs = [sent(pair, same(d)) for d in depths]
-    cross = sent(line, same(nz))
-
-    far_pair = sent(pair, far)
-    far_line = sent(line, far)
-    far_perm = sent(cluster_perm, far)
     far_pairs = [sent(far_pair, slanted(d)) for d in depths]
     far_cross = sent(cross, far)
 

time: 212 us -> 214 us (level)
  waiting for transfers between devices: 50.7 us -> 72.6 us
  starting transfers between devices: 88.8 us -> 78.4 us
  Pallas kernels: 59.8 us -> 53.9 us
  local copies, waits for them, and re-layouts: 7.13 us -> 4.57 us
    ppermute x32 -> x33, waiting for transfers between devices: 50.7 us -> 72.6 us  [sent(): return lax.ppermute(value, AXES, pairs)]
    ppermute x32 -> x33, starting transfers between devices: 88.8 us -> 78.4 us  [sent(): return lax.ppermute(value, AXES, pairs)]
    pallas_call x4, Pallas kernels: 34.8 us -> 29 us  [products(): pl.pallas_call(functools.partial(product_kernel, back, part), out_shape=[...]
    unnamed x64 -> x40, local copies, waits for them, and re-layouts: 5.38 us -> 2.82 us
  transfers between devices with their start and end apart: 32 -> 33, of which waited for: 10 -> 10; matrix products, arithmetic and copies ran while one was open for 1% -> 0% of each run, Pallas kernels for 27% -> 24%
where the time goes in v3:
time: 214 us; the launch traced here: 211 us
  starting transfers between devices  78.4 us (37%)
  waiting for transfers between devices  72.6 us (34%)
  Pallas kernels  53.9 us (25%)
  local copies, waits for them, and re-layouts  4.57 us (2%)
    ppermute x33, starting transfers between devices, sent(): return lax.ppermute(value, AXES, pairs)  78.4 us
    ppermute x33, waiting for transfers between devices, sent(): return lax.ppermute(value, AXES, pairs)  72.6 us
    pallas_call x4, Pallas kernels, products(): pl.pallas_call(functools.partial(product_kernel, back, part), out_shape=[...  29 us
    pallas_call x1, Pallas kernels, orthogonal(): pl.pallas_call(functools.partial(factor_kernel, scale), in_specs=[pl.Bloc...  19 us
  transfers between devices with their start and end apart: 33, of which 10 were waited for; matrix products, arithmetic and copies ran while one was open for 0% of the time, Pallas kernels for 24%

profile of v3, /device:TPU:0, one launch (start us, length us, event | category | flops | bytes accessed | tf_op | source)
XLA Modules:
  0.0 210.7 jit_solution(9652996752908893308)
XLA Ops:
  0.6 1.0 fusion.1
  1.7 0.0 copy-start.2
  1.7 4.2 %collective-permute-start.8 = (bf16[256,256]{1,0:T(8,128)(2,1)S(1)}, bf16[256,256]{1,0:T(8,128)(2,1)S(1)}, u32[]{:S(2)}, u32[]{:S(2)}) collective-permute-start(bf16[256,256]{1,0:T(8,128)(2,1)S(1)} %get-tuple-element.46), channel_id=1, source_target_pairs={{0,3},{1,2},{2,1},{3,0},{4,7},{5,6},{6,5},{7,4},{8,11},{9,10},{10,... | collective-permute-start | bytes 393224 | tf_op jit(solution)/shard_map/ppermute | solution.py:24
  5.9 0.9 collective-permute-start.6
  6.8 3.0 %collective-permute-start.12 = (bf16[256,256]{1,0:T(8,128)(2,1)S(1)}, bf16[256,256]{1,0:T(8,128)(2,1)S(1)}, u32[]{:S(2)}, u32[]{:S(2)}) collective-permute-start(bf16[256,256]{1,0:T(8,128)(2,1)S(1)} %get-tuple-element.45), channel_id=1, source_target_pairs={{0,4},{1,5},{2,6},{3,7},{4,0},{5,1},{6,2},{7,3},{8,12},{9,13},{10,... | collective-permute-start | bytes 393224 | tf_op jit(solution)/shard_map/ppermute | solution.py:24
  9.9 3.0 %collective-permute-start.2 = (bf16[256,256]{1,0:T(8,128)(2,1)S(1)}, bf16[256,256]{1,0:T(8,128)(2,1)S(1)}, u32[]{:S(2)}, u32[]{:S(2)}) collective-permute-start(bf16[256,256]{1,0:T(8,128)(2,1)S(1)} %get-tuple-element.45), channel_id=1, source_target_pairs={{0,100},{1,93},{2,86},{3,79},{4,0},{5,121},{6,114},{7,107},{8,108}... | collective-permute-start | bytes 393224 | tf_op jit(solution)/shard_map/ppermute | solution.py:24
  12.8 0.0 collective-permute-done.8
  12.8 0.7 collective-permute-start.1
  13.5 0.3 collective-permute-done.7
  13.8 0.0 collective-permute-done.6
  13.8 0.1 pad_maximum_fusion.refs_4_
  13.8 5.7 %collective-permute-start.10 = (bf16[4,256,256]{2,1,0:T(8,128)(2,1)S(1)}, bf16[4,256,256]{2,1,0:T(8,128)(2,1)S(1)}, u32[]{:S(2)}, u32[]{:S(2)}) collective-permute-start(bf16[4,256,256]{2,1,0:T(8,128)(2,1)S(1)} %pad_maximum_fusion.refs_4_), channel_id=1, source_target_pairs={{0,4},{1,5},{2,6},{3,7},{4,0},{5,1},{6,2},{7,3},{8,12},{9,13},{10,... | collective-permute-start | bytes 1572872 | tf_op jit(solution)/shard_map/ppermute | solution.py:24
  19.6 0.0 collective-permute-done.12
  19.6 3.2 %collective-permute-start.15 = (bf16[2,256,256]{2,1,0:T(8,128)(2,1)S(1)}, bf16[2,256,256]{2,1,0:T(8,128)(2,1)S(1)}, u32[]{:S(2)}, u32[]{:S(2)}) collective-permute-start(bf16[2,256,256]{2,1,0:T(8,128)(2,1)S(1)} %pad_maximum_fusion.2.refs_0_), channel_id=1, source_target_pairs={{0,3},{1,2},{2,1},{3,0},{4,7},{5,6},{6,5},{7,4},{8,11},{9,10},{10,... | collective-permute-start | bytes 786440 | tf_op jit(solution)/shard_map/ppermute | solution.py:24
  22.8 0.1 collective-permute-start.14
  22.9 0.0 collective-permute-done.2
  22.9 0.9 collective-permute-start.13
  23.8 0.1 pad_add_fusion.ids_ref
  23.9 3.7 %collective-permute-start.5 = (bf16[2,256,256]{2,1,0:T(8,128)(2,1)S(1)}, bf16[2,256,256]{2,1,0:T(8,128)(2,1)S(1)}, u32[]{:S(2)}, u32[]{:S(2)}) collective-permute-start(bf16[2,256,256]{2,1,0:T(8,128)(2,1)S(1)} %pad_maximum_fusion.1.refs_0_), channel_id=1, source_target_pairs={{0,107},{1,122},{2,9},{3,24},{4,111},{5,126},{6,13},{7,28},{8,115}... | collective-permute-start | bytes 786440 | tf_op jit(solution)/shard_map/ppermute | solution.py:24
  27.6 13.3 %collective-permute-done.15.refs_3_ = bf16[2,256,256]{2,1,0:T(8,128)(2,1)S(1)} collective-permute-done((bf16[2,256,256]{2,1,0:T(8,128)(2,1)S(1)}, bf16[2,256,256]{2,1,0:T(8,128)(2,1)S(1)}, u32[]{:S(2)}, u32[]{:S(2)}) %collective-permute-start.15) | collective-permute-done | bytes 262176 | tf_op jit(solution)/shard_map/ppermute | solution.py:24
  40.9 0.0 collective-permute-start.4
  40.9 4.9 %collective-permute-start.3 = (bf16[2,256,256]{2,1,0:T(8,128)(2,1)S(1)}, bf16[2,256,256]{2,1,0:T(8,128)(2,1)S(1)}, u32[]{:S(2)}, u32[]{:S(2)}) collective-permute-start(bf16[2,256,256]{2,1,0:T(8,128)(2,1)S(1)} %pad_maximum_fusion.1.refs_0_), channel_id=1, source_target_pairs={{0,121},{1,8},{2,123},{3,10},{4,125},{5,12},{6,127},{7,14},{8,1},{... | collective-permute-start | bytes 786440 | tf_op jit(solution)/shard_map/ppermute | solution.py:24
  45.9 7.9 %shard_map.59 = s16[4,2,272,256]{3,2,1,0:T(8,128)(2,1)} custom-call(s32[4]{0:T(128)S(1)} %pad_add_fusion.ids_ref, f32[2]{0:T(128)S(1)} %fusion.weight_ref, s32[2,1,2048]{2,1,0:T(1,128)S(1)} %copy-done.2, bf16[2,256,256]{2,1,0:T(8,128)(2,1)S(1)} %pad_maximum_fusion.2.refs_0_, bf16[2,256,256]{2,1,0:T(8,128)(2,1)S(1)} %collective-permute-done.13.refs_1_, ...), custom_call_target="tpu_custom_call" | custom-call | flops 4294967296 | bytes 11534336 | tf_op jit(solution)/shard_map/pallas_call | solution.py:114
  53.8 9.8 %collective-permute-start.16 = (s16[4,2,272,256]{3,2,1,0:T(8,128)(2,1)}, s16[4,2,272,256]{3,2,1,0:T(8,128)(2,1)}, u32[]{:S(2)}, u32[]{:S(2)}) collective-permute-start(s16[4,2,272,256]{3,2,1,0:T(8,128)(2,1)} %shard_map.59), channel_id=1, source_target_pairs={{0,0},{1,9},{2,18},{3,27},{4,36},{5,45},{6,54},{7,63},{8,8},{9,17}... | collective-permute-start | bytes 3342344 | tf_op jit(solution)/shard_map/ppermute | solution.py:24
  63.6 6.8 %shard_map.62 = (s16[2,272,256]{2,1,0:T(8,128)(2,1)S(1)}, s16[2,272,256]{2,1,0:T(8,128)(2,1)S(1)}, s16[2,272,256]{2,1,0:T(8,128)(2,1)S(1)}, s16[2,272,256]{2,1,0:T(8,128)(2,1)S(1)}) custom-call(s32[4]{0:T(128)S(1)} %pad_add_fusion.ids_ref, f32[2]{0:T(128)S(1)} %fusion.weight_ref, s32[2,1,2048]{2,1,0:T(1,128)S(1)} %copy-done.2, ...), custom_call_target="tpu_custom_call" | custom-call | flops 4294967296 | bytes 11534336 | tf_op jit(solution)/shard_map/pallas_call | solution.py:114
  70.4 0.0 copy-start
  70.4 0.7 copy-done
  71.1 0.1 collective-permute-start.24
  71.2 0.7 collective-permute-start.9
  71.9 0.7 collective-permute-start.11
  72.6 0.3 collective-permute-start.25
  72.9 10.2 %collective-permute-done.24.refs_1_ = s16[2,272,256]{2,1,0:T(8,128)(2,1)S(1)} collective-permute-done((s16[2,272,256]{2,1,0:T(8,128)(2,1)S(1)}, s16[2,272,256]{2,1,0:T(8,128)(2,1)S(1)}, u32[]{:S(2)}, u32[]{:S(2)}) %collective-permute-start.24) | collective-permute-done | bytes 278560 | tf_op jit(solution)/shard_map/ppermute | solution.py:24
  83.2 6.9 %collective-permute-start.26 = (s16[2,272,256]{2,1,0:T(8,128)(2,1)S(1)}, s16[2,272,256]{2,1,0:T(8,128)(2,1)}, u32[]{:S(2)}, u32[]{:S(2)}) collective-permute-start(s16[2,272,256]{2,1,0:T(8,128)(2,1)S(1)} %get-tuple-element.38), channel_id=1, source_target_pairs={{0,107},{1,122},{2,9},{3,24},{4,111},{5,126},{6,13},{7,28},{8,115}... | collective-permute-start | bytes 835592 | tf_op jit(solution)/shard_map/ppermute | solution.py:24
  90.0 28.3 %collective-permute-done.25.refs_2_ = s16[2,272,256]{2,1,0:T(8,128)(2,1)S(1)} collective-permute-done((s16[2,272,256]{2,1,0:T(8,128)(2,1)S(1)}, s16[2,272,256]{2,1,0:T(8,128)(2,1)S(1)}, u32[]{:S(2)}, u32[]{:S(2)}) %collective-permute-start.25) | collective-permute-done | bytes 278560 | tf_op jit(solution)/shard_map/ppermute | solution.py:24
  118.4 0.8 collective-permute-start
  119.2 2.3 %sum_back.1 = s16[2,272,256]{2,1,0:T(8,128)(2,1)} custom-call(s16[2,272,256]{2,1,0:T(8,128)(2,1)} %copy-done, s16[2,272,256]{2,1,0:T(8,128)(2,1)} %copy-done.6, s16[2,272,256]{2,1,0:T(8,128)(2,1)} %copy-done.7, s16[2,272,256]{2,1,0:T(8,128)(2,1)} %collective-permute-done.26.refs_3_), custom_call_target="tpu_custom_call" | custom-call | tf_op jit(solution)/shard_map/sum_back/pallas_call | solution.py:140
  121.5 2.5 %collective-permute-start.27 = (s16[2,272,256]{2,1,0:T(8,128)(2,1)}, s16[2,272,256]{2,1,0:T(8,128)(2,1)S(1)}, u32[]{:S(2)}, u32[]{:S(2)}) collective-permute-start(s16[2,272,256]{2,1,0:T(8,128)(2,1)} %sum_back.1), channel_id=1, source_target_pairs={{0,4},{1,13},{2,22},{3,31},{4,32},{5,41},{6,50},{7,59},{8,12},{9,2... | collective-permute-start | bytes 835592 | tf_op jit(solution)/shard_map/ppermute | solution.py:24
  124.0 6.8 %shard_map.61 = (s16[2,272,256]{2,1,0:T(8,128)(2,1)S(1)}, s16[2,272,256]{2,1,0:T(8,128)(2,1)S(1)}, s16[2,272,256]{2,1,0:T(8,128)(2,1)S(1)}, s16[2,272,256]{2,1,0:T(8,128)(2,1)S(1)}) custom-call(s32[4]{0:T(128)S(1)} %pad_add_fusion.ids_ref, f32[2]{0:T(128)S(1)} %fusion.weight_ref, s32[2,1,2048]{2,1,0:T(1,128)S(1)} %collective-permute-done.perm_ref, ...), custom_call_target="tpu_custom_call" | custom-call | flops 4294967296 | bytes 11534336 | tf_op jit(solution)/shard_map/pallas_call | solution.py:114
  130.8 1.3 collective-permute-start.20
  132.0 0.7 collective-permute-start.22
  132.7 8.2 %collective-permute-start.23 = (s16[2,272,256]{2,1,0:T(8,128)(2,1)S(1)}, s16[2,272,256]{2,1,0:T(8,128)(2,1)S(1)}, u32[]{:S(2)}, u32[]{:S(2)}) collective-permute-start(s16[2,272,256]{2,1,0:T(8,128)(2,1)S(1)} %get-tuple-element.30), channel_id=1, source_target_pairs={{0,7},{1,6},{2,5},{3,4},{4,3},{5,2},{6,1},{7,0},{8,15},{9,14},{10,... | collective-permute-start | bytes 835592 | tf_op jit(solution)/shard_map/ppermute | solution.py:24
  140.9 7.5 %shard_map.60 = (s16[2,272,256]{2,1,0:T(8,128)(2,1)S(1)}, s16[2,272,256]{2,1,0:T(8,128)(2,1)S(1)}, s16[2,272,256]{2,1,0:T(8,128)(2,1)S(1)}, s16[2,272,256]{2,1,0:T(8,128)(2,1)S(1)}) custom-call(s32[4]{0:T(128)S(1)} %pad_add_fusion.ids_ref, f32[2]{0:T(128)S(1)} %fusion.weight_ref, s32[2,1,2048]{2,1,0:T(1,128)S(1)} %collective-permute-done.perm_ref, ...), custom_call_target="tpu_custom_call" | custom-call | flops 4294967296 | bytes 11534336 | tf_op jit(solution)/shard_map/pallas_call | solution.py:114
  148.4 0.0 copy-start.1
  148.5 0.7 copy-done.1
  149.2 8.0 %collective-permute-start.18 = (s16[2,272,256]{2,1,0:T(8,128)(2,1)S(1)}, s16[2,272,256]{2,1,0:T(8,128)(2,1)S(1)}, u32[]{:S(2)}, u32[]{:S(2)}) collective-permute-start(s16[2,272,256]{2,1,0:T(8,128)(2,1)S(1)} %get-tuple-element.25), channel_id=1, source_target_pairs={{0,2},{1,3},{2,0},{3,1},{4,6},{5,7},{6,4},{7,5},{8,10},{9,11},{10,... | collective-permute-start | bytes 835592 | tf_op jit(solution)/shard_map/ppermute | solution.py:24
  157.2 0.6 collective-permute-start.19
  157.8 6.9 %collective-permute-done.18.refs_2_ = s16[2,272,256]{2,1,0:T(8,128)(2,1)S(1)} collective-permute-done((s16[2,272,256]{2,1,0:T(8,128)(2,1)S(1)}, s16[2,272,256]{2,1,0:T(8,128)(2,1)S(1)}, u32[]{:S(2)}, u32[]{:S(2)}) %collective-permute-start.18) | collective-permute-done | bytes 278560 | tf_op jit(solution)/shard_map/ppermute | solution.py:24
  164.7 2.9 %collective-permute-done.19.refs_3_ = s16[2,272,256]{2,1,0:T(8,128)(2,1)S(1)} collective-permute-done((s16[2,272,256]{2,1,0:T(8,128)(2,1)S(1)}, s16[2,272,256]{2,1,0:T(8,128)(2,1)S(1)}, u32[]{:S(2)}, u32[]{:S(2)}) %collective-permute-start.19) | collective-permute-done | bytes 278560 | tf_op jit(solution)/shard_map/ppermute | solution.py:24
  167.7 0.7 copy-done.15
  168.3 3.7 %gram.1 = (f32[2,256,256]{2,1,0:T(8,128)}, f32[256,256]{1,0:T(8,128)}, f32[384,128]{1,0:T(8,128)}) custom-call(s32[4]{0:T(128)} %copy-done.3, s16[2,272,256]{2,1,0:T(8,128)(2,1)} %copy-done.1, s16[2,272,256]{2,1,0:T(8,128)(2,1)} %copy-done.13, s16[2,272,256]{2,1,0:T(8,128)(2,1)} %copy-done.14, s16[2,272,256]{2,1,0:T(8,128)(2,1)} %copy-done.15, ...), custom_call_target="tpu_custom_call" | custom-call | tf_op jit(solution)/shard_map/gram/pallas_call | solution.py:169
  172.1 1.0 collective-permute-start.31
  173.1 1.6 collective-permute-start.30
  174.7 1.6 collective-permute-start.29
  176.2 5.4 %collective-permute-done.31.refs_3_ = f32[384,128]{1,0:T(8,128)S(1)} collective-permute-done((f32[384,128]{1,0:T(8,128)}, f32[384,128]{1,0:T(8,128)S(1)}, u32[]{:S(2)}, u32[]{:S(2)}) %collective-permute-start.31) | collective-permute-done | bytes 196640 | tf_op jit(solution)/shard_map/ppermute | solution.py:24
  181.6 0.5 collective-permute-done.30.refs_2_
  182.1 0.2 collective-permute-done.29.refs_1_
  182.3 0.0 copy-done.16
  182.3 0.5 copy-done.17
  182.8 0.2 copy-done.18
  182.9 19.0 %orthogonal.1 = (f32[2,256,256]{2,1,0:T(8,128)}, f32[256,256]{1,0:T(8,128)}) custom-call(s32[4]{0:T(128)} %copy-done.3, f32[2,256,256]{2,1,0:T(8,128)} %get-tuple-element.39.samples_ref, f32[256,256]{1,0:T(8,128)} %get-tuple-element.40.other_ref, f32[384,128]{1,0:T(8,128)} %get-tuple-element.41.refs_0_, f32[384,128]{1,0:T(8,128)} %copy-done.18, ...), custom_call_target="tpu_custom_call" | custom-call | tf_op jit(solution)/shard_map/orthogonal/pallas_call | solution.py:282
  201.9 3.4 %collective-permute-start.32 = (f32[256,256]{1,0:T(8,128)}, f32[256,256]{1,0:T(8,128)S(1)}, u32[]{:S(2)}, u32[]{:S(2)}) collective-permute-start(f32[256,256]{1,0:T(8,128)} %get-tuple-element.43), channel_id=1, source_target_pairs={{0,4},{1,5},{2,6},{3,7},{4,0},{5,1},{6,2},{7,3},{8,12},{9,13},{10,... | collective-permute-start | bytes 786440 | tf_op jit(solution)/shard_map/ppermute | solution.py:24
  205.3 0.0 copy-start.5
  205.3 4.6 %collective-permute-done.32 = f32[256,256]{1,0:T(8,128)S(1)} collective-permute-done((f32[256,256]{1,0:T(8,128)}, f32[256,256]{1,0:T(8,128)S(1)}, u32[]{:S(2)}, u32[]{:S(2)}) %collective-permute-start.32) | collective-permute-done | bytes 262176 | tf_op jit(solution)/shard_map/ppermute | solution.py:24
  210.0 0.7 bitcast_dynamic-update-slice_fusion
  (57 shorter events, 0.2 us)
Async XLA Ops:
  0.6 23.2 %copy-start.19 = (s32[2,1,1]{0,2,1:T(1,128)S(1)}, s32[2,1,1]{0,2,1:T(1,128)}, u32[]{:S(2)}) copy-start(s32[2,1,1]{0,2,1:T(1,128)} %param.7) | copy-start | bytes 28
  1.7 44.2 %copy-start.2 = (s32[2,1,2048]{2,1,0:T(1,128)S(1)}, s32[2,1,2048]{2,1,0:T(1,128)}, u32[]{:S(2)}) copy-start(s32[2,1,2048]{2,1,0:T(1,128)} %perm_ref.3) | copy-start | bytes 49156
  1.7 11.2 %collective-permute-start.8 = (bf16[256,256]{1,0:T(8,128)(2,1)S(1)}, bf16[256,256]{1,0:T(8,128)(2,1)S(1)}, u32[]{:S(2)}, u32[]{:S(2)}) collective-permute-start(bf16[256,256]{1,0:T(8,128)(2,1)S(1)} %get-tuple-element.46), channel_id=1, source_target_pairs={{0,3},{1,2},{2,1},{3,0},{4,7},{5,6},{6,5},{7,4},{8,11},{9,10},{10,... | collective-permute-start | bytes 393224 | tf_op jit(solution)/shard_map/ppermute | solution.py:24
  5.9 7.9 %collective-permute-start.7 = (bf16[256,256]{1,0:T(8,128)(2,1)S(1)}, bf16[256,256]{1,0:T(8,128)(2,1)S(1)}, u32[]{:S(2)}, u32[]{:S(2)}) collective-permute-start(bf16[256,256]{1,0:T(8,128)(2,1)S(1)} %get-tuple-element.46), channel_id=1, source_target_pairs={{0,2},{1,3},{2,0},{3,1},{4,6},{5,7},{6,4},{7,5},{8,10},{9,11},{10,... | collective-permute-start | bytes 393224 | tf_op jit(solution)/shard_map/ppermute | solution.py:24
  5.9 7.9 %collective-permute-start.6 = (bf16[256,256]{1,0:T(8,128)(2,1)S(1)}, bf16[256,256]{1,0:T(8,128)(2,1)S(1)}, u32[]{:S(2)}, u32[]{:S(2)}) collective-permute-start(bf16[256,256]{1,0:T(8,128)(2,1)S(1)} %get-tuple-element.46), channel_id=1, source_target_pairs={{0,1},{1,0},{2,3},{3,2},{4,5},{5,4},{6,7},{7,6},{8,9},{9,8},{10,11... | collective-permute-start | bytes 393224 | tf_op jit(solution)/shard_map/ppermute | solution.py:24
  6.8 12.7 %collective-permute-start.12 = (bf16[256,256]{1,0:T(8,128)(2,1)S(1)}, bf16[256,256]{1,0:T(8,128)(2,1)S(1)}, u32[]{:S(2)}, u32[]{:S(2)}) collective-permute-start(bf16[256,256]{1,0:T(8,128)(2,1)S(1)} %get-tuple-element.45), channel_id=1, source_target_pairs={{0,4},{1,5},{2,6},{3,7},{4,0},{5,1},{6,2},{7,3},{8,12},{9,13},{10,... | collective-permute-start | bytes 393224 | tf_op jit(solution)/shard_map/ppermute | solution.py:24
  9.9 13.1 %collective-permute-start.2 = (bf16[256,256]{1,0:T(8,128)(2,1)S(1)}, bf16[256,256]{1,0:T(8,128)(2,1)S(1)}, u32[]{:S(2)}, u32[]{:S(2)}) collective-permute-start(bf16[256,256]{1,0:T(8,128)(2,1)S(1)} %get-tuple-element.45), channel_id=1, source_target_pairs={{0,100},{1,93},{2,86},{3,79},{4,0},{5,121},{6,114},{7,107},{8,108}... | collective-permute-start | bytes 393224 | tf_op jit(solution)/shard_map/ppermute | solution.py:24
  12.8 11.1 %collective-permute-start.1 = (bf16[256,256]{1,0:T(8,128)(2,1)S(1)}, bf16[256,256]{1,0:T(8,128)(2,1)S(1)}, u32[]{:S(2)}, u32[]{:S(2)}) collective-permute-start(bf16[256,256]{1,0:T(8,128)(2,1)S(1)} %get-tuple-element.45), channel_id=1, source_target_pairs={{0,0},{1,121},{2,114},{3,107},{4,100},{5,93},{6,86},{7,79},{8,8},{... | collective-permute-start | bytes 393224 | tf_op jit(solution)/shard_map/ppermute | solution.py:24
  13.8 32.0 %collective-permute-start.10 = (bf16[4,256,256]{2,1,0:T(8,128)(2,1)S(1)}, bf16[4,256,256]{2,1,0:T(8,128)(2,1)S(1)}, u32[]{:S(2)}, u32[]{:S(2)}) collective-permute-start(bf16[4,256,256]{2,1,0:T(8,128)(2,1)S(1)} %pad_maximum_fusion.refs_4_), channel_id=1, source_target_pairs={{0,4},{1,5},{2,6},{3,7},{4,0},{5,1},{6,2},{7,3},{8,12},{9,13},{10,... | collective-permute-start | bytes 1572872 | tf_op jit(solution)/shard_map/ppermute | solution.py:24
  19.6 21.3 %collective-permute-start.15 = (bf16[2,256,256]{2,1,0:T(8,128)(2,1)S(1)}, bf16[2,256,256]{2,1,0:T(8,128)(2,1)S(1)}, u32[]{:S(2)}, u32[]{:S(2)}) collective-permute-start(bf16[2,256,256]{2,1,0:T(8,128)(2,1)S(1)} %pad_maximum_fusion.2.refs_0_), channel_id=1, source_target_pairs={{0,3},{1,2},{2,1},{3,0},{4,7},{5,6},{6,5},{7,4},{8,11},{9,10},{10,... | collective-permute-start | bytes 786440 | tf_op jit(solution)/shard_map/ppermute | solution.py:24
  22.8 18.1 %collective-permute-start.14 = (bf16[2,256,256]{2,1,0:T(8,128)(2,1)S(1)}, bf16[2,256,256]{2,1,0:T(8,128)(2,1)S(1)}, u32[]{:S(2)}, u32[]{:S(2)}) collective-permute-start(bf16[2,256,256]{2,1,0:T(8,128)(2,1)S(1)} %pad_maximum_fusion.2.refs_0_), channel_id=1, source_target_pairs={{0,2},{1,3},{2,0},{3,1},{4,6},{5,7},{6,4},{7,5},{8,10},{9,11},{10,... | collective-permute-start | bytes 786440 | tf_op jit(solution)/shard_map/ppermute | solution.py:24
  22.9 22.9 %collective-permute-start.13 = (bf16[2,256,256]{2,1,0:T(8,128)(2,1)S(1)}, bf16[2,256,256]{2,1,0:T(8,128)(2,1)S(1)}, u32[]{:S(2)}, u32[]{:S(2)}) collective-permute-start(bf16[2,256,256]{2,1,0:T(8,128)(2,1)S(1)} %pad_maximum_fusion.2.refs_0_), channel_id=1, source_target_pairs={{0,1},{1,0},{2,3},{3,2},{4,5},{5,4},{6,7},{7,6},{8,9},{9,8},{10,11... | collective-permute-start | bytes 786440 | tf_op jit(solution)/shard_map/ppermute | solution.py:24
  23.9 117.1 %copy-start.3 = (s32[4]{0:T(128)}, s32[4]{0:T(128)S(1)}, u32[]{:S(2)}) copy-start(s32[4]{0:T(128)S(1)} %pad_add_fusion.ids_ref) | copy-start | bytes 52
  23.9 47.2 %collective-permute-start.5 = (bf16[2,256,256]{2,1,0:T(8,128)(2,1)S(1)}, bf16[2,256,256]{2,1,0:T(8,128)(2,1)S(1)}, u32[]{:S(2)}, u32[]{:S(2)}) collective-permute-start(bf16[2,256,256]{2,1,0:T(8,128)(2,1)S(1)} %pad_maximum_fusion.1.refs_0_), channel_id=1, source_target_pairs={{0,107},{1,122},{2,9},{3,24},{4,111},{5,126},{6,13},{7,28},{8,115}... | collective-permute-start | bytes 786440 | tf_op jit(solution)/shard_map/ppermute | solution.py:24
  40.9 30.2 %collective-permute-start.4 = (bf16[2,256,256]{2,1,0:T(8,128)(2,1)S(1)}, bf16[2,256,256]{2,1,0:T(8,128)(2,1)S(1)}, u32[]{:S(2)}, u32[]{:S(2)}) collective-permute-start(bf16[2,256,256]{2,1,0:T(8,128)(2,1)S(1)} %pad_maximum_fusion.1.refs_0_), channel_id=1, source_target_pairs={{0,114},{1,115},{2,16},{3,17},{4,118},{5,119},{6,20},{7,21},{8,122... | collective-permute-start | bytes 786440 | tf_op jit(solution)/shard_map/ppermute | solution.py:24
  40.9 30.2 %collective-permute-start.3 = (bf16[2,256,256]{2,1,0:T(8,128)(2,1)S(1)}, bf16[2,256,256]{2,1,0:T(8,128)(2,1)S(1)}, u32[]{:S(2)}, u32[]{:S(2)}) collective-permute-start(bf16[2,256,256]{2,1,0:T(8,128)(2,1)S(1)} %pad_maximum_fusion.1.refs_0_), channel_id=1, source_target_pairs={{0,121},{1,8},{2,123},{3,10},{4,125},{5,12},{6,127},{7,14},{8,1},{... | collective-permute-start | bytes 786440 | tf_op jit(solution)/shard_map/ppermute | solution.py:24
  53.8 79.0 %collective-permute-start.16 = (s16[4,2,272,256]{3,2,1,0:T(8,128)(2,1)}, s16[4,2,272,256]{3,2,1,0:T(8,128)(2,1)}, u32[]{:S(2)}, u32[]{:S(2)}) collective-permute-start(s16[4,2,272,256]{3,2,1,0:T(8,128)(2,1)} %shard_map.59), channel_id=1, source_target_pairs={{0,0},{1,9},{2,18},{3,27},{4,36},{5,45},{6,54},{7,63},{8,8},{9,17}... | collective-permute-start | bytes 3342344 | tf_op jit(solution)/shard_map/ppermute | solution.py:24
  70.4 0.7 copy-start
  71.1 12.0 %collective-permute-start.24 = (s16[2,272,256]{2,1,0:T(8,128)(2,1)S(1)}, s16[2,272,256]{2,1,0:T(8,128)(2,1)S(1)}, u32[]{:S(2)}, u32[]{:S(2)}) collective-permute-start(s16[2,272,256]{2,1,0:T(8,128)(2,1)S(1)} %get-tuple-element.36), channel_id=1, source_target_pairs={{0,121},{1,8},{2,123},{3,10},{4,125},{5,12},{6,127},{7,14},{8,1},{... | collective-permute-start | bytes 835592 | tf_op jit(solution)/shard_map/ppermute | solution.py:24
  71.2 52.8 %collective-permute-start.9 = (bf16[4,256,256]{2,1,0:T(8,128)(2,1)S(1)}, bf16[4,256,256]{2,1,0:T(8,128)(2,1)S(1)}, u32[]{:S(2)}, u32[]{:S(2)}) collective-permute-start(bf16[4,256,256]{2,1,0:T(8,128)(2,1)S(1)} %pad_maximum_fusion.refs_4_), channel_id=1, source_target_pairs={{0,0},{1,121},{2,114},{3,107},{4,100},{5,93},{6,86},{7,79},{8,8},{... | collective-permute-start | bytes 1572872 | tf_op jit(solution)/shard_map/ppermute | solution.py:24
  71.9 52.1 %collective-permute-start.11 = (bf16[4,256,256]{2,1,0:T(8,128)(2,1)S(1)}, bf16[4,256,256]{2,1,0:T(8,128)(2,1)S(1)}, u32[]{:S(2)}, u32[]{:S(2)}) collective-permute-start(bf16[4,256,256]{2,1,0:T(8,128)(2,1)S(1)} %collective-permute-done.10.refs_5_), channel_id=1, source_target_pairs={{0,0},{1,121},{2,114},{3,107},{4,100},{5,93},{6,86},{7,79},{8,8},{... | collective-permute-start | bytes 1572872 | tf_op jit(solution)/shard_map/ppermute | solution.py:24
  72.6 45.7 %collective-permute-start.25 = (s16[2,272,256]{2,1,0:T(8,128)(2,1)S(1)}, s16[2,272,256]{2,1,0:T(8,128)(2,1)S(1)}, u32[]{:S(2)}, u32[]{:S(2)}) collective-permute-start(s16[2,272,256]{2,1,0:T(8,128)(2,1)S(1)} %get-tuple-element.37), channel_id=1, source_target_pairs={{0,114},{1,115},{2,16},{3,17},{4,118},{5,119},{6,20},{7,21},{8,122... | collective-permute-start | bytes 835592 | tf_op jit(solution)/shard_map/ppermute | solution.py:24
  83.2 36.0 %copy-start.6 = (s16[2,272,256]{2,1,0:T(8,128)(2,1)}, s16[2,272,256]{2,1,0:T(8,128)(2,1)S(1)}, u32[]{:S(2)}) copy-start(s16[2,272,256]{2,1,0:T(8,128)(2,1)S(1)} %collective-permute-done.24.refs_1_) | copy-start | bytes 835588
  83.2 36.1 %collective-permute-start.26 = (s16[2,272,256]{2,1,0:T(8,128)(2,1)S(1)}, s16[2,272,256]{2,1,0:T(8,128)(2,1)}, u32[]{:S(2)}, u32[]{:S(2)}) collective-permute-start(s16[2,272,256]{2,1,0:T(8,128)(2,1)S(1)} %get-tuple-element.38), channel_id=1, source_target_pairs={{0,107},{1,122},{2,9},{3,24},{4,111},{5,126},{6,13},{7,28},{8,115}... | collective-permute-start | bytes 835592 | tf_op jit(solution)/shard_map/ppermute | solution.py:24
  118.3 0.9 copy-start.7
  118.4 5.6 %collective-permute-start = (s32[2,1,2048]{2,1,0:T(1,128)S(1)}, s32[2,1,2048]{2,1,0:T(1,128)S(1)}, u32[]{:S(2)}, u32[]{:S(2)}) collective-permute-start(s32[2,1,2048]{2,1,0:T(1,128)S(1)} %copy-done.2), channel_id=1, source_target_pairs={{0,0},{1,121},{2,114},{3,107},{4,100},{5,93},{6,86},{7,79},{8,8},{... | collective-permute-start | bytes 49160 | tf_op jit(solution)/shard_map/ppermute | solution.py:24
  121.5 27.6 %collective-permute-start.27 = (s16[2,272,256]{2,1,0:T(8,128)(2,1)}, s16[2,272,256]{2,1,0:T(8,128)(2,1)S(1)}, u32[]{:S(2)}, u32[]{:S(2)}) collective-permute-start(s16[2,272,256]{2,1,0:T(8,128)(2,1)} %sum_back.1), channel_id=1, source_target_pairs={{0,4},{1,13},{2,22},{3,31},{4,32},{5,41},{6,50},{7,59},{8,12},{9,2... | collective-permute-start | bytes 835592 | tf_op jit(solution)/shard_map/ppermute | solution.py:24
  130.8 18.4 %collective-permute-start.20 = (s16[2,272,256]{2,1,0:T(8,128)(2,1)S(1)}, s16[2,272,256]{2,1,0:T(8,128)(2,1)S(1)}, u32[]{:S(2)}, u32[]{:S(2)}) collective-permute-start(s16[2,272,256]{2,1,0:T(8,128)(2,1)S(1)} %get-tuple-element.27), channel_id=1, source_target_pairs={{0,4},{1,5},{2,6},{3,7},{4,0},{5,1},{6,2},{7,3},{8,12},{9,13},{10,... | collective-permute-start | bytes 835592 | tf_op jit(solution)/shard_map/ppermute | solution.py:24
  132.0 25.2 %collective-permute-start.21 = (s16[2,272,256]{2,1,0:T(8,128)(2,1)S(1)}, s16[2,272,256]{2,1,0:T(8,128)(2,1)S(1)}, u32[]{:S(2)}, u32[]{:S(2)}) collective-permute-start(s16[2,272,256]{2,1,0:T(8,128)(2,1)S(1)} %get-tuple-element.28), channel_id=1, source_target_pairs={{0,5},{1,4},{2,7},{3,6},{4,1},{5,0},{6,3},{7,2},{8,13},{9,12},{10,... | collective-permute-start | bytes 835592 | tf_op jit(solution)/shard_map/ppermute | solution.py:24
  132.0 25.7 %collective-permute-start.22 = (s16[2,272,256]{2,1,0:T(8,128)(2,1)S(1)}, s16[2,272,256]{2,1,0:T(8,128)(2,1)S(1)}, u32[]{:S(2)}, u32[]{:S(2)}) collective-permute-start(s16[2,272,256]{2,1,0:T(8,128)(2,1)S(1)} %get-tuple-element.29), channel_id=1, source_target_pairs={{0,6},{1,7},{2,4},{3,5},{4,2},{5,3},{6,0},{7,1},{8,14},{9,15},{10,... | collective-permute-start | bytes 835592 | tf_op jit(solution)/shard_map/ppermute | solution.py:24
  132.7 25.1 %collective-permute-start.23 = (s16[2,272,256]{2,1,0:T(8,128)(2,1)S(1)}, s16[2,272,256]{2,1,0:T(8,128)(2,1)S(1)}, u32[]{:S(2)}, u32[]{:S(2)}) collective-permute-start(s16[2,272,256]{2,1,0:T(8,128)(2,1)S(1)} %get-tuple-element.30), channel_id=1, source_target_pairs={{0,7},{1,6},{2,5},{3,4},{4,3},{5,2},{6,1},{7,0},{8,15},{9,14},{10,... | collective-permute-start | bytes 835592 | tf_op jit(solution)/shard_map/ppermute | solution.py:24
  148.4 0.7 copy-start.1
  149.2 18.5 %copy-start.8 = (s16[2,272,256]{2,1,0:T(8,128)(2,1)}, s16[2,272,256]{2,1,0:T(8,128)(2,1)S(1)}, u32[]{:S(2)}) copy-start(s16[2,272,256]{2,1,0:T(8,128)(2,1)S(1)} %collective-permute-done.27.refs_8_) | copy-start | bytes 835588
  149.2 8.7 %collective-permute-start.17 = (s16[2,272,256]{2,1,0:T(8,128)(2,1)S(1)}, s16[2,272,256]{2,1,0:T(8,128)(2,1)S(1)}, u32[]{:S(2)}, u32[]{:S(2)}) collective-permute-start(s16[2,272,256]{2,1,0:T(8,128)(2,1)S(1)} %get-tuple-element.24), channel_id=1, source_target_pairs={{0,1},{1,0},{2,3},{3,2},{4,5},{5,4},{6,7},{7,6},{8,9},{9,8},{10,11... | collective-permute-start | bytes 835592 | tf_op jit(solution)/shard_map/ppermute | solution.py:24
  149.2 18.5 %copy-start.9 = (s16[2,272,256]{2,1,0:T(8,128)(2,1)}, s16[2,272,256]{2,1,0:T(8,128)(2,1)S(1)}, u32[]{:S(2)}) copy-start(s16[2,272,256]{2,1,0:T(8,128)(2,1)S(1)} %collective-permute-done.20.refs_4_) | copy-start | bytes 835588
  149.2 15.5 %collective-permute-start.18 = (s16[2,272,256]{2,1,0:T(8,128)(2,1)S(1)}, s16[2,272,256]{2,1,0:T(8,128)(2,1)S(1)}, u32[]{:S(2)}, u32[]{:S(2)}) collective-permute-start(s16[2,272,256]{2,1,0:T(8,128)(2,1)S(1)} %get-tuple-element.25), channel_id=1, source_target_pairs={{0,2},{1,3},{2,0},{3,1},{4,6},{5,7},{6,4},{7,5},{8,10},{9,11},{10,... | collective-permute-start | bytes 835592 | tf_op jit(solution)/shard_map/ppermute | solution.py:24
  157.2 10.4 %copy-start.10 = (s16[2,272,256]{2,1,0:T(8,128)(2,1)}, s16[2,272,256]{2,1,0:T(8,128)(2,1)S(1)}, u32[]{:S(2)}) copy-start(s16[2,272,256]{2,1,0:T(8,128)(2,1)S(1)} %collective-permute-done.21.refs_5_) | copy-start | bytes 835588
  157.2 10.4 %collective-permute-start.19 = (s16[2,272,256]{2,1,0:T(8,128)(2,1)S(1)}, s16[2,272,256]{2,1,0:T(8,128)(2,1)S(1)}, u32[]{:S(2)}, u32[]{:S(2)}) collective-permute-start(s16[2,272,256]{2,1,0:T(8,128)(2,1)S(1)} %get-tuple-element.26), channel_id=1, source_target_pairs={{0,3},{1,2},{2,1},{3,0},{4,7},{5,6},{6,5},{7,4},{8,11},{9,10},{10,... | collective-permute-start | bytes 835592 | tf_op jit(solution)/shard_map/ppermute | solution.py:24
  157.8 9.8 %copy-start.11 = (s16[2,272,256]{2,1,0:T(8,128)(2,1)}, s16[2,272,256]{2,1,0:T(8,128)(2,1)S(1)}, u32[]{:S(2)}) copy-start(s16[2,272,256]{2,1,0:T(8,128)(2,1)S(1)} %collective-permute-done.22.refs_6_) | copy-start | bytes 835588
  157.8 9.8 %copy-start.12 = (s16[2,272,256]{2,1,0:T(8,128)(2,1)}, s16[2,272,256]{2,1,0:T(8,128)(2,1)S(1)}, u32[]{:S(2)}) copy-start(s16[2,272,256]{2,1,0:T(8,128)(2,1)S(1)} %collective-permute-done.23.refs_7_) | copy-start | bytes 835588
  157.8 9.8 %copy-start.13 = (s16[2,272,256]{2,1,0:T(8,128)(2,1)}, s16[2,272,256]{2,1,0:T(8,128)(2,1)S(1)}, u32[]{:S(2)}) copy-start(s16[2,272,256]{2,1,0:T(8,128)(2,1)S(1)} %collective-permute-done.17.refs_1_) | copy-start | bytes 835588
  164.7 2.9 %copy-start.14 = (s16[2,272,256]{2,1,0:T(8,128)(2,1)}, s16[2,272,256]{2,1,0:T(8,128)(2,1)S(1)}, u32[]{:S(2)}) copy-start(s16[2,272,256]{2,1,0:T(8,128)(2,1)S(1)} %collective-permute-done.18.refs_2_) | copy-start | bytes 835588
  167.6 0.7 copy-start.15
  172.1 33.2 %copy-start.4 = (f32[2,256,256]{2,1,0:T(8,128)S(1)}, f32[2,256,256]{2,1,0:T(8,128)}, u32[]{:S(2)}) copy-start(f32[2,256,256]{2,1,0:T(8,128)} %get-tuple-element.39.samples_ref) | copy-start | bytes 1572868
  172.1 33.2 %collective-permute-start.28 = (f32[256,256]{1,0:T(8,128)}, f32[256,256]{1,0:T(8,128)S(1)}, u32[]{:S(2)}, u32[]{:S(2)}) collective-permute-start(f32[256,256]{1,0:T(8,128)} %get-tuple-element.40.other_ref), channel_id=1, source_target_pairs={{0,4},{1,5},{2,6},{3,7},{4,0},{5,1},{6,2},{7,3},{8,12},{9,13},{10,... | collective-permute-start | bytes 786440 | tf_op jit(solution)/shard_map/ppermute | solution.py:24
  172.1 9.5 %collective-permute-start.31 = (f32[384,128]{1,0:T(8,128)}, f32[384,128]{1,0:T(8,128)S(1)}, u32[]{:S(2)}, u32[]{:S(2)}) collective-permute-start(f32[384,128]{1,0:T(8,128)} %get-tuple-element.41.refs_0_), channel_id=1, source_target_pairs={{0,3},{1,2},{2,1},{3,0},{4,7},{5,6},{6,5},{7,4},{8,11},{9,10},{10,... | collective-permute-start | bytes 589832 | tf_op jit(solution)/shard_map/ppermute | solution.py:24
  173.1 9.0 %collective-permute-start.30 = (f32[384,128]{1,0:T(8,128)}, f32[384,128]{1,0:T(8,128)S(1)}, u32[]{:S(2)}, u32[]{:S(2)}) collective-permute-start(f32[384,128]{1,0:T(8,128)} %get-tuple-element.41.refs_0_), channel_id=1, source_target_pairs={{0,2},{1,3},{2,0},{3,1},{4,6},{5,7},{6,4},{7,5},{8,10},{9,11},{10,... | collective-permute-start | bytes 589832 | tf_op jit(solution)/shard_map/ppermute | solution.py:24
  174.7 7.6 %collective-permute-start.29 = (f32[384,128]{1,0:T(8,128)}, f32[384,128]{1,0:T(8,128)S(1)}, u32[]{:S(2)}, u32[]{:S(2)}) collective-permute-start(f32[384,128]{1,0:T(8,128)} %get-tuple-element.41.refs_0_), channel_id=1, source_target_pairs={{0,1},{1,0},{2,3},{3,2},{4,5},{5,4},{6,7},{7,6},{8,9},{9,8},{10,11... | collective-permute-start | bytes 589832 | tf_op jit(solution)/shard_map/ppermute | solution.py:24
  181.6 0.7 copy-start.16
  182.1 0.7 copy-start.17
  182.3 0.7 copy-start.18
  201.9 8.1 %collective-permute-start.32 = (f32[256,256]{1,0:T(8,128)}, f32[256,256]{1,0:T(8,128)S(1)}, u32[]{:S(2)}, u32[]{:S(2)}) collective-permute-start(f32[256,256]{1,0:T(8,128)} %get-tuple-element.43), channel_id=1, source_target_pairs={{0,4},{1,5},{2,6},{3,7},{4,0},{5,1},{6,2},{7,3},{8,12},{9,13},{10,... | collective-permute-start | bytes 786440 | tf_op jit(solution)/shard_map/ppermute | solution.py:24
  205.3 5.4 %copy-start.5 = (f32[2,256,256]{2,1,0:T(8,128)}, f32[2,256,256]{2,1,0:T(8,128)S(1)}, u32[]{:S(2)}) copy-start(f32[2,256,256]{2,1,0:T(8,128)S(1)} %bitcast_dynamic-update-slice_fusion.1) | copy-start | bytes 1572868

commit v4 on v3

--- a/solution.py
+++ b/solution.py
@@ -127,17 +127,23 @@
     )(ids, weight, perm, *pairs, plane, cross, tiles, *more)
 
 
-def sum_kernel(*refs):
-    *in_refs, out_ref = refs
+def sum_kernel(count, *refs):
+    out_ref = refs[-1]
     for a in range(2):
-        total = decoded(in_refs[0][a])
-        for ref in in_refs[1:]:
+        total = decoded(refs[0][a])
+        for ref in refs[1:count]:
             total = total + decoded(ref[a])
         out_ref[a] = coded(total)
 
 
-def summed(codes):
-    return pl.pallas_call(sum_kernel, out_shape=jax.ShapeDtypeStruct(codes[0].shape, jnp.int16), name="sum_back")(*codes)
+def summed(codes, after=()):
+    vmem, unread = pl.BlockSpec(memory_space=pltpu.VMEM), pl.BlockSpec(memory_space=pl.ANY)
+    return pl.pallas_call(
+        functools.partial(sum_kernel, len(codes)),
+        in_specs=[vmem] * len(codes) + [unread] * len(after),
+        out_shape=jax.ShapeDtypeStruct(codes[0].shape, jnp.int16),
+        name="sum",
+    )(*codes, *after)
 
 
 def gram_kernel(ids_ref, *refs):
@@ -337,12 +343,12 @@
     back, far_pairs = lax.optimization_barrier((back, far_pairs))
     back = [back[0]] + [sent(back[d], slanted(d)) for d in depths]
     given = products(ids, weight, far_perm, *far_blocks, tiles, False, 1)
-    given = [sent(code, same(nz + d)) for d, code in enumerate(given)]
+    given = [given[0]] + [sent(given[d], same(d)) for d in depths]
     kept = products(ids, weight, far_perm, *far_blocks, tiles, False, 0, (more,))
+    arrived = sent(summed(back, kept[:1]), lambda r, c: (r + c, c))
     kept = [kept[0]] + [sent(kept[d], same(d)) for d in depths]
-    arrived = summed(back)
-    arrived = sent(arrived, lambda r, c: (r + c, c ^ nz))
-    samples, swapped, gram = gram_of(ids, [*kept, *given, arrived])
+    crossed = sent(summed([*given, arrived]), same(nz))
+    samples, swapped, gram = gram_of(ids, [*kept, crossed])
     grams = [gram] + [sent(gram, same(d)) for d in depths]
     basis, swapped_basis = orthogonal(ids, samples, swapped, grams, 1.0 / tile_len)
 

time: 214 us -> 207 us (0.967); the launches traced: 211 us -> 207 us
  starting transfers between devices: 78.4 us -> 74.7 us
  waiting for transfers between devices: 72.6 us -> 70.2 us
    ppermute x33, starting transfers between devices: 78.4 us -> 74.7 us  [sent(): return lax.ppermute(value, AXES, pairs)]
    pallas_call x1 -> x2, Pallas kernels: 2.29 us -> 4.75 us  [summed(): pl.pallas_call(functools.partial(sum_kernel, len(codes)), in_specs=[vmem]...]
    ppermute x33, waiting for transfers between devices: 72.6 us -> 70.2 us  [sent(): return lax.ppermute(value, AXES, pairs)]
    unnamed x40 -> x44, local copies, waits for them, and re-layouts: 2.82 us -> 4.47 us
  transfers between devices with their start and end apart: 33 -> 33, of which waited for: 10 -> 14; matrix products, arithmetic and copies ran while one was open for 0% -> 0% of each run, Pallas kernels for 24% -> 25%
where the time goes in v4:
time: 207 us
  starting transfers between devices  74.7 us (36%)
  waiting for transfers between devices  70.2 us (34%)
  Pallas kernels  54.2 us (26%)
  local copies, waits for them, and re-layouts  6.22 us (3%)
    ppermute x33, starting transfers between devices, sent(): return lax.ppermute(value, AXES, pairs)  74.7 us
    ppermute x33, waiting for transfers between devices, sent(): return lax.ppermute(value, AXES, pairs)  70.2 us
    pallas_call x4, Pallas kernels, products(): pl.pallas_call(functools.partial(product_kernel, back, part), out_shape=[...  27.4 us
    pallas_call x1, Pallas kernels, orthogonal(): pl.pallas_call(functools.partial(factor_kernel, scale), in_specs=[pl.Bloc...  19 us
    pallas_call x2, Pallas kernels, summed(): pl.pallas_call(functools.partial(sum_kernel, len(codes)), in_specs=[vmem]...  4.75 us
    unnamed x44, local copies, waits for them, and re-layouts  4.47 us
  transfers between devices with their start and end apart: 33, of which 14 were waited for; matrix products, arithmetic and copies ran while one was open for 0% of the time, Pallas kernels for 25%

profile of v4, /device:TPU:0, one launch (start us, length us, event | category | flops | bytes accessed | tf_op | source)
XLA Modules:
  0.0 206.5 jit_solution(10743214602095350023)
XLA Ops:
  0.7 1.0 fusion.1
  1.7 4.1 %collective-permute-start.7 = (bf16[256,256]{1,0:T(8,128)(2,1)S(1)}, bf16[256,256]{1,0:T(8,128)(2,1)S(1)}, u32[]{:S(2)}, u32[]{:S(2)}) collective-permute-start(bf16[256,256]{1,0:T(8,128)(2,1)S(1)} %get-tuple-element.46), channel_id=1, source_target_pairs={{0,2},{1,3},{2,0},{3,1},{4,6},{5,7},{6,4},{7,5},{8,10},{9,11},{10,... | collective-permute-start | bytes 393224 | tf_op jit(solution)/shard_map/ppermute | solution.py:24
  5.7 0.7 collective-permute-start.8
  6.4 0.3 collective-permute-start.6
  6.8 3.0 %collective-permute-start.12 = (bf16[256,256]{1,0:T(8,128)(2,1)S(1)}, bf16[256,256]{1,0:T(8,128)(2,1)S(1)}, u32[]{:S(2)}, u32[]{:S(2)}) collective-permute-start(bf16[256,256]{1,0:T(8,128)(2,1)S(1)} %get-tuple-element.45), channel_id=1, source_target_pairs={{0,4},{1,5},{2,6},{3,7},{4,0},{5,1},{6,2},{7,3},{8,12},{9,13},{10,... | collective-permute-start | bytes 393224 | tf_op jit(solution)/shard_map/ppermute | solution.py:24
  9.8 2.3 %collective-permute-done.8 = bf16[256,256]{1,0:T(8,128)(2,1)S(1)} collective-permute-done((bf16[256,256]{1,0:T(8,128)(2,1)S(1)}, bf16[256,256]{1,0:T(8,128)(2,1)S(1)}, u32[]{:S(2)}, u32[]{:S(2)}) %collective-permute-start.8) | collective-permute-done | bytes 131104 | tf_op jit(solution)/shard_map/ppermute | solution.py:24
  12.0 0.8 collective-permute-done.6
  12.8 0.1 pad_maximum_fusion.refs_4_
  12.9 3.1 %collective-permute-start.10 = (bf16[4,256,256]{2,1,0:T(8,128)(2,1)S(1)}, bf16[4,256,256]{2,1,0:T(8,128)(2,1)S(1)}, u32[]{:S(2)}, u32[]{:S(2)}) collective-permute-start(bf16[4,256,256]{2,1,0:T(8,128)(2,1)S(1)} %pad_maximum_fusion.refs_4_), channel_id=1, source_target_pairs={{0,4},{1,5},{2,6},{3,7},{4,0},{5,1},{6,2},{7,3},{8,12},{9,13},{10,... | collective-permute-start | bytes 1572872 | tf_op jit(solution)/shard_map/ppermute | solution.py:24
  16.0 0.7 collective-permute-start.1
  16.7 4.2 %collective-permute-start.13 = (bf16[2,256,256]{2,1,0:T(8,128)(2,1)S(1)}, bf16[2,256,256]{2,1,0:T(8,128)(2,1)S(1)}, u32[]{:S(2)}, u32[]{:S(2)}) collective-permute-start(bf16[2,256,256]{2,1,0:T(8,128)(2,1)S(1)} %pad_maximum_fusion.2.refs_0_), channel_id=1, source_target_pairs={{0,1},{1,0},{2,3},{3,2},{4,5},{5,4},{6,7},{7,6},{8,9},{9,8},{10,11... | collective-permute-start | bytes 786440 | tf_op jit(solution)/shard_map/ppermute | solution.py:24
  20.9 3.5 %collective-permute-start.14 = (bf16[2,256,256]{2,1,0:T(8,128)(2,1)S(1)}, bf16[2,256,256]{2,1,0:T(8,128)(2,1)S(1)}, u32[]{:S(2)}, u32[]{:S(2)}) collective-permute-start(bf16[2,256,256]{2,1,0:T(8,128)(2,1)S(1)} %pad_maximum_fusion.2.refs_0_), channel_id=1, source_target_pairs={{0,2},{1,3},{2,0},{3,1},{4,6},{5,7},{6,4},{7,5},{8,10},{9,11},{10,... | collective-permute-start | bytes 786440 | tf_op jit(solution)/shard_map/ppermute | solution.py:24
  24.5 0.1 pad_add_fusion.ids_ref
  24.5 2.2 %collective-permute-done.13.refs_1_ = bf16[2,256,256]{2,1,0:T(8,128)(2,1)S(1)} collective-permute-done((bf16[2,256,256]{2,1,0:T(8,128)(2,1)S(1)}, bf16[2,256,256]{2,1,0:T(8,128)(2,1)S(1)}, u32[]{:S(2)}, u32[]{:S(2)}) %collective-permute-start.13) | collective-permute-done | bytes 262176 | tf_op jit(solution)/shard_map/ppermute | solution.py:24
  26.7 3.9 %collective-permute-start.2 = (bf16[256,256]{1,0:T(8,128)(2,1)S(1)}, bf16[256,256]{1,0:T(8,128)(2,1)S(1)}, u32[]{:S(2)}, u32[]{:S(2)}) collective-permute-start(bf16[256,256]{1,0:T(8,128)(2,1)S(1)} %get-tuple-element.45), channel_id=1, source_target_pairs={{0,100},{1,93},{2,86},{3,79},{4,0},{5,121},{6,114},{7,107},{8,108}... | collective-permute-start | bytes 393224 | tf_op jit(solution)/shard_map/ppermute | solution.py:24
  30.7 6.5 %collective-permute-done.14.refs_2_ = bf16[2,256,256]{2,1,0:T(8,128)(2,1)S(1)} collective-permute-done((bf16[2,256,256]{2,1,0:T(8,128)(2,1)S(1)}, bf16[2,256,256]{2,1,0:T(8,128)(2,1)S(1)}, u32[]{:S(2)}, u32[]{:S(2)}) %collective-permute-start.14) | collective-permute-done | bytes 262176 | tf_op jit(solution)/shard_map/ppermute | solution.py:24
  37.2 2.6 %collective-permute-done.15.refs_3_ = bf16[2,256,256]{2,1,0:T(8,128)(2,1)S(1)} collective-permute-done((bf16[2,256,256]{2,1,0:T(8,128)(2,1)S(1)}, bf16[2,256,256]{2,1,0:T(8,128)(2,1)S(1)}, u32[]{:S(2)}, u32[]{:S(2)}) %collective-permute-start.15) | collective-permute-done | bytes 262176 | tf_op jit(solution)/shard_map/ppermute | solution.py:24
  39.8 6.8 %shard_map.59 = s16[4,2,272,256]{3,2,1,0:T(8,128)(2,1)S(1)} custom-call(s32[4]{0:T(128)S(1)} %pad_add_fusion.ids_ref, f32[2]{0:T(128)S(1)} %fusion.weight_ref, s32[2,1,2048]{2,1,0:T(1,128)S(1)} %copy-done.3, bf16[2,256,256]{2,1,0:T(8,128)(2,1)S(1)} %pad_maximum_fusion.2.refs_0_, bf16[2,256,256]{2,1,0:T(8,128)(2,1)S(1)} %collective-permute-done.13.refs_1_, ...), custom_call_target="tpu_custom_call" | custom-call | flops 4294967296 | bytes 11534336 | tf_op jit(solution)/shard_map/pallas_call | solution.py:114
  46.6 0.7 collective-permute-start.16
  47.4 3.1 %collective-permute-start.3 = (bf16[2,256,256]{2,1,0:T(8,128)(2,1)S(1)}, bf16[2,256,256]{2,1,0:T(8,128)(2,1)S(1)}, u32[]{:S(2)}, u32[]{:S(2)}) collective-permute-start(bf16[2,256,256]{2,1,0:T(8,128)(2,1)S(1)} %pad_maximum_fusion.1.refs_0_), channel_id=1, source_target_pairs={{0,121},{1,8},{2,123},{3,10},{4,125},{5,12},{6,127},{7,14},{8,1},{... | collective-permute-start | bytes 786440 | tf_op jit(solution)/shard_map/ppermute | solution.py:24
  50.5 2.7 %collective-permute-start.4 = (bf16[2,256,256]{2,1,0:T(8,128)(2,1)S(1)}, bf16[2,256,256]{2,1,0:T(8,128)(2,1)S(1)}, u32[]{:S(2)}, u32[]{:S(2)}) collective-permute-start(bf16[2,256,256]{2,1,0:T(8,128)(2,1)S(1)} %pad_maximum_fusion.1.refs_0_), channel_id=1, source_target_pairs={{0,114},{1,115},{2,16},{3,17},{4,118},{5,119},{6,20},{7,21},{8,122... | collective-permute-start | bytes 786440 | tf_op jit(solution)/shard_map/ppermute | solution.py:24
  53.2 0.7 collective-permute-start.9
  53.9 0.7 collective-permute-start.11
  54.6 25.1 %collective-permute-done.3.refs_1_ = bf16[2,256,256]{2,1,0:T(8,128)(2,1)S(1)} collective-permute-done((bf16[2,256,256]{2,1,0:T(8,128)(2,1)S(1)}, bf16[2,256,256]{2,1,0:T(8,128)(2,1)S(1)}, u32[]{:S(2)}, u32[]{:S(2)}) %collective-permute-start.3) | collective-permute-done | bytes 262176 | tf_op jit(solution)/shard_map/ppermute | solution.py:24
  79.7 0.7 collective-permute-start
  80.3 8.0 %collective-permute-done.4.refs_2_ = bf16[2,256,256]{2,1,0:T(8,128)(2,1)S(1)} collective-permute-done((bf16[2,256,256]{2,1,0:T(8,128)(2,1)S(1)}, bf16[2,256,256]{2,1,0:T(8,128)(2,1)S(1)}, u32[]{:S(2)}, u32[]{:S(2)}) %collective-permute-start.4) | collective-permute-done | bytes 262176 | tf_op jit(solution)/shard_map/ppermute | solution.py:24
  88.4 6.8 %shard_map.62 = (s16[2,272,256]{2,1,0:T(8,128)(2,1)S(1)}, s16[2,272,256]{2,1,0:T(8,128)(2,1)S(1)}, s16[2,272,256]{2,1,0:T(8,128)(2,1)S(1)}, s16[2,272,256]{2,1,0:T(8,128)(2,1)S(1)}) custom-call(s32[4]{0:T(128)S(1)} %pad_add_fusion.ids_ref, f32[2]{0:T(128)S(1)} %fusion.weight_ref, s32[2,1,2048]{2,1,0:T(1,128)S(1)} %copy-done.3, ...), custom_call_target="tpu_custom_call" | custom-call | flops 4294967296 | bytes 11534336 | tf_op jit(solution)/shard_map/pallas_call | solution.py:114
  95.2 0.7 copy-done.2
  95.9 1.6 collective-permute-done.5.refs_3_
  97.5 12.0 %collective-permute-start.24 = (s16[2,272,256]{2,1,0:T(8,128)(2,1)S(1)}, s16[2,272,256]{2,1,0:T(8,128)(2,1)S(1)}, u32[]{:S(2)}, u32[]{:S(2)}) collective-permute-start(s16[2,272,256]{2,1,0:T(8,128)(2,1)S(1)} %get-tuple-element.37), channel_id=1, source_target_pairs={{0,114},{1,115},{2,16},{3,17},{4,118},{5,119},{6,20},{7,21},{8,122... | collective-permute-start | bytes 835592 | tf_op jit(solution)/shard_map/ppermute | solution.py:24
  109.5 7.0 %shard_map.61 = (s16[2,272,256]{2,1,0:T(8,128)(2,1)S(1)}, s16[2,272,256]{2,1,0:T(8,128)(2,1)S(1)}, s16[2,272,256]{2,1,0:T(8,128)(2,1)S(1)}, s16[2,272,256]{2,1,0:T(8,128)(2,1)S(1)}) custom-call(s32[4]{0:T(128)S(1)} %pad_add_fusion.ids_ref, f32[2]{0:T(128)S(1)} %fusion.weight_ref, s32[2,1,2048]{2,1,0:T(1,128)S(1)} %collective-permute-done.perm_ref, ...), custom_call_target="tpu_custom_call" | custom-call | flops 4294967296 | bytes 11534336 | tf_op jit(solution)/shard_map/pallas_call | solution.py:114
  116.4 0.0 copy-start.1
  116.4 5.2 %collective-permute-start.20 = (s16[2,272,256]{2,1,0:T(8,128)(2,1)S(1)}, s16[2,272,256]{2,1,0:T(8,128)(2,1)S(1)}, u32[]{:S(2)}, u32[]{:S(2)}) collective-permute-start(s16[2,272,256]{2,1,0:T(8,128)(2,1)S(1)} %get-tuple-element.28), channel_id=1, source_target_pairs={{0,1},{1,0},{2,3},{3,2},{4,5},{5,4},{6,7},{7,6},{8,9},{9,8},{10,11... | collective-permute-start | bytes 835592 | tf_op jit(solution)/shard_map/ppermute | solution.py:24
  121.7 6.8 %shard_map.60 = (s16[2,272,256]{2,1,0:T(8,128)(2,1)S(1)}, s16[2,272,256]{2,1,0:T(8,128)(2,1)S(1)}, s16[2,272,256]{2,1,0:T(8,128)(2,1)S(1)}, s16[2,272,256]{2,1,0:T(8,128)(2,1)S(1)}) custom-call(s32[4]{0:T(128)S(1)} %pad_add_fusion.ids_ref, f32[2]{0:T(128)S(1)} %fusion.weight_ref, s32[2,1,2048]{2,1,0:T(1,128)S(1)} %collective-permute-done.perm_ref, ...), custom_call_target="tpu_custom_call" | custom-call | flops 4294967296 | bytes 11534336 | tf_op jit(solution)/shard_map/pallas_call | solution.py:114
  128.6 0.7 copy-done
  129.3 2.8 %collective-permute-start.22 = (s16[2,272,256]{2,1,0:T(8,128)(2,1)S(1)}, s16[2,272,256]{2,1,0:T(8,128)(2,1)S(1)}, u32[]{:S(2)}, u32[]{:S(2)}) collective-permute-start(s16[2,272,256]{2,1,0:T(8,128)(2,1)S(1)} %get-tuple-element.30), channel_id=1, source_target_pairs={{0,3},{1,2},{2,1},{3,0},{4,7},{5,6},{6,5},{7,4},{8,11},{9,10},{10,... | collective-permute-start | bytes 835592 | tf_op jit(solution)/shard_map/ppermute | solution.py:24
  132.1 0.7 copy-done.10
  132.7 0.1 copy-done.12
  132.9 2.3 %sum.2 = s16[2,272,256]{2,1,0:T(8,128)(2,1)} custom-call(s16[2,272,256]{2,1,0:T(8,128)(2,1)} %copy-done.2, s16[2,272,256]{2,1,0:T(8,128)(2,1)} %copy-done.9, s16[2,272,256]{2,1,0:T(8,128)(2,1)} %copy-done.10, s16[2,272,256]{2,1,0:T(8,128)(2,1)} %copy-done.12, s16[2,272,256]{2,1,0:T(8,128)(2,1)} %copy-done), custom_call_target="tpu_custom_call" | custom-call | tf_op jit(solution)/shard_map/sum/pallas_call | solution.py:141
  135.2 1.6 collective-permute-start.26
  136.8 1.1 collective-permute-start.17
  137.9 1.2 collective-permute-start.18
  139.1 2.4 %collective-permute-start.19 = (s16[2,272,256]{2,1,0:T(8,128)(2,1)S(1)}, s16[2,272,256]{2,1,0:T(8,128)(2,1)S(1)}, u32[]{:S(2)}, u32[]{:S(2)}) collective-permute-start(s16[2,272,256]{2,1,0:T(8,128)(2,1)S(1)} %get-tuple-element.26), channel_id=1, source_target_pairs={{0,3},{1,2},{2,1},{3,0},{4,7},{5,6},{6,5},{7,4},{8,11},{9,10},{10,... | collective-permute-start | bytes 835592 | tf_op jit(solution)/shard_map/ppermute | solution.py:24
  141.5 0.7 copy-done.13
  142.2 0.1 copy-done.16
  142.3 2.5 %sum.3 = s16[2,272,256]{2,1,0:T(8,128)(2,1)} custom-call(s16[2,272,256]{2,1,0:T(8,128)(2,1)} %copy-done.1, s16[2,272,256]{2,1,0:T(8,128)(2,1)} %copy-done.7, s16[2,272,256]{2,1,0:T(8,128)(2,1)} %copy-done.8, s16[2,272,256]{2,1,0:T(8,128)(2,1)} %copy-done.13, s16[2,272,256]{2,1,0:T(8,128)(2,1)} %copy-done.16), custom_call_target="tpu_custom_call" | custom-call | tf_op jit(solution)/shard_map/sum/pallas_call | solution.py:141
  144.8 7.7 %collective-permute-start.27 = (s16[2,272,256]{2,1,0:T(8,128)(2,1)}, s16[2,272,256]{2,1,0:T(8,128)(2,1)S(1)}, u32[]{:S(2)}, u32[]{:S(2)}) collective-permute-start(s16[2,272,256]{2,1,0:T(8,128)(2,1)} %sum.3), channel_id=1, source_target_pairs={{0,4},{1,5},{2,6},{3,7},{4,0},{5,1},{6,2},{7,3},{8,12},{9,13},{10,... | collective-permute-start | bytes 835592 | tf_op jit(solution)/shard_map/ppermute | solution.py:24
  152.5 0.0 collective-permute-done.18.refs_2_
  152.5 2.6 %collective-permute-done.19.refs_3_ = s16[2,272,256]{2,1,0:T(8,128)(2,1)S(1)} collective-permute-done((s16[2,272,256]{2,1,0:T(8,128)(2,1)S(1)}, s16[2,272,256]{2,1,0:T(8,128)(2,1)S(1)}, u32[]{:S(2)}, u32[]{:S(2)}) %collective-permute-start.19) | collective-permute-done | bytes 278560 | tf_op jit(solution)/shard_map/ppermute | solution.py:24
  155.1 3.7 %collective-permute-done.27.refs_4_ = s16[2,272,256]{2,1,0:T(8,128)(2,1)S(1)} collective-permute-done((s16[2,272,256]{2,1,0:T(8,128)(2,1)}, s16[2,272,256]{2,1,0:T(8,128)(2,1)S(1)}, u32[]{:S(2)}, u32[]{:S(2)}) %collective-permute-start.27) | collective-permute-done | bytes 278560 | tf_op jit(solution)/shard_map/ppermute | solution.py:24
  158.9 0.7 copy-done.17
  159.6 3.1 %gram.1 = (f32[2,256,256]{2,1,0:T(8,128)}, f32[256,256]{1,0:T(8,128)}, f32[384,128]{1,0:T(8,128)}) custom-call(s32[4]{0:T(128)} %copy-done.4, s16[2,272,256]{2,1,0:T(8,128)(2,1)} %copy-done, s16[2,272,256]{2,1,0:T(8,128)(2,1)} %copy-done.11, s16[2,272,256]{2,1,0:T(8,128)(2,1)} %copy-done.14, s16[2,272,256]{2,1,0:T(8,128)(2,1)} %copy-done.15, ...), custom_call_target="tpu_custom_call" | custom-call | tf_op jit(solution)/shard_map/gram/pallas_call | solution.py:175
  162.7 3.3 %collective-permute-start.28 = (f32[256,256]{1,0:T(8,128)}, f32[256,256]{1,0:T(8,128)S(1)}, u32[]{:S(2)}, u32[]{:S(2)}) collective-permute-start(f32[256,256]{1,0:T(8,128)} %get-tuple-element.40.other_ref), channel_id=1, source_target_pairs={{0,4},{1,5},{2,6},{3,7},{4,0},{5,1},{6,2},{7,3},{8,12},{9,13},{10,... | collective-permute-start | bytes 786440 | tf_op jit(solution)/shard_map/ppermute | solution.py:24
  165.9 1.2 collective-permute-start.30
  167.1 3.5 %collective-permute-start.31 = (f32[384,128]{1,0:T(8,128)}, f32[384,128]{1,0:T(8,128)S(1)}, u32[]{:S(2)}, u32[]{:S(2)}) collective-permute-start(f32[384,128]{1,0:T(8,128)} %get-tuple-element.41.refs_0_), channel_id=1, source_target_pairs={{0,3},{1,2},{2,1},{3,0},{4,7},{5,6},{6,5},{7,4},{8,11},{9,10},{10,... | collective-permute-start | bytes 589832 | tf_op jit(solution)/shard_map/ppermute | solution.py:24
  170.6 2.6 %collective-permute-done.29.refs_1_ = f32[384,128]{1,0:T(8,128)S(1)} collective-permute-done((f32[384,128]{1,0:T(8,128)}, f32[384,128]{1,0:T(8,128)S(1)}, u32[]{:S(2)}, u32[]{:S(2)}) %collective-permute-start.29) | collective-permute-done | bytes 196640 | tf_op jit(solution)/shard_map/ppermute | solution.py:24
  173.3 2.1 collective-permute-done.30.refs_2_
  175.3 2.5 %collective-permute-done.31.refs_3_ = f32[384,128]{1,0:T(8,128)S(1)} collective-permute-done((f32[384,128]{1,0:T(8,128)}, f32[384,128]{1,0:T(8,128)S(1)}, u32[]{:S(2)}, u32[]{:S(2)}) %collective-permute-start.31) | collective-permute-done | bytes 196640 | tf_op jit(solution)/shard_map/ppermute | solution.py:24
  177.8 0.7 copy-done.20
  178.5 19.0 %orthogonal.1 = (f32[2,256,256]{2,1,0:T(8,128)}, f32[256,256]{1,0:T(8,128)}) custom-call(s32[4]{0:T(128)} %copy-done.4, f32[2,256,256]{2,1,0:T(8,128)} %get-tuple-element.39.samples_ref, f32[256,256]{1,0:T(8,128)} %get-tuple-element.40.other_ref, f32[384,128]{1,0:T(8,128)} %get-tuple-element.41.refs_0_, f32[384,128]{1,0:T(8,128)} %copy-done.18, ...), custom_call_target="tpu_custom_call" | custom-call | tf_op jit(solution)/shard_map/orthogonal/pallas_call | solution.py:288
  197.5 0.6 collective-permute-start.32
  198.1 0.0 copy-start.6
  198.1 7.7 %collective-permute-done.32 = f32[256,256]{1,0:T(8,128)S(1)} collective-permute-done((f32[256,256]{1,0:T(8,128)}, f32[256,256]{1,0:T(8,128)S(1)}, u32[]{:S(2)}, u32[]{:S(2)}) %collective-permute-start.32) | collective-permute-done | bytes 262176 | tf_op jit(solution)/shard_map/ppermute | solution.py:24
  205.8 0.7 bitcast_dynamic-update-slice_fusion
  (62 shorter events, 0.2 us)
Async XLA Ops:
  0.6 23.9 %copy-start.21 = (s32[2,1,1]{0,2,1:T(1,128)S(1)}, s32[2,1,1]{0,2,1:T(1,128)}, u32[]{:S(2)}) copy-start(s32[2,1,1]{0,2,1:T(1,128)} %param.7) | copy-start | bytes 28
  0.6 39.1 %copy-start.3 = (s32[2,1,2048]{2,1,0:T(1,128)S(1)}, s32[2,1,2048]{2,1,0:T(1,128)}, u32[]{:S(2)}) copy-start(s32[2,1,2048]{2,1,0:T(1,128)} %perm_ref.3) | copy-start | bytes 49156
  1.7 8.1 %collective-permute-start.7 = (bf16[256,256]{1,0:T(8,128)(2,1)S(1)}, bf16[256,256]{1,0:T(8,128)(2,1)S(1)}, u32[]{:S(2)}, u32[]{:S(2)}) collective-permute-start(bf16[256,256]{1,0:T(8,128)(2,1)S(1)} %get-tuple-element.46), channel_id=1, source_target_pairs={{0,2},{1,3},{2,0},{3,1},{4,6},{5,7},{6,4},{7,5},{8,10},{9,11},{10,... | collective-permute-start | bytes 393224 | tf_op jit(solution)/shard_map/ppermute | solution.py:24
  5.7 6.3 %collective-permute-start.8 = (bf16[256,256]{1,0:T(8,128)(2,1)S(1)}, bf16[256,256]{1,0:T(8,128)(2,1)S(1)}, u32[]{:S(2)}, u32[]{:S(2)}) collective-permute-start(bf16[256,256]{1,0:T(8,128)(2,1)S(1)} %get-tuple-element.46), channel_id=1, source_target_pairs={{0,3},{1,2},{2,1},{3,0},{4,7},{5,6},{6,5},{7,4},{8,11},{9,10},{10,... | collective-permute-start | bytes 393224 | tf_op jit(solution)/shard_map/ppermute | solution.py:24
  6.4 6.4 %collective-permute-start.6 = (bf16[256,256]{1,0:T(8,128)(2,1)S(1)}, bf16[256,256]{1,0:T(8,128)(2,1)S(1)}, u32[]{:S(2)}, u32[]{:S(2)}) collective-permute-start(bf16[256,256]{1,0:T(8,128)(2,1)S(1)} %get-tuple-element.46), channel_id=1, source_target_pairs={{0,1},{1,0},{2,3},{3,2},{4,5},{5,4},{6,7},{7,6},{8,9},{9,8},{10,11... | collective-permute-start | bytes 393224 | tf_op jit(solution)/shard_map/ppermute | solution.py:24
  6.8 9.9 %collective-permute-start.12 = (bf16[256,256]{1,0:T(8,128)(2,1)S(1)}, bf16[256,256]{1,0:T(8,128)(2,1)S(1)}, u32[]{:S(2)}, u32[]{:S(2)}) collective-permute-start(bf16[256,256]{1,0:T(8,128)(2,1)S(1)} %get-tuple-element.45), channel_id=1, source_target_pairs={{0,4},{1,5},{2,6},{3,7},{4,0},{5,1},{6,2},{7,3},{8,12},{9,13},{10,... | collective-permute-start | bytes 393224 | tf_op jit(solution)/shard_map/ppermute | solution.py:24
  12.9 26.9 %collective-permute-start.10 = (bf16[4,256,256]{2,1,0:T(8,128)(2,1)S(1)}, bf16[4,256,256]{2,1,0:T(8,128)(2,1)S(1)}, u32[]{:S(2)}, u32[]{:S(2)}) collective-permute-start(bf16[4,256,256]{2,1,0:T(8,128)(2,1)S(1)} %pad_maximum_fusion.refs_4_), channel_id=1, source_target_pairs={{0,4},{1,5},{2,6},{3,7},{4,0},{5,1},{6,2},{7,3},{8,12},{9,13},{10,... | collective-permute-start | bytes 1572872 | tf_op jit(solution)/shard_map/ppermute | solution.py:24
  16.0 31.3 %collective-permute-start.1 = (bf16[256,256]{1,0:T(8,128)(2,1)S(1)}, bf16[256,256]{1,0:T(8,128)(2,1)S(1)}, u32[]{:S(2)}, u32[]{:S(2)}) collective-permute-start(bf16[256,256]{1,0:T(8,128)(2,1)S(1)} %get-tuple-element.45), channel_id=1, source_target_pairs={{0,0},{1,121},{2,114},{3,107},{4,100},{5,93},{6,86},{7,79},{8,8},{... | collective-permute-start | bytes 393224 | tf_op jit(solution)/shard_map/ppermute | solution.py:24
  16.7 10.0 %collective-permute-start.13 = (bf16[2,256,256]{2,1,0:T(8,128)(2,1)S(1)}, bf16[2,256,256]{2,1,0:T(8,128)(2,1)S(1)}, u32[]{:S(2)}, u32[]{:S(2)}) collective-permute-start(bf16[2,256,256]{2,1,0:T(8,128)(2,1)S(1)} %pad_maximum_fusion.2.refs_0_), channel_id=1, source_target_pairs={{0,1},{1,0},{2,3},{3,2},{4,5},{5,4},{6,7},{7,6},{8,9},{9,8},{10,11... | collective-permute-start | bytes 786440 | tf_op jit(solution)/shard_map/ppermute | solution.py:24
  20.9 16.3 %collective-permute-start.14 = (bf16[2,256,256]{2,1,0:T(8,128)(2,1)S(1)}, bf16[2,256,256]{2,1,0:T(8,128)(2,1)S(1)}, u32[]{:S(2)}, u32[]{:S(2)}) collective-permute-start(bf16[2,256,256]{2,1,0:T(8,128)(2,1)S(1)} %pad_maximum_fusion.2.refs_0_), channel_id=1, source_target_pairs={{0,2},{1,3},{2,0},{3,1},{4,6},{5,7},{6,4},{7,5},{8,10},{9,11},{10,... | collective-permute-start | bytes 786440 | tf_op jit(solution)/shard_map/ppermute | solution.py:24
  24.5 15.3 %collective-permute-start.15 = (bf16[2,256,256]{2,1,0:T(8,128)(2,1)S(1)}, bf16[2,256,256]{2,1,0:T(8,128)(2,1)S(1)}, u32[]{:S(2)}, u32[]{:S(2)}) collective-permute-start(bf16[2,256,256]{2,1,0:T(8,128)(2,1)S(1)} %pad_maximum_fusion.2.refs_0_), channel_id=1, source_target_pairs={{0,3},{1,2},{2,1},{3,0},{4,7},{5,6},{6,5},{7,4},{8,11},{9,10},{10,... | collective-permute-start | bytes 786440 | tf_op jit(solution)/shard_map/ppermute | solution.py:24
  24.5 97.1 %copy-start.4 = (s32[4]{0:T(128)}, s32[4]{0:T(128)S(1)}, u32[]{:S(2)}) copy-start(s32[4]{0:T(128)S(1)} %pad_add_fusion.ids_ref) | copy-start | bytes 52
  26.7 20.6 %collective-permute-start.2 = (bf16[256,256]{1,0:T(8,128)(2,1)S(1)}, bf16[256,256]{1,0:T(8,128)(2,1)S(1)}, u32[]{:S(2)}, u32[]{:S(2)}) collective-permute-start(bf16[256,256]{1,0:T(8,128)(2,1)S(1)} %get-tuple-element.45), channel_id=1, source_target_pairs={{0,100},{1,93},{2,86},{3,79},{4,0},{5,121},{6,114},{7,107},{8,108}... | collective-permute-start | bytes 393224 | tf_op jit(solution)/shard_map/ppermute | solution.py:24
  46.6 75.1 %collective-permute-start.16 = (s16[4,2,272,256]{3,2,1,0:T(8,128)(2,1)S(1)}, s16[4,2,272,256]{3,2,1,0:T(8,128)(2,1)S(1)}, u32[]{:S(2)}, u32[]{:S(2)}) collective-permute-start(s16[4,2,272,256]{3,2,1,0:T(8,128)(2,1)S(1)} %shard_map.59), channel_id=1, source_target_pairs={{0,0},{1,9},{2,18},{3,27},{4,36},{5,45},{6,54},{7,63},{8,8},{9,17}... | collective-permute-start | bytes 3342344 | tf_op jit(solution)/shard_map/ppermute | solution.py:24
  47.4 32.3 %collective-permute-start.3 = (bf16[2,256,256]{2,1,0:T(8,128)(2,1)S(1)}, bf16[2,256,256]{2,1,0:T(8,128)(2,1)S(1)}, u32[]{:S(2)}, u32[]{:S(2)}) collective-permute-start(bf16[2,256,256]{2,1,0:T(8,128)(2,1)S(1)} %pad_maximum_fusion.1.refs_0_), channel_id=1, source_target_pairs={{0,121},{1,8},{2,123},{3,10},{4,125},{5,12},{6,127},{7,14},{8,1},{... | collective-permute-start | bytes 786440 | tf_op jit(solution)/shard_map/ppermute | solution.py:24
  50.5 37.9 %collective-permute-start.4 = (bf16[2,256,256]{2,1,0:T(8,128)(2,1)S(1)}, bf16[2,256,256]{2,1,0:T(8,128)(2,1)S(1)}, u32[]{:S(2)}, u32[]{:S(2)}) collective-permute-start(bf16[2,256,256]{2,1,0:T(8,128)(2,1)S(1)} %pad_maximum_fusion.1.refs_0_), channel_id=1, source_target_pairs={{0,114},{1,115},{2,16},{3,17},{4,118},{5,119},{6,20},{7,21},{8,122... | collective-permute-start | bytes 786440 | tf_op jit(solution)/shard_map/ppermute | solution.py:24
  53.2 56.3 %collective-permute-start.9 = (bf16[4,256,256]{2,1,0:T(8,128)(2,1)S(1)}, bf16[4,256,256]{2,1,0:T(8,128)(2,1)S(1)}, u32[]{:S(2)}, u32[]{:S(2)}) collective-permute-start(bf16[4,256,256]{2,1,0:T(8,128)(2,1)S(1)} %pad_maximum_fusion.refs_4_), channel_id=1, source_target_pairs={{0,0},{1,121},{2,114},{3,107},{4,100},{5,93},{6,86},{7,79},{8,8},{... | collective-permute-start | bytes 1572872 | tf_op jit(solution)/shard_map/ppermute | solution.py:24
  53.9 55.6 %collective-permute-start.11 = (bf16[4,256,256]{2,1,0:T(8,128)(2,1)S(1)}, bf16[4,256,256]{2,1,0:T(8,128)(2,1)S(1)}, u32[]{:S(2)}, u32[]{:S(2)}) collective-permute-start(bf16[4,256,256]{2,1,0:T(8,128)(2,1)S(1)} %collective-permute-done.10.refs_5_), channel_id=1, source_target_pairs={{0,0},{1,121},{2,114},{3,107},{4,100},{5,93},{6,86},{7,79},{8,8},{... | collective-permute-start | bytes 1572872 | tf_op jit(solution)/shard_map/ppermute | solution.py:24
  79.7 17.8 %collective-permute-start = (s32[2,1,2048]{2,1,0:T(1,128)S(1)}, s32[2,1,2048]{2,1,0:T(1,128)S(1)}, u32[]{:S(2)}, u32[]{:S(2)}) collective-permute-start(s32[2,1,2048]{2,1,0:T(1,128)S(1)} %copy-done.3), channel_id=1, source_target_pairs={{0,0},{1,121},{2,114},{3,107},{4,100},{5,93},{6,86},{7,79},{8,8},{... | collective-permute-start | bytes 49160 | tf_op jit(solution)/shard_map/ppermute | solution.py:24
  88.4 9.1 %collective-permute-start.5 = (bf16[2,256,256]{2,1,0:T(8,128)(2,1)S(1)}, bf16[2,256,256]{2,1,0:T(8,128)(2,1)S(1)}, u32[]{:S(2)}, u32[]{:S(2)}) collective-permute-start(bf16[2,256,256]{2,1,0:T(8,128)(2,1)S(1)} %pad_maximum_fusion.1.refs_0_), channel_id=1, source_target_pairs={{0,107},{1,122},{2,9},{3,24},{4,111},{5,126},{6,13},{7,28},{8,115}... | collective-permute-start | bytes 786440 | tf_op jit(solution)/shard_map/ppermute | solution.py:24
  95.2 0.7 copy-start.2
  97.5 31.8 %collective-permute-start.23 = (s16[2,272,256]{2,1,0:T(8,128)(2,1)S(1)}, s16[2,272,256]{2,1,0:T(8,128)(2,1)S(1)}, u32[]{:S(2)}, u32[]{:S(2)}) collective-permute-start(s16[2,272,256]{2,1,0:T(8,128)(2,1)S(1)} %get-tuple-element.36), channel_id=1, source_target_pairs={{0,121},{1,8},{2,123},{3,10},{4,125},{5,12},{6,127},{7,14},{8,1},{... | collective-permute-start | bytes 835592 | tf_op jit(solution)/shard_map/ppermute | solution.py:24
  97.5 34.6 %collective-permute-start.24 = (s16[2,272,256]{2,1,0:T(8,128)(2,1)S(1)}, s16[2,272,256]{2,1,0:T(8,128)(2,1)S(1)}, u32[]{:S(2)}, u32[]{:S(2)}) collective-permute-start(s16[2,272,256]{2,1,0:T(8,128)(2,1)S(1)} %get-tuple-element.37), channel_id=1, source_target_pairs={{0,114},{1,115},{2,16},{3,17},{4,118},{5,119},{6,20},{7,21},{8,122... | collective-permute-start | bytes 835592 | tf_op jit(solution)/shard_map/ppermute | solution.py:24
  109.5 22.6 %collective-permute-start.25 = (s16[2,272,256]{2,1,0:T(8,128)(2,1)S(1)}, s16[2,272,256]{2,1,0:T(8,128)(2,1)S(1)}, u32[]{:S(2)}, u32[]{:S(2)}) collective-permute-start(s16[2,272,256]{2,1,0:T(8,128)(2,1)S(1)} %get-tuple-element.38), channel_id=1, source_target_pairs={{0,107},{1,122},{2,9},{3,24},{4,111},{5,126},{6,13},{7,28},{8,115}... | collective-permute-start | bytes 835592 | tf_op jit(solution)/shard_map/ppermute | solution.py:24
  116.4 12.1 %copy-start.1 = (s16[2,272,256]{2,1,0:T(8,128)(2,1)}, s16[2,272,256]{2,1,0:T(8,128)(2,1)S(1)}, u32[]{:S(2)}) copy-start(s16[2,272,256]{2,1,0:T(8,128)(2,1)S(1)} %get-tuple-element.27.refs_0_) | copy-start | bytes 835588
  116.4 21.4 %collective-permute-start.20 = (s16[2,272,256]{2,1,0:T(8,128)(2,1)S(1)}, s16[2,272,256]{2,1,0:T(8,128)(2,1)S(1)}, u32[]{:S(2)}, u32[]{:S(2)}) collective-permute-start(s16[2,272,256]{2,1,0:T(8,128)(2,1)S(1)} %get-tuple-element.28), channel_id=1, source_target_pairs={{0,1},{1,0},{2,3},{3,2},{4,5},{5,4},{6,7},{7,6},{8,9},{9,8},{10,11... | collective-permute-start | bytes 835592 | tf_op jit(solution)/shard_map/ppermute | solution.py:24
  121.7 17.4 %collective-permute-start.21 = (s16[2,272,256]{2,1,0:T(8,128)(2,1)S(1)}, s16[2,272,256]{2,1,0:T(8,128)(2,1)S(1)}, u32[]{:S(2)}, u32[]{:S(2)}) collective-permute-start(s16[2,272,256]{2,1,0:T(8,128)(2,1)S(1)} %get-tuple-element.29), channel_id=1, source_target_pairs={{0,2},{1,3},{2,0},{3,1},{4,6},{5,7},{6,4},{7,5},{8,10},{9,11},{10,... | collective-permute-start | bytes 835592 | tf_op jit(solution)/shard_map/ppermute | solution.py:24
  128.6 0.7 copy-start
  129.3 2.8 %copy-start.9 = (s16[2,272,256]{2,1,0:T(8,128)(2,1)}, s16[2,272,256]{2,1,0:T(8,128)(2,1)S(1)}, u32[]{:S(2)}) copy-start(s16[2,272,256]{2,1,0:T(8,128)(2,1)S(1)} %collective-permute-done.23.refs_1_) | copy-start | bytes 835588
  129.3 12.2 %collective-permute-start.22 = (s16[2,272,256]{2,1,0:T(8,128)(2,1)S(1)}, s16[2,272,256]{2,1,0:T(8,128)(2,1)S(1)}, u32[]{:S(2)}, u32[]{:S(2)}) collective-permute-start(s16[2,272,256]{2,1,0:T(8,128)(2,1)S(1)} %get-tuple-element.30), channel_id=1, source_target_pairs={{0,3},{1,2},{2,1},{3,0},{4,7},{5,6},{6,5},{7,4},{8,11},{9,10},{10,... | collective-permute-start | bytes 835592 | tf_op jit(solution)/shard_map/ppermute | solution.py:24
  132.0 0.7 copy-start.10
  132.0 0.8 copy-start.12
  135.2 6.3 %collective-permute-start.26 = (s16[2,272,256]{2,1,0:T(8,128)(2,1)}, s16[2,272,256]{2,1,0:T(8,128)(2,1)S(1)}, u32[]{:S(2)}, u32[]{:S(2)}) collective-permute-start(s16[2,272,256]{2,1,0:T(8,128)(2,1)} %sum.2), channel_id=1, source_target_pairs={{0,0},{1,9},{2,18},{3,27},{4,36},{5,45},{6,54},{7,63},{8,8},{9,17}... | collective-permute-start | bytes 835592 | tf_op jit(solution)/shard_map/ppermute | solution.py:24
  136.8 15.7 %collective-permute-start.17 = (s16[2,272,256]{2,1,0:T(8,128)(2,1)S(1)}, s16[2,272,256]{2,1,0:T(8,128)(2,1)S(1)}, u32[]{:S(2)}, u32[]{:S(2)}) collective-permute-start(s16[2,272,256]{2,1,0:T(8,128)(2,1)S(1)} %get-tuple-element.24), channel_id=1, source_target_pairs={{0,1},{1,0},{2,3},{3,2},{4,5},{5,4},{6,7},{7,6},{8,9},{9,8},{10,11... | collective-permute-start | bytes 835592 | tf_op jit(solution)/shard_map/ppermute | solution.py:24
  137.9 3.6 %copy-start.7 = (s16[2,272,256]{2,1,0:T(8,128)(2,1)}, s16[2,272,256]{2,1,0:T(8,128)(2,1)S(1)}, u32[]{:S(2)}) copy-start(s16[2,272,256]{2,1,0:T(8,128)(2,1)S(1)} %collective-permute-done.20.refs_1_) | copy-start | bytes 835588
  137.9 14.6 %collective-permute-start.18 = (s16[2,272,256]{2,1,0:T(8,128)(2,1)S(1)}, s16[2,272,256]{2,1,0:T(8,128)(2,1)S(1)}, u32[]{:S(2)}, u32[]{:S(2)}) collective-permute-start(s16[2,272,256]{2,1,0:T(8,128)(2,1)S(1)} %get-tuple-element.25), channel_id=1, source_target_pairs={{0,2},{1,3},{2,0},{3,1},{4,6},{5,7},{6,4},{7,5},{8,10},{9,11},{10,... | collective-permute-start | bytes 835592 | tf_op jit(solution)/shard_map/ppermute | solution.py:24
  139.1 2.4 %copy-start.8 = (s16[2,272,256]{2,1,0:T(8,128)(2,1)}, s16[2,272,256]{2,1,0:T(8,128)(2,1)S(1)}, u32[]{:S(2)}) copy-start(s16[2,272,256]{2,1,0:T(8,128)(2,1)S(1)} %collective-permute-done.21.refs_2_) | copy-start | bytes 835588
  139.1 16.0 %collective-permute-start.19 = (s16[2,272,256]{2,1,0:T(8,128)(2,1)S(1)}, s16[2,272,256]{2,1,0:T(8,128)(2,1)S(1)}, u32[]{:S(2)}, u32[]{:S(2)}) collective-permute-start(s16[2,272,256]{2,1,0:T(8,128)(2,1)S(1)} %get-tuple-element.26), channel_id=1, source_target_pairs={{0,3},{1,2},{2,1},{3,0},{4,7},{5,6},{6,5},{7,4},{8,11},{9,10},{10,... | collective-permute-start | bytes 835592 | tf_op jit(solution)/shard_map/ppermute | solution.py:24
  141.5 0.7 copy-start.13
  141.5 0.8 copy-start.16
  144.8 14.1 %collective-permute-start.27 = (s16[2,272,256]{2,1,0:T(8,128)(2,1)}, s16[2,272,256]{2,1,0:T(8,128)(2,1)S(1)}, u32[]{:S(2)}, u32[]{:S(2)}) collective-permute-start(s16[2,272,256]{2,1,0:T(8,128)(2,1)} %sum.3), channel_id=1, source_target_pairs={{0,4},{1,5},{2,6},{3,7},{4,0},{5,1},{6,2},{7,3},{8,12},{9,13},{10,... | collective-permute-start | bytes 835592 | tf_op jit(solution)/shard_map/ppermute | solution.py:24
  152.5 6.4 %copy-start.11 = (s16[2,272,256]{2,1,0:T(8,128)(2,1)}, s16[2,272,256]{2,1,0:T(8,128)(2,1)S(1)}, u32[]{:S(2)}) copy-start(s16[2,272,256]{2,1,0:T(8,128)(2,1)S(1)} %collective-permute-done.17.refs_1_) | copy-start | bytes 835588
  152.5 6.3 %copy-start.14 = (s16[2,272,256]{2,1,0:T(8,128)(2,1)}, s16[2,272,256]{2,1,0:T(8,128)(2,1)S(1)}, u32[]{:S(2)}) copy-start(s16[2,272,256]{2,1,0:T(8,128)(2,1)S(1)} %collective-permute-done.18.refs_2_) | copy-start | bytes 835588
  155.1 3.8 %copy-start.15 = (s16[2,272,256]{2,1,0:T(8,128)(2,1)}, s16[2,272,256]{2,1,0:T(8,128)(2,1)S(1)}, u32[]{:S(2)}) copy-start(s16[2,272,256]{2,1,0:T(8,128)(2,1)S(1)} %collective-permute-done.19.refs_3_) | copy-start | bytes 835588
  158.9 0.7 copy-start.17
  162.7 35.4 %copy-start.5 = (f32[2,256,256]{2,1,0:T(8,128)S(1)}, f32[2,256,256]{2,1,0:T(8,128)}, u32[]{:S(2)}) copy-start(f32[2,256,256]{2,1,0:T(8,128)} %get-tuple-element.39.samples_ref) | copy-start | bytes 1572868
  162.7 35.4 %collective-permute-start.28 = (f32[256,256]{1,0:T(8,128)}, f32[256,256]{1,0:T(8,128)S(1)}, u32[]{:S(2)}, u32[]{:S(2)}) collective-permute-start(f32[256,256]{1,0:T(8,128)} %get-tuple-element.40.other_ref), channel_id=1, source_target_pairs={{0,4},{1,5},{2,6},{3,7},{4,0},{5,1},{6,2},{7,3},{8,12},{9,13},{10,... | collective-permute-start | bytes 786440 | tf_op jit(solution)/shard_map/ppermute | solution.py:24
  165.9 7.3 %collective-permute-start.29 = (f32[384,128]{1,0:T(8,128)}, f32[384,128]{1,0:T(8,128)S(1)}, u32[]{:S(2)}, u32[]{:S(2)}) collective-permute-start(f32[384,128]{1,0:T(8,128)} %get-tuple-element.41.refs_0_), channel_id=1, source_target_pairs={{0,1},{1,0},{2,3},{3,2},{4,5},{5,4},{6,7},{7,6},{8,9},{9,8},{10,11... | collective-permute-start | bytes 589832 | tf_op jit(solution)/shard_map/ppermute | solution.py:24
  165.9 9.4 %collective-permute-start.30 = (f32[384,128]{1,0:T(8,128)}, f32[384,128]{1,0:T(8,128)S(1)}, u32[]{:S(2)}, u32[]{:S(2)}) collective-permute-start(f32[384,128]{1,0:T(8,128)} %get-tuple-element.41.refs_0_), channel_id=1, source_target_pairs={{0,2},{1,3},{2,0},{3,1},{4,6},{5,7},{6,4},{7,5},{8,10},{9,11},{10,... | collective-permute-start | bytes 589832 | tf_op jit(solution)/shard_map/ppermute | solution.py:24
  167.1 10.7 %collective-permute-start.31 = (f32[384,128]{1,0:T(8,128)}, f32[384,128]{1,0:T(8,128)S(1)}, u32[]{:S(2)}, u32[]{:S(2)}) collective-permute-start(f32[384,128]{1,0:T(8,128)} %get-tuple-element.41.refs_0_), channel_id=1, source_target_pairs={{0,3},{1,2},{2,1},{3,0},{4,7},{5,6},{6,5},{7,4},{8,11},{9,10},{10,... | collective-permute-start | bytes 589832 | tf_op jit(solution)/shard_map/ppermute | solution.py:24
  173.3 4.6 %copy-start.18 = (f32[384,128]{1,0:T(8,128)}, f32[384,128]{1,0:T(8,128)S(1)}, u32[]{:S(2)}) copy-start(f32[384,128]{1,0:T(8,128)S(1)} %collective-permute-done.29.refs_1_) | copy-start | bytes 589828
  175.3 2.5 %copy-start.19 = (f32[384,128]{1,0:T(8,128)}, f32[384,128]{1,0:T(8,128)S(1)}, u32[]{:S(2)}) copy-start(f32[384,128]{1,0:T(8,128)S(1)} %collective-permute-done.30.refs_2_) | copy-start | bytes 589828
  177.8 0.7 copy-start.20
  197.5 8.3 %collective-permute-start.32 = (f32[256,256]{1,0:T(8,128)}, f32[256,256]{1,0:T(8,128)S(1)}, u32[]{:S(2)}, u32[]{:S(2)}) collective-permute-start(f32[256,256]{1,0:T(8,128)} %get-tuple-element.43), channel_id=1, source_target_pairs={{0,4},{1,5},{2,6},{3,7},{4,0},{5,1},{6,2},{7,3},{8,12},{9,13},{10,... | collective-permute-start | bytes 786440 | tf_op jit(solution)/shard_map/ppermute | solution.py:24
  198.1 8.4 %copy-start.6 = (f32[2,256,256]{2,1,0:T(8,128)}, f32[2,256,256]{2,1,0:T(8,128)S(1)}, u32[]{:S(2)}) copy-start(f32[2,256,256]{2,1,0:T(8,128)S(1)} %bitcast_dynamic-update-slice_fusion.1) | copy-start | bytes 1572868

commit v5 on v4

--- a/solution.py
+++ b/solution.py
@@ -235,11 +235,10 @@
             new_v = new_v + factor * inverse[t : t + 1, :]
         new_u = jnp.where(lane >= at + sub, new_u * scale, 0.0)
         new_v = new_v * scale
-        for t in range(size):
-            factor = jnp.broadcast_to(tall[:, t : t + 1], (n, n))
-            old_a = old_a - factor * u[t : t + 1, :]
-            old_m = old_m - factor * v[t : t + 1, :]
-        a_ref[...], m_ref[...] = old_a, old_m
+        update = jnp.dot(
+            tall, jnp.concatenate([u, v], axis=1), preferred_element_type=jnp.float32, precision=EXACT
+        )
+        a_ref[...], m_ref[...] = old_a - update[:, :n], old_m - update[:, n:]
         out_ref[pl.ds(at, size), :] = new_v
         u_ref[...], v_ref[...] = new_u, new_v
         tall_ref[...] = new_u.T
@@ -278,7 +277,7 @@
         for m, value in enumerate(made):
             columns = slice(m * half, (m + 1) * half)
             if n:
-                out_ref[:, columns] = value
+                out_ref[:, columns] = coded(value)
             else:
                 basis_ref[plane, :, columns] = value
 
@@ -288,7 +287,10 @@
     return pl.pallas_call(
         functools.partial(factor_kernel, scale),
         in_specs=[pl.BlockSpec(memory_space=pltpu.SMEM)] + [pl.BlockSpec(memory_space=pltpu.VMEM)] * (2 + len(grams)),
-        out_shape=[jax.ShapeDtypeStruct(x.shape, jnp.float32) for x in (samples, other)],
+        out_shape=[
+            jax.ShapeDtypeStruct(samples.shape, jnp.float32),
+            jax.ShapeDtypeStruct((other.shape[0] + EXTRA, other.shape[1]), jnp.int16),
+        ],
         scratch_shapes=[
             pltpu.VMEM(shape, jnp.float32) for shape in [(half, half)] * 4 + [(half, 8), (8, half), (8, half)]
         ],
@@ -345,17 +347,20 @@
     given = products(ids, weight, far_perm, *far_blocks, tiles, False, 1)
     given = [given[0]] + [sent(given[d], same(d)) for d in depths]
     kept = products(ids, weight, far_perm, *far_blocks, tiles, False, 0, (more,))
-    arrived = sent(summed(back, kept[:1]), lambda r, c: (r + c, c))
+    after = kept[:1]
     kept = [kept[0]] + [sent(kept[d], same(d)) for d in depths]
-    crossed = sent(summed([*given, arrived]), same(nz))
-    samples, swapped, gram = gram_of(ids, [*kept, crossed])
+    crossed = summed(given, after)
+    crossed = sent(crossed, same(nz))
+    arrived = summed(back, after)
+    arrived = sent(arrived, lambda r, c: (r + c, c ^ nz))
+    samples, swapped, gram = gram_of(ids, [*kept, crossed, arrived])
     grams = [gram] + [sent(gram, same(d)) for d in depths]
     basis, swapped_basis = orthogonal(ids, samples, swapped, grams, 1.0 / tile_len)
 
     def placed(array, theirs):
-        return lax.dynamic_update_index_in_dim(array, sent(theirs, same(nz)), 1 - plane, 0)
-
-    return (placed(samples, swapped), placed(basis, swapped_basis))
+        return lax.dynamic_update_index_in_dim(array, theirs, 1 - plane, 0)
+
+    return (placed(samples, sent(swapped, same(nz))), placed(basis, decoded(sent(swapped_basis, same(nz)))))
 
 
 def solution(mesh):

time: 207 us -> 206 us (level)
  waiting for transfers between devices: 70.2 us -> 76.1 us
  starting transfers between devices: 74.7 us -> 69 us
    ppermute x33, waiting for transfers between devices: 70.2 us -> 76.1 us  [sent(): return lax.ppermute(value, AXES, pairs)]
    ppermute x33, starting transfers between devices: 74.7 us -> 69 us  [sent(): return lax.ppermute(value, AXES, pairs)]
  transfers between devices with their start and end apart: 33 -> 33, of which waited for: 14 -> 18; matrix products, arithmetic and copies ran while one was open for 0% -> 0% of each run, Pallas kernels for 25% -> 24%
where the time goes in v5:
time: 206 us
  waiting for transfers between devices  76.1 us (37%)
  starting transfers between devices  69 us (33%)
  Pallas kernels  53.4 us (26%)
  local copies, waits for them, and re-layouts  5.46 us (3%)
    ppermute x33, waiting for transfers between devices, sent(): return lax.ppermute(value, AXES, pairs)  76.1 us
    ppermute x33, starting transfers between devices, sent(): return lax.ppermute(value, AXES, pairs)  69 us
    pallas_call x4, Pallas kernels, products(): pl.pallas_call(functools.partial(product_kernel, back, part), out_shape=[...  27.4 us
    pallas_call x1, Pallas kernels, orthogonal(): pl.pallas_call(functools.partial(factor_kernel, scale), in_specs=[pl.Bloc...  18.1 us
    pallas_call x2, Pallas kernels, summed(): pl.pallas_call(functools.partial(sum_kernel, len(codes)), in_specs=[vmem]...  4.61 us
    unnamed x44, local copies, waits for them, and re-layouts  4.43 us
  transfers between devices with their start and end apart: 33, of which 18 were waited for; matrix products, arithmetic and copies ran while one was open for 0% of the time, Pallas kernels for 24%

profile of v5, /device:TPU:0, one launch (start us, length us, event | category | flops | bytes accessed | tf_op | source)
XLA Modules:
  0.0 205.9 jit_solution(11409275319005162249)
XLA Ops:
  0.7 1.0 fusion.5
  1.7 4.1 %collective-permute-start.7 = (bf16[256,256]{1,0:T(8,128)(2,1)S(1)}, bf16[256,256]{1,0:T(8,128)(2,1)S(1)}, u32[]{:S(2)}, u32[]{:S(2)}) collective-permute-start(bf16[256,256]{1,0:T(8,128)(2,1)S(1)} %get-tuple-element.46), channel_id=1, source_target_pairs={{0,2},{1,3},{2,0},{3,1},{4,6},{5,7},{6,4},{7,5},{8,10},{9,11},{10,... | collective-permute-start | bytes 393224 | tf_op jit(solution)/shard_map/ppermute | solution.py:24
  5.7 0.7 collective-permute-start.8
  6.4 0.3 collective-permute-start.6
  6.8 3.0 %collective-permute-start.12 = (bf16[256,256]{1,0:T(8,128)(2,1)S(1)}, bf16[256,256]{1,0:T(8,128)(2,1)S(1)}, u32[]{:S(2)}, u32[]{:S(2)}) collective-permute-start(bf16[256,256]{1,0:T(8,128)(2,1)S(1)} %get-tuple-element.45), channel_id=1, source_target_pairs={{0,4},{1,5},{2,6},{3,7},{4,0},{5,1},{6,2},{7,3},{8,12},{9,13},{10,... | collective-permute-start | bytes 393224 | tf_op jit(solution)/shard_map/ppermute | solution.py:24
  9.8 2.3 %collective-permute-done.8 = bf16[256,256]{1,0:T(8,128)(2,1)S(1)} collective-permute-done((bf16[256,256]{1,0:T(8,128)(2,1)S(1)}, bf16[256,256]{1,0:T(8,128)(2,1)S(1)}, u32[]{:S(2)}, u32[]{:S(2)}) %collective-permute-start.8) | collective-permute-done | bytes 131104 | tf_op jit(solution)/shard_map/ppermute | solution.py:24
  12.0 0.8 collective-permute-done.6
  12.9 3.1 %collective-permute-start.10 = (bf16[4,256,256]{2,1,0:T(8,128)(2,1)S(1)}, bf16[4,256,256]{2,1,0:T(8,128)(2,1)S(1)}, u32[]{:S(2)}, u32[]{:S(2)}) collective-permute-start(bf16[4,256,256]{2,1,0:T(8,128)(2,1)S(1)} %pad_maximum_fusion.refs_4_), channel_id=1, source_target_pairs={{0,4},{1,5},{2,6},{3,7},{4,0},{5,1},{6,2},{7,3},{8,12},{9,13},{10,... | collective-permute-start | bytes 1572872 | tf_op jit(solution)/shard_map/ppermute | solution.py:24
  16.0 0.7 collective-permute-start.1
  16.7 4.2 %collective-permute-start.13 = (bf16[2,256,256]{2,1,0:T(8,128)(2,1)S(1)}, bf16[2,256,256]{2,1,0:T(8,128)(2,1)S(1)}, u32[]{:S(2)}, u32[]{:S(2)}) collective-permute-start(bf16[2,256,256]{2,1,0:T(8,128)(2,1)S(1)} %pad_maximum_fusion.2.refs_0_), channel_id=1, source_target_pairs={{0,1},{1,0},{2,3},{3,2},{4,5},{5,4},{6,7},{7,6},{8,9},{9,8},{10,11... | collective-permute-start | bytes 786440 | tf_op jit(solution)/shard_map/ppermute | solution.py:24
  20.9 3.5 %collective-permute-start.14 = (bf16[2,256,256]{2,1,0:T(8,128)(2,1)S(1)}, bf16[2,256,256]{2,1,0:T(8,128)(2,1)S(1)}, u32[]{:S(2)}, u32[]{:S(2)}) collective-permute-start(bf16[2,256,256]{2,1,0:T(8,128)(2,1)S(1)} %pad_maximum_fusion.2.refs_0_), channel_id=1, source_target_pairs={{0,2},{1,3},{2,0},{3,1},{4,6},{5,7},{6,4},{7,5},{8,10},{9,11},{10,... | collective-permute-start | bytes 786440 | tf_op jit(solution)/shard_map/ppermute | solution.py:24
  24.5 0.1 pad_add_fusion.ids_ref
  24.5 2.2 %collective-permute-done.13.refs_1_ = bf16[2,256,256]{2,1,0:T(8,128)(2,1)S(1)} collective-permute-done((bf16[2,256,256]{2,1,0:T(8,128)(2,1)S(1)}, bf16[2,256,256]{2,1,0:T(8,128)(2,1)S(1)}, u32[]{:S(2)}, u32[]{:S(2)}) %collective-permute-start.13) | collective-permute-done | bytes 262176 | tf_op jit(solution)/shard_map/ppermute | solution.py:24
  26.7 3.9 %collective-permute-start.2 = (bf16[256,256]{1,0:T(8,128)(2,1)S(1)}, bf16[256,256]{1,0:T(8,128)(2,1)S(1)}, u32[]{:S(2)}, u32[]{:S(2)}) collective-permute-start(bf16[256,256]{1,0:T(8,128)(2,1)S(1)} %get-tuple-element.45), channel_id=1, source_target_pairs={{0,100},{1,93},{2,86},{3,79},{4,0},{5,121},{6,114},{7,107},{8,108}... | collective-permute-start | bytes 393224 | tf_op jit(solution)/shard_map/ppermute | solution.py:24
  30.7 6.5 %collective-permute-done.14.refs_2_ = bf16[2,256,256]{2,1,0:T(8,128)(2,1)S(1)} collective-permute-done((bf16[2,256,256]{2,1,0:T(8,128)(2,1)S(1)}, bf16[2,256,256]{2,1,0:T(8,128)(2,1)S(1)}, u32[]{:S(2)}, u32[]{:S(2)}) %collective-permute-start.14) | collective-permute-done | bytes 262176 | tf_op jit(solution)/shard_map/ppermute | solution.py:24
  37.2 2.6 %collective-permute-done.15.refs_3_ = bf16[2,256,256]{2,1,0:T(8,128)(2,1)S(1)} collective-permute-done((bf16[2,256,256]{2,1,0:T(8,128)(2,1)S(1)}, bf16[2,256,256]{2,1,0:T(8,128)(2,1)S(1)}, u32[]{:S(2)}, u32[]{:S(2)}) %collective-permute-start.15) | collective-permute-done | bytes 262176 | tf_op jit(solution)/shard_map/ppermute | solution.py:24
  39.8 6.8 %shard_map.59 = s16[4,2,272,256]{3,2,1,0:T(8,128)(2,1)S(1)} custom-call(s32[4]{0:T(128)S(1)} %pad_add_fusion.ids_ref, f32[2]{0:T(128)S(1)} %fusion.4.weight_ref, s32[2,1,2048]{2,1,0:T(1,128)S(1)} %copy-done.3, bf16[2,256,256]{2,1,0:T(8,128)(2,1)S(1)} %pad_maximum_fusion.2.refs_0_, bf16[2,256,256]{2,1,0:T(8,128)(2,1)S(1)} %collective-permute-done.13.refs_1_, ...), custom_call_target="tpu_custom_call" | custom-call | flops 4294967296 | bytes 11534336 | tf_op jit(solution)/shard_map/pallas_call | solution.py:114
  46.6 0.7 collective-permute-start.16
  47.4 3.1 %collective-permute-start.3 = (bf16[2,256,256]{2,1,0:T(8,128)(2,1)S(1)}, bf16[2,256,256]{2,1,0:T(8,128)(2,1)S(1)}, u32[]{:S(2)}, u32[]{:S(2)}) collective-permute-start(bf16[2,256,256]{2,1,0:T(8,128)(2,1)S(1)} %pad_maximum_fusion.1.refs_0_), channel_id=1, source_target_pairs={{0,121},{1,8},{2,123},{3,10},{4,125},{5,12},{6,127},{7,14},{8,1},{... | collective-permute-start | bytes 786440 | tf_op jit(solution)/shard_map/ppermute | solution.py:24
  50.5 2.7 %collective-permute-start.4 = (bf16[2,256,256]{2,1,0:T(8,128)(2,1)S(1)}, bf16[2,256,256]{2,1,0:T(8,128)(2,1)S(1)}, u32[]{:S(2)}, u32[]{:S(2)}) collective-permute-start(bf16[2,256,256]{2,1,0:T(8,128)(2,1)S(1)} %pad_maximum_fusion.1.refs_0_), channel_id=1, source_target_pairs={{0,114},{1,115},{2,16},{3,17},{4,118},{5,119},{6,20},{7,21},{8,122... | collective-permute-start | bytes 786440 | tf_op jit(solution)/shard_map/ppermute | solution.py:24
  53.2 0.7 collective-permute-start.9
  53.9 0.7 collective-permute-start.11
  54.6 25.1 %collective-permute-done.3.refs_1_ = bf16[2,256,256]{2,1,0:T(8,128)(2,1)S(1)} collective-permute-done((bf16[2,256,256]{2,1,0:T(8,128)(2,1)S(1)}, bf16[2,256,256]{2,1,0:T(8,128)(2,1)S(1)}, u32[]{:S(2)}, u32[]{:S(2)}) %collective-permute-start.3) | collective-permute-done | bytes 262176 | tf_op jit(solution)/shard_map/ppermute | solution.py:24
  79.7 0.7 collective-permute-start
  80.3 8.0 %collective-permute-done.4.refs_2_ = bf16[2,256,256]{2,1,0:T(8,128)(2,1)S(1)} collective-permute-done((bf16[2,256,256]{2,1,0:T(8,128)(2,1)S(1)}, bf16[2,256,256]{2,1,0:T(8,128)(2,1)S(1)}, u32[]{:S(2)}, u32[]{:S(2)}) %collective-permute-start.4) | collective-permute-done | bytes 262176 | tf_op jit(solution)/shard_map/ppermute | solution.py:24
  88.4 6.8 %shard_map.62 = (s16[2,272,256]{2,1,0:T(8,128)(2,1)S(1)}, s16[2,272,256]{2,1,0:T(8,128)(2,1)S(1)}, s16[2,272,256]{2,1,0:T(8,128)(2,1)S(1)}, s16[2,272,256]{2,1,0:T(8,128)(2,1)S(1)}) custom-call(s32[4]{0:T(128)S(1)} %pad_add_fusion.ids_ref, f32[2]{0:T(128)S(1)} %fusion.4.weight_ref, s32[2,1,2048]{2,1,0:T(1,128)S(1)} %copy-done.3, ...), custom_call_target="tpu_custom_call" | custom-call | flops 4294967296 | bytes 11534336 | tf_op jit(solution)/shard_map/pallas_call | solution.py:114
  95.2 0.7 copy-done.1
  95.9 1.6 collective-permute-done.5.refs_3_
  97.5 12.0 %collective-permute-start.25 = (s16[2,272,256]{2,1,0:T(8,128)(2,1)S(1)}, s16[2,272,256]{2,1,0:T(8,128)(2,1)S(1)}, u32[]{:S(2)}, u32[]{:S(2)}) collective-permute-start(s16[2,272,256]{2,1,0:T(8,128)(2,1)S(1)} %get-tuple-element.37), channel_id=1, source_target_pairs={{0,114},{1,115},{2,16},{3,17},{4,118},{5,119},{6,20},{7,21},{8,122... | collective-permute-start | bytes 835592 | tf_op jit(solution)/shard_map/ppermute | solution.py:24
  109.5 7.0 %shard_map.61 = (s16[2,272,256]{2,1,0:T(8,128)(2,1)S(1)}, s16[2,272,256]{2,1,0:T(8,128)(2,1)S(1)}, s16[2,272,256]{2,1,0:T(8,128)(2,1)S(1)}, s16[2,272,256]{2,1,0:T(8,128)(2,1)S(1)}) custom-call(s32[4]{0:T(128)S(1)} %pad_add_fusion.ids_ref, f32[2]{0:T(128)S(1)} %fusion.4.weight_ref, s32[2,1,2048]{2,1,0:T(1,128)S(1)} %collective-permute-done.perm_ref, ...), custom_call_target="tpu_custom_call" | custom-call | flops 4294967296 | bytes 11534336 | tf_op jit(solution)/shard_map/pallas_call | solution.py:114
  116.5 5.2 %collective-permute-start.20 = (s16[2,272,256]{2,1,0:T(8,128)(2,1)S(1)}, s16[2,272,256]{2,1,0:T(8,128)(2,1)S(1)}, u32[]{:S(2)}, u32[]{:S(2)}) collective-permute-start(s16[2,272,256]{2,1,0:T(8,128)(2,1)S(1)} %get-tuple-element.28), channel_id=1, source_target_pairs={{0,1},{1,0},{2,3},{3,2},{4,5},{5,4},{6,7},{7,6},{8,9},{9,8},{10,11... | collective-permute-start | bytes 835592 | tf_op jit(solution)/shard_map/ppermute | solution.py:24
  121.7 2.8 %collective-permute-start.22 = (s16[2,272,256]{2,1,0:T(8,128)(2,1)S(1)}, s16[2,272,256]{2,1,0:T(8,128)(2,1)S(1)}, u32[]{:S(2)}, u32[]{:S(2)}) collective-permute-start(s16[2,272,256]{2,1,0:T(8,128)(2,1)S(1)} %get-tuple-element.30), channel_id=1, source_target_pairs={{0,3},{1,2},{2,1},{3,0},{4,7},{5,6},{6,5},{7,4},{8,11},{9,10},{10,... | collective-permute-start | bytes 835592 | tf_op jit(solution)/shard_map/ppermute | solution.py:24
  124.5 6.8 %shard_map.60 = (s16[2,272,256]{2,1,0:T(8,128)(2,1)S(1)}, s16[2,272,256]{2,1,0:T(8,128)(2,1)S(1)}, s16[2,272,256]{2,1,0:T(8,128)(2,1)S(1)}, s16[2,272,256]{2,1,0:T(8,128)(2,1)S(1)}) custom-call(s32[4]{0:T(128)S(1)} %pad_add_fusion.ids_ref, f32[2]{0:T(128)S(1)} %fusion.4.weight_ref, s32[2,1,2048]{2,1,0:T(1,128)S(1)} %collective-permute-done.perm_ref, ...), custom_call_target="tpu_custom_call" | custom-call | flops 4294967296 | bytes 11534336 | tf_op jit(solution)/shard_map/pallas_call | solution.py:114
  131.3 0.7 copy-done
  132.1 0.7 copy-done.8
  132.8 0.1 copy-done.10
  132.9 2.3 %sum.3 = s16[2,272,256]{2,1,0:T(8,128)(2,1)} custom-call(s16[2,272,256]{2,1,0:T(8,128)(2,1)} %copy-done.1, s16[2,272,256]{2,1,0:T(8,128)(2,1)} %copy-done.7, s16[2,272,256]{2,1,0:T(8,128)(2,1)} %copy-done.8, s16[2,272,256]{2,1,0:T(8,128)(2,1)} %copy-done.10, s16[2,272,256]{2,1,0:T(8,128)(2,1)} %copy-done), custom_call_target="tpu_custom_call" | custom-call | tf_op jit(solution)/shard_map/sum/pallas_call | solution.py:141
  135.2 2.1 %collective-permute-start.27 = (s16[2,272,256]{2,1,0:T(8,128)(2,1)}, s16[2,272,256]{2,1,0:T(8,128)(2,1)S(1)}, u32[]{:S(2)}, u32[]{:S(2)}) collective-permute-start(s16[2,272,256]{2,1,0:T(8,128)(2,1)} %sum.3), channel_id=1, source_target_pairs={{0,4},{1,13},{2,22},{3,31},{4,32},{5,41},{6,50},{7,59},{8,12},{9,2... | collective-permute-start | bytes 835592 | tf_op jit(solution)/shard_map/ppermute | solution.py:24
  137.3 0.4 collective-permute-done.22.refs_3_
  137.7 0.3 copy-done.9
  138.0 0.1 copy-done.11
  138.1 0.3 copy-done.12
  138.4 2.3 %sum.2 = s16[2,272,256]{2,1,0:T(8,128)(2,1)} custom-call(s16[2,272,256]{2,1,0:T(8,128)(2,1)} %copy-done.2, s16[2,272,256]{2,1,0:T(8,128)(2,1)} %copy-done.9, s16[2,272,256]{2,1,0:T(8,128)(2,1)} %copy-done.11, s16[2,272,256]{2,1,0:T(8,128)(2,1)} %copy-done.12, s16[2,272,256]{2,1,0:T(8,128)(2,1)} %copy-done), custom_call_target="tpu_custom_call" | custom-call | tf_op jit(solution)/shard_map/sum/pallas_call | solution.py:141
  140.7 2.0 collective-permute-start.23
  142.7 4.6 %collective-permute-start.18 = (s16[2,272,256]{2,1,0:T(8,128)(2,1)S(1)}, s16[2,272,256]{2,1,0:T(8,128)(2,1)S(1)}, u32[]{:S(2)}, u32[]{:S(2)}) collective-permute-start(s16[2,272,256]{2,1,0:T(8,128)(2,1)S(1)} %get-tuple-element.25), channel_id=1, source_target_pairs={{0,2},{1,3},{2,0},{3,1},{4,6},{5,7},{6,4},{7,5},{8,10},{9,11},{10,... | collective-permute-start | bytes 835592 | tf_op jit(solution)/shard_map/ppermute | solution.py:24
  147.3 0.1 collective-permute-start.19
  147.4 1.1 collective-permute-done.27.refs_5_
  148.5 2.6 %collective-permute-done.23.refs_4_ = s16[2,272,256]{2,1,0:T(8,128)(2,1)S(1)} collective-permute-done((s16[2,272,256]{2,1,0:T(8,128)(2,1)}, s16[2,272,256]{2,1,0:T(8,128)(2,1)S(1)}, u32[]{:S(2)}, u32[]{:S(2)}) %collective-permute-start.23) | collective-permute-done | bytes 278560 | tf_op jit(solution)/shard_map/ppermute | solution.py:24
  151.1 1.1 collective-permute-done.17.refs_1_
  152.2 7.0 %collective-permute-done.18.refs_2_ = s16[2,272,256]{2,1,0:T(8,128)(2,1)S(1)} collective-permute-done((s16[2,272,256]{2,1,0:T(8,128)(2,1)S(1)}, s16[2,272,256]{2,1,0:T(8,128)(2,1)S(1)}, u32[]{:S(2)}, u32[]{:S(2)}) %collective-permute-start.18) | collective-permute-done | bytes 278560 | tf_op jit(solution)/shard_map/ppermute | solution.py:24
  159.2 2.6 %collective-permute-done.19.refs_3_ = s16[2,272,256]{2,1,0:T(8,128)(2,1)S(1)} collective-permute-done((s16[2,272,256]{2,1,0:T(8,128)(2,1)S(1)}, s16[2,272,256]{2,1,0:T(8,128)(2,1)S(1)}, u32[]{:S(2)}, u32[]{:S(2)}) %collective-permute-start.19) | collective-permute-done | bytes 278560 | tf_op jit(solution)/shard_map/ppermute | solution.py:24
  161.8 0.7 copy-done.17
  162.5 3.3 %gram.1 = (f32[2,256,256]{2,1,0:T(8,128)}, f32[256,256]{1,0:T(8,128)}, f32[384,128]{1,0:T(8,128)}) custom-call(s32[4]{0:T(128)} %copy-done.4, s16[2,272,256]{2,1,0:T(8,128)(2,1)} %copy-done, s16[2,272,256]{2,1,0:T(8,128)(2,1)} %copy-done.15, s16[2,272,256]{2,1,0:T(8,128)(2,1)} %copy-done.16, s16[2,272,256]{2,1,0:T(8,128)(2,1)} %copy-done.17, ...), custom_call_target="tpu_custom_call" | custom-call | tf_op jit(solution)/shard_map/gram/pallas_call | solution.py:175
  165.8 2.2 %collective-permute-start.28 = (f32[256,256]{1,0:T(8,128)}, f32[256,256]{1,0:T(8,128)S(1)}, u32[]{:S(2)}, u32[]{:S(2)}) collective-permute-start(f32[256,256]{1,0:T(8,128)} %get-tuple-element.40.other_ref), channel_id=1, source_target_pairs={{0,4},{1,5},{2,6},{3,7},{4,0},{5,1},{6,2},{7,3},{8,12},{9,13},{10,... | collective-permute-start | bytes 786440 | tf_op jit(solution)/shard_map/ppermute | solution.py:24
  168.0 1.7 collective-permute-start.30
  169.7 3.0 %collective-permute-start.31 = (f32[384,128]{1,0:T(8,128)}, f32[384,128]{1,0:T(8,128)S(1)}, u32[]{:S(2)}, u32[]{:S(2)}) collective-permute-start(f32[384,128]{1,0:T(8,128)} %get-tuple-element.41.refs_0_), channel_id=1, source_target_pairs={{0,3},{1,2},{2,1},{3,0},{4,7},{5,6},{6,5},{7,4},{8,11},{9,10},{10,... | collective-permute-start | bytes 589832 | tf_op jit(solution)/shard_map/ppermute | solution.py:24
  172.7 2.6 %collective-permute-done.29.refs_1_ = f32[384,128]{1,0:T(8,128)S(1)} collective-permute-done((f32[384,128]{1,0:T(8,128)}, f32[384,128]{1,0:T(8,128)S(1)}, u32[]{:S(2)}, u32[]{:S(2)}) %collective-permute-start.29) | collective-permute-done | bytes 196640 | tf_op jit(solution)/shard_map/ppermute | solution.py:24
  175.3 2.2 %collective-permute-done.30.refs_2_ = f32[384,128]{1,0:T(8,128)S(1)} collective-permute-done((f32[384,128]{1,0:T(8,128)}, f32[384,128]{1,0:T(8,128)S(1)}, u32[]{:S(2)}, u32[]{:S(2)}) %collective-permute-start.30) | collective-permute-done | bytes 196640 | tf_op jit(solution)/shard_map/ppermute | solution.py:24
  177.5 2.1 %collective-permute-done.31.refs_3_ = f32[384,128]{1,0:T(8,128)S(1)} collective-permute-done((f32[384,128]{1,0:T(8,128)}, f32[384,128]{1,0:T(8,128)S(1)}, u32[]{:S(2)}, u32[]{:S(2)}) %collective-permute-start.31) | collective-permute-done | bytes 196640 | tf_op jit(solution)/shard_map/ppermute | solution.py:24
  179.5 0.7 copy-done.20
  180.2 18.1 %orthogonal.1 = (f32[2,256,256]{2,1,0:T(8,128)}, s16[272,256]{1,0:T(8,128)(2,1)}) custom-call(s32[4]{0:T(128)} %copy-done.4, f32[2,256,256]{2,1,0:T(8,128)} %get-tuple-element.39.samples_ref, f32[256,256]{1,0:T(8,128)} %get-tuple-element.40.other_ref, f32[384,128]{1,0:T(8,128)} %get-tuple-element.41.refs_0_, f32[384,128]{1,0:T(8,128)} %copy-done.18, ...), custom_call_target="tpu_custom_call" | custom-call | tf_op jit(solution)/shard_map/orthogonal/pallas_call | solution.py:287
  198.3 1.3 collective-permute-start.32
  199.7 5.5 %collective-permute-done.32 = s16[272,256]{1,0:T(8,128)(2,1)S(1)} collective-permute-done((s16[272,256]{1,0:T(8,128)(2,1)}, s16[272,256]{1,0:T(8,128)(2,1)S(1)}, u32[]{:S(2)}, u32[]{:S(2)}) %collective-permute-start.32) | collective-permute-done | bytes 139296 | tf_op jit(solution)/shard_map/ppermute | solution.py:24
  205.2 0.7 fusion.1
  (64 shorter events, 0.3 us)
Async XLA Ops:
  0.6 23.9 %copy-start.21 = (s32[2,1,1]{0,2,1:T(1,128)S(1)}, s32[2,1,1]{0,2,1:T(1,128)}, u32[]{:S(2)}) copy-start(s32[2,1,1]{0,2,1:T(1,128)} %param.7) | copy-start | bytes 28
  0.6 39.1 %copy-start.3 = (s32[2,1,2048]{2,1,0:T(1,128)S(1)}, s32[2,1,2048]{2,1,0:T(1,128)}, u32[]{:S(2)}) copy-start(s32[2,1,2048]{2,1,0:T(1,128)} %perm_ref.3) | copy-start | bytes 49156
  1.7 8.1 %collective-permute-start.7 = (bf16[256,256]{1,0:T(8,128)(2,1)S(1)}, bf16[256,256]{1,0:T(8,128)(2,1)S(1)}, u32[]{:S(2)}, u32[]{:S(2)}) collective-permute-start(bf16[256,256]{1,0:T(8,128)(2,1)S(1)} %get-tuple-element.46), channel_id=1, source_target_pairs={{0,2},{1,3},{2,0},{3,1},{4,6},{5,7},{6,4},{7,5},{8,10},{9,11},{10,... | collective-permute-start | bytes 393224 | tf_op jit(solution)/shard_map/ppermute | solution.py:24
  5.7 6.3 %collective-permute-start.8 = (bf16[256,256]{1,0:T(8,128)(2,1)S(1)}, bf16[256,256]{1,0:T(8,128)(2,1)S(1)}, u32[]{:S(2)}, u32[]{:S(2)}) collective-permute-start(bf16[256,256]{1,0:T(8,128)(2,1)S(1)} %get-tuple-element.46), channel_id=1, source_target_pairs={{0,3},{1,2},{2,1},{3,0},{4,7},{5,6},{6,5},{7,4},{8,11},{9,10},{10,... | collective-permute-start | bytes 393224 | tf_op jit(solution)/shard_map/ppermute | solution.py:24
  6.4 6.4 %collective-permute-start.6 = (bf16[256,256]{1,0:T(8,128)(2,1)S(1)}, bf16[256,256]{1,0:T(8,128)(2,1)S(1)}, u32[]{:S(2)}, u32[]{:S(2)}) collective-permute-start(bf16[256,256]{1,0:T(8,128)(2,1)S(1)} %get-tuple-element.46), channel_id=1, source_target_pairs={{0,1},{1,0},{2,3},{3,2},{4,5},{5,4},{6,7},{7,6},{8,9},{9,8},{10,11... | collective-permute-start | bytes 393224 | tf_op jit(solution)/shard_map/ppermute | solution.py:24
  6.8 9.9 %collective-permute-start.12 = (bf16[256,256]{1,0:T(8,128)(2,1)S(1)}, bf16[256,256]{1,0:T(8,128)(2,1)S(1)}, u32[]{:S(2)}, u32[]{:S(2)}) collective-permute-start(bf16[256,256]{1,0:T(8,128)(2,1)S(1)} %get-tuple-element.45), channel_id=1, source_target_pairs={{0,4},{1,5},{2,6},{3,7},{4,0},{5,1},{6,2},{7,3},{8,12},{9,13},{10,... | collective-permute-start | bytes 393224 | tf_op jit(solution)/shard_map/ppermute | solution.py:24
  12.9 26.9 %collective-permute-start.10 = (bf16[4,256,256]{2,1,0:T(8,128)(2,1)S(1)}, bf16[4,256,256]{2,1,0:T(8,128)(2,1)S(1)}, u32[]{:S(2)}, u32[]{:S(2)}) collective-permute-start(bf16[4,256,256]{2,1,0:T(8,128)(2,1)S(1)} %pad_maximum_fusion.refs_4_), channel_id=1, source_target_pairs={{0,4},{1,5},{2,6},{3,7},{4,0},{5,1},{6,2},{7,3},{8,12},{9,13},{10,... | collective-permute-start | bytes 1572872 | tf_op jit(solution)/shard_map/ppermute | solution.py:24
  16.0 31.3 %collective-permute-start.1 = (bf16[256,256]{1,0:T(8,128)(2,1)S(1)}, bf16[256,256]{1,0:T(8,128)(2,1)S(1)}, u32[]{:S(2)}, u32[]{:S(2)}) collective-permute-start(bf16[256,256]{1,0:T(8,128)(2,1)S(1)} %get-tuple-element.45), channel_id=1, source_target_pairs={{0,0},{1,121},{2,114},{3,107},{4,100},{5,93},{6,86},{7,79},{8,8},{... | collective-permute-start | bytes 393224 | tf_op jit(solution)/shard_map/ppermute | solution.py:24
  16.7 10.0 %collective-permute-start.13 = (bf16[2,256,256]{2,1,0:T(8,128)(2,1)S(1)}, bf16[2,256,256]{2,1,0:T(8,128)(2,1)S(1)}, u32[]{:S(2)}, u32[]{:S(2)}) collective-permute-start(bf16[2,256,256]{2,1,0:T(8,128)(2,1)S(1)} %pad_maximum_fusion.2.refs_0_), channel_id=1, source_target_pairs={{0,1},{1,0},{2,3},{3,2},{4,5},{5,4},{6,7},{7,6},{8,9},{9,8},{10,11... | collective-permute-start | bytes 786440 | tf_op jit(solution)/shard_map/ppermute | solution.py:24
  20.9 16.3 %collective-permute-start.14 = (bf16[2,256,256]{2,1,0:T(8,128)(2,1)S(1)}, bf16[2,256,256]{2,1,0:T(8,128)(2,1)S(1)}, u32[]{:S(2)}, u32[]{:S(2)}) collective-permute-start(bf16[2,256,256]{2,1,0:T(8,128)(2,1)S(1)} %pad_maximum_fusion.2.refs_0_), channel_id=1, source_target_pairs={{0,2},{1,3},{2,0},{3,1},{4,6},{5,7},{6,4},{7,5},{8,10},{9,11},{10,... | collective-permute-start | bytes 786440 | tf_op jit(solution)/shard_map/ppermute | solution.py:24
  24.5 15.3 %collective-permute-start.15 = (bf16[2,256,256]{2,1,0:T(8,128)(2,1)S(1)}, bf16[2,256,256]{2,1,0:T(8,128)(2,1)S(1)}, u32[]{:S(2)}, u32[]{:S(2)}) collective-permute-start(bf16[2,256,256]{2,1,0:T(8,128)(2,1)S(1)} %pad_maximum_fusion.2.refs_0_), channel_id=1, source_target_pairs={{0,3},{1,2},{2,1},{3,0},{4,7},{5,6},{6,5},{7,4},{8,11},{9,10},{10,... | collective-permute-start | bytes 786440 | tf_op jit(solution)/shard_map/ppermute | solution.py:24
  24.5 99.9 %copy-start.4 = (s32[4]{0:T(128)}, s32[4]{0:T(128)S(1)}, u32[]{:S(2)}) copy-start(s32[4]{0:T(128)S(1)} %pad_add_fusion.ids_ref) | copy-start | bytes 52
  26.7 20.6 %collective-permute-start.2 = (bf16[256,256]{1,0:T(8,128)(2,1)S(1)}, bf16[256,256]{1,0:T(8,128)(2,1)S(1)}, u32[]{:S(2)}, u32[]{:S(2)}) collective-permute-start(bf16[256,256]{1,0:T(8,128)(2,1)S(1)} %get-tuple-element.45), channel_id=1, source_target_pairs={{0,100},{1,93},{2,86},{3,79},{4,0},{5,121},{6,114},{7,107},{8,108}... | collective-permute-start | bytes 393224 | tf_op jit(solution)/shard_map/ppermute | solution.py:24
  46.6 75.1 %collective-permute-start.16 = (s16[4,2,272,256]{3,2,1,0:T(8,128)(2,1)S(1)}, s16[4,2,272,256]{3,2,1,0:T(8,128)(2,1)S(1)}, u32[]{:S(2)}, u32[]{:S(2)}) collective-permute-start(s16[4,2,272,256]{3,2,1,0:T(8,128)(2,1)S(1)} %shard_map.59), channel_id=1, source_target_pairs={{0,0},{1,9},{2,18},{3,27},{4,36},{5,45},{6,54},{7,63},{8,8},{9,17}... | collective-permute-start | bytes 3342344 | tf_op jit(solution)/shard_map/ppermute | solution.py:24
  47.4 32.3 %collective-permute-start.3 = (bf16[2,256,256]{2,1,0:T(8,128)(2,1)S(1)}, bf16[2,256,256]{2,1,0:T(8,128)(2,1)S(1)}, u32[]{:S(2)}, u32[]{:S(2)}) collective-permute-start(bf16[2,256,256]{2,1,0:T(8,128)(2,1)S(1)} %pad_maximum_fusion.1.refs_0_), channel_id=1, source_target_pairs={{0,121},{1,8},{2,123},{3,10},{4,125},{5,12},{6,127},{7,14},{8,1},{... | collective-permute-start | bytes 786440 | tf_op jit(solution)/shard_map/ppermute | solution.py:24
  50.5 37.9 %collective-permute-start.4 = (bf16[2,256,256]{2,1,0:T(8,128)(2,1)S(1)}, bf16[2,256,256]{2,1,0:T(8,128)(2,1)S(1)}, u32[]{:S(2)}, u32[]{:S(2)}) collective-permute-start(bf16[2,256,256]{2,1,0:T(8,128)(2,1)S(1)} %pad_maximum_fusion.1.refs_0_), channel_id=1, source_target_pairs={{0,114},{1,115},{2,16},{3,17},{4,118},{5,119},{6,20},{7,21},{8,122... | collective-permute-start | bytes 786440 | tf_op jit(solution)/shard_map/ppermute | solution.py:24
  53.2 56.3 %collective-permute-start.9 = (bf16[4,256,256]{2,1,0:T(8,128)(2,1)S(1)}, bf16[4,256,256]{2,1,0:T(8,128)(2,1)S(1)}, u32[]{:S(2)}, u32[]{:S(2)}) collective-permute-start(bf16[4,256,256]{2,1,0:T(8,128)(2,1)S(1)} %pad_maximum_fusion.refs_4_), channel_id=1, source_target_pairs={{0,0},{1,121},{2,114},{3,107},{4,100},{5,93},{6,86},{7,79},{8,8},{... | collective-permute-start | bytes 1572872 | tf_op jit(solution)/shard_map/ppermute | solution.py:24
  53.9 55.6 %collective-permute-start.11 = (bf16[4,256,256]{2,1,0:T(8,128)(2,1)S(1)}, bf16[4,256,256]{2,1,0:T(8,128)(2,1)S(1)}, u32[]{:S(2)}, u32[]{:S(2)}) collective-permute-start(bf16[4,256,256]{2,1,0:T(8,128)(2,1)S(1)} %collective-permute-done.10.refs_5_), channel_id=1, source_target_pairs={{0,0},{1,121},{2,114},{3,107},{4,100},{5,93},{6,86},{7,79},{8,8},{... | collective-permute-start | bytes 1572872 | tf_op jit(solution)/shard_map/ppermute | solution.py:24
  79.7 17.8 %collective-permute-start = (s32[2,1,2048]{2,1,0:T(1,128)S(1)}, s32[2,1,2048]{2,1,0:T(1,128)S(1)}, u32[]{:S(2)}, u32[]{:S(2)}) collective-permute-start(s32[2,1,2048]{2,1,0:T(1,128)S(1)} %copy-done.3), channel_id=1, source_target_pairs={{0,0},{1,121},{2,114},{3,107},{4,100},{5,93},{6,86},{7,79},{8,8},{... | collective-permute-start | bytes 49160 | tf_op jit(solution)/shard_map/ppermute | solution.py:24
  88.4 9.1 %collective-permute-start.5 = (bf16[2,256,256]{2,1,0:T(8,128)(2,1)S(1)}, bf16[2,256,256]{2,1,0:T(8,128)(2,1)S(1)}, u32[]{:S(2)}, u32[]{:S(2)}) collective-permute-start(bf16[2,256,256]{2,1,0:T(8,128)(2,1)S(1)} %pad_maximum_fusion.1.refs_0_), channel_id=1, source_target_pairs={{0,107},{1,122},{2,9},{3,24},{4,111},{5,126},{6,13},{7,28},{8,115}... | collective-permute-start | bytes 786440 | tf_op jit(solution)/shard_map/ppermute | solution.py:24
  95.2 0.7 copy-start.1
  97.5 24.2 %collective-permute-start.24 = (s16[2,272,256]{2,1,0:T(8,128)(2,1)S(1)}, s16[2,272,256]{2,1,0:T(8,128)(2,1)S(1)}, u32[]{:S(2)}, u32[]{:S(2)}) collective-permute-start(s16[2,272,256]{2,1,0:T(8,128)(2,1)S(1)} %get-tuple-element.36), channel_id=1, source_target_pairs={{0,121},{1,8},{2,123},{3,10},{4,125},{5,12},{6,127},{7,14},{8,1},{... | collective-permute-start | bytes 835592 | tf_op jit(solution)/shard_map/ppermute | solution.py:24
  97.5 34.6 %collective-permute-start.25 = (s16[2,272,256]{2,1,0:T(8,128)(2,1)S(1)}, s16[2,272,256]{2,1,0:T(8,128)(2,1)S(1)}, u32[]{:S(2)}, u32[]{:S(2)}) collective-permute-start(s16[2,272,256]{2,1,0:T(8,128)(2,1)S(1)} %get-tuple-element.37), channel_id=1, source_target_pairs={{0,114},{1,115},{2,16},{3,17},{4,118},{5,119},{6,20},{7,21},{8,122... | collective-permute-start | bytes 835592 | tf_op jit(solution)/shard_map/ppermute | solution.py:24
  109.5 22.6 %collective-permute-start.26 = (s16[2,272,256]{2,1,0:T(8,128)(2,1)S(1)}, s16[2,272,256]{2,1,0:T(8,128)(2,1)S(1)}, u32[]{:S(2)}, u32[]{:S(2)}) collective-permute-start(s16[2,272,256]{2,1,0:T(8,128)(2,1)S(1)} %get-tuple-element.38), channel_id=1, source_target_pairs={{0,107},{1,122},{2,9},{3,24},{4,111},{5,126},{6,13},{7,28},{8,115}... | collective-permute-start | bytes 835592 | tf_op jit(solution)/shard_map/ppermute | solution.py:24
  116.4 14.9 %copy-start.2 = (s16[2,272,256]{2,1,0:T(8,128)(2,1)}, s16[2,272,256]{2,1,0:T(8,128)(2,1)S(1)}, u32[]{:S(2)}) copy-start(s16[2,272,256]{2,1,0:T(8,128)(2,1)S(1)} %get-tuple-element.27.refs_0_) | copy-start | bytes 835588
  116.5 20.8 %collective-permute-start.20 = (s16[2,272,256]{2,1,0:T(8,128)(2,1)S(1)}, s16[2,272,256]{2,1,0:T(8,128)(2,1)S(1)}, u32[]{:S(2)}, u32[]{:S(2)}) collective-permute-start(s16[2,272,256]{2,1,0:T(8,128)(2,1)S(1)} %get-tuple-element.28), channel_id=1, source_target_pairs={{0,1},{1,0},{2,3},{3,2},{4,5},{5,4},{6,7},{7,6},{8,9},{9,8},{10,11... | collective-permute-start | bytes 835592 | tf_op jit(solution)/shard_map/ppermute | solution.py:24
  121.7 9.6 %copy-start.7 = (s16[2,272,256]{2,1,0:T(8,128)(2,1)}, s16[2,272,256]{2,1,0:T(8,128)(2,1)S(1)}, u32[]{:S(2)}) copy-start(s16[2,272,256]{2,1,0:T(8,128)(2,1)S(1)} %collective-permute-done.24.refs_1_) | copy-start | bytes 835588
  121.7 15.6 %collective-permute-start.21 = (s16[2,272,256]{2,1,0:T(8,128)(2,1)S(1)}, s16[2,272,256]{2,1,0:T(8,128)(2,1)S(1)}, u32[]{:S(2)}, u32[]{:S(2)}) collective-permute-start(s16[2,272,256]{2,1,0:T(8,128)(2,1)S(1)} %get-tuple-element.29), channel_id=1, source_target_pairs={{0,2},{1,3},{2,0},{3,1},{4,6},{5,7},{6,4},{7,5},{8,10},{9,11},{10,... | collective-permute-start | bytes 835592 | tf_op jit(solution)/shard_map/ppermute | solution.py:24
  121.7 16.0 %collective-permute-start.22 = (s16[2,272,256]{2,1,0:T(8,128)(2,1)S(1)}, s16[2,272,256]{2,1,0:T(8,128)(2,1)S(1)}, u32[]{:S(2)}, u32[]{:S(2)}) collective-permute-start(s16[2,272,256]{2,1,0:T(8,128)(2,1)S(1)} %get-tuple-element.30), channel_id=1, source_target_pairs={{0,3},{1,2},{2,1},{3,0},{4,7},{5,6},{6,5},{7,4},{8,11},{9,10},{10,... | collective-permute-start | bytes 835592 | tf_op jit(solution)/shard_map/ppermute | solution.py:24
  131.3 0.7 copy-start
  132.0 0.7 copy-start.8
  132.1 0.8 copy-start.10
  135.2 13.4 %collective-permute-start.27 = (s16[2,272,256]{2,1,0:T(8,128)(2,1)}, s16[2,272,256]{2,1,0:T(8,128)(2,1)S(1)}, u32[]{:S(2)}, u32[]{:S(2)}) collective-permute-start(s16[2,272,256]{2,1,0:T(8,128)(2,1)} %sum.3), channel_id=1, source_target_pairs={{0,4},{1,13},{2,22},{3,31},{4,32},{5,41},{6,50},{7,59},{8,12},{9,2... | collective-permute-start | bytes 835592 | tf_op jit(solution)/shard_map/ppermute | solution.py:24
  137.3 0.7 copy-start.9
  137.3 0.8 copy-start.11
  137.7 0.7 copy-start.12
  140.7 10.4 %collective-permute-start.23 = (s16[2,272,256]{2,1,0:T(8,128)(2,1)}, s16[2,272,256]{2,1,0:T(8,128)(2,1)S(1)}, u32[]{:S(2)}, u32[]{:S(2)}) collective-permute-start(s16[2,272,256]{2,1,0:T(8,128)(2,1)} %sum.2), channel_id=1, source_target_pairs={{0,4},{1,5},{2,6},{3,7},{4,0},{5,1},{6,2},{7,3},{8,12},{9,13},{10,... | collective-permute-start | bytes 835592 | tf_op jit(solution)/shard_map/ppermute | solution.py:24
  142.7 9.5 %collective-permute-start.17 = (s16[2,272,256]{2,1,0:T(8,128)(2,1)S(1)}, s16[2,272,256]{2,1,0:T(8,128)(2,1)S(1)}, u32[]{:S(2)}, u32[]{:S(2)}) collective-permute-start(s16[2,272,256]{2,1,0:T(8,128)(2,1)S(1)} %get-tuple-element.24), channel_id=1, source_target_pairs={{0,1},{1,0},{2,3},{3,2},{4,5},{5,4},{6,7},{7,6},{8,9},{9,8},{10,11... | collective-permute-start | bytes 835592 | tf_op jit(solution)/shard_map/ppermute | solution.py:24
  142.7 16.5 %collective-permute-start.18 = (s16[2,272,256]{2,1,0:T(8,128)(2,1)S(1)}, s16[2,272,256]{2,1,0:T(8,128)(2,1)S(1)}, u32[]{:S(2)}, u32[]{:S(2)}) collective-permute-start(s16[2,272,256]{2,1,0:T(8,128)(2,1)S(1)} %get-tuple-element.25), channel_id=1, source_target_pairs={{0,2},{1,3},{2,0},{3,1},{4,6},{5,7},{6,4},{7,5},{8,10},{9,11},{10,... | collective-permute-start | bytes 835592 | tf_op jit(solution)/shard_map/ppermute | solution.py:24
  147.3 14.5 %collective-permute-start.19 = (s16[2,272,256]{2,1,0:T(8,128)(2,1)S(1)}, s16[2,272,256]{2,1,0:T(8,128)(2,1)S(1)}, u32[]{:S(2)}, u32[]{:S(2)}) collective-permute-start(s16[2,272,256]{2,1,0:T(8,128)(2,1)S(1)} %get-tuple-element.26), channel_id=1, source_target_pairs={{0,3},{1,2},{2,1},{3,0},{4,7},{5,6},{6,5},{7,4},{8,11},{9,10},{10,... | collective-permute-start | bytes 835592 | tf_op jit(solution)/shard_map/ppermute | solution.py:24
  148.5 13.2 %copy-start.13 = (s16[2,272,256]{2,1,0:T(8,128)(2,1)}, s16[2,272,256]{2,1,0:T(8,128)(2,1)S(1)}, u32[]{:S(2)}) copy-start(s16[2,272,256]{2,1,0:T(8,128)(2,1)S(1)} %collective-permute-done.27.refs_5_) | copy-start | bytes 835588
  151.1 10.7 %copy-start.14 = (s16[2,272,256]{2,1,0:T(8,128)(2,1)}, s16[2,272,256]{2,1,0:T(8,128)(2,1)S(1)}, u32[]{:S(2)}) copy-start(s16[2,272,256]{2,1,0:T(8,128)(2,1)S(1)} %collective-permute-done.23.refs_4_) | copy-start | bytes 835588
  152.2 9.6 %copy-start.15 = (s16[2,272,256]{2,1,0:T(8,128)(2,1)}, s16[2,272,256]{2,1,0:T(8,128)(2,1)S(1)}, u32[]{:S(2)}) copy-start(s16[2,272,256]{2,1,0:T(8,128)(2,1)S(1)} %collective-permute-done.17.refs_1_) | copy-start | bytes 835588
  159.2 2.6 %copy-start.16 = (s16[2,272,256]{2,1,0:T(8,128)(2,1)}, s16[2,272,256]{2,1,0:T(8,128)(2,1)S(1)}, u32[]{:S(2)}) copy-start(s16[2,272,256]{2,1,0:T(8,128)(2,1)S(1)} %collective-permute-done.18.refs_2_) | copy-start | bytes 835588
  161.8 0.7 copy-start.17
  165.8 33.8 %copy-start.5 = (f32[2,256,256]{2,1,0:T(8,128)S(1)}, f32[2,256,256]{2,1,0:T(8,128)}, u32[]{:S(2)}) copy-start(f32[2,256,256]{2,1,0:T(8,128)} %get-tuple-element.39.samples_ref) | copy-start | bytes 1572868
  165.8 33.8 %collective-permute-start.28 = (f32[256,256]{1,0:T(8,128)}, f32[256,256]{1,0:T(8,128)S(1)}, u32[]{:S(2)}, u32[]{:S(2)}) collective-permute-start(f32[256,256]{1,0:T(8,128)} %get-tuple-element.40.other_ref), channel_id=1, source_target_pairs={{0,4},{1,5},{2,6},{3,7},{4,0},{5,1},{6,2},{7,3},{8,12},{9,13},{10,... | collective-permute-start | bytes 786440 | tf_op jit(solution)/shard_map/ppermute | solution.py:24
  168.0 7.3 %collective-permute-start.29 = (f32[384,128]{1,0:T(8,128)}, f32[384,128]{1,0:T(8,128)S(1)}, u32[]{:S(2)}, u32[]{:S(2)}) collective-permute-start(f32[384,128]{1,0:T(8,128)} %get-tuple-element.41.refs_0_), channel_id=1, source_target_pairs={{0,1},{1,0},{2,3},{3,2},{4,5},{5,4},{6,7},{7,6},{8,9},{9,8},{10,11... | collective-permute-start | bytes 589832 | tf_op jit(solution)/shard_map/ppermute | solution.py:24
  168.0 9.5 %collective-permute-start.30 = (f32[384,128]{1,0:T(8,128)}, f32[384,128]{1,0:T(8,128)S(1)}, u32[]{:S(2)}, u32[]{:S(2)}) collective-permute-start(f32[384,128]{1,0:T(8,128)} %get-tuple-element.41.refs_0_), channel_id=1, source_target_pairs={{0,2},{1,3},{2,0},{3,1},{4,6},{5,7},{6,4},{7,5},{8,10},{9,11},{10,... | collective-permute-start | bytes 589832 | tf_op jit(solution)/shard_map/ppermute | solution.py:24
  169.7 9.8 %collective-permute-start.31 = (f32[384,128]{1,0:T(8,128)}, f32[384,128]{1,0:T(8,128)S(1)}, u32[]{:S(2)}, u32[]{:S(2)}) collective-permute-start(f32[384,128]{1,0:T(8,128)} %get-tuple-element.41.refs_0_), channel_id=1, source_target_pairs={{0,3},{1,2},{2,1},{3,0},{4,7},{5,6},{6,5},{7,4},{8,11},{9,10},{10,... | collective-permute-start | bytes 589832 | tf_op jit(solution)/shard_map/ppermute | solution.py:24
  175.3 4.3 %copy-start.18 = (f32[384,128]{1,0:T(8,128)}, f32[384,128]{1,0:T(8,128)S(1)}, u32[]{:S(2)}) copy-start(f32[384,128]{1,0:T(8,128)S(1)} %collective-permute-done.29.refs_1_) | copy-start | bytes 589828
  177.5 2.1 %copy-start.19 = (f32[384,128]{1,0:T(8,128)}, f32[384,128]{1,0:T(8,128)S(1)}, u32[]{:S(2)}) copy-start(f32[384,128]{1,0:T(8,128)S(1)} %collective-permute-done.30.refs_2_) | copy-start | bytes 589828
  179.5 0.7 copy-start.20
  198.3 6.8 %collective-permute-start.32 = (s16[272,256]{1,0:T(8,128)(2,1)}, s16[272,256]{1,0:T(8,128)(2,1)S(1)}, u32[]{:S(2)}, u32[]{:S(2)}) collective-permute-start(s16[272,256]{1,0:T(8,128)(2,1)} %get-tuple-element.43), channel_id=1, source_target_pairs={{0,4},{1,5},{2,6},{3,7},{4,0},{5,1},{6,2},{7,3},{8,12},{9,13},{10,... | collective-permute-start | bytes 417800 | tf_op jit(solution)/shard_map/ppermute | solution.py:24
  199.6 6.3 %copy-start.6 = (f32[2,256,256]{2,1,0:T(8,128)}, f32[2,256,256]{2,1,0:T(8,128)S(1)}, u32[]{:S(2)}) copy-start(f32[2,256,256]{2,1,0:T(8,128)S(1)} %bitcast_dynamic-update-slice_fusion) | copy-start | bytes 1572868

commit v6 on v5

--- a/solution.py
+++ b/solution.py
@@ -128,22 +128,23 @@
 
 
 def sum_kernel(count, *refs):
-    out_ref = refs[-1]
-    for a in range(2):
-        total = decoded(refs[0][a])
-        for ref in refs[1:count]:
-            total = total + decoded(ref[a])
-        out_ref[a] = coded(total)
-
-
-def summed(codes, after=()):
+    first_ref, second_ref = refs[-2:]
+    for out_ref, codes in ((first_ref, refs[:count]), (second_ref, refs[count : 2 * count])):
+        for a in range(2):
+            total = decoded(codes[0][a])
+            for ref in codes[1:]:
+                total = total + decoded(ref[a])
+            out_ref[a] = coded(total)
+
+
+def summed(first, second, after):
     vmem, unread = pl.BlockSpec(memory_space=pltpu.VMEM), pl.BlockSpec(memory_space=pl.ANY)
     return pl.pallas_call(
-        functools.partial(sum_kernel, len(codes)),
-        in_specs=[vmem] * len(codes) + [unread] * len(after),
-        out_shape=jax.ShapeDtypeStruct(codes[0].shape, jnp.int16),
+        functools.partial(sum_kernel, len(first)),
+        in_specs=[vmem] * (2 * len(first)) + [unread],
+        out_shape=[jax.ShapeDtypeStruct(first[0].shape, jnp.int16)] * 2,
         name="sum",
-    )(*codes, *after)
+    )(*first, *second, after)
 
 
 def gram_kernel(ids_ref, *refs):
@@ -342,16 +343,14 @@
     (more,) = products(ids, weight, perm, *own_blocks, tiles, True, 0)
     more = sent(more, lambda r, c: (r + c, c))
     back = products(ids, weight, perm, *own_blocks, tiles, True, 1)
-    back, far_pairs = lax.optimization_barrier((back, far_pairs))
     back = [back[0]] + [sent(back[d], slanted(d)) for d in depths]
     given = products(ids, weight, far_perm, *far_blocks, tiles, False, 1)
     given = [given[0]] + [sent(given[d], same(d)) for d in depths]
     kept = products(ids, weight, far_perm, *far_blocks, tiles, False, 0, (more,))
-    after = kept[:1]
+    after = kept[0]
     kept = [kept[0]] + [sent(kept[d], same(d)) for d in depths]
-    crossed = summed(given, after)
+    crossed, arrived = summed(given, back, after)
     crossed = sent(crossed, same(nz))
-    arrived = summed(back, after)
     arrived = sent(arrived, lambda r, c: (r + c, c ^ nz))
     samples, swapped, gram = gram_of(ids, [*kept, crossed, arrived])
     grams = [gram] + [sent(gram, same(d)) for d in depths]

time: 206 us -> 215 us (1.044)
  starting transfers between devices: 69 us -> 103 us
  waiting for transfers between devices: 76.1 us -> 53.8 us
    ppermute x33, starting transfers between devices: 69 us -> 103 us  [sent(): return lax.ppermute(value, AXES, pairs)]
    ppermute x33, waiting for transfers between devices: 76.1 us -> 53.8 us  [sent(): return lax.ppermute(value, AXES, pairs)]
    pallas_call x2 -> x1, Pallas kernels: 4.61 us -> 3.01 us  [summed(): pl.pallas_call(functools.partial(sum_kernel, len(first)), in_specs=[vmem]...]
  transfers between devices with their start and end apart: 33 -> 33, of which waited for: 18 -> 15; matrix products, arithmetic and copies ran while one was open for 0% -> 0% of each run, Pallas kernels for 24% -> 23%
where the time goes in v6:
time: 215 us; the launch traced here: 214 us
  starting transfers between devices  103 us (48%)
  waiting for transfers between devices  53.8 us (25%)
  Pallas kernels  51.8 us (24%)
  local copies, waits for them, and re-layouts  3.92 us (2%)
    ppermute x33, starting transfers between devices, sent(): return lax.ppermute(value, AXES, pairs)  103 us
    ppermute x33, waiting for transfers between devices, sent(): return lax.ppermute(value, AXES, pairs)  53.8 us
    pallas_call x4, Pallas kernels, products(): pl.pallas_call(functools.partial(product_kernel, back, part), out_shape=[...  27.4 us
    pallas_call x1, Pallas kernels, orthogonal(): pl.pallas_call(functools.partial(factor_kernel, scale), in_specs=[pl.Bloc...  18.1 us
  transfers between devices with their start and end apart: 33, of which 15 were waited for; matrix products, arithmetic and copies ran while one was open for 0% of the time, Pallas kernels for 23%

profile of v6, /device:TPU:0, one launch (start us, length us, event | category | flops | bytes accessed | tf_op | source)
XLA Modules:
  0.0 214.2 jit_solution(11921094628416687195)
XLA Ops:
  0.7 1.0 fusion.5
  1.7 4.2 %collective-permute-start.8 = (bf16[256,256]{1,0:T(8,128)(2,1)S(1)}, bf16[256,256]{1,0:T(8,128)(2,1)S(1)}, u32[]{:S(2)}, u32[]{:S(2)}) collective-permute-start(bf16[256,256]{1,0:T(8,128)(2,1)S(1)} %get-tuple-element.42), channel_id=1, source_target_pairs={{0,3},{1,2},{2,1},{3,0},{4,7},{5,6},{6,5},{7,4},{8,11},{9,10},{10,... | collective-permute-start | bytes 393224 | tf_op jit(solution)/shard_map/ppermute | solution.py:24
  5.9 0.0 collective-permute-start.7
  5.9 0.9 collective-permute-start.6
  6.8 3.0 %collective-permute-start.12 = (bf16[256,256]{1,0:T(8,128)(2,1)S(1)}, bf16[256,256]{1,0:T(8,128)(2,1)S(1)}, u32[]{:S(2)}, u32[]{:S(2)}) collective-permute-start(bf16[256,256]{1,0:T(8,128)(2,1)S(1)} %get-tuple-element.41), channel_id=1, source_target_pairs={{0,4},{1,5},{2,6},{3,7},{4,0},{5,1},{6,2},{7,3},{8,12},{9,13},{10,... | collective-permute-start | bytes 393224 | tf_op jit(solution)/shard_map/ppermute | solution.py:24
  9.9 1.6 collective-permute-done.8
  11.5 2.3 %collective-permute-done.7 = bf16[256,256]{1,0:T(8,128)(2,1)S(1)} collective-permute-done((bf16[256,256]{1,0:T(8,128)(2,1)S(1)}, bf16[256,256]{1,0:T(8,128)(2,1)S(1)}, u32[]{:S(2)}, u32[]{:S(2)}) %collective-permute-start.7) | collective-permute-done | bytes 131104 | tf_op jit(solution)/shard_map/ppermute | solution.py:24
  13.8 0.0 collective-permute-done.6
  13.8 0.1 pad_maximum_fusion.refs_4_
  13.8 3.1 %collective-permute-start.10 = (bf16[4,256,256]{2,1,0:T(8,128)(2,1)S(1)}, bf16[4,256,256]{2,1,0:T(8,128)(2,1)S(1)}, u32[]{:S(2)}, u32[]{:S(2)}) collective-permute-start(bf16[4,256,256]{2,1,0:T(8,128)(2,1)S(1)} %pad_maximum_fusion.refs_4_), channel_id=1, source_target_pairs={{0,4},{1,5},{2,6},{3,7},{4,0},{5,1},{6,2},{7,3},{8,12},{9,13},{10,... | collective-permute-start | bytes 1572872 | tf_op jit(solution)/shard_map/ppermute | solution.py:24
  16.9 3.0 %collective-permute-start.2 = (bf16[256,256]{1,0:T(8,128)(2,1)S(1)}, bf16[256,256]{1,0:T(8,128)(2,1)S(1)}, u32[]{:S(2)}, u32[]{:S(2)}) collective-permute-start(bf16[256,256]{1,0:T(8,128)(2,1)S(1)} %get-tuple-element.41), channel_id=1, source_target_pairs={{0,100},{1,93},{2,86},{3,79},{4,0},{5,121},{6,114},{7,107},{8,108}... | collective-permute-start | bytes 393224 | tf_op jit(solution)/shard_map/ppermute | solution.py:24
  19.9 0.0 collective-permute-done.12
  19.9 0.1 collective-permute-start.13
  20.0 2.7 %collective-permute-start.14 = (bf16[2,256,256]{2,1,0:T(8,128)(2,1)S(1)}, bf16[2,256,256]{2,1,0:T(8,128)(2,1)S(1)}, u32[]{:S(2)}, u32[]{:S(2)}) collective-permute-start(bf16[2,256,256]{2,1,0:T(8,128)(2,1)S(1)} %pad_maximum_fusion.2.refs_0_), channel_id=1, source_target_pairs={{0,2},{1,3},{2,0},{3,1},{4,6},{5,7},{6,4},{7,5},{8,10},{9,11},{10,... | collective-permute-start | bytes 786440 | tf_op jit(solution)/shard_map/ppermute | solution.py:24
  22.7 2.0 collective-permute-start.15
  24.7 0.1 pad_add_fusion.ids_ref
  24.8 4.4 %collective-permute-done.13.refs_1_ = bf16[2,256,256]{2,1,0:T(8,128)(2,1)S(1)} collective-permute-done((bf16[2,256,256]{2,1,0:T(8,128)(2,1)S(1)}, bf16[2,256,256]{2,1,0:T(8,128)(2,1)S(1)}, u32[]{:S(2)}, u32[]{:S(2)}) %collective-permute-start.13) | collective-permute-done | bytes 262176 | tf_op jit(solution)/shard_map/ppermute | solution.py:24
  29.2 0.7 collective-permute-start.1
  29.9 4.9 %collective-permute-done.14.refs_2_ = bf16[2,256,256]{2,1,0:T(8,128)(2,1)S(1)} collective-permute-done((bf16[2,256,256]{2,1,0:T(8,128)(2,1)S(1)}, bf16[2,256,256]{2,1,0:T(8,128)(2,1)S(1)}, u32[]{:S(2)}, u32[]{:S(2)}) %collective-permute-start.14) | collective-permute-done | bytes 262176 | tf_op jit(solution)/shard_map/ppermute | solution.py:24
  34.8 3.9 %collective-permute-done.15.refs_3_ = bf16[2,256,256]{2,1,0:T(8,128)(2,1)S(1)} collective-permute-done((bf16[2,256,256]{2,1,0:T(8,128)(2,1)S(1)}, bf16[2,256,256]{2,1,0:T(8,128)(2,1)S(1)}, u32[]{:S(2)}, u32[]{:S(2)}) %collective-permute-start.15) | collective-permute-done | bytes 262176 | tf_op jit(solution)/shard_map/ppermute | solution.py:24
  38.6 6.8 %shard_map.59 = s16[4,2,272,256]{3,2,1,0:T(8,128)(2,1)S(1)} custom-call(s32[4]{0:T(128)S(1)} %pad_add_fusion.ids_ref, f32[2]{0:T(128)S(1)} %fusion.4.weight_ref, s32[2,1,2048]{2,1,0:T(1,128)S(1)} %copy-done.3, bf16[2,256,256]{2,1,0:T(8,128)(2,1)S(1)} %pad_maximum_fusion.2.refs_0_, bf16[2,256,256]{2,1,0:T(8,128)(2,1)S(1)} %collective-permute-done.13.refs_1_, ...), custom_call_target="tpu_custom_call" | custom-call | flops 4294967296 | bytes 11534336 | tf_op jit(solution)/shard_map/pallas_call | solution.py:114
  45.4 0.7 collective-permute-start.16
  46.2 3.3 %collective-permute-start.3 = (bf16[2,256,256]{2,1,0:T(8,128)(2,1)S(1)}, bf16[2,256,256]{2,1,0:T(8,128)(2,1)S(1)}, u32[]{:S(2)}, u32[]{:S(2)}) collective-permute-start(bf16[2,256,256]{2,1,0:T(8,128)(2,1)S(1)} %pad_maximum_fusion.1.refs_0_), channel_id=1, source_target_pairs={{0,121},{1,8},{2,123},{3,10},{4,125},{5,12},{6,127},{7,14},{8,1},{... | collective-permute-start | bytes 786440 | tf_op jit(solution)/shard_map/ppermute | solution.py:24
  49.6 0.7 collective-permute-start.9
  50.2 0.7 collective-permute-start.11
  50.9 0.7 collective-permute-start
  51.6 50.9 %collective-permute-start.4 = (bf16[2,256,256]{2,1,0:T(8,128)(2,1)S(1)}, bf16[2,256,256]{2,1,0:T(8,128)(2,1)S(1)}, u32[]{:S(2)}, u32[]{:S(2)}) collective-permute-start(bf16[2,256,256]{2,1,0:T(8,128)(2,1)S(1)} %pad_maximum_fusion.1.refs_0_), channel_id=1, source_target_pairs={{0,114},{1,115},{2,16},{3,17},{4,118},{5,119},{6,20},{7,21},{8,122... | collective-permute-start | bytes 786440 | tf_op jit(solution)/shard_map/ppermute | solution.py:24
  102.5 6.8 %shard_map.62 = (s16[2,272,256]{2,1,0:T(8,128)(2,1)S(1)}, s16[2,272,256]{2,1,0:T(8,128)(2,1)S(1)}, s16[2,272,256]{2,1,0:T(8,128)(2,1)S(1)}, s16[2,272,256]{2,1,0:T(8,128)(2,1)S(1)}) custom-call(s32[4]{0:T(128)S(1)} %pad_add_fusion.ids_ref, f32[2]{0:T(128)S(1)} %fusion.4.weight_ref, s32[2,1,2048]{2,1,0:T(1,128)S(1)} %copy-done.3, ...), custom_call_target="tpu_custom_call" | custom-call | flops 4294967296 | bytes 11534336 | tf_op jit(solution)/shard_map/pallas_call | solution.py:114
  109.3 0.1 collective-permute-start.23
  109.4 2.2 %collective-permute-done.5.refs_3_ = bf16[2,256,256]{2,1,0:T(8,128)(2,1)S(1)} collective-permute-done((bf16[2,256,256]{2,1,0:T(8,128)(2,1)S(1)}, bf16[2,256,256]{2,1,0:T(8,128)(2,1)S(1)}, u32[]{:S(2)}, u32[]{:S(2)}) %collective-permute-start.5) | collective-permute-done | bytes 262176 | tf_op jit(solution)/shard_map/ppermute | solution.py:24
  111.6 5.2 %collective-permute-start.24 = (s16[2,272,256]{2,1,0:T(8,128)(2,1)S(1)}, s16[2,272,256]{2,1,0:T(8,128)(2,1)S(1)}, u32[]{:S(2)}, u32[]{:S(2)}) collective-permute-start(s16[2,272,256]{2,1,0:T(8,128)(2,1)S(1)} %get-tuple-element.31), channel_id=1, source_target_pairs={{0,114},{1,115},{2,16},{3,17},{4,118},{5,119},{6,20},{7,21},{8,122... | collective-permute-start | bytes 835592 | tf_op jit(solution)/shard_map/ppermute | solution.py:24
  116.8 7.0 %shard_map.61 = (s16[2,272,256]{2,1,0:T(8,128)(2,1)S(1)}, s16[2,272,256]{2,1,0:T(8,128)(2,1)S(1)}, s16[2,272,256]{2,1,0:T(8,128)(2,1)S(1)}, s16[2,272,256]{2,1,0:T(8,128)(2,1)S(1)}) custom-call(s32[4]{0:T(128)S(1)} %pad_add_fusion.ids_ref, f32[2]{0:T(128)S(1)} %fusion.4.weight_ref, s32[2,1,2048]{2,1,0:T(1,128)S(1)} %collective-permute-done.perm_ref, ...), custom_call_target="tpu_custom_call" | custom-call | flops 4294967296 | bytes 11534336 | tf_op jit(solution)/shard_map/pallas_call | solution.py:114
  123.8 0.0 copy-start.2
  123.8 0.1 collective-permute-start.20
  123.9 0.8 collective-permute-start.21
  124.7 3.9 %collective-permute-start.22 = (s16[2,272,256]{2,1,0:T(8,128)(2,1)S(1)}, s16[2,272,256]{2,1,0:T(8,128)(2,1)S(1)}, u32[]{:S(2)}, u32[]{:S(2)}) collective-permute-start(s16[2,272,256]{2,1,0:T(8,128)(2,1)S(1)} %get-tuple-element.28), channel_id=1, source_target_pairs={{0,3},{1,2},{2,1},{3,0},{4,7},{5,6},{6,5},{7,4},{8,11},{9,10},{10,... | collective-permute-start | bytes 835592 | tf_op jit(solution)/shard_map/ppermute | solution.py:24
  128.6 6.8 %shard_map.60 = (s16[2,272,256]{2,1,0:T(8,128)(2,1)S(1)}, s16[2,272,256]{2,1,0:T(8,128)(2,1)S(1)}, s16[2,272,256]{2,1,0:T(8,128)(2,1)S(1)}, s16[2,272,256]{2,1,0:T(8,128)(2,1)S(1)}) custom-call(s32[4]{0:T(128)S(1)} %pad_add_fusion.ids_ref, f32[2]{0:T(128)S(1)} %fusion.4.weight_ref, s32[2,1,2048]{2,1,0:T(1,128)S(1)} %collective-permute-done.perm_ref, ...), custom_call_target="tpu_custom_call" | custom-call | flops 4294967296 | bytes 11534336 | tf_op jit(solution)/shard_map/pallas_call | solution.py:114
  135.4 0.0 copy-start
  135.5 0.7 copy-done
  136.2 1.4 collective-permute-start.18
  137.6 3.2 %collective-permute-start.19 = (s16[2,272,256]{2,1,0:T(8,128)(2,1)S(1)}, s16[2,272,256]{2,1,0:T(8,128)(2,1)S(1)}, u32[]{:S(2)}, u32[]{:S(2)}) collective-permute-start(s16[2,272,256]{2,1,0:T(8,128)(2,1)S(1)} %get-tuple-element.24), channel_id=1, source_target_pairs={{0,3},{1,2},{2,1},{3,0},{4,7},{5,6},{6,5},{7,4},{8,11},{9,10},{10,... | collective-permute-start | bytes 835592 | tf_op jit(solution)/shard_map/ppermute | solution.py:24
  140.9 1.2 collective-permute-done.22.refs_3_
  142.1 0.7 copy-done.12
  142.8 3.0 %sum.1 = (s16[2,272,256]{2,1,0:T(8,128)(2,1)}, s16[2,272,256]{2,1,0:T(8,128)(2,1)}) custom-call(s16[2,272,256]{2,1,0:T(8,128)(2,1)} %copy-done.2, s16[2,272,256]{2,1,0:T(8,128)(2,1)} %copy-done.10, s16[2,272,256]{2,1,0:T(8,128)(2,1)} %copy-done.11, s16[2,272,256]{2,1,0:T(8,128)(2,1)} %copy-done.12, s16[2,272,256]{2,1,0:T(8,128)(2,1)} %copy-done.1, ...), custom_call_target="tpu_custom_call" | custom-call | tf_op jit(solution)/shard_map/sum/pallas_call | solution.py:142
  145.8 1.0 collective-permute-start.26
  146.8 2.5 %collective-permute-start.27 = (s16[2,272,256]{2,1,0:T(8,128)(2,1)}, s16[2,272,256]{2,1,0:T(8,128)(2,1)S(1)}, u32[]{:S(2)}, u32[]{:S(2)}) collective-permute-start(s16[2,272,256]{2,1,0:T(8,128)(2,1)} %get-tuple-element.34), channel_id=1, source_target_pairs={{0,4},{1,13},{2,22},{3,31},{4,32},{5,41},{6,50},{7,59},{8,12},{9,2... | collective-permute-start | bytes 835592 | tf_op jit(solution)/shard_map/ppermute | solution.py:24
  149.3 1.2 collective-permute-done.18.refs_2_
  150.5 3.1 %collective-permute-done.19.refs_3_ = s16[2,272,256]{2,1,0:T(8,128)(2,1)S(1)} collective-permute-done((s16[2,272,256]{2,1,0:T(8,128)(2,1)S(1)}, s16[2,272,256]{2,1,0:T(8,128)(2,1)S(1)}, u32[]{:S(2)}, u32[]{:S(2)}) %collective-permute-start.19) | collective-permute-done | bytes 278560 | tf_op jit(solution)/shard_map/ppermute | solution.py:24
  153.6 3.5 %collective-permute-done.26.refs_4_ = s16[2,272,256]{2,1,0:T(8,128)(2,1)S(1)} collective-permute-done((s16[2,272,256]{2,1,0:T(8,128)(2,1)}, s16[2,272,256]{2,1,0:T(8,128)(2,1)S(1)}, u32[]{:S(2)}, u32[]{:S(2)}) %collective-permute-start.26) | collective-permute-done | bytes 278560 | tf_op jit(solution)/shard_map/ppermute | solution.py:24
  157.0 10.7 %collective-permute-done.27.refs_5_ = s16[2,272,256]{2,1,0:T(8,128)(2,1)S(1)} collective-permute-done((s16[2,272,256]{2,1,0:T(8,128)(2,1)}, s16[2,272,256]{2,1,0:T(8,128)(2,1)S(1)}, u32[]{:S(2)}, u32[]{:S(2)}) %collective-permute-start.27) | collective-permute-done | bytes 278560 | tf_op jit(solution)/shard_map/ppermute | solution.py:24
  167.8 0.7 copy-done.17
  168.5 3.3 %gram.1 = (f32[2,256,256]{2,1,0:T(8,128)}, f32[256,256]{1,0:T(8,128)}, f32[384,128]{1,0:T(8,128)}) custom-call(s32[4]{0:T(128)} %copy-done.4, s16[2,272,256]{2,1,0:T(8,128)(2,1)} %copy-done, s16[2,272,256]{2,1,0:T(8,128)(2,1)} %copy-done.13, s16[2,272,256]{2,1,0:T(8,128)(2,1)} %copy-done.14, s16[2,272,256]{2,1,0:T(8,128)(2,1)} %copy-done.15, ...), custom_call_target="tpu_custom_call" | custom-call | tf_op jit(solution)/shard_map/gram/pallas_call | solution.py:176
  171.8 0.1 collective-permute-start.29
  171.9 2.5 %collective-permute-start.30 = (f32[384,128]{1,0:T(8,128)}, f32[384,128]{1,0:T(8,128)S(1)}, u32[]{:S(2)}, u32[]{:S(2)}) collective-permute-start(f32[384,128]{1,0:T(8,128)} %get-tuple-element.37.refs_0_), channel_id=1, source_target_pairs={{0,2},{1,3},{2,0},{3,1},{4,6},{5,7},{6,4},{7,5},{8,10},{9,11},{10,... | collective-permute-start | bytes 589832 | tf_op jit(solution)/shard_map/ppermute | solution.py:24
  174.4 2.2 %collective-permute-start.31 = (f32[384,128]{1,0:T(8,128)}, f32[384,128]{1,0:T(8,128)S(1)}, u32[]{:S(2)}, u32[]{:S(2)}) collective-permute-start(f32[384,128]{1,0:T(8,128)} %get-tuple-element.37.refs_0_), channel_id=1, source_target_pairs={{0,3},{1,2},{2,1},{3,0},{4,7},{5,6},{6,5},{7,4},{8,11},{9,10},{10,... | collective-permute-start | bytes 589832 | tf_op jit(solution)/shard_map/ppermute | solution.py:24
  176.6 2.0 collective-permute-done.29.refs_1_
  178.6 4.6 %collective-permute-done.30.refs_2_ = f32[384,128]{1,0:T(8,128)S(1)} collective-permute-done((f32[384,128]{1,0:T(8,128)}, f32[384,128]{1,0:T(8,128)S(1)}, u32[]{:S(2)}, u32[]{:S(2)}) %collective-permute-start.30) | collective-permute-done | bytes 196640 | tf_op jit(solution)/shard_map/ppermute | solution.py:24
  183.2 3.9 %collective-permute-done.31.refs_3_ = f32[384,128]{1,0:T(8,128)S(1)} collective-permute-done((f32[384,128]{1,0:T(8,128)}, f32[384,128]{1,0:T(8,128)S(1)}, u32[]{:S(2)}, u32[]{:S(2)}) %collective-permute-start.31) | collective-permute-done | bytes 196640 | tf_op jit(solution)/shard_map/ppermute | solution.py:24
  187.1 0.7 copy-done.20
  187.8 18.1 %orthogonal.1 = (f32[2,256,256]{2,1,0:T(8,128)}, s16[272,256]{1,0:T(8,128)(2,1)}) custom-call(s32[4]{0:T(128)} %copy-done.4, f32[2,256,256]{2,1,0:T(8,128)} %get-tuple-element.35.samples_ref, f32[256,256]{1,0:T(8,128)} %get-tuple-element.36.other_ref, f32[384,128]{1,0:T(8,128)} %get-tuple-element.37.refs_0_, f32[384,128]{1,0:T(8,128)} %copy-done.18, ...), custom_call_target="tpu_custom_call" | custom-call | tf_op jit(solution)/shard_map/orthogonal/pallas_call | solution.py:288
  205.9 3.1 %collective-permute-start.32 = (s16[272,256]{1,0:T(8,128)(2,1)}, s16[272,256]{1,0:T(8,128)(2,1)S(1)}, u32[]{:S(2)}, u32[]{:S(2)}) collective-permute-start(s16[272,256]{1,0:T(8,128)(2,1)} %get-tuple-element.39), channel_id=1, source_target_pairs={{0,4},{1,5},{2,6},{3,7},{4,0},{5,1},{6,2},{7,3},{8,12},{9,13},{10,... | collective-permute-start | bytes 417800 | tf_op jit(solution)/shard_map/ppermute | solution.py:24
  209.0 0.0 copy-start.6
  209.0 4.4 %collective-permute-done.32 = s16[272,256]{1,0:T(8,128)(2,1)S(1)} collective-permute-done((s16[272,256]{1,0:T(8,128)(2,1)}, s16[272,256]{1,0:T(8,128)(2,1)S(1)}, u32[]{:S(2)}, u32[]{:S(2)}) %collective-permute-start.32) | collective-permute-done | bytes 139296 | tf_op jit(solution)/shard_map/ppermute | solution.py:24
  213.5 0.7 fusion.1
  (63 shorter events, 0.2 us)
Async XLA Ops:
  0.6 24.2 %copy-start.21 = (s32[2,1,1]{0,2,1:T(1,128)S(1)}, s32[2,1,1]{0,2,1:T(1,128)}, u32[]{:S(2)}) copy-start(s32[2,1,1]{0,2,1:T(1,128)} %param.7) | copy-start | bytes 28
  0.6 38.0 %copy-start.3 = (s32[2,1,2048]{2,1,0:T(1,128)S(1)}, s32[2,1,2048]{2,1,0:T(1,128)}, u32[]{:S(2)}) copy-start(s32[2,1,2048]{2,1,0:T(1,128)} %perm_ref.3) | copy-start | bytes 49156
  1.7 9.8 %collective-permute-start.8 = (bf16[256,256]{1,0:T(8,128)(2,1)S(1)}, bf16[256,256]{1,0:T(8,128)(2,1)S(1)}, u32[]{:S(2)}, u32[]{:S(2)}) collective-permute-start(bf16[256,256]{1,0:T(8,128)(2,1)S(1)} %get-tuple-element.42), channel_id=1, source_target_pairs={{0,3},{1,2},{2,1},{3,0},{4,7},{5,6},{6,5},{7,4},{8,11},{9,10},{10,... | collective-permute-start | bytes 393224 | tf_op jit(solution)/shard_map/ppermute | solution.py:24
  5.9 7.9 %collective-permute-start.7 = (bf16[256,256]{1,0:T(8,128)(2,1)S(1)}, bf16[256,256]{1,0:T(8,128)(2,1)S(1)}, u32[]{:S(2)}, u32[]{:S(2)}) collective-permute-start(bf16[256,256]{1,0:T(8,128)(2,1)S(1)} %get-tuple-element.42), channel_id=1, source_target_pairs={{0,2},{1,3},{2,0},{3,1},{4,6},{5,7},{6,4},{7,5},{8,10},{9,11},{10,... | collective-permute-start | bytes 393224 | tf_op jit(solution)/shard_map/ppermute | solution.py:24
  5.9 7.9 %collective-permute-start.6 = (bf16[256,256]{1,0:T(8,128)(2,1)S(1)}, bf16[256,256]{1,0:T(8,128)(2,1)S(1)}, u32[]{:S(2)}, u32[]{:S(2)}) collective-permute-start(bf16[256,256]{1,0:T(8,128)(2,1)S(1)} %get-tuple-element.42), channel_id=1, source_target_pairs={{0,1},{1,0},{2,3},{3,2},{4,5},{5,4},{6,7},{7,6},{8,9},{9,8},{10,11... | collective-permute-start | bytes 393224 | tf_op jit(solution)/shard_map/ppermute | solution.py:24
  6.8 13.1 %collective-permute-start.12 = (bf16[256,256]{1,0:T(8,128)(2,1)S(1)}, bf16[256,256]{1,0:T(8,128)(2,1)S(1)}, u32[]{:S(2)}, u32[]{:S(2)}) collective-permute-start(bf16[256,256]{1,0:T(8,128)(2,1)S(1)} %get-tuple-element.41), channel_id=1, source_target_pairs={{0,4},{1,5},{2,6},{3,7},{4,0},{5,1},{6,2},{7,3},{8,12},{9,13},{10,... | collective-permute-start | bytes 393224 | tf_op jit(solution)/shard_map/ppermute | solution.py:24
  13.8 24.8 %collective-permute-start.10 = (bf16[4,256,256]{2,1,0:T(8,128)(2,1)S(1)}, bf16[4,256,256]{2,1,0:T(8,128)(2,1)S(1)}, u32[]{:S(2)}, u32[]{:S(2)}) collective-permute-start(bf16[4,256,256]{2,1,0:T(8,128)(2,1)S(1)} %pad_maximum_fusion.refs_4_), channel_id=1, source_target_pairs={{0,4},{1,5},{2,6},{3,7},{4,0},{5,1},{6,2},{7,3},{8,12},{9,13},{10,... | collective-permute-start | bytes 1572872 | tf_op jit(solution)/shard_map/ppermute | solution.py:24
  16.9 29.2 %collective-permute-start.2 = (bf16[256,256]{1,0:T(8,128)(2,1)S(1)}, bf16[256,256]{1,0:T(8,128)(2,1)S(1)}, u32[]{:S(2)}, u32[]{:S(2)}) collective-permute-start(bf16[256,256]{1,0:T(8,128)(2,1)S(1)} %get-tuple-element.41), channel_id=1, source_target_pairs={{0,100},{1,93},{2,86},{3,79},{4,0},{5,121},{6,114},{7,107},{8,108}... | collective-permute-start | bytes 393224 | tf_op jit(solution)/shard_map/ppermute | solution.py:24
  19.9 9.3 %collective-permute-start.13 = (bf16[2,256,256]{2,1,0:T(8,128)(2,1)S(1)}, bf16[2,256,256]{2,1,0:T(8,128)(2,1)S(1)}, u32[]{:S(2)}, u32[]{:S(2)}) collective-permute-start(bf16[2,256,256]{2,1,0:T(8,128)(2,1)S(1)} %pad_maximum_fusion.2.refs_0_), channel_id=1, source_target_pairs={{0,1},{1,0},{2,3},{3,2},{4,5},{5,4},{6,7},{7,6},{8,9},{9,8},{10,11... | collective-permute-start | bytes 786440 | tf_op jit(solution)/shard_map/ppermute | solution.py:24
  20.0 14.7 %collective-permute-start.14 = (bf16[2,256,256]{2,1,0:T(8,128)(2,1)S(1)}, bf16[2,256,256]{2,1,0:T(8,128)(2,1)S(1)}, u32[]{:S(2)}, u32[]{:S(2)}) collective-permute-start(bf16[2,256,256]{2,1,0:T(8,128)(2,1)S(1)} %pad_maximum_fusion.2.refs_0_), channel_id=1, source_target_pairs={{0,2},{1,3},{2,0},{3,1},{4,6},{5,7},{6,4},{7,5},{8,10},{9,11},{10,... | collective-permute-start | bytes 786440 | tf_op jit(solution)/shard_map/ppermute | solution.py:24
  22.7 15.9 %collective-permute-start.15 = (bf16[2,256,256]{2,1,0:T(8,128)(2,1)S(1)}, bf16[2,256,256]{2,1,0:T(8,128)(2,1)S(1)}, u32[]{:S(2)}, u32[]{:S(2)}) collective-permute-start(bf16[2,256,256]{2,1,0:T(8,128)(2,1)S(1)} %pad_maximum_fusion.2.refs_0_), channel_id=1, source_target_pairs={{0,3},{1,2},{2,1},{3,0},{4,7},{5,6},{6,5},{7,4},{8,11},{9,10},{10,... | collective-permute-start | bytes 786440 | tf_op jit(solution)/shard_map/ppermute | solution.py:24
  24.8 103.8 %copy-start.4 = (s32[4]{0:T(128)}, s32[4]{0:T(128)S(1)}, u32[]{:S(2)}) copy-start(s32[4]{0:T(128)S(1)} %pad_add_fusion.ids_ref) | copy-start | bytes 52
  29.2 17.0 %collective-permute-start.1 = (bf16[256,256]{1,0:T(8,128)(2,1)S(1)}, bf16[256,256]{1,0:T(8,128)(2,1)S(1)}, u32[]{:S(2)}, u32[]{:S(2)}) collective-permute-start(bf16[256,256]{1,0:T(8,128)(2,1)S(1)} %get-tuple-element.41), channel_id=1, source_target_pairs={{0,0},{1,121},{2,114},{3,107},{4,100},{5,93},{6,86},{7,79},{8,8},{... | collective-permute-start | bytes 393224 | tf_op jit(solution)/shard_map/ppermute | solution.py:24
  45.4 79.2 %collective-permute-start.16 = (s16[4,2,272,256]{3,2,1,0:T(8,128)(2,1)S(1)}, s16[4,2,272,256]{3,2,1,0:T(8,128)(2,1)S(1)}, u32[]{:S(2)}, u32[]{:S(2)}) collective-permute-start(s16[4,2,272,256]{3,2,1,0:T(8,128)(2,1)S(1)} %shard_map.59), channel_id=1, source_target_pairs={{0,0},{1,9},{2,18},{3,27},{4,36},{5,45},{6,54},{7,63},{8,8},{9,17}... | collective-permute-start | bytes 3342344 | tf_op jit(solution)/shard_map/ppermute | solution.py:24
  46.2 56.3 %collective-permute-start.3 = (bf16[2,256,256]{2,1,0:T(8,128)(2,1)S(1)}, bf16[2,256,256]{2,1,0:T(8,128)(2,1)S(1)}, u32[]{:S(2)}, u32[]{:S(2)}) collective-permute-start(bf16[2,256,256]{2,1,0:T(8,128)(2,1)S(1)} %pad_maximum_fusion.1.refs_0_), channel_id=1, source_target_pairs={{0,121},{1,8},{2,123},{3,10},{4,125},{5,12},{6,127},{7,14},{8,1},{... | collective-permute-start | bytes 786440 | tf_op jit(solution)/shard_map/ppermute | solution.py:24
  49.6 67.2 %collective-permute-start.9 = (bf16[4,256,256]{2,1,0:T(8,128)(2,1)S(1)}, bf16[4,256,256]{2,1,0:T(8,128)(2,1)S(1)}, u32[]{:S(2)}, u32[]{:S(2)}) collective-permute-start(bf16[4,256,256]{2,1,0:T(8,128)(2,1)S(1)} %pad_maximum_fusion.refs_4_), channel_id=1, source_target_pairs={{0,0},{1,121},{2,114},{3,107},{4,100},{5,93},{6,86},{7,79},{8,8},{... | collective-permute-start | bytes 1572872 | tf_op jit(solution)/shard_map/ppermute | solution.py:24
  50.2 66.5 %collective-permute-start.11 = (bf16[4,256,256]{2,1,0:T(8,128)(2,1)S(1)}, bf16[4,256,256]{2,1,0:T(8,128)(2,1)S(1)}, u32[]{:S(2)}, u32[]{:S(2)}) collective-permute-start(bf16[4,256,256]{2,1,0:T(8,128)(2,1)S(1)} %collective-permute-done.10.refs_5_), channel_id=1, source_target_pairs={{0,0},{1,121},{2,114},{3,107},{4,100},{5,93},{6,86},{7,79},{8,8},{... | collective-permute-start | bytes 1572872 | tf_op jit(solution)/shard_map/ppermute | solution.py:24
  50.9 0.7 collective-permute-start
  51.6 57.7 %collective-permute-start.4 = (bf16[2,256,256]{2,1,0:T(8,128)(2,1)S(1)}, bf16[2,256,256]{2,1,0:T(8,128)(2,1)S(1)}, u32[]{:S(2)}, u32[]{:S(2)}) collective-permute-start(bf16[2,256,256]{2,1,0:T(8,128)(2,1)S(1)} %pad_maximum_fusion.1.refs_0_), channel_id=1, source_target_pairs={{0,114},{1,115},{2,16},{3,17},{4,118},{5,119},{6,20},{7,21},{8,122... | collective-permute-start | bytes 786440 | tf_op jit(solution)/shard_map/ppermute | solution.py:24
  102.5 9.1 %collective-permute-start.5 = (bf16[2,256,256]{2,1,0:T(8,128)(2,1)S(1)}, bf16[2,256,256]{2,1,0:T(8,128)(2,1)S(1)}, u32[]{:S(2)}, u32[]{:S(2)}) collective-permute-start(bf16[2,256,256]{2,1,0:T(8,128)(2,1)S(1)} %pad_maximum_fusion.1.refs_0_), channel_id=1, source_target_pairs={{0,107},{1,122},{2,9},{3,24},{4,111},{5,126},{6,13},{7,28},{8,115}... | collective-permute-start | bytes 786440 | tf_op jit(solution)/shard_map/ppermute | solution.py:24
  109.3 14.4 %copy-start.1 = (s16[2,272,256]{2,1,0:T(8,128)(2,1)}, s16[2,272,256]{2,1,0:T(8,128)(2,1)S(1)}, u32[]{:S(2)}) copy-start(s16[2,272,256]{2,1,0:T(8,128)(2,1)S(1)} %get-tuple-element.29.refs_4_) | copy-start | bytes 835588
  109.3 14.5 %collective-permute-start.23 = (s16[2,272,256]{2,1,0:T(8,128)(2,1)S(1)}, s16[2,272,256]{2,1,0:T(8,128)(2,1)S(1)}, u32[]{:S(2)}, u32[]{:S(2)}) collective-permute-start(s16[2,272,256]{2,1,0:T(8,128)(2,1)S(1)} %get-tuple-element.30), channel_id=1, source_target_pairs={{0,121},{1,8},{2,123},{3,10},{4,125},{5,12},{6,127},{7,14},{8,1},{... | collective-permute-start | bytes 835592 | tf_op jit(solution)/shard_map/ppermute | solution.py:24
  111.6 24.5 %collective-permute-start.24 = (s16[2,272,256]{2,1,0:T(8,128)(2,1)S(1)}, s16[2,272,256]{2,1,0:T(8,128)(2,1)S(1)}, u32[]{:S(2)}, u32[]{:S(2)}) collective-permute-start(s16[2,272,256]{2,1,0:T(8,128)(2,1)S(1)} %get-tuple-element.31), channel_id=1, source_target_pairs={{0,114},{1,115},{2,16},{3,17},{4,118},{5,119},{6,20},{7,21},{8,122... | collective-permute-start | bytes 835592 | tf_op jit(solution)/shard_map/ppermute | solution.py:24
  116.8 19.4 %collective-permute-start.25 = (s16[2,272,256]{2,1,0:T(8,128)(2,1)S(1)}, s16[2,272,256]{2,1,0:T(8,128)(2,1)S(1)}, u32[]{:S(2)}, u32[]{:S(2)}) collective-permute-start(s16[2,272,256]{2,1,0:T(8,128)(2,1)S(1)} %get-tuple-element.32), channel_id=1, source_target_pairs={{0,107},{1,122},{2,9},{3,24},{4,111},{5,126},{6,13},{7,28},{8,115}... | collective-permute-start | bytes 835592 | tf_op jit(solution)/shard_map/ppermute | solution.py:24
  123.8 11.7 %copy-start.2 = (s16[2,272,256]{2,1,0:T(8,128)(2,1)}, s16[2,272,256]{2,1,0:T(8,128)(2,1)S(1)}, u32[]{:S(2)}) copy-start(s16[2,272,256]{2,1,0:T(8,128)(2,1)S(1)} %get-tuple-element.25.refs_0_) | copy-start | bytes 835588
  123.8 13.9 %collective-permute-start.20 = (s16[2,272,256]{2,1,0:T(8,128)(2,1)S(1)}, s16[2,272,256]{2,1,0:T(8,128)(2,1)S(1)}, u32[]{:S(2)}, u32[]{:S(2)}) collective-permute-start(s16[2,272,256]{2,1,0:T(8,128)(2,1)S(1)} %get-tuple-element.26), channel_id=1, source_target_pairs={{0,1},{1,0},{2,3},{3,2},{4,5},{5,4},{6,7},{7,6},{8,9},{9,8},{10,11... | collective-permute-start | bytes 835592 | tf_op jit(solution)/shard_map/ppermute | solution.py:24
  123.9 11.6 %copy-start.7 = (s16[2,272,256]{2,1,0:T(8,128)(2,1)}, s16[2,272,256]{2,1,0:T(8,128)(2,1)S(1)}, u32[]{:S(2)}) copy-start(s16[2,272,256]{2,1,0:T(8,128)(2,1)S(1)} %collective-permute-done.23.refs_5_) | copy-start | bytes 835588
  123.9 17.0 %collective-permute-start.21 = (s16[2,272,256]{2,1,0:T(8,128)(2,1)S(1)}, s16[2,272,256]{2,1,0:T(8,128)(2,1)S(1)}, u32[]{:S(2)}, u32[]{:S(2)}) collective-permute-start(s16[2,272,256]{2,1,0:T(8,128)(2,1)S(1)} %get-tuple-element.27), channel_id=1, source_target_pairs={{0,2},{1,3},{2,0},{3,1},{4,6},{5,7},{6,4},{7,5},{8,10},{9,11},{10,... | collective-permute-start | bytes 835592 | tf_op jit(solution)/shard_map/ppermute | solution.py:24
  124.7 17.4 %collective-permute-start.22 = (s16[2,272,256]{2,1,0:T(8,128)(2,1)S(1)}, s16[2,272,256]{2,1,0:T(8,128)(2,1)S(1)}, u32[]{:S(2)}, u32[]{:S(2)}) collective-permute-start(s16[2,272,256]{2,1,0:T(8,128)(2,1)S(1)} %get-tuple-element.28), channel_id=1, source_target_pairs={{0,3},{1,2},{2,1},{3,0},{4,7},{5,6},{6,5},{7,4},{8,11},{9,10},{10,... | collective-permute-start | bytes 835592 | tf_op jit(solution)/shard_map/ppermute | solution.py:24
  135.4 0.7 copy-start
  136.2 5.9 %copy-start.8 = (s16[2,272,256]{2,1,0:T(8,128)(2,1)}, s16[2,272,256]{2,1,0:T(8,128)(2,1)S(1)}, u32[]{:S(2)}) copy-start(s16[2,272,256]{2,1,0:T(8,128)(2,1)S(1)} %collective-permute-done.24.refs_6_) | copy-start | bytes 835588
  136.2 13.2 %collective-permute-start.17 = (s16[2,272,256]{2,1,0:T(8,128)(2,1)S(1)}, s16[2,272,256]{2,1,0:T(8,128)(2,1)S(1)}, u32[]{:S(2)}, u32[]{:S(2)}) collective-permute-start(s16[2,272,256]{2,1,0:T(8,128)(2,1)S(1)} %get-tuple-element.22), channel_id=1, source_target_pairs={{0,1},{1,0},{2,3},{3,2},{4,5},{5,4},{6,7},{7,6},{8,9},{9,8},{10,11... | collective-permute-start | bytes 835592 | tf_op jit(solution)/shard_map/ppermute | solution.py:24
  136.2 5.9 %copy-start.9 = (s16[2,272,256]{2,1,0:T(8,128)(2,1)}, s16[2,272,256]{2,1,0:T(8,128)(2,1)S(1)}, u32[]{:S(2)}) copy-start(s16[2,272,256]{2,1,0:T(8,128)(2,1)S(1)} %collective-permute-done.25.refs_7_) | copy-start | bytes 835588
  136.2 14.3 %collective-permute-start.18 = (s16[2,272,256]{2,1,0:T(8,128)(2,1)S(1)}, s16[2,272,256]{2,1,0:T(8,128)(2,1)S(1)}, u32[]{:S(2)}, u32[]{:S(2)}) collective-permute-start(s16[2,272,256]{2,1,0:T(8,128)(2,1)S(1)} %get-tuple-element.23), channel_id=1, source_target_pairs={{0,2},{1,3},{2,0},{3,1},{4,6},{5,7},{6,4},{7,5},{8,10},{9,11},{10,... | collective-permute-start | bytes 835592 | tf_op jit(solution)/shard_map/ppermute | solution.py:24
  137.6 4.4 %copy-start.10 = (s16[2,272,256]{2,1,0:T(8,128)(2,1)}, s16[2,272,256]{2,1,0:T(8,128)(2,1)S(1)}, u32[]{:S(2)}) copy-start(s16[2,272,256]{2,1,0:T(8,128)(2,1)S(1)} %collective-permute-done.20.refs_1_) | copy-start | bytes 835588
  137.6 15.9 %collective-permute-start.19 = (s16[2,272,256]{2,1,0:T(8,128)(2,1)S(1)}, s16[2,272,256]{2,1,0:T(8,128)(2,1)S(1)}, u32[]{:S(2)}, u32[]{:S(2)}) collective-permute-start(s16[2,272,256]{2,1,0:T(8,128)(2,1)S(1)} %get-tuple-element.24), channel_id=1, source_target_pairs={{0,3},{1,2},{2,1},{3,0},{4,7},{5,6},{6,5},{7,4},{8,11},{9,10},{10,... | collective-permute-start | bytes 835592 | tf_op jit(solution)/shard_map/ppermute | solution.py:24
  140.9 1.2 copy-start.11
  142.0 0.7 copy-start.12
  145.8 11.2 %collective-permute-start.26 = (s16[2,272,256]{2,1,0:T(8,128)(2,1)}, s16[2,272,256]{2,1,0:T(8,128)(2,1)S(1)}, u32[]{:S(2)}, u32[]{:S(2)}) collective-permute-start(s16[2,272,256]{2,1,0:T(8,128)(2,1)} %get-tuple-element.33), channel_id=1, source_target_pairs={{0,4},{1,5},{2,6},{3,7},{4,0},{5,1},{6,2},{7,3},{8,12},{9,13},{10,... | collective-permute-start | bytes 835592 | tf_op jit(solution)/shard_map/ppermute | solution.py:24
  146.8 20.9 %collective-permute-start.27 = (s16[2,272,256]{2,1,0:T(8,128)(2,1)}, s16[2,272,256]{2,1,0:T(8,128)(2,1)S(1)}, u32[]{:S(2)}, u32[]{:S(2)}) collective-permute-start(s16[2,272,256]{2,1,0:T(8,128)(2,1)} %get-tuple-element.34), channel_id=1, source_target_pairs={{0,4},{1,13},{2,22},{3,31},{4,32},{5,41},{6,50},{7,59},{8,12},{9,2... | collective-permute-start | bytes 835592 | tf_op jit(solution)/shard_map/ppermute | solution.py:24
  149.3 18.4 %copy-start.13 = (s16[2,272,256]{2,1,0:T(8,128)(2,1)}, s16[2,272,256]{2,1,0:T(8,128)(2,1)S(1)}, u32[]{:S(2)}) copy-start(s16[2,272,256]{2,1,0:T(8,128)(2,1)S(1)} %collective-permute-done.17.refs_1_) | copy-start | bytes 835588
  150.5 17.2 %copy-start.14 = (s16[2,272,256]{2,1,0:T(8,128)(2,1)}, s16[2,272,256]{2,1,0:T(8,128)(2,1)S(1)}, u32[]{:S(2)}) copy-start(s16[2,272,256]{2,1,0:T(8,128)(2,1)S(1)} %collective-permute-done.18.refs_2_) | copy-start | bytes 835588
  153.6 14.2 %copy-start.15 = (s16[2,272,256]{2,1,0:T(8,128)(2,1)}, s16[2,272,256]{2,1,0:T(8,128)(2,1)S(1)}, u32[]{:S(2)}) copy-start(s16[2,272,256]{2,1,0:T(8,128)(2,1)S(1)} %collective-permute-done.19.refs_3_) | copy-start | bytes 835588
  157.0 10.7 %copy-start.16 = (s16[2,272,256]{2,1,0:T(8,128)(2,1)}, s16[2,272,256]{2,1,0:T(8,128)(2,1)S(1)}, u32[]{:S(2)}) copy-start(s16[2,272,256]{2,1,0:T(8,128)(2,1)S(1)} %collective-permute-done.26.refs_4_) | copy-start | bytes 835588
  167.8 0.7 copy-start.17
  171.8 37.2 %copy-start.5 = (f32[2,256,256]{2,1,0:T(8,128)S(1)}, f32[2,256,256]{2,1,0:T(8,128)}, u32[]{:S(2)}) copy-start(f32[2,256,256]{2,1,0:T(8,128)} %get-tuple-element.35.samples_ref) | copy-start | bytes 1572868
  171.8 37.2 %collective-permute-start.28 = (f32[256,256]{1,0:T(8,128)}, f32[256,256]{1,0:T(8,128)S(1)}, u32[]{:S(2)}, u32[]{:S(2)}) collective-permute-start(f32[256,256]{1,0:T(8,128)} %get-tuple-element.36.other_ref), channel_id=1, source_target_pairs={{0,4},{1,5},{2,6},{3,7},{4,0},{5,1},{6,2},{7,3},{8,12},{9,13},{10,... | collective-permute-start | bytes 786440 | tf_op jit(solution)/shard_map/ppermute | solution.py:24
  171.8 6.8 %collective-permute-start.29 = (f32[384,128]{1,0:T(8,128)}, f32[384,128]{1,0:T(8,128)S(1)}, u32[]{:S(2)}, u32[]{:S(2)}) collective-permute-start(f32[384,128]{1,0:T(8,128)} %get-tuple-element.37.refs_0_), channel_id=1, source_target_pairs={{0,1},{1,0},{2,3},{3,2},{4,5},{5,4},{6,7},{7,6},{8,9},{9,8},{10,11... | collective-permute-start | bytes 589832 | tf_op jit(solution)/shard_map/ppermute | solution.py:24
  171.9 11.3 %collective-permute-start.30 = (f32[384,128]{1,0:T(8,128)}, f32[384,128]{1,0:T(8,128)S(1)}, u32[]{:S(2)}, u32[]{:S(2)}) collective-permute-start(f32[384,128]{1,0:T(8,128)} %get-tuple-element.37.refs_0_), channel_id=1, source_target_pairs={{0,2},{1,3},{2,0},{3,1},{4,6},{5,7},{6,4},{7,5},{8,10},{9,11},{10,... | collective-permute-start | bytes 589832 | tf_op jit(solution)/shard_map/ppermute | solution.py:24
  174.4 12.7 %collective-permute-start.31 = (f32[384,128]{1,0:T(8,128)}, f32[384,128]{1,0:T(8,128)S(1)}, u32[]{:S(2)}, u32[]{:S(2)}) collective-permute-start(f32[384,128]{1,0:T(8,128)} %get-tuple-element.37.refs_0_), channel_id=1, source_target_pairs={{0,3},{1,2},{2,1},{3,0},{4,7},{5,6},{6,5},{7,4},{8,11},{9,10},{10,... | collective-permute-start | bytes 589832 | tf_op jit(solution)/shard_map/ppermute | solution.py:24
  178.6 8.5 %copy-start.18 = (f32[384,128]{1,0:T(8,128)}, f32[384,128]{1,0:T(8,128)S(1)}, u32[]{:S(2)}) copy-start(f32[384,128]{1,0:T(8,128)S(1)} %collective-permute-done.29.refs_1_) | copy-start | bytes 589828
  183.2 3.9 %copy-start.19 = (f32[384,128]{1,0:T(8,128)}, f32[384,128]{1,0:T(8,128)S(1)}, u32[]{:S(2)}) copy-start(f32[384,128]{1,0:T(8,128)S(1)} %collective-permute-done.30.refs_2_) | copy-start | bytes 589828
  187.1 0.7 copy-start.20
  205.9 7.6 %collective-permute-start.32 = (s16[272,256]{1,0:T(8,128)(2,1)}, s16[272,256]{1,0:T(8,128)(2,1)S(1)}, u32[]{:S(2)}, u32[]{:S(2)}) collective-permute-start(s16[272,256]{1,0:T(8,128)(2,1)} %get-tuple-element.39), channel_id=1, source_target_pairs={{0,4},{1,5},{2,6},{3,7},{4,0},{5,1},{6,2},{7,3},{8,12},{9,13},{10,... | collective-permute-start | bytes 417800 | tf_op jit(solution)/shard_map/ppermute | solution.py:24
  209.0 5.2 %copy-start.6 = (f32[2,256,256]{2,1,0:T(8,128)}, f32[2,256,256]{2,1,0:T(8,128)S(1)}, u32[]{:S(2)}) copy-start(f32[2,256,256]{2,1,0:T(8,128)S(1)} %bitcast_dynamic-update-slice_fusion) | copy-start | bytes 1572868

commit v7 on v5

--- a/solution.py
+++ b/solution.py
@@ -47,9 +47,7 @@
 
 def product_kernel(back, part, ids_ref, weight_ref, perm_ref, *refs):
     *pair_refs, plane_ref, cross_ref, tiles_ref = refs[:7]
-    joins = not back and part == 0
-    more_ref = refs[7] if joins else None
-    *out_refs, tile_ref, raw_ref, omega_ref, sems = refs[8 if joins else 7 :]
+    *out_refs, tile_ref, raw_ref, omega_ref, sems = refs[7:]
     nz, points, _ = plane_ref.shape
     length = raw_ref.shape[1]
     step = 512
@@ -95,17 +93,14 @@
                 value = jnp.dot(omega_ref[...], tile_ref[:, pl.ds(at, points)], preferred_element_type=jnp.float32).T
             else:
                 value = jnp.dot(tile_ref[pl.ds(at, points), :], omega_ref[...], preferred_element_type=jnp.float32)
-            value = value * weight
-            if joins:
-                value = value + decoded(more_ref[d, a])
-            code = coded(value)
+            code = coded(value * weight)
             if len(out_refs) == 1:
                 out_refs[0][d, a] = code
             else:
                 out_refs[d][a] = code
 
 
-def products(ids, weight, perm, pairs, plane, cross, tiles, back, part, more=()):
+def products(ids, weight, perm, pairs, plane, cross, tiles, back, part):
     nz, points, probes = plane.shape
     length = tiles.shape[1]
     block = (2, points + EXTRA, probes)
@@ -114,7 +109,7 @@
     return pl.pallas_call(
         functools.partial(product_kernel, back, part),
         out_shape=[jax.ShapeDtypeStruct(shape, jnp.int16) for shape in shapes],
-        in_specs=[smem, smem] + [vmem] * (3 + nz) + [pl.BlockSpec(memory_space=pl.ANY)] + [vmem] * len(more),
+        in_specs=[smem, smem] + [vmem] * (3 + nz) + [pl.BlockSpec(memory_space=pl.ANY)],
         out_specs=[vmem] * len(shapes),
         scratch_shapes=[
             pltpu.VMEM(tiles.shape[1:], jnp.bfloat16),
@@ -124,7 +119,22 @@
         ],
         compiler_params=pltpu.CompilerParams(vmem_limit_bytes=40 << 20),
         cost_estimate=pl.CostEstimate(flops=4 * length * length * probes, bytes_accessed=11 << 20, transcendentals=0),
-    )(ids, weight, perm, *pairs, plane, cross, tiles, *more)
+    )(ids, weight, perm, *pairs, plane, cross, tiles)
+
+
+def join_kernel(nz, *refs):
+    more_ref = refs[nz]
+    for d in range(nz):
+        for a in range(2):
+            refs[nz + 1 + d][a] = coded(decoded(refs[d][a]) + decoded(more_ref[d, a]))
+
+
+def joined(codes, more):
+    return pl.pallas_call(
+        functools.partial(join_kernel, len(codes)),
+        out_shape=[jax.ShapeDtypeStruct(x.shape, jnp.int16) for x in codes],
+        name="join",
+    )(*codes, more)
 
 
 def sum_kernel(count, *refs):
@@ -346,7 +356,7 @@
     back = [back[0]] + [sent(back[d], slanted(d)) for d in depths]
     given = products(ids, weight, far_perm, *far_blocks, tiles, False, 1)
     given = [given[0]] + [sent(given[d], same(d)) for d in depths]
-    kept = products(ids, weight, far_perm, *far_blocks, tiles, False, 0, (more,))
+    kept = joined(products(ids, weight, far_perm, *far_blocks, tiles, False, 0), more)
     after = kept[:1]
     kept = [kept[0]] + [sent(kept[d], same(d)) for d in depths]
     crossed = summed(given, after)

time: 206 us -> 211 us (1.024)
  Pallas kernels: 53.4 us -> 56.5 us
  local copies, waits for them, and re-layouts: 5.46 us -> 8.3 us
    pallas_call x0 -> x1, Pallas kernels: none -> 3.19 us  [joined(): pl.pallas_call(functools.partial(join_kernel, len(codes)), out_shape=[jax...]
    unnamed x44 -> x58, local copies, waits for them, and re-layouts: 4.43 us -> 7.27 us
  transfers between devices with their start and end apart: 33 -> 33, of which waited for: 18 -> 16; matrix products, arithmetic and copies ran while one was open for 0% -> 0% of each run, Pallas kernels for 24% -> 25%
where the time goes in v7:
time: 211 us; the launch traced here: 210 us
  waiting for transfers between devices  76.3 us (36%)
  starting transfers between devices  67.4 us (32%)
  Pallas kernels  56.5 us (27%)
  local copies, waits for them, and re-layouts  8.3 us (4%)
    ppermute x33, waiting for transfers between devices, sent(): return lax.ppermute(value, AXES, pairs)  76.3 us
    ppermute x33, starting transfers between devices, sent(): return lax.ppermute(value, AXES, pairs)  67.4 us
    pallas_call x4, Pallas kernels, products(): pl.pallas_call(functools.partial(product_kernel, back, part), out_shape=[...  27.3 us
    pallas_call x1, Pallas kernels, orthogonal(): pl.pallas_call(functools.partial(factor_kernel, scale), in_specs=[pl.Bloc...  18.1 us
    unnamed x58, local copies, waits for them, and re-layouts  7.27 us
    pallas_call x2, Pallas kernels, summed(): pl.pallas_call(functools.partial(sum_kernel, len(codes)), in_specs=[vmem]...  4.57 us
  transfers between devices with their start and end apart: 33, of which 16 were waited for; matrix products, arithmetic and copies ran while one was open for 0% of the time, Pallas kernels for 25%

profile of v7, /device:TPU:0, one launch (start us, length us, event | category | flops | bytes accessed | tf_op | source)
XLA Modules:
  0.0 210.4 jit_solution(7880155430477152757)
XLA Ops:
  0.7 1.0 fusion.5
  1.7 4.1 %collective-permute-start.7 = (bf16[256,256]{1,0:T(8,128)(2,1)S(1)}, bf16[256,256]{1,0:T(8,128)(2,1)S(1)}, u32[]{:S(2)}, u32[]{:S(2)}) collective-permute-start(bf16[256,256]{1,0:T(8,128)(2,1)S(1)} %get-tuple-element.54), channel_id=1, source_target_pairs={{0,2},{1,3},{2,0},{3,1},{4,6},{5,7},{6,4},{7,5},{8,10},{9,11},{10,... | collective-permute-start | bytes 393224 | tf_op jit(solution)/shard_map/ppermute | solution.py:24
  5.7 0.7 collective-permute-start.8
  6.4 0.3 collective-permute-start.6
  6.8 3.0 %collective-permute-start.12 = (bf16[256,256]{1,0:T(8,128)(2,1)S(1)}, bf16[256,256]{1,0:T(8,128)(2,1)S(1)}, u32[]{:S(2)}, u32[]{:S(2)}) collective-permute-start(bf16[256,256]{1,0:T(8,128)(2,1)S(1)} %get-tuple-element.53), channel_id=1, source_target_pairs={{0,4},{1,5},{2,6},{3,7},{4,0},{5,1},{6,2},{7,3},{8,12},{9,13},{10,... | collective-permute-start | bytes 393224 | tf_op jit(solution)/shard_map/ppermute | solution.py:24
  9.8 2.3 %collective-permute-done.8 = bf16[256,256]{1,0:T(8,128)(2,1)S(1)} collective-permute-done((bf16[256,256]{1,0:T(8,128)(2,1)S(1)}, bf16[256,256]{1,0:T(8,128)(2,1)S(1)}, u32[]{:S(2)}, u32[]{:S(2)}) %collective-permute-start.8) | collective-permute-done | bytes 131104 | tf_op jit(solution)/shard_map/ppermute | solution.py:24
  12.0 0.8 collective-permute-done.6
  12.9 3.1 %collective-permute-start.10 = (bf16[4,256,256]{2,1,0:T(8,128)(2,1)S(1)}, bf16[4,256,256]{2,1,0:T(8,128)(2,1)S(1)}, u32[]{:S(2)}, u32[]{:S(2)}) collective-permute-start(bf16[4,256,256]{2,1,0:T(8,128)(2,1)S(1)} %pad_maximum_fusion.refs_4_), channel_id=1, source_target_pairs={{0,4},{1,5},{2,6},{3,7},{4,0},{5,1},{6,2},{7,3},{8,12},{9,13},{10,... | collective-permute-start | bytes 1572872 | tf_op jit(solution)/shard_map/ppermute | solution.py:24
  16.0 0.7 collective-permute-start.1
  16.7 4.2 %collective-permute-start.13 = (bf16[2,256,256]{2,1,0:T(8,128)(2,1)S(1)}, bf16[2,256,256]{2,1,0:T(8,128)(2,1)S(1)}, u32[]{:S(2)}, u32[]{:S(2)}) collective-permute-start(bf16[2,256,256]{2,1,0:T(8,128)(2,1)S(1)} %pad_maximum_fusion.2.refs_0_), channel_id=1, source_target_pairs={{0,1},{1,0},{2,3},{3,2},{4,5},{5,4},{6,7},{7,6},{8,9},{9,8},{10,11... | collective-permute-start | bytes 786440 | tf_op jit(solution)/shard_map/ppermute | solution.py:24
  20.9 3.5 %collective-permute-start.14 = (bf16[2,256,256]{2,1,0:T(8,128)(2,1)S(1)}, bf16[2,256,256]{2,1,0:T(8,128)(2,1)S(1)}, u32[]{:S(2)}, u32[]{:S(2)}) collective-permute-start(bf16[2,256,256]{2,1,0:T(8,128)(2,1)S(1)} %pad_maximum_fusion.2.refs_0_), channel_id=1, source_target_pairs={{0,2},{1,3},{2,0},{3,1},{4,6},{5,7},{6,4},{7,5},{8,10},{9,11},{10,... | collective-permute-start | bytes 786440 | tf_op jit(solution)/shard_map/ppermute | solution.py:24
  24.5 2.2 %collective-permute-done.13.refs_1_ = bf16[2,256,256]{2,1,0:T(8,128)(2,1)S(1)} collective-permute-done((bf16[2,256,256]{2,1,0:T(8,128)(2,1)S(1)}, bf16[2,256,256]{2,1,0:T(8,128)(2,1)S(1)}, u32[]{:S(2)}, u32[]{:S(2)}) %collective-permute-start.13) | collective-permute-done | bytes 262176 | tf_op jit(solution)/shard_map/ppermute | solution.py:24
  26.7 3.9 %collective-permute-start.2 = (bf16[256,256]{1,0:T(8,128)(2,1)S(1)}, bf16[256,256]{1,0:T(8,128)(2,1)S(1)}, u32[]{:S(2)}, u32[]{:S(2)}) collective-permute-start(bf16[256,256]{1,0:T(8,128)(2,1)S(1)} %get-tuple-element.53), channel_id=1, source_target_pairs={{0,100},{1,93},{2,86},{3,79},{4,0},{5,121},{6,114},{7,107},{8,108}... | collective-permute-start | bytes 393224 | tf_op jit(solution)/shard_map/ppermute | solution.py:24
  30.7 6.5 %collective-permute-done.14.refs_2_ = bf16[2,256,256]{2,1,0:T(8,128)(2,1)S(1)} collective-permute-done((bf16[2,256,256]{2,1,0:T(8,128)(2,1)S(1)}, bf16[2,256,256]{2,1,0:T(8,128)(2,1)S(1)}, u32[]{:S(2)}, u32[]{:S(2)}) %collective-permute-start.14) | collective-permute-done | bytes 262176 | tf_op jit(solution)/shard_map/ppermute | solution.py:24
  37.2 2.6 %collective-permute-done.15.refs_3_ = bf16[2,256,256]{2,1,0:T(8,128)(2,1)S(1)} collective-permute-done((bf16[2,256,256]{2,1,0:T(8,128)(2,1)S(1)}, bf16[2,256,256]{2,1,0:T(8,128)(2,1)S(1)}, u32[]{:S(2)}, u32[]{:S(2)}) %collective-permute-start.15) | collective-permute-done | bytes 262176 | tf_op jit(solution)/shard_map/ppermute | solution.py:24
  39.8 6.8 %shard_map.60 = s16[4,2,272,256]{3,2,1,0:T(8,128)(2,1)S(1)} custom-call(s32[4]{0:T(128)S(1)} %pad_add_fusion.ids_ref, f32[2]{0:T(128)S(1)} %fusion.4.weight_ref, s32[2,1,2048]{2,1,0:T(1,128)S(1)} %copy-done.6, bf16[2,256,256]{2,1,0:T(8,128)(2,1)S(1)} %pad_maximum_fusion.2.refs_0_, bf16[2,256,256]{2,1,0:T(8,128)(2,1)S(1)} %collective-permute-done.13.refs_1_, ...), custom_call_target="tpu_custom_call" | custom-call | flops 4294967296 | bytes 11534336 | tf_op jit(solution)/shard_map/pallas_call | solution.py:109
  46.6 0.7 collective-permute-start.16
  47.4 3.1 %collective-permute-start.3 = (bf16[2,256,256]{2,1,0:T(8,128)(2,1)S(1)}, bf16[2,256,256]{2,1,0:T(8,128)(2,1)S(1)}, u32[]{:S(2)}, u32[]{:S(2)}) collective-permute-start(bf16[2,256,256]{2,1,0:T(8,128)(2,1)S(1)} %pad_maximum_fusion.1.refs_0_), channel_id=1, source_target_pairs={{0,121},{1,8},{2,123},{3,10},{4,125},{5,12},{6,127},{7,14},{8,1},{... | collective-permute-start | bytes 786440 | tf_op jit(solution)/shard_map/ppermute | solution.py:24
  50.5 2.7 %collective-permute-start.4 = (bf16[2,256,256]{2,1,0:T(8,128)(2,1)S(1)}, bf16[2,256,256]{2,1,0:T(8,128)(2,1)S(1)}, u32[]{:S(2)}, u32[]{:S(2)}) collective-permute-start(bf16[2,256,256]{2,1,0:T(8,128)(2,1)S(1)} %pad_maximum_fusion.1.refs_0_), channel_id=1, source_target_pairs={{0,114},{1,115},{2,16},{3,17},{4,118},{5,119},{6,20},{7,21},{8,122... | collective-permute-start | bytes 786440 | tf_op jit(solution)/shard_map/ppermute | solution.py:24
  53.2 0.7 collective-permute-start.9
  53.9 0.7 collective-permute-start.11
  54.6 25.1 %collective-permute-done.3.refs_1_ = bf16[2,256,256]{2,1,0:T(8,128)(2,1)S(1)} collective-permute-done((bf16[2,256,256]{2,1,0:T(8,128)(2,1)S(1)}, bf16[2,256,256]{2,1,0:T(8,128)(2,1)S(1)}, u32[]{:S(2)}, u32[]{:S(2)}) %collective-permute-start.3) | collective-permute-done | bytes 262176 | tf_op jit(solution)/shard_map/ppermute | solution.py:24
  79.7 0.7 collective-permute-start
  80.3 8.0 %collective-permute-done.4.refs_2_ = bf16[2,256,256]{2,1,0:T(8,128)(2,1)S(1)} collective-permute-done((bf16[2,256,256]{2,1,0:T(8,128)(2,1)S(1)}, bf16[2,256,256]{2,1,0:T(8,128)(2,1)S(1)}, u32[]{:S(2)}, u32[]{:S(2)}) %collective-permute-start.4) | collective-permute-done | bytes 262176 | tf_op jit(solution)/shard_map/ppermute | solution.py:24
  88.4 6.8 %shard_map.62 = (s16[2,272,256]{2,1,0:T(8,128)(2,1)S(1)}, s16[2,272,256]{2,1,0:T(8,128)(2,1)S(1)}, s16[2,272,256]{2,1,0:T(8,128)(2,1)S(1)}, s16[2,272,256]{2,1,0:T(8,128)(2,1)S(1)}) custom-call(s32[4]{0:T(128)S(1)} %pad_add_fusion.ids_ref, f32[2]{0:T(128)S(1)} %fusion.4.weight_ref, s32[2,1,2048]{2,1,0:T(1,128)S(1)} %copy-done.6, ...), custom_call_target="tpu_custom_call" | custom-call | flops 4294967296 | bytes 11534336 | tf_op jit(solution)/shard_map/pallas_call | solution.py:109
  95.2 0.7 copy-done
  95.9 1.6 collective-permute-done.5.refs_3_
  97.5 12.0 %collective-permute-start.25 = (s16[2,272,256]{2,1,0:T(8,128)(2,1)S(1)}, s16[2,272,256]{2,1,0:T(8,128)(2,1)S(1)}, u32[]{:S(2)}, u32[]{:S(2)}) collective-permute-start(s16[2,272,256]{2,1,0:T(8,128)(2,1)S(1)} %get-tuple-element.45), channel_id=1, source_target_pairs={{0,114},{1,115},{2,16},{3,17},{4,118},{5,119},{6,20},{7,21},{8,122... | collective-permute-start | bytes 835592 | tf_op jit(solution)/shard_map/ppermute | solution.py:24
  109.5 7.0 %shard_map.61 = (s16[2,272,256]{2,1,0:T(8,128)(2,1)S(1)}, s16[2,272,256]{2,1,0:T(8,128)(2,1)S(1)}, s16[2,272,256]{2,1,0:T(8,128)(2,1)S(1)}, s16[2,272,256]{2,1,0:T(8,128)(2,1)S(1)}) custom-call(s32[4]{0:T(128)S(1)} %pad_add_fusion.ids_ref, f32[2]{0:T(128)S(1)} %fusion.4.weight_ref, s32[2,1,2048]{2,1,0:T(1,128)S(1)} %collective-permute-done.perm_ref, ...), custom_call_target="tpu_custom_call" | custom-call | flops 4294967296 | bytes 11534336 | tf_op jit(solution)/shard_map/pallas_call | solution.py:109
  116.4 0.7 copy-done.1
  117.2 5.1 %collective-permute-start.20 = (s16[2,272,256]{2,1,0:T(8,128)(2,1)S(1)}, s16[2,272,256]{2,1,0:T(8,128)(2,1)S(1)}, u32[]{:S(2)}, u32[]{:S(2)}) collective-permute-start(s16[2,272,256]{2,1,0:T(8,128)(2,1)S(1)} %get-tuple-element.36), channel_id=1, source_target_pairs={{0,1},{1,0},{2,3},{3,2},{4,5},{5,4},{6,7},{7,6},{8,9},{9,8},{10,11... | collective-permute-start | bytes 835592 | tf_op jit(solution)/shard_map/ppermute | solution.py:24
  122.3 2.7 %collective-permute-start.22 = (s16[2,272,256]{2,1,0:T(8,128)(2,1)S(1)}, s16[2,272,256]{2,1,0:T(8,128)(2,1)S(1)}, u32[]{:S(2)}, u32[]{:S(2)}) collective-permute-start(s16[2,272,256]{2,1,0:T(8,128)(2,1)S(1)} %get-tuple-element.38), channel_id=1, source_target_pairs={{0,3},{1,2},{2,1},{3,0},{4,7},{5,6},{6,5},{7,4},{8,11},{9,10},{10,... | collective-permute-start | bytes 835592 | tf_op jit(solution)/shard_map/ppermute | solution.py:24
  125.1 6.8 %shard_map.59 = (s16[2,272,256]{2,1,0:T(8,128)(2,1)S(1)}, s16[2,272,256]{2,1,0:T(8,128)(2,1)S(1)}, s16[2,272,256]{2,1,0:T(8,128)(2,1)S(1)}, s16[2,272,256]{2,1,0:T(8,128)(2,1)S(1)}) custom-call(s32[4]{0:T(128)S(1)} %pad_add_fusion.ids_ref, f32[2]{0:T(128)S(1)} %fusion.4.weight_ref, s32[2,1,2048]{2,1,0:T(1,128)S(1)} %collective-permute-done.perm_ref, ...), custom_call_target="tpu_custom_call" | custom-call | flops 4294967296 | bytes 11534336 | tf_op jit(solution)/shard_map/pallas_call | solution.py:109
  131.9 0.7 copy-done.2
  132.6 0.7 copy-done.3
  133.3 0.7 copy-done.4
  134.0 0.7 copy-done.5
  134.7 3.2 %join.1 = (s16[2,272,256]{2,1,0:T(8,128)(2,1)}, s16[2,272,256]{2,1,0:T(8,128)(2,1)}, s16[2,272,256]{2,1,0:T(8,128)(2,1)}, s16[2,272,256]{2,1,0:T(8,128)(2,1)}) custom-call(s16[2,272,256]{2,1,0:T(8,128)(2,1)} %copy-done.2, s16[2,272,256]{2,1,0:T(8,128)(2,1)} %copy-done.3, s16[2,272,256]{2,1,0:T(8,128)(2,1)} %copy-done.4, s16[2,272,256]{2,1,0:T(8,128)(2,1)} %copy-done.5, ...), custom_call_target="tpu_custom_call" | custom-call | tf_op jit(solution)/shard_map/join/pallas_call | solution.py:133
  137.9 0.7 copy-done.12
  138.6 0.1 copy-done.14
  138.7 2.3 %sum.3 = s16[2,272,256]{2,1,0:T(8,128)(2,1)} custom-call(s16[2,272,256]{2,1,0:T(8,128)(2,1)} %copy-done, s16[2,272,256]{2,1,0:T(8,128)(2,1)} %copy-done.11, s16[2,272,256]{2,1,0:T(8,128)(2,1)} %copy-done.12, s16[2,272,256]{2,1,0:T(8,128)(2,1)} %copy-done.14, s16[2,272,256]{2,1,0:T(8,128)(2,1)} %get-tuple-element.31.refs_4_.refs_0_), custom_call_target="tpu_custom_call" | custom-call | tf_op jit(solution)/shard_map/sum/pallas_call | solution.py:151
  141.0 2.2 %collective-permute-start.27 = (s16[2,272,256]{2,1,0:T(8,128)(2,1)}, s16[2,272,256]{2,1,0:T(8,128)(2,1)S(1)}, u32[]{:S(2)}, u32[]{:S(2)}) collective-permute-start(s16[2,272,256]{2,1,0:T(8,128)(2,1)} %sum.3), channel_id=1, source_target_pairs={{0,4},{1,13},{2,22},{3,31},{4,32},{5,41},{6,50},{7,59},{8,12},{9,2... | collective-permute-start | bytes 835592 | tf_op jit(solution)/shard_map/ppermute | solution.py:24
  143.2 0.7 copy-done.13
  143.9 0.1 copy-done.15
  144.1 2.3 %sum.2 = s16[2,272,256]{2,1,0:T(8,128)(2,1)} custom-call(s16[2,272,256]{2,1,0:T(8,128)(2,1)} %copy-done.1, s16[2,272,256]{2,1,0:T(8,128)(2,1)} %copy-done.13, s16[2,272,256]{2,1,0:T(8,128)(2,1)} %copy-done.15, s16[2,272,256]{2,1,0:T(8,128)(2,1)} %copy-done.16, s16[2,272,256]{2,1,0:T(8,128)(2,1)} %get-tuple-element.31.refs_4_.refs_0_), custom_call_target="tpu_custom_call" | custom-call | tf_op jit(solution)/shard_map/sum/pallas_call | solution.py:151
  146.4 1.5 collective-permute-start.18
  147.8 3.2 %collective-permute-start.19 = (s16[2,272,256]{2,1,0:T(8,128)(2,1)S(1)}, s16[2,272,256]{2,1,0:T(8,128)(2,1)S(1)}, u32[]{:S(2)}, u32[]{:S(2)}) collective-permute-start(s16[2,272,256]{2,1,0:T(8,128)(2,1)S(1)} %copy-done.25), channel_id=1, source_target_pairs={{0,3},{1,2},{2,1},{3,0},{4,7},{5,6},{6,5},{7,4},{8,11},{9,10},{10,... | collective-permute-start | bytes 835592 | tf_op jit(solution)/shard_map/ppermute | solution.py:24
  151.1 3.3 %collective-permute-done.27.refs_5_ = s16[2,272,256]{2,1,0:T(8,128)(2,1)S(1)} collective-permute-done((s16[2,272,256]{2,1,0:T(8,128)(2,1)}, s16[2,272,256]{2,1,0:T(8,128)(2,1)S(1)}, u32[]{:S(2)}, u32[]{:S(2)}) %collective-permute-start.27) | collective-permute-done | bytes 278560 | tf_op jit(solution)/shard_map/ppermute | solution.py:24
  154.4 2.1 %collective-permute-done.23.refs_4_ = s16[2,272,256]{2,1,0:T(8,128)(2,1)S(1)} collective-permute-done((s16[2,272,256]{2,1,0:T(8,128)(2,1)}, s16[2,272,256]{2,1,0:T(8,128)(2,1)S(1)}, u32[]{:S(2)}, u32[]{:S(2)}) %collective-permute-start.23) | collective-permute-done | bytes 278560 | tf_op jit(solution)/shard_map/ppermute | solution.py:24
  156.5 4.1 %collective-permute-done.18.refs_2_ = s16[2,272,256]{2,1,0:T(8,128)(2,1)S(1)} collective-permute-done((s16[2,272,256]{2,1,0:T(8,128)(2,1)S(1)}, s16[2,272,256]{2,1,0:T(8,128)(2,1)S(1)}, u32[]{:S(2)}, u32[]{:S(2)}) %collective-permute-start.18) | collective-permute-done | bytes 278560 | tf_op jit(solution)/shard_map/ppermute | solution.py:24
  160.6 2.6 %collective-permute-done.19.refs_3_ = s16[2,272,256]{2,1,0:T(8,128)(2,1)S(1)} collective-permute-done((s16[2,272,256]{2,1,0:T(8,128)(2,1)S(1)}, s16[2,272,256]{2,1,0:T(8,128)(2,1)S(1)}, u32[]{:S(2)}, u32[]{:S(2)}) %collective-permute-start.19) | collective-permute-done | bytes 278560 | tf_op jit(solution)/shard_map/ppermute | solution.py:24
  163.2 0.7 copy-done.21
  163.9 3.3 %gram.1 = (f32[2,256,256]{2,1,0:T(8,128)}, f32[256,256]{1,0:T(8,128)}, f32[384,128]{1,0:T(8,128)}) custom-call(s32[4]{0:T(128)} %copy-done.7, s16[2,272,256]{2,1,0:T(8,128)(2,1)} %get-tuple-element.31.refs_4_.refs_0_, s16[2,272,256]{2,1,0:T(8,128)(2,1)} %copy-done.19, s16[2,272,256]{2,1,0:T(8,128)(2,1)} %copy-done.20, s16[2,272,256]{2,1,0:T(8,128)(2,1)} %copy-done.21, ...), custom_call_target="tpu_custom_call" | custom-call | tf_op jit(solution)/shard_map/gram/pallas_call | solution.py:185
  167.2 3.2 %collective-permute-start.28 = (f32[256,256]{1,0:T(8,128)}, f32[256,256]{1,0:T(8,128)S(1)}, u32[]{:S(2)}, u32[]{:S(2)}) collective-permute-start(f32[256,256]{1,0:T(8,128)} %get-tuple-element.48.other_ref), channel_id=1, source_target_pairs={{0,4},{1,5},{2,6},{3,7},{4,0},{5,1},{6,2},{7,3},{8,12},{9,13},{10,... | collective-permute-start | bytes 786440 | tf_op jit(solution)/shard_map/ppermute | solution.py:24
  170.4 4.4 %collective-permute-start.30 = (f32[384,128]{1,0:T(8,128)}, f32[384,128]{1,0:T(8,128)S(1)}, u32[]{:S(2)}, u32[]{:S(2)}) collective-permute-start(f32[384,128]{1,0:T(8,128)} %get-tuple-element.49.refs_0_), channel_id=1, source_target_pairs={{0,2},{1,3},{2,0},{3,1},{4,6},{5,7},{6,4},{7,5},{8,10},{9,11},{10,... | collective-permute-start | bytes 589832 | tf_op jit(solution)/shard_map/ppermute | solution.py:24
  174.8 0.3 collective-permute-start.31
  175.1 2.8 %collective-permute-done.29.refs_1_ = f32[384,128]{1,0:T(8,128)S(1)} collective-permute-done((f32[384,128]{1,0:T(8,128)}, f32[384,128]{1,0:T(8,128)S(1)}, u32[]{:S(2)}, u32[]{:S(2)}) %collective-permute-start.29) | collective-permute-done | bytes 196640 | tf_op jit(solution)/shard_map/ppermute | solution.py:24
  177.9 4.0 %collective-permute-done.30.refs_2_ = f32[384,128]{1,0:T(8,128)S(1)} collective-permute-done((f32[384,128]{1,0:T(8,128)}, f32[384,128]{1,0:T(8,128)S(1)}, u32[]{:S(2)}, u32[]{:S(2)}) %collective-permute-start.30) | collective-permute-done | bytes 196640 | tf_op jit(solution)/shard_map/ppermute | solution.py:24
  182.0 2.1 %collective-permute-done.31.refs_3_ = f32[384,128]{1,0:T(8,128)S(1)} collective-permute-done((f32[384,128]{1,0:T(8,128)}, f32[384,128]{1,0:T(8,128)S(1)}, u32[]{:S(2)}, u32[]{:S(2)}) %collective-permute-start.31) | collective-permute-done | bytes 196640 | tf_op jit(solution)/shard_map/ppermute | solution.py:24
  184.1 0.7 copy-done.24
  184.7 18.1 %orthogonal.1 = (f32[2,256,256]{2,1,0:T(8,128)}, s16[272,256]{1,0:T(8,128)(2,1)}) custom-call(s32[4]{0:T(128)} %copy-done.7, f32[2,256,256]{2,1,0:T(8,128)} %get-tuple-element.47.samples_ref, f32[256,256]{1,0:T(8,128)} %get-tuple-element.48.other_ref, f32[384,128]{1,0:T(8,128)} %get-tuple-element.49.refs_0_, f32[384,128]{1,0:T(8,128)} %copy-done.22, ...), custom_call_target="tpu_custom_call" | custom-call | tf_op jit(solution)/shard_map/orthogonal/pallas_call | solution.py:297
  202.9 0.6 collective-permute-start.32
  203.5 6.1 %collective-permute-done.32 = s16[272,256]{1,0:T(8,128)(2,1)S(1)} collective-permute-done((s16[272,256]{1,0:T(8,128)(2,1)}, s16[272,256]{1,0:T(8,128)(2,1)S(1)}, u32[]{:S(2)}, u32[]{:S(2)}) %collective-permute-start.32) | collective-permute-done | bytes 139296 | tf_op jit(solution)/shard_map/ppermute | solution.py:24
  209.7 0.7 fusion.1
  (79 shorter events, 0.5 us)
Async XLA Ops:
  0.6 23.9 %copy-start.28 = (s32[2,1,1]{0,2,1:T(1,128)S(1)}, s32[2,1,1]{0,2,1:T(1,128)}, u32[]{:S(2)}) copy-start(s32[2,1,1]{0,2,1:T(1,128)} %param.7) | copy-start | bytes 28
  0.6 39.1 %copy-start.6 = (s32[2,1,2048]{2,1,0:T(1,128)S(1)}, s32[2,1,2048]{2,1,0:T(1,128)}, u32[]{:S(2)}) copy-start(s32[2,1,2048]{2,1,0:T(1,128)} %perm_ref.3) | copy-start | bytes 49156
  1.7 8.1 %collective-permute-start.7 = (bf16[256,256]{1,0:T(8,128)(2,1)S(1)}, bf16[256,256]{1,0:T(8,128)(2,1)S(1)}, u32[]{:S(2)}, u32[]{:S(2)}) collective-permute-start(bf16[256,256]{1,0:T(8,128)(2,1)S(1)} %get-tuple-element.54), channel_id=1, source_target_pairs={{0,2},{1,3},{2,0},{3,1},{4,6},{5,7},{6,4},{7,5},{8,10},{9,11},{10,... | collective-permute-start | bytes 393224 | tf_op jit(solution)/shard_map/ppermute | solution.py:24
  5.7 6.3 %collective-permute-start.8 = (bf16[256,256]{1,0:T(8,128)(2,1)S(1)}, bf16[256,256]{1,0:T(8,128)(2,1)S(1)}, u32[]{:S(2)}, u32[]{:S(2)}) collective-permute-start(bf16[256,256]{1,0:T(8,128)(2,1)S(1)} %get-tuple-element.54), channel_id=1, source_target_pairs={{0,3},{1,2},{2,1},{3,0},{4,7},{5,6},{6,5},{7,4},{8,11},{9,10},{10,... | collective-permute-start | bytes 393224 | tf_op jit(solution)/shard_map/ppermute | solution.py:24
  6.4 6.4 %collective-permute-start.6 = (bf16[256,256]{1,0:T(8,128)(2,1)S(1)}, bf16[256,256]{1,0:T(8,128)(2,1)S(1)}, u32[]{:S(2)}, u32[]{:S(2)}) collective-permute-start(bf16[256,256]{1,0:T(8,128)(2,1)S(1)} %get-tuple-element.54), channel_id=1, source_target_pairs={{0,1},{1,0},{2,3},{3,2},{4,5},{5,4},{6,7},{7,6},{8,9},{9,8},{10,11... | collective-permute-start | bytes 393224 | tf_op jit(solution)/shard_map/ppermute | solution.py:24
  6.8 9.9 %collective-permute-start.12 = (bf16[256,256]{1,0:T(8,128)(2,1)S(1)}, bf16[256,256]{1,0:T(8,128)(2,1)S(1)}, u32[]{:S(2)}, u32[]{:S(2)}) collective-permute-start(bf16[256,256]{1,0:T(8,128)(2,1)S(1)} %get-tuple-element.53), channel_id=1, source_target_pairs={{0,4},{1,5},{2,6},{3,7},{4,0},{5,1},{6,2},{7,3},{8,12},{9,13},{10,... | collective-permute-start | bytes 393224 | tf_op jit(solution)/shard_map/ppermute | solution.py:24
  12.9 26.9 %collective-permute-start.10 = (bf16[4,256,256]{2,1,0:T(8,128)(2,1)S(1)}, bf16[4,256,256]{2,1,0:T(8,128)(2,1)S(1)}, u32[]{:S(2)}, u32[]{:S(2)}) collective-permute-start(bf16[4,256,256]{2,1,0:T(8,128)(2,1)S(1)} %pad_maximum_fusion.refs_4_), channel_id=1, source_target_pairs={{0,4},{1,5},{2,6},{3,7},{4,0},{5,1},{6,2},{7,3},{8,12},{9,13},{10,... | collective-permute-start | bytes 1572872 | tf_op jit(solution)/shard_map/ppermute | solution.py:24
  16.0 31.3 %collective-permute-start.1 = (bf16[256,256]{1,0:T(8,128)(2,1)S(1)}, bf16[256,256]{1,0:T(8,128)(2,1)S(1)}, u32[]{:S(2)}, u32[]{:S(2)}) collective-permute-start(bf16[256,256]{1,0:T(8,128)(2,1)S(1)} %get-tuple-element.53), channel_id=1, source_target_pairs={{0,0},{1,121},{2,114},{3,107},{4,100},{5,93},{6,86},{7,79},{8,8},{... | collective-permute-start | bytes 393224 | tf_op jit(solution)/shard_map/ppermute | solution.py:24
  16.7 10.0 %collective-permute-start.13 = (bf16[2,256,256]{2,1,0:T(8,128)(2,1)S(1)}, bf16[2,256,256]{2,1,0:T(8,128)(2,1)S(1)}, u32[]{:S(2)}, u32[]{:S(2)}) collective-permute-start(bf16[2,256,256]{2,1,0:T(8,128)(2,1)S(1)} %pad_maximum_fusion.2.refs_0_), channel_id=1, source_target_pairs={{0,1},{1,0},{2,3},{3,2},{4,5},{5,4},{6,7},{7,6},{8,9},{9,8},{10,11... | collective-permute-start | bytes 786440 | tf_op jit(solution)/shard_map/ppermute | solution.py:24
  20.9 16.3 %collective-permute-start.14 = (bf16[2,256,256]{2,1,0:T(8,128)(2,1)S(1)}, bf16[2,256,256]{2,1,0:T(8,128)(2,1)S(1)}, u32[]{:S(2)}, u32[]{:S(2)}) collective-permute-start(bf16[2,256,256]{2,1,0:T(8,128)(2,1)S(1)} %pad_maximum_fusion.2.refs_0_), channel_id=1, source_target_pairs={{0,2},{1,3},{2,0},{3,1},{4,6},{5,7},{6,4},{7,5},{8,10},{9,11},{10,... | collective-permute-start | bytes 786440 | tf_op jit(solution)/shard_map/ppermute | solution.py:24
  24.5 15.3 %collective-permute-start.15 = (bf16[2,256,256]{2,1,0:T(8,128)(2,1)S(1)}, bf16[2,256,256]{2,1,0:T(8,128)(2,1)S(1)}, u32[]{:S(2)}, u32[]{:S(2)}) collective-permute-start(bf16[2,256,256]{2,1,0:T(8,128)(2,1)S(1)} %pad_maximum_fusion.2.refs_0_), channel_id=1, source_target_pairs={{0,3},{1,2},{2,1},{3,0},{4,7},{5,6},{6,5},{7,4},{8,11},{9,10},{10,... | collective-permute-start | bytes 786440 | tf_op jit(solution)/shard_map/ppermute | solution.py:24
  24.5 100.5 %copy-start.7 = (s32[4]{0:T(128)}, s32[4]{0:T(128)S(1)}, u32[]{:S(2)}) copy-start(s32[4]{0:T(128)S(1)} %pad_add_fusion.ids_ref) | copy-start | bytes 52
  26.7 20.6 %collective-permute-start.2 = (bf16[256,256]{1,0:T(8,128)(2,1)S(1)}, bf16[256,256]{1,0:T(8,128)(2,1)S(1)}, u32[]{:S(2)}, u32[]{:S(2)}) collective-permute-start(bf16[256,256]{1,0:T(8,128)(2,1)S(1)} %get-tuple-element.53), channel_id=1, source_target_pairs={{0,100},{1,93},{2,86},{3,79},{4,0},{5,121},{6,114},{7,107},{8,108}... | collective-permute-start | bytes 393224 | tf_op jit(solution)/shard_map/ppermute | solution.py:24
  46.6 75.7 %collective-permute-start.16 = (s16[4,2,272,256]{3,2,1,0:T(8,128)(2,1)S(1)}, s16[4,2,272,256]{3,2,1,0:T(8,128)(2,1)S(1)}, u32[]{:S(2)}, u32[]{:S(2)}) collective-permute-start(s16[4,2,272,256]{3,2,1,0:T(8,128)(2,1)S(1)} %shard_map.60), channel_id=1, source_target_pairs={{0,0},{1,9},{2,18},{3,27},{4,36},{5,45},{6,54},{7,63},{8,8},{9,17}... | collective-permute-start | bytes 3342344 | tf_op jit(solution)/shard_map/ppermute | solution.py:24
  47.4 32.3 %collective-permute-start.3 = (bf16[2,256,256]{2,1,0:T(8,128)(2,1)S(1)}, bf16[2,256,256]{2,1,0:T(8,128)(2,1)S(1)}, u32[]{:S(2)}, u32[]{:S(2)}) collective-permute-start(bf16[2,256,256]{2,1,0:T(8,128)(2,1)S(1)} %pad_maximum_fusion.1.refs_0_), channel_id=1, source_target_pairs={{0,121},{1,8},{2,123},{3,10},{4,125},{5,12},{6,127},{7,14},{8,1},{... | collective-permute-start | bytes 786440 | tf_op jit(solution)/shard_map/ppermute | solution.py:24
  50.5 37.9 %collective-permute-start.4 = (bf16[2,256,256]{2,1,0:T(8,128)(2,1)S(1)}, bf16[2,256,256]{2,1,0:T(8,128)(2,1)S(1)}, u32[]{:S(2)}, u32[]{:S(2)}) collective-permute-start(bf16[2,256,256]{2,1,0:T(8,128)(2,1)S(1)} %pad_maximum_fusion.1.refs_0_), channel_id=1, source_target_pairs={{0,114},{1,115},{2,16},{3,17},{4,118},{5,119},{6,20},{7,21},{8,122... | collective-permute-start | bytes 786440 | tf_op jit(solution)/shard_map/ppermute | solution.py:24
  53.2 56.3 %collective-permute-start.9 = (bf16[4,256,256]{2,1,0:T(8,128)(2,1)S(1)}, bf16[4,256,256]{2,1,0:T(8,128)(2,1)S(1)}, u32[]{:S(2)}, u32[]{:S(2)}) collective-permute-start(bf16[4,256,256]{2,1,0:T(8,128)(2,1)S(1)} %pad_maximum_fusion.refs_4_), channel_id=1, source_target_pairs={{0,0},{1,121},{2,114},{3,107},{4,100},{5,93},{6,86},{7,79},{8,8},{... | collective-permute-start | bytes 1572872 | tf_op jit(solution)/shard_map/ppermute | solution.py:24
  53.9 55.6 %collective-permute-start.11 = (bf16[4,256,256]{2,1,0:T(8,128)(2,1)S(1)}, bf16[4,256,256]{2,1,0:T(8,128)(2,1)S(1)}, u32[]{:S(2)}, u32[]{:S(2)}) collective-permute-start(bf16[4,256,256]{2,1,0:T(8,128)(2,1)S(1)} %collective-permute-done.10.refs_5_), channel_id=1, source_target_pairs={{0,0},{1,121},{2,114},{3,107},{4,100},{5,93},{6,86},{7,79},{8,8},{... | collective-permute-start | bytes 1572872 | tf_op jit(solution)/shard_map/ppermute | solution.py:24
  79.7 17.8 %collective-permute-start = (s32[2,1,2048]{2,1,0:T(1,128)S(1)}, s32[2,1,2048]{2,1,0:T(1,128)S(1)}, u32[]{:S(2)}, u32[]{:S(2)}) collective-permute-start(s32[2,1,2048]{2,1,0:T(1,128)S(1)} %copy-done.6), channel_id=1, source_target_pairs={{0,0},{1,121},{2,114},{3,107},{4,100},{5,93},{6,86},{7,79},{8,8},{... | collective-permute-start | bytes 49160 | tf_op jit(solution)/shard_map/ppermute | solution.py:24
  88.4 9.1 %collective-permute-start.5 = (bf16[2,256,256]{2,1,0:T(8,128)(2,1)S(1)}, bf16[2,256,256]{2,1,0:T(8,128)(2,1)S(1)}, u32[]{:S(2)}, u32[]{:S(2)}) collective-permute-start(bf16[2,256,256]{2,1,0:T(8,128)(2,1)S(1)} %pad_maximum_fusion.1.refs_0_), channel_id=1, source_target_pairs={{0,107},{1,122},{2,9},{3,24},{4,111},{5,126},{6,13},{7,28},{8,115}... | collective-permute-start | bytes 786440 | tf_op jit(solution)/shard_map/ppermute | solution.py:24
  95.2 0.7 copy-start
  97.5 24.8 %collective-permute-start.24 = (s16[2,272,256]{2,1,0:T(8,128)(2,1)S(1)}, s16[2,272,256]{2,1,0:T(8,128)(2,1)S(1)}, u32[]{:S(2)}, u32[]{:S(2)}) collective-permute-start(s16[2,272,256]{2,1,0:T(8,128)(2,1)S(1)} %get-tuple-element.44), channel_id=1, source_target_pairs={{0,121},{1,8},{2,123},{3,10},{4,125},{5,12},{6,127},{7,14},{8,1},{... | collective-permute-start | bytes 835592 | tf_op jit(solution)/shard_map/ppermute | solution.py:24
  97.5 40.4 %collective-permute-start.25 = (s16[2,272,256]{2,1,0:T(8,128)(2,1)S(1)}, s16[2,272,256]{2,1,0:T(8,128)(2,1)S(1)}, u32[]{:S(2)}, u32[]{:S(2)}) collective-permute-start(s16[2,272,256]{2,1,0:T(8,128)(2,1)S(1)} %get-tuple-element.45), channel_id=1, source_target_pairs={{0,114},{1,115},{2,16},{3,17},{4,118},{5,119},{6,20},{7,21},{8,122... | collective-permute-start | bytes 835592 | tf_op jit(solution)/shard_map/ppermute | solution.py:24
  109.5 28.4 %collective-permute-start.26 = (s16[2,272,256]{2,1,0:T(8,128)(2,1)S(1)}, s16[2,272,256]{2,1,0:T(8,128)(2,1)S(1)}, u32[]{:S(2)}, u32[]{:S(2)}) collective-permute-start(s16[2,272,256]{2,1,0:T(8,128)(2,1)S(1)} %get-tuple-element.46), channel_id=1, source_target_pairs={{0,107},{1,122},{2,9},{3,24},{4,111},{5,126},{6,13},{7,28},{8,115}... | collective-permute-start | bytes 835592 | tf_op jit(solution)/shard_map/ppermute | solution.py:24
  116.4 0.7 copy-start.1
  117.2 26.0 %collective-permute-start.20 = (s16[2,272,256]{2,1,0:T(8,128)(2,1)S(1)}, s16[2,272,256]{2,1,0:T(8,128)(2,1)S(1)}, u32[]{:S(2)}, u32[]{:S(2)}) collective-permute-start(s16[2,272,256]{2,1,0:T(8,128)(2,1)S(1)} %get-tuple-element.36), channel_id=1, source_target_pairs={{0,1},{1,0},{2,3},{3,2},{4,5},{5,4},{6,7},{7,6},{8,9},{9,8},{10,11... | collective-permute-start | bytes 835592 | tf_op jit(solution)/shard_map/ppermute | solution.py:24
  122.3 9.5 %copy-start.11 = (s16[2,272,256]{2,1,0:T(8,128)(2,1)}, s16[2,272,256]{2,1,0:T(8,128)(2,1)S(1)}, u32[]{:S(2)}) copy-start(s16[2,272,256]{2,1,0:T(8,128)(2,1)S(1)} %collective-permute-done.24.refs_1_) | copy-start | bytes 835588
  122.3 20.9 %collective-permute-start.21 = (s16[2,272,256]{2,1,0:T(8,128)(2,1)S(1)}, s16[2,272,256]{2,1,0:T(8,128)(2,1)S(1)}, u32[]{:S(2)}, u32[]{:S(2)}) collective-permute-start(s16[2,272,256]{2,1,0:T(8,128)(2,1)S(1)} %get-tuple-element.37), channel_id=1, source_target_pairs={{0,2},{1,3},{2,0},{3,1},{4,6},{5,7},{6,4},{7,5},{8,10},{9,11},{10,... | collective-permute-start | bytes 835592 | tf_op jit(solution)/shard_map/ppermute | solution.py:24
  122.3 9.5 %copy-start.8 = (s16[4,2,272,256]{3,2,1,0:T(8,128)(2,1)}, s16[4,2,272,256]{3,2,1,0:T(8,128)(2,1)S(1)}, u32[]{:S(2)}) copy-start(s16[4,2,272,256]{3,2,1,0:T(8,128)(2,1)S(1)} %collective-permute-done.16.refs_4_) | copy-start | bytes 3342340
  122.3 20.9 %collective-permute-start.22 = (s16[2,272,256]{2,1,0:T(8,128)(2,1)S(1)}, s16[2,272,256]{2,1,0:T(8,128)(2,1)S(1)}, u32[]{:S(2)}, u32[]{:S(2)}) collective-permute-start(s16[2,272,256]{2,1,0:T(8,128)(2,1)S(1)} %get-tuple-element.38), channel_id=1, source_target_pairs={{0,3},{1,2},{2,1},{3,0},{4,7},{5,6},{6,5},{7,4},{8,11},{9,10},{10,... | collective-permute-start | bytes 835592 | tf_op jit(solution)/shard_map/ppermute | solution.py:24
  131.9 0.7 copy-start.2
  132.6 0.7 copy-start.3
  133.3 0.7 copy-start.4
  134.0 0.7 copy-start.5
  137.9 0.7 copy-start.12
  137.9 0.8 copy-start.14
  141.0 5.4 %copy-start.27 = (s16[2,272,256]{2,1,0:T(8,128)(2,1)S(1)}, s16[2,272,256]{2,1,0:T(8,128)(2,1)}, u32[]{:S(2)}) copy-start(s16[2,272,256]{2,1,0:T(8,128)(2,1)} %get-tuple-element.32) | copy-start | bytes 835588
  141.0 5.4 %copy-start.26 = (s16[2,272,256]{2,1,0:T(8,128)(2,1)S(1)}, s16[2,272,256]{2,1,0:T(8,128)(2,1)}, u32[]{:S(2)}) copy-start(s16[2,272,256]{2,1,0:T(8,128)(2,1)} %get-tuple-element.33) | copy-start | bytes 835588
  141.0 6.9 %copy-start.25 = (s16[2,272,256]{2,1,0:T(8,128)(2,1)S(1)}, s16[2,272,256]{2,1,0:T(8,128)(2,1)}, u32[]{:S(2)}) copy-start(s16[2,272,256]{2,1,0:T(8,128)(2,1)} %get-tuple-element.34) | copy-start | bytes 835588
  141.0 13.4 %collective-permute-start.27 = (s16[2,272,256]{2,1,0:T(8,128)(2,1)}, s16[2,272,256]{2,1,0:T(8,128)(2,1)S(1)}, u32[]{:S(2)}, u32[]{:S(2)}) collective-permute-start(s16[2,272,256]{2,1,0:T(8,128)(2,1)} %sum.3), channel_id=1, source_target_pairs={{0,4},{1,13},{2,22},{3,31},{4,32},{5,41},{6,50},{7,59},{8,12},{9,2... | collective-permute-start | bytes 835592 | tf_op jit(solution)/shard_map/ppermute | solution.py:24
  143.2 0.7 copy-start.13
  143.2 0.8 copy-start.15
  143.2 0.8 copy-start.16
  146.3 10.2 %collective-permute-start.23 = (s16[2,272,256]{2,1,0:T(8,128)(2,1)}, s16[2,272,256]{2,1,0:T(8,128)(2,1)S(1)}, u32[]{:S(2)}, u32[]{:S(2)}) collective-permute-start(s16[2,272,256]{2,1,0:T(8,128)(2,1)} %sum.2), channel_id=1, source_target_pairs={{0,4},{1,5},{2,6},{3,7},{4,0},{5,1},{6,2},{7,3},{8,12},{9,13},{10,... | collective-permute-start | bytes 835592 | tf_op jit(solution)/shard_map/ppermute | solution.py:24
  146.4 10.2 %collective-permute-start.17 = (s16[2,272,256]{2,1,0:T(8,128)(2,1)S(1)}, s16[2,272,256]{2,1,0:T(8,128)(2,1)S(1)}, u32[]{:S(2)}, u32[]{:S(2)}) collective-permute-start(s16[2,272,256]{2,1,0:T(8,128)(2,1)S(1)} %copy-done.27), channel_id=1, source_target_pairs={{0,1},{1,0},{2,3},{3,2},{4,5},{5,4},{6,7},{7,6},{8,9},{9,8},{10,11... | collective-permute-start | bytes 835592 | tf_op jit(solution)/shard_map/ppermute | solution.py:24
  146.4 14.3 %collective-permute-start.18 = (s16[2,272,256]{2,1,0:T(8,128)(2,1)S(1)}, s16[2,272,256]{2,1,0:T(8,128)(2,1)S(1)}, u32[]{:S(2)}, u32[]{:S(2)}) collective-permute-start(s16[2,272,256]{2,1,0:T(8,128)(2,1)S(1)} %copy-done.26), channel_id=1, source_target_pairs={{0,2},{1,3},{2,0},{3,1},{4,6},{5,7},{6,4},{7,5},{8,10},{9,11},{10,... | collective-permute-start | bytes 835592 | tf_op jit(solution)/shard_map/ppermute | solution.py:24
  147.8 15.4 %collective-permute-start.19 = (s16[2,272,256]{2,1,0:T(8,128)(2,1)S(1)}, s16[2,272,256]{2,1,0:T(8,128)(2,1)S(1)}, u32[]{:S(2)}, u32[]{:S(2)}) collective-permute-start(s16[2,272,256]{2,1,0:T(8,128)(2,1)S(1)} %copy-done.25), channel_id=1, source_target_pairs={{0,3},{1,2},{2,1},{3,0},{4,7},{5,6},{6,5},{7,4},{8,11},{9,10},{10,... | collective-permute-start | bytes 835592 | tf_op jit(solution)/shard_map/ppermute | solution.py:24
  154.4 8.8 %copy-start.17 = (s16[2,272,256]{2,1,0:T(8,128)(2,1)}, s16[2,272,256]{2,1,0:T(8,128)(2,1)S(1)}, u32[]{:S(2)}) copy-start(s16[2,272,256]{2,1,0:T(8,128)(2,1)S(1)} %collective-permute-done.27.refs_5_) | copy-start | bytes 835588
  156.5 6.7 %copy-start.18 = (s16[2,272,256]{2,1,0:T(8,128)(2,1)}, s16[2,272,256]{2,1,0:T(8,128)(2,1)S(1)}, u32[]{:S(2)}) copy-start(s16[2,272,256]{2,1,0:T(8,128)(2,1)S(1)} %collective-permute-done.23.refs_4_) | copy-start | bytes 835588
  156.5 6.7 %copy-start.19 = (s16[2,272,256]{2,1,0:T(8,128)(2,1)}, s16[2,272,256]{2,1,0:T(8,128)(2,1)S(1)}, u32[]{:S(2)}) copy-start(s16[2,272,256]{2,1,0:T(8,128)(2,1)S(1)} %collective-permute-done.17.refs_1_) | copy-start | bytes 835588
  160.6 2.6 %copy-start.20 = (s16[2,272,256]{2,1,0:T(8,128)(2,1)}, s16[2,272,256]{2,1,0:T(8,128)(2,1)S(1)}, u32[]{:S(2)}) copy-start(s16[2,272,256]{2,1,0:T(8,128)(2,1)S(1)} %collective-permute-done.18.refs_2_) | copy-start | bytes 835588
  163.2 0.7 copy-start.21
  167.2 36.3 %copy-start.9 = (f32[2,256,256]{2,1,0:T(8,128)S(1)}, f32[2,256,256]{2,1,0:T(8,128)}, u32[]{:S(2)}) copy-start(f32[2,256,256]{2,1,0:T(8,128)} %get-tuple-element.47.samples_ref) | copy-start | bytes 1572868
  167.2 36.2 %collective-permute-start.28 = (f32[256,256]{1,0:T(8,128)}, f32[256,256]{1,0:T(8,128)S(1)}, u32[]{:S(2)}, u32[]{:S(2)}) collective-permute-start(f32[256,256]{1,0:T(8,128)} %get-tuple-element.48.other_ref), channel_id=1, source_target_pairs={{0,4},{1,5},{2,6},{3,7},{4,0},{5,1},{6,2},{7,3},{8,12},{9,13},{10,... | collective-permute-start | bytes 786440 | tf_op jit(solution)/shard_map/ppermute | solution.py:24
  170.4 7.5 %collective-permute-start.29 = (f32[384,128]{1,0:T(8,128)}, f32[384,128]{1,0:T(8,128)S(1)}, u32[]{:S(2)}, u32[]{:S(2)}) collective-permute-start(f32[384,128]{1,0:T(8,128)} %get-tuple-element.49.refs_0_), channel_id=1, source_target_pairs={{0,1},{1,0},{2,3},{3,2},{4,5},{5,4},{6,7},{7,6},{8,9},{9,8},{10,11... | collective-permute-start | bytes 589832 | tf_op jit(solution)/shard_map/ppermute | solution.py:24
  170.4 11.5 %collective-permute-start.30 = (f32[384,128]{1,0:T(8,128)}, f32[384,128]{1,0:T(8,128)S(1)}, u32[]{:S(2)}, u32[]{:S(2)}) collective-permute-start(f32[384,128]{1,0:T(8,128)} %get-tuple-element.49.refs_0_), channel_id=1, source_target_pairs={{0,2},{1,3},{2,0},{3,1},{4,6},{5,7},{6,4},{7,5},{8,10},{9,11},{10,... | collective-permute-start | bytes 589832 | tf_op jit(solution)/shard_map/ppermute | solution.py:24
  174.8 9.2 %collective-permute-start.31 = (f32[384,128]{1,0:T(8,128)}, f32[384,128]{1,0:T(8,128)S(1)}, u32[]{:S(2)}, u32[]{:S(2)}) collective-permute-start(f32[384,128]{1,0:T(8,128)} %get-tuple-element.49.refs_0_), channel_id=1, source_target_pairs={{0,3},{1,2},{2,1},{3,0},{4,7},{5,6},{6,5},{7,4},{8,11},{9,10},{10,... | collective-permute-start | bytes 589832 | tf_op jit(solution)/shard_map/ppermute | solution.py:24
  177.9 6.1 %copy-start.22 = (f32[384,128]{1,0:T(8,128)}, f32[384,128]{1,0:T(8,128)S(1)}, u32[]{:S(2)}) copy-start(f32[384,128]{1,0:T(8,128)S(1)} %collective-permute-done.29.refs_1_) | copy-start | bytes 589828
  182.0 2.1 %copy-start.23 = (f32[384,128]{1,0:T(8,128)}, f32[384,128]{1,0:T(8,128)S(1)}, u32[]{:S(2)}) copy-start(f32[384,128]{1,0:T(8,128)S(1)} %collective-permute-done.30.refs_2_) | copy-start | bytes 589828
  184.1 0.7 copy-start.24
  202.9 6.8 %collective-permute-start.32 = (s16[272,256]{1,0:T(8,128)(2,1)}, s16[272,256]{1,0:T(8,128)(2,1)S(1)}, u32[]{:S(2)}, u32[]{:S(2)}) collective-permute-start(s16[272,256]{1,0:T(8,128)(2,1)} %get-tuple-element.51), channel_id=1, source_target_pairs={{0,4},{1,5},{2,6},{3,7},{4,0},{5,1},{6,2},{7,3},{8,12},{9,13},{10,... | collective-permute-start | bytes 417800 | tf_op jit(solution)/shard_map/ppermute | solution.py:24
  203.5 6.9 %copy-start.10 = (f32[2,256,256]{2,1,0:T(8,128)}, f32[2,256,256]{2,1,0:T(8,128)S(1)}, u32[]{:S(2)}) copy-start(f32[2,256,256]{2,1,0:T(8,128)S(1)} %bitcast_dynamic-update-slice_fusion) | copy-start | bytes 1572868
